TPU v7x, 32 devices: a whole 2x2x4 slice. The times are simulated.
32 devices in a mesh: row: 4 (over y, core), col: 8 (over z, x).
Axes of the slice: x: 2, y: 2, z: 4, core: 2. Of those that a mesh axis runs over, the one named last changes fastest.
Arguments:
- state: bfloat16 [128, 768, 128], P('row', 'col'), may hold values from -0.94921875 to 0.94921875
- grad: bfloat16 [128, 768, 128], P('row', 'col'), may hold values from -6 to 6
- kernel: bfloat16 [3, 3, 128, 128], replicated, may hold values from -0.1875 to 0.1875
- ray_matrix: bfloat16 [8, 4, 64, 1024], replicated, may hold values from -0.1875 to 0.1875
- ray_weight: float32 [256, 64, 128], P(('row', 'col')), may hold values from 0.2 to 2
- hits: int32 [4, 24, 16], replicated, may hold values from 0 to 255, as said below
- offsets: int32 [4, 24, 16], P('row', 'col'), may hold values from 0 to 3
- block_slot: int32 [256], replicated, may hold values from 0 to 255, as said below
- angle_count: int32 [8], replicated, may hold values from 16 to 32
Outputs:
- adjoint: float32 [128, 768, 128], P('row', 'col')
Inputs may be any that keep to these rules, and one draw needn't show every extreme that they name: `hits`: of the listed pairs of the tiles of one device, at most 3 name blocks whose owner slots lie in one device's range [d * 8, (d + 1) * 8), and exactly 3 do so for some owner d of each device. Devices are numbered row * 8 + col, in the order of the mesh, row first. `block_slot`: A permutation of the ray blocks' slots.
All inputs are finite; a program needn't handle non-finite values.
Results may differ from a plain program's by a relative error of at most 0.0049.
Values may be sent and summed in bfloat16 or wider, within the bound.
No kernel may reach another device: no remote copies, remote signals or barrier semaphores. Data moves between devices by JAX's collectives and lax.ppermute only.
A program may use at most 128 MiB of HBM per device.

v0:
```python
import jax
import jax.numpy as jnp
from jax import lax
from jax.sharding import PartitionSpec as P

PIX = 32
ANGLES = 8
HITS = 16
ITERS = 2


relax_rate = 0.25


def with_halo(block, sides, width):
    for axis, dim in sides:
        count = lax.axis_size(axis)
        forward = [(i, i + 1) for i in range(count - 1)]
        backward = [(target, source) for source, target in forward]
        low = lax.ppermute(
            lax.slice_in_dim(block, block.shape[dim] - width, None, axis=dim), axis, forward
        )
        high = lax.ppermute(lax.slice_in_dim(block, 0, width, axis=dim), axis, backward)
        block = jnp.concatenate([low, block, high], axis=dim)
    return block


def conv_pull(padded, kernel, rows_dev, cols_dev, chans):
    total = jnp.zeros((rows_dev * cols_dev, chans), jnp.float32)
    for shift_row in range(3):
        for shift_col in range(3):
            window = padded[
                2 - shift_row : 2 - shift_row + rows_dev, 2 - shift_col : 2 - shift_col + cols_dev
            ]
            total = total + jnp.dot(
                window.reshape(rows_dev * cols_dev, chans),
                kernel[shift_row, shift_col].T,
                preferred_element_type=jnp.float32,
            )
    return total.reshape(rows_dev, cols_dev, chans)


def on_device(state, grad, kernel, ray_matrix, ray_weight, hits, offsets, block_slot, angle_count):
    rows_dev, cols_dev, chans = state.shape
    bins = ray_matrix.shape[2]
    tile_pix = ray_matrix.shape[3]
    row_count = lax.axis_size("row")
    col_count = lax.axis_size("col")
    device_count = row_count * col_count
    myself = lax.axis_index("row") * col_count + lax.axis_index("col")
    tile_rows = rows_dev // PIX
    tile_cols = cols_dev // PIX
    tile_count = tile_rows * tile_cols
    pair_count = tile_count * HITS
    blk_dev = ray_weight.shape[0]
    block_total = blk_dev * device_count
    blk_ang = block_total // ANGLES
    capacity = max(2, (pair_count + device_count - 2) // device_count + 1)
    width = bins * chans
    everyone = hits.reshape(row_count, tile_rows, col_count, tile_cols, HITS)
    everyone = everyone.transpose(0, 2, 1, 3, 4).reshape(device_count, pair_count)
    storage = block_slot[everyone]
    target = storage // blk_dev
    local_slot = storage % blk_dev
    earlier = jnp.arange(pair_count)[None, :] < jnp.arange(pair_count)[:, None]
    ranking = jnp.sum(
        ((target[:, :, None] == target[:, None, :]) & earlier[None]).astype(jnp.int32), axis=2
    )
    my_hits = lax.dynamic_index_in_dim(everyone, myself, 0, keepdims=False)
    my_target = lax.dynamic_index_in_dim(target, myself, 0, keepdims=False)
    my_rank = lax.dynamic_index_in_dim(ranking, myself, 0, keepdims=False)
    slot_of = my_target * capacity + my_rank
    fill_table = slot_of[None, :] == jnp.arange(device_count * capacity, dtype=jnp.int32)[:, None]
    source = jnp.sum(
        fill_table.astype(jnp.int32) * jnp.arange(pair_count, dtype=jnp.int32)[None, :], axis=1
    )
    filled = jnp.any(fill_table, axis=1).astype(jnp.float32)
    matched = (target[:, None, :] == myself) & (
        ranking[:, None, :] == jnp.arange(capacity, dtype=jnp.int32)[None, :, None]
    )
    recv_local = jnp.sum(matched.astype(jnp.int32) * local_slot[:, None, :], axis=2)
    recv_local = recv_local + blk_dev * (1 - jnp.any(matched, axis=2).astype(jnp.int32))
    recv_local = recv_local.reshape(device_count * capacity)
    collect = (jnp.arange(blk_dev, dtype=jnp.int32)[:, None] == recv_local[None, :]).astype(
        jnp.float32
    )
    own_place = myself * blk_dev + jnp.arange(blk_dev, dtype=jnp.int32)
    owner_hit = (block_slot[None, :] == own_place[:, None]).astype(jnp.int32)
    own_block = jnp.sum(owner_hit * jnp.arange(block_total, dtype=jnp.int32)[None, :], axis=1)
    inuse = (own_block % blk_ang < angle_count[own_block // blk_ang]).astype(jnp.float32)
    scaling = (inuse[:, None, None] * ray_weight).reshape(blk_dev, width)
    offset_flat = offsets.reshape(tile_count, HITS)
    matrices = ray_matrix[my_hits.reshape(tile_count, HITS) // blk_ang, offset_flat]
    matrices = matrices.reshape(tile_count, HITS * bins, tile_pix)
    derivative = 1.0 - jnp.square(state.astype(jnp.float32))
    cotangent = grad.astype(jnp.float32)
    adjoint = cotangent
    for turn in range(ITERS):
        scaled = (derivative * adjoint).astype(jnp.bfloat16)
        padded = with_halo(scaled, (("row", 0), ("col", 1)), 1)
        pulled = conv_pull(padded, kernel, rows_dev, cols_dev, chans)
        pulled_low = pulled.astype(jnp.bfloat16)
        pulled_tiles = pulled_low.reshape(tile_rows, PIX, tile_cols, PIX, chans)
        pulled_tiles = pulled_tiles.transpose(0, 2, 1, 3, 4).reshape(tile_count, tile_pix, chans)
        partial_value = jnp.einsum(
            "tkp,tpc->tkc", matrices, pulled_tiles, preferred_element_type=jnp.float32
        )
        partial_value = partial_value.reshape(pair_count, width)
        outgoing = partial_value[source] * filled[:, None]
        incoming = lax.all_to_all(outgoing, ("row", "col"), split_axis=0, concat_axis=0, tiled=True)
        sinogram = jnp.dot(
            collect, incoming, precision=lax.Precision.HIGHEST, preferred_element_type=jnp.float32
        )
        weighted = (scaling * sinogram).astype(jnp.bfloat16)
        extended = jnp.concatenate([weighted, jnp.zeros((1, width), jnp.bfloat16)], axis=0)
        replies = extended[recv_local]
        returned = lax.all_to_all(replies, ("row", "col"), split_axis=0, concat_axis=0, tiled=True)
        per_pair = returned[slot_of].reshape(tile_count, HITS * bins, chans)
        backed = jnp.einsum("tkp,tkc->tpc", matrices, per_pair, preferred_element_type=jnp.float32)
        backed = backed.reshape(tile_rows, tile_cols, PIX, PIX, chans).transpose(0, 2, 1, 3, 4)
        backed = backed.reshape(rows_dev, cols_dev, chans)
        adjoint = cotangent + (pulled - relax_rate * backed)
    return adjoint


def solution(mesh):
    placed = (
        P("row", "col", None),
        P("row", "col", None),
        P(),
        P(),
        P(("row", "col"), None, None),
        P(),
        P("row", "col", None),
        P(),
        P(),
    )
    return jax.shard_map(
        on_device, mesh=mesh, in_specs=placed, out_specs=P("row", "col", None), check_vma=False
    )
```

profile of v0, /device:TPU:0, one launch (start us, length us, event | category | flops | bytes accessed | tf_op | source)
XLA Modules:
  0.0 443.8 jit_solution(7397985115216791992)
XLA Ops:
  0.0 1.7 fusion.4
  3.0 3.0 collective-permute-start
  6.5 9.5 %gather_fusion.2 = s32[1536]{0:T(1024)S(1)} fusion(s32[256]{0:T(256)S(1)} %copy-done.2, s32[2048]{0:T(1024)S(1)} %pad_clamp_fusion), kind=kCustom, calls=%fused_computation.2 | custom fusion | bytes 18432 | tf_op jit(solution)/shard_map/gather | solution.py:62
  17.5 7.5 %gather_fusion = bf16[48,64,1024]{2,1,0:T(8,128)(2,1)} fusion(bf16[8,4,64,1024]{3,2,1,0:T(8,128)(2,1)} %param.12, s32[48]{0:T(128)S(1)} %reshape.570), kind=kCustom, calls=%fused_computation | custom fusion | bytes 12583296 | tf_op jit(solution)/shard_map/gather | solution.py:93
  26.4 5.5 %collective-permute-start.3 = (bf16[34,1,128]{2,1,0:T(2,128)(2,1)S(1)}, bf16[34,1,128]{2,1,0:T(2,128)(2,1)S(1)}, u32[]{:S(2)}, u32[]{:S(2)}) collective-permute-start(bf16[34,1,128]{2,1,0:T(2,128)(2,1)S(1)} %get-tuple-element.28), channel_id=1, source_target_pairs={{0,1},{1,2},{2,3},{3,4},{4,5},{5,6},{6,7},{8,9},{9,10},{10,11},{11... | collective-permute-start | bytes 26120 | tf_op jit(solution)/shard_map/ppermute | solution.py:20
  40.2 1.8 fusion.78
  42.3 3.2 gather_fusion.3
  45.5 5.0 %gather.35 = f32[32,3,8192]{2,1,0:T(4,128)} reshape(f32[96,8192]{1,0:T(8,128)} %gather_fusion.3) | data formatting | bytes 6291456 | tf_op jit(solution)/shard_map/gather | solution.py:109
  50.5 5.5 %broadcast_multiply_fusion.1 = f32[32,3,8192]{2,1,0:T(4,128)} fusion(f32[32,3,8192]{2,1,0:T(4,128)} %gather.35, f32[32,3]{1,0:T(8,128)S(1)} %reshape.569), kind=kLoop, calls=%fused_computation.33 | loop fusion | flops 786432 | bytes 6291840 | tf_op jit(solution)/shard_map/mul | solution.py:109
  56.0 8.3 %all-to-all-start = ((f32[32,3,8192]{2,1,0:T(4,128)}), f32[32,3,8192]{2,1,0:T(4,128)}, u32[]{:S(2)}, u32[]{:S(2)}) async-start(f32[32,3,8192]{2,1,0:T(4,128)} %broadcast_multiply_fusion.1), calls=%async_computation | async-start | bytes 8388608 | tf_op jit(solution)/shard_map/all_to_all | solution.py:110
  66.0 93.2 %all-to-all-done = f32[32,3,8192]{2,1,0:T(4,128)} async-done(((f32[32,3,8192]{2,1,0:T(4,128)}), f32[32,3,8192]{2,1,0:T(4,128)}, u32[]{:S(2)}, u32[]{:S(2)}) %all-to-all-start) | async-done | bytes 3145760 | tf_op jit(solution)/shard_map/all_to_all | solution.py:110
  159.2 3.7 all_to_all.29
  164.1 1.5 gather_fusion.4
  165.7 2.4 all_to_all.30
  168.1 3.5 all-to-all-start.1
  171.6 49.9 %all-to-all-done.1 = bf16[32,3,8192]{2,1,0:T(4,128)(2,1)} async-done(((bf16[32,3,8192]{2,1,0:T(4,128)(2,1)}), bf16[32,3,8192]{2,1,0:T(4,128)(2,1)}, u32[]{:S(2)}, u32[]{:S(2)}) %all-to-all-start.1) | async-done | bytes 1572896 | tf_op jit(solution)/shard_map/all_to_all | solution.py:117
  221.5 3.2 all_to_all.32
  226.0 5.1 %convolution_multiply_fusion.3 = f32[3,1024,128]{2,1,0:T(8,128)S(1)} fusion(bf16[3,1024,1024]{2,1,0:T(8,128)(2,1)} %bitcast.147, bf16[3,1024,128]{2,1,0:T(8,128)(2,1)S(1)} %reshape.555), kind=kOutput, calls=%fused_computation.39 | convolution fusion | flops 805699584 | bytes 8650752 | tf_op jit(solution)/shard_map/tkp,tkc->tpc/dot_general | solution.py:119
  234.8 3.2 collective-permute-start.4
  240.1 4.8 %collective-permute-start.7 = (bf16[34,1,128]{2,1,0:T(2,128)(2,1)S(1)}, bf16[34,1,128]{2,1,0:T(2,128)(2,1)S(1)}, u32[]{:S(2)}, u32[]{:S(2)}) collective-permute-start(bf16[34,1,128]{2,1,0:T(2,128)(2,1)S(1)} %get-tuple-element.24), channel_id=1, source_target_pairs={{0,1},{1,2},{2,3},{3,4},{4,5},{5,6},{6,7},{8,9},{9,10},{10,11},{11... | collective-permute-start | bytes 26120 | tf_op jit(solution)/shard_map/ppermute | solution.py:20
  249.9 1.5 fusion.77
  253.1 1.8 fusion.79
  255.1 3.2 gather_fusion.6
  258.4 5.0 %gather.39 = f32[32,3,8192]{2,1,0:T(4,128)} reshape(f32[96,8192]{1,0:T(8,128)} %gather_fusion.6) | data formatting | bytes 6291456 | tf_op jit(solution)/shard_map/gather | solution.py:109
  263.3 3.2 broadcast_multiply_fusion
  266.5 101.7 %all_to_all.42 = f32[32,3,8192]{2,1,0:T(4,128)} all-to-all(f32[32,3,8192]{2,1,0:T(4,128)S(1)} %broadcast_multiply_fusion), channel_id=1, replica_groups=mesh['row'=4,'col'=8] {'row','col'}, dimensions={0} | all-to-all | bytes 6291456 | tf_op jit(solution)/shard_map/all_to_all | solution.py:110
  368.2 3.7 all_to_all.34
  373.2 2.7 gather_fusion.7
  375.8 2.7 all_to_all.35
  378.6 52.4 %all_to_all.43 = bf16[32,3,8192]{2,1,0:T(4,128)(2,1)} all-to-all(bf16[32,3,8192]{2,1,0:T(4,128)(2,1)S(1)} %all_to_all.35), channel_id=1, replica_groups=mesh['row'=4,'col'=8] {'row','col'}, dimensions={0} | all-to-all | bytes 3145728 | tf_op jit(solution)/shard_map/all_to_all | solution.py:117
  430.9 3.2 all_to_all.37
  435.5 5.1 %convolution_multiply_fusion.2 = f32[3,1024,128]{2,1,0:T(8,128)S(1)} fusion(bf16[3,1024,1024]{2,1,0:T(8,128)(2,1)} %bitcast.148, bf16[3,1024,128]{2,1,0:T(8,128)(2,1)S(1)} %reshape.568), kind=kOutput, calls=%fused_computation.38 | convolution fusion | flops 805699584 | bytes 8650752 | tf_op jit(solution)/shard_map/tkp,tkc->tpc/dot_general | solution.py:119
  (130 shorter events, 35.5 us)
Async XLA Ops:
  0.0 65.2 %copy-start = (s32[8]{0:T(128)S(1)}, s32[8]{0:T(128)}, u32[]{:S(2)}) copy-start(s32[8]{0:T(128)} %param.17) | copy-start | bytes 100
  0.0 6.1 %copy-start.11 = (s32[4,24,16]{1,2,0:T(8,128)S(1)}, s32[4,24,16]{1,2,0:T(8,128)}, u32[]{:S(2)}) copy-start(s32[4,24,16]{1,2,0:T(8,128)} %param.14) | copy-start | bytes 18436
  0.0 6.4 %copy-start.2 = (s32[256]{0:T(256)S(1)}, s32[256]{0:T(256)}, u32[]{:S(2)}) copy-start(s32[256]{0:T(256)} %param.16) | copy-start | bytes 3076
  1.7 23.2 %collective-permute-start.1 = (bf16[1,96,128]{2,1,0:T(8,128)(2,1)S(1)}, bf16[1,96,128]{2,1,0:T(8,128)(2,1)S(1)}, u32[]{:S(2)}, u32[]{:S(2)}) collective-permute-start(bf16[1,96,128]{2,1,0:T(8,128)(2,1)S(1)} %get-tuple-element.36), channel_id=1, source_target_pairs={{8,0},{16,8},{24,16},{9,1},{17,9},{25,17},{10,2},{18,10},{26,18},{... | collective-permute-start | bytes 73736 | tf_op jit(solution)/shard_map/ppermute | solution.py:23
  3.0 21.9 %collective-permute-start = (bf16[1,96,128]{2,1,0:T(8,128)(2,1)S(1)}, bf16[1,96,128]{2,1,0:T(8,128)(2,1)S(1)}, u32[]{:S(2)}, u32[]{:S(2)}) collective-permute-start(bf16[1,96,128]{2,1,0:T(8,128)(2,1)S(1)} %get-tuple-element.35), channel_id=1, source_target_pairs={{0,8},{8,16},{16,24},{1,9},{9,17},{17,25},{2,10},{10,18},{18,26},{... | collective-permute-start | bytes 73736 | tf_op jit(solution)/shard_map/ppermute | solution.py:20
  6.5 10.8 %copy-start.12 = (s32[1,3,16]{2,0,1:T(1,128)S(1)}, s32[1,3,16]{2,0,1:T(1,128)}, u32[]{:S(2)}) copy-start(s32[1,3,16]{2,0,1:T(1,128)} %param.15) | copy-start | bytes 580
  24.9 7.1 %copy-start.8 = (bf16[3,3,128,128]{3,2,1,0:T(8,128)(2,1)S(1)}, bf16[3,3,128,128]{3,2,1,0:T(8,128)(2,1)}, u32[]{:S(2)}) copy-start(bf16[3,3,128,128]{3,2,1,0:T(8,128)(2,1)} %param.11) | copy-start | bytes 884740
  25.0 7.4 %collective-permute-start.2 = (bf16[34,1,128]{2,1,0:T(2,128)(2,1)S(1)}, bf16[34,1,128]{2,1,0:T(2,128)(2,1)S(1)}, u32[]{:S(2)}, u32[]{:S(2)}) collective-permute-start(bf16[34,1,128]{2,1,0:T(2,128)(2,1)S(1)} %get-tuple-element.27), channel_id=1, source_target_pairs={{1,0},{2,1},{3,2},{4,3},{5,4},{6,5},{7,6},{9,8},{10,9},{11,10},{12... | collective-permute-start | bytes 26120 | tf_op jit(solution)/shard_map/ppermute | solution.py:23
  26.4 6.9 %collective-permute-start.3 = (bf16[34,1,128]{2,1,0:T(2,128)(2,1)S(1)}, bf16[34,1,128]{2,1,0:T(2,128)(2,1)S(1)}, u32[]{:S(2)}, u32[]{:S(2)}) collective-permute-start(bf16[34,1,128]{2,1,0:T(2,128)(2,1)S(1)} %get-tuple-element.28), channel_id=1, source_target_pairs={{0,1},{1,2},{2,3},{3,4},{4,5},{5,6},{6,7},{8,9},{9,10},{10,11},{11... | collective-permute-start | bytes 26120 | tf_op jit(solution)/shard_map/ppermute | solution.py:20
  36.7 2.8 slice-start
  37.1 3.1 slice-start.1
  56.0 9.9 %copy-start.10 = (f32[8,64,128]{2,1,0:T(8,128)S(1)}, f32[8,64,128]{2,1,0:T(8,128)}, u32[]{:S(2)}) copy-start(f32[8,64,128]{2,1,0:T(8,128)} %param.13) | copy-start | bytes 786436
  56.0 103.2 %all-to-all-start = ((f32[32,3,8192]{2,1,0:T(4,128)}), f32[32,3,8192]{2,1,0:T(4,128)}, u32[]{:S(2)}, u32[]{:S(2)}) async-start(f32[32,3,8192]{2,1,0:T(4,128)} %broadcast_multiply_fusion.1), calls=%async_computation | async-start | bytes 8388608 | tf_op jit(solution)/shard_map/all_to_all | solution.py:110
  168.1 53.4 %all-to-all-start.1 = ((bf16[32,3,8192]{2,1,0:T(4,128)(2,1)}), bf16[32,3,8192]{2,1,0:T(4,128)(2,1)}, u32[]{:S(2)}, u32[]{:S(2)}) async-start(bf16[32,3,8192]{2,1,0:T(4,128)(2,1)} %all_to_all.30), calls=%async_computation.1 | async-start | bytes 4194304 | tf_op jit(solution)/shard_map/all_to_all | solution.py:117
  231.2 1.1 copy-start.3
  231.2 1.6 copy-start.5
  231.2 1.8 copy-start.7
  233.5 4.5 %collective-permute-start.5 = (bf16[1,96,128]{2,1,0:T(8,128)(2,1)S(1)}, bf16[1,96,128]{2,1,0:T(8,128)(2,1)S(1)}, u32[]{:S(2)}, u32[]{:S(2)}) collective-permute-start(bf16[1,96,128]{2,1,0:T(8,128)(2,1)S(1)} %get-tuple-element.32), channel_id=1, source_target_pairs={{8,0},{16,8},{24,16},{9,1},{17,9},{25,17},{10,2},{18,10},{26,18},{... | collective-permute-start | bytes 73736 | tf_op jit(solution)/shard_map/ppermute | solution.py:23
  234.8 10.2 %copy-start.9 = (bf16[3,3,128,128]{3,2,1,0:T(8,128)(2,1)S(1)}, bf16[3,3,128,128]{3,2,1,0:T(8,128)(2,1)}, u32[]{:S(2)}) copy-start(bf16[3,3,128,128]{3,2,1,0:T(8,128)(2,1)} %param.11) | copy-start | bytes 884740
  234.8 4.0 collective-permute-start.4
  238.8 6.6 %collective-permute-start.6 = (bf16[34,1,128]{2,1,0:T(2,128)(2,1)S(1)}, bf16[34,1,128]{2,1,0:T(2,128)(2,1)S(1)}, u32[]{:S(2)}, u32[]{:S(2)}) collective-permute-start(bf16[34,1,128]{2,1,0:T(2,128)(2,1)S(1)} %get-tuple-element.23), channel_id=1, source_target_pairs={{1,0},{2,1},{3,2},{4,3},{5,4},{6,5},{7,6},{9,8},{10,9},{11,10},{12... | collective-permute-start | bytes 26120 | tf_op jit(solution)/shard_map/ppermute | solution.py:23
  240.1 6.0 %collective-permute-start.7 = (bf16[34,1,128]{2,1,0:T(2,128)(2,1)S(1)}, bf16[34,1,128]{2,1,0:T(2,128)(2,1)S(1)}, u32[]{:S(2)}, u32[]{:S(2)}) collective-permute-start(bf16[34,1,128]{2,1,0:T(2,128)(2,1)S(1)} %get-tuple-element.24), channel_id=1, source_target_pairs={{0,1},{1,2},{2,3},{3,4},{4,5},{5,6},{6,7},{8,9},{9,10},{10,11},{11... | collective-permute-start | bytes 26120 | tf_op jit(solution)/shard_map/ppermute | solution.py:20
  249.5 2.8 slice-start.2
  249.9 3.1 slice-start.3
  440.6 1.1 copy-start.4
  440.6 1.6 copy-start.6
  440.8 3.0 copy-start.1
where the time goes:
time: 445 us; the launch traced here: 444 us
  blocking collectives  154 us (35%)
  waiting for transfers between devices  146 us (33%)
  local copies, waits for them, and re-layouts  69.3 us (16%)
  starting transfers between devices  33.6 us (8%)
  matrix products  25.1 us (6%)
  other arithmetic  15.4 us (3%)
    all_to_all x1, blocking collectives, on_device(): lax.all_to_all(outgoing, ('row', 'col'), split_axis=0, concat_axis=0, til...  102 us
    all_to_all x1, waiting for transfers between devices, on_device(): lax.all_to_all(outgoing, ('row', 'col'), split_axis=0, concat_axis=0, til...  93.2 us
    all_to_all x1, blocking collectives, on_device(): lax.all_to_all(replies, ('row', 'col'), split_axis=0, concat_axis=0, tile...  52.4 us
    all_to_all x1, waiting for transfers between devices, on_device(): lax.all_to_all(replies, ('row', 'col'), split_axis=0, concat_axis=0, tile...  49.9 us
    ppermute x4, starting transfers between devices, with_halo(): lax.ppermute(lax.slice_in_dim(block, block.shape[dim] - width, None, axis...  16.5 us
    gather x4, local copies, waits for them, and re-layouts, on_device(): outgoing = partial_value[source] * filled[:, None]  16.3 us
    all_to_all x4, local copies, waits for them, and re-layouts, on_device(): lax.all_to_all(replies, ('row', 'col'), split_axis=0, concat_axis=0, tile...  11.4 us
    dot_general x2, matrix products, on_device(): jnp.einsum('tkp,tkc->tpc', matrices, per_pair, preferred_element_type=jnp...  10.2 us
  transfers between devices with their start and end apart: 10, of which 5 were waited for; matrix products, arithmetic and copies ran while one was open for 5% of the time, Pallas kernels for 0%

commit v1 on v0

v1 whole, which is shorter than its diff:
```python
import functools

import jax
import jax.numpy as jnp
from jax import lax
from jax.experimental import pallas as pl
from jax.experimental.pallas import tpu as pltpu
from jax.sharding import Mesh, PartitionSpec as P

PIX = 32
ANGLES = 8
HITS = 16
ITERS = 2
RING = 4

relax_rate = 0.25

COL = ("zh", "zl", "x")
GROUP = ("row", "zl", "x")


def fetch_matrices(mat_idx, ray_ref, held, sems, pairs):
    def body(q, carry):
        pltpu.make_async_copy(ray_ref.at[mat_idx[q]], held.at[q], sems.at[q]).start()
        return carry

    lax.fori_loop(0, pairs, body, 0)


def await_matrices(mat_idx, ray_ref, held, sems, first, count):
    for k in range(count):
        q = first + k
        pltpu.make_async_copy(ray_ref.at[mat_idx[q]], held.at[q], sems.at[q]).wait()


def project_kernel(
    mat_idx, send_slot, scaled, above, below, left, right, taps, ray_ref,
    pulled_out, out, held, sems, wide, cols3, *, tiles, hits, tile_cols,
):
    t = pl.program_id(0)
    rows, cols, chans = scaled.shape
    bins, tile_pix = held.shape[1:]

    @pl.when(t == 0)
    def _():
        fetch_matrices(mat_idx, ray_ref, held, sems, tiles * hits)
        f32 = jnp.float32
        wide[0, 8 : 8 + cols, :] = above[...].astype(f32)
        wide[rows + 1, 8 : 8 + cols, :] = below[...].astype(f32)
        wide[1 : rows + 1, 8 : 8 + cols, :] = scaled[...].astype(f32)
        lefts = left[...].astype(f32)
        rights = right[...].astype(f32)
        for r in range(rows + 2):
            wide[r, 7:8, :] = lefts[r : r + 1, :]
            wide[r, 8 + cols : 9 + cols, :] = rights[r : r + 1, :]
        for dc in range(3):
            cols3[:, :, dc * chans : (dc + 1) * chans] = wide[:, 7 + dc : 7 + dc + cols, :].astype(
                jnp.bfloat16
            )
        out[...] = jnp.zeros_like(out)

    r0 = (t // tile_cols) * PIX
    c0 = pl.multiple_of((t % tile_cols) * PIX, PIX)
    acc = None
    for dr in range(3):
        window = cols3[pl.ds(r0 + dr, PIX), pl.ds(c0, PIX), :].reshape(tile_pix, 3 * chans)
        term = jnp.dot(window, taps[dr], preferred_element_type=jnp.float32)
        acc = term if acc is None else acc + term
    pulled_out[0] = acc
    low = acc.astype(jnp.bfloat16)
    first = t * hits
    await_matrices(mat_idx, ray_ref, held, sems, first, hits)
    matrix = held[pl.ds(first, hits)].reshape(hits * bins, tile_pix)
    part = jnp.dot(matrix, low, preferred_element_type=jnp.float32).astype(jnp.bfloat16)
    for k in range(hits):
        out[send_slot[first + k]] = part[k * bins : (k + 1) * bins, :]


def combine_kernel(table, recv, total, low, acc):
    acc[...] = jnp.zeros_like(acc)

    def body(j, carry):
        acc[table[j]] += recv[j].astype(jnp.float32)
        return carry

    lax.fori_loop(0, recv.shape[0], body, 0, unroll=8)
    total[...] = acc[: total.shape[0]]
    low[...] = acc[: total.shape[0]].astype(jnp.bfloat16)


def reply_kernel(table, total, other, scaling, out, held):
    n = total.shape[0]
    held[:n] = (scaling[...] * (total[...] + other[...].astype(jnp.float32))).astype(jnp.bfloat16)
    held[n] = jnp.zeros(held.shape[1:], jnp.bfloat16)

    def body(j, carry):
        out[j] = held[table[j]]
        return carry

    lax.fori_loop(0, out.shape[0], body, 0, unroll=8)


def back_kernel(
    mat_idx, send_slot, returned, pulled, grad, state, ray_ref, out, held, sems, picked,
    *, tiles, hits, last,
):
    t = pl.program_id(0)
    bins, tile_pix = held.shape[1:]
    chans = returned.shape[2]

    @pl.when(t == 0)
    def _():
        fetch_matrices(mat_idx, ray_ref, held, sems, tiles * hits)

    first = t * hits
    for k in range(hits):
        picked[k * bins : (k + 1) * bins, :] = returned[send_slot[first + k]]
    await_matrices(mat_idx, ray_ref, held, sems, first, hits)
    matrix = held[pl.ds(first, hits)].reshape(hits * bins, tile_pix)
    backed = lax.dot_general(
        matrix, picked[...], (((0,), (0,)), ((), ())), preferred_element_type=jnp.float32
    )
    change = (pulled[0] - relax_rate * backed).reshape(PIX, PIX, chans)
    adjoint = grad[...].astype(jnp.float32) + change
    if last:
        out[...] = adjoint
    else:
        value = state[...].astype(jnp.float32)
        out[...] = ((1.0 - value * value) * adjoint).astype(jnp.bfloat16)


def halo_of(scaled):
    rows, cols, chans = scaled.shape
    nr = lax.axis_size("row")
    nc = lax.axis_size(COL)
    up = [(i, i + 1) for i in range(nr - 1)]
    down = [(b, a) for a, b in up]
    right = [(i, i + 1) for i in range(nc - 1)]
    left = [(b, a) for a, b in right]
    above = lax.ppermute(scaled[rows - 1], "row", up)
    below = lax.ppermute(scaled[0], "row", down)
    last = jnp.concatenate([above[cols - 1 :], scaled[:, cols - 1], below[cols - 1 :]], axis=0)
    first = jnp.concatenate([above[:1], scaled[:, 0], below[:1]], axis=0)
    lefts = lax.ppermute(last, COL, right)
    rights = lax.ppermute(first, COL, left)
    return above, below, lefts, rights


def on_device(state, grad, kernel, ray_matrix, ray_weight, hits, offsets, block_slot, angle_count):
    f32, bf16, i32 = jnp.float32, jnp.bfloat16, jnp.int32
    rows_dev, cols_dev, chans = state.shape
    angles, spots, bins, tile_pix = ray_matrix.shape
    nr = lax.axis_size("row")
    nx = lax.axis_size("x")
    nc = lax.axis_size(COL)
    devices = nr * nc
    row, zh, zl, x = (lax.axis_index(a) for a in ("row",) + COL)
    tile_rows = rows_dev // PIX
    tile_cols = cols_dev // PIX
    tiles = tile_rows * tile_cols
    pairs = tiles * HITS
    blk_dev = ray_weight.shape[0]
    blocks = blk_dev * devices
    blk_ang = blocks // ANGLES
    cap = 2 * max(2, (pairs + devices - 2) // devices + 1)
    cap = min(cap, pairs)
    peers = nr * 2 * nx
    slots = peers * cap
    dense = 2 * blk_dev

    scaled = (
        (1.0 - jnp.square(state.astype(f32))) * grad.astype(f32)
    ).astype(bf16)
    halo = halo_of(scaled)

    everyone = hits.reshape(nr, tile_rows, nc, tile_cols, HITS).transpose(0, 2, 1, 3, 4)
    everyone = everyone.reshape(nr, 2, 2, nx, pairs)
    group = lax.dynamic_index_in_dim(everyone, zh, 1, keepdims=False).reshape(peers, pairs)
    storage = jnp.sum(
        jnp.where(group[:, :, None] == jnp.arange(blocks, dtype=i32), block_slot, 0), axis=2
    )
    owner = storage // blk_dev
    local = storage % blk_dev
    owner_z = (owner % nc) // nx
    owner_zh = owner_z // 2
    owner_zl = owner_z % 2
    side = jnp.where(owner_zh == zh, owner_zl, 1 - owner_zl)
    peer = ((owner // nc) * 2 + side) * nx + owner % nx
    place = owner_zh * blk_dev + local
    earlier = jnp.arange(pairs)[None, :] < jnp.arange(pairs)[:, None]
    ranking = jnp.sum(
        ((peer[:, :, None] == peer[:, None, :]) & earlier[None]).astype(i32), axis=2
    )
    me = (row * 2 + zl) * nx + x
    my_hits = lax.dynamic_index_in_dim(group, me, 0, keepdims=False)
    send_slot = lax.dynamic_index_in_dim(peer * cap + ranking, me, 0, keepdims=False)
    matched = (peer[:, None, :] == me) & (
        ranking[:, None, :] == jnp.arange(cap, dtype=i32)[None, :, None]
    )
    table = dense + jnp.sum(jnp.where(matched, place[:, None, :] - dense, 0), axis=2)
    table = table.reshape(slots)
    mat_idx = (my_hits // blk_ang) * spots + offsets.reshape(pairs)

    own_place = (row * nc + (zh * 2 + zl) * nx + x) * blk_dev + jnp.arange(blk_dev, dtype=i32)
    number = jnp.arange(blocks, dtype=i32)
    used = (
        (number % blk_ang).reshape(ANGLES, blk_ang) < angle_count[:, None]
    ).reshape(1, blocks)
    inuse = jnp.any((block_slot[None, :] == own_place[:, None]) & used, axis=1).astype(f32)
    own_scale = inuse[:, None, None] * ray_weight
    swap = [(z, RING - 1 - z) for z in range(RING)]

    def exchange(value):
        return lax.ppermute(value, ("zh", "zl"), swap)

    other_scale = exchange(own_scale)
    scaling = jnp.concatenate(
        [jnp.where(zh == 0, own_scale, other_scale), jnp.where(zh == 0, other_scale, own_scale)]
    )
    taps = kernel[::-1, ::-1].transpose(0, 1, 3, 2).reshape(3, 3 * chans, chans)
    rays = ray_matrix.reshape(angles * spots, bins, tile_pix)

    whole = lambda shape: pl.BlockSpec(shape, lambda t, *_: (0,) * len(shape))
    hbm = pl.BlockSpec(memory_space=pl.ANY)
    by_tile = pl.BlockSpec((PIX, PIX, chans), lambda t, *_: (t // tile_cols, t % tile_cols, 0))
    by_index = pl.BlockSpec((1, tile_pix, chans), lambda t, *_: (t, 0, 0))
    matrices = [
        pltpu.VMEM((pairs, bins, tile_pix), bf16),
        pltpu.SemaphoreType.DMA((pairs,)),
    ]
    block = (bins, chans)

    project = pl.pallas_call(
        functools.partial(project_kernel, tiles=tiles, hits=HITS, tile_cols=tile_cols),
        out_shape=(
            jax.ShapeDtypeStruct((tiles, tile_pix, chans), f32),
            jax.ShapeDtypeStruct((slots,) + block, bf16),
        ),
        grid_spec=pltpu.PrefetchScalarGridSpec(
            num_scalar_prefetch=2,
            grid=(tiles,),
            in_specs=[
                whole((rows_dev, cols_dev, chans)),
                whole((cols_dev, chans)),
                whole((cols_dev, chans)),
                whole((rows_dev + 2, chans)),
                whole((rows_dev + 2, chans)),
                whole((3, 3 * chans, chans)),
                hbm,
            ],
            out_specs=(by_index, whole((slots,) + block)),
            scratch_shapes=matrices
            + [
                pltpu.VMEM((rows_dev + 2, cols_dev + 16, chans), f32),
                pltpu.VMEM((rows_dev + 2, cols_dev, 3 * chans), bf16),
            ],
        ),
        name="project",
    )
    combine = pl.pallas_call(
        combine_kernel,
        out_shape=(
            jax.ShapeDtypeStruct((dense,) + block, f32),
            jax.ShapeDtypeStruct((dense,) + block, bf16),
        ),
        grid_spec=pltpu.PrefetchScalarGridSpec(
            num_scalar_prefetch=1,
            grid=(1,),
            in_specs=[whole((slots,) + block)],
            out_specs=(whole((dense,) + block), whole((dense,) + block)),
            scratch_shapes=[pltpu.VMEM((dense + 1,) + block, f32)],
        ),
        name="combine",
    )
    reply = pl.pallas_call(
        reply_kernel,
        out_shape=jax.ShapeDtypeStruct((slots,) + block, bf16),
        grid_spec=pltpu.PrefetchScalarGridSpec(
            num_scalar_prefetch=1,
            grid=(1,),
            in_specs=[whole((dense,) + block)] * 3,
            out_specs=whole((slots,) + block),
            scratch_shapes=[pltpu.VMEM((dense + 1,) + block, bf16)],
        ),
        name="reply",
    )

    def back(last):
        return pl.pallas_call(
            functools.partial(back_kernel, tiles=tiles, hits=HITS, last=last),
            out_shape=jax.ShapeDtypeStruct(state.shape, f32 if last else bf16),
            grid_spec=pltpu.PrefetchScalarGridSpec(
                num_scalar_prefetch=2,
                grid=(tiles,),
                in_specs=[whole((slots,) + block), by_index, by_tile, by_tile, hbm],
                out_specs=by_tile,
                scratch_shapes=matrices + [pltpu.VMEM((HITS * bins, chans), bf16)],
            ),
            name="back",
        )

    def across(value):
        value = value.reshape((peers, cap) + block)
        value = lax.all_to_all(value, GROUP, split_axis=0, concat_axis=0, tiled=True)
        return value.reshape((slots,) + block)

    for turn in range(ITERS):
        if turn:
            halo = halo_of(scaled)
        pulled, outgoing = project(mat_idx, send_slot, scaled, *halo, taps, rays)
        total, low = combine(table, across(outgoing))
        replies = reply(table, total, exchange(low), scaling)
        last = turn == ITERS - 1
        scaled = back(last)(mat_idx, send_slot, across(replies), pulled, grad, state, rays)
    return scaled


def solution(mesh):
    nr, nc = mesh.devices.shape
    fine = Mesh(mesh.devices.reshape(nr, 2, RING // 2, nc // RING), ("row",) + COL)
    image = P("row", COL, None)
    placed = (
        image,
        image,
        P(),
        P(),
        P(("row",) + COL, None, None),
        P(),
        image,
        P(),
        P(),
    )
    return jax.shard_map(
        on_device, mesh=fine, in_specs=placed, out_specs=image, check_vma=False
    )
```

time: 445 us -> 225 us (0.51)
  waiting for transfers between devices: 146 us -> 40.5 us
  blocking collectives: 154 us -> 84.1 us
  local copies, waits for them, and re-layouts: 69.3 us -> 7.57 us
  Pallas kernels: 0 us -> 53.1 us
  matrix products: 25.1 us -> 0 us
  other arithmetic: 15.4 us -> 5.46 us
    all_to_all x2 -> x1, waiting for transfers between devices: 143 us -> 16.6 us  [across(): lax.all_to_all(value, GROUP, split_axis=0, concat_axis=0, tiled=True)]
    all_to_all x2 -> x3, blocking collectives: 154 us -> 84.1 us  [across(): lax.all_to_all(value, GROUP, split_axis=0, concat_axis=0, tiled=True)]
    pallas_call x0 -> x8, Pallas kernels: none -> 53.1 us  [the longest x2 22.2 us: on_device(): pulled, outgoing = project(mat_idx, send_slot, scaled, *halo, taps, rays)]
    gather x12 -> x0, local copies, waits for them, and re-layouts: 40.3 us -> none  [the longest x4 16.3 us: on_device(): outgoing = partial_value[source] * filled[:, None]]
    dot_general x24 -> x0, matrix products: 25.1 us -> none  [the longest x2 10.2 us: on_device(): jnp.einsum('tkp,tkc->tpc', matrices, per_pair, preferred_element_type=jnp...]
    ppermute x8 -> x11, waiting for transfers between devices: 2.48 us -> 24 us  [the longest x3 16 us: exchange(): return lax.ppermute(value, ('zh', 'zl'), swap)]
    all_to_all x6 -> x0, local copies, waits for them, and re-layouts: 18.9 us -> none  [the longest x4 11.4 us: on_device(): lax.all_to_all(replies, ('row', 'col'), split_axis=0, concat_axis=0, tile...]
    mul x2 -> x1, other arithmetic: 8.68 us -> 0.09 us  [on_device(): own_scale = inuse[:, None, None] * ray_weight]
  transfers between devices with their start and end apart: 10 -> 12, of which waited for: 5 -> 6; matrix products, arithmetic and copies ran while one was open for 5% -> 3% of each run, Pallas kernels for 0% -> 2%
where the time goes in v1:
time: 225 us; the launch traced here: 224 us
  blocking collectives  84.1 us (37%)
  Pallas kernels  53.1 us (24%)
  waiting for transfers between devices  40.5 us (18%)
  starting transfers between devices  32.5 us (14%)
  local copies, waits for them, and re-layouts  7.57 us (3%)
  other arithmetic  5.46 us (2%)
    all_to_all x3, blocking collectives, across(): lax.all_to_all(value, GROUP, split_axis=0, concat_axis=0, tiled=True)  84.1 us
    pallas_call x2, Pallas kernels, on_device(): pulled, outgoing = project(mat_idx, send_slot, scaled, *halo, taps, rays)  22.2 us
    pallas_call x2, Pallas kernels, on_device(): back(last)(mat_idx, send_slot, across(replies), pulled, grad, state, rays)  17.3 us
    all_to_all x1, waiting for transfers between devices, across(): lax.all_to_all(value, GROUP, split_axis=0, concat_axis=0, tiled=True)  16.6 us
    ppermute x3, waiting for transfers between devices, exchange(): return lax.ppermute(value, ('zh', 'zl'), swap)  16 us
    ppermute x2, starting transfers between devices, halo_of(): lefts = lax.ppermute(last, COL, right)  8.01 us
    ppermute x2, waiting for transfers between devices, halo_of(): rights = lax.ppermute(first, COL, left)  7.07 us
    pallas_call x2, Pallas kernels, on_device(): total, low = combine(table, across(outgoing))  7.04 us
  transfers between devices with their start and end apart: 12, of which 6 were waited for; matrix products, arithmetic and copies ran while one was open for 3% of the time, Pallas kernels for 2%

profile of v1, /device:TPU:0, one launch (start us, length us, event | category | flops | bytes accessed | tf_op | source)
XLA Modules:
  0.0 223.8 jit_solution(17223876057521122860)
XLA Ops:
  0.0 1.7 multiply_convert_fusion.scaled
  1.8 1.3 collective-permute-start.1
  3.1 3.0 %collective-permute-start = (bf16[96,128]{1,0:T(8,128)(2,1)S(1)}, bf16[96,128]{1,0:T(8,128)(2,1)S(1)}, u32[]{:S(2)}, u32[]{:S(2)}) collective-permute-start(bf16[96,128]{1,0:T(8,128)(2,1)S(1)} %get-tuple-element.30), channel_id=1, source_target_pairs={{0,8},{8,16},{16,24},{1,9},{9,17},{17,25},{2,10},{10,18},{18,26},{... | collective-permute-start | bytes 73736 | tf_op jit(solution)/shard_map/ppermute | solution.py:140
  8.3 4.9 %collective-permute-start.2 = (bf16[34,128]{1,0:T(8,128)(2,1)S(1)}, bf16[34,128]{1,0:T(8,128)(2,1)S(1)}, u32[]{:S(2)}, u32[]{:S(2)}) collective-permute-start(bf16[34,128]{1,0:T(8,128)(2,1)S(1)} %pad_maximum_fusion.1), channel_id=1, source_target_pairs={{0,1},{1,2},{2,3},{3,4},{4,5},{5,6},{6,7},{8,9},{9,10},{10,11},{11... | collective-permute-start | bytes 26120 | tf_op jit(solution)/shard_map/ppermute | solution.py:144
  13.2 1.3 collective-permute-start.3
  15.1 0.9 copy.19
  16.0 2.8 %collective-permute-done.3.right = bf16[34,128]{1,0:T(8,128)(2,1)S(1)} collective-permute-done((bf16[34,128]{1,0:T(8,128)(2,1)S(1)}, bf16[34,128]{1,0:T(8,128)(2,1)S(1)}, u32[]{:S(2)}, u32[]{:S(2)}) %collective-permute-start.3) | collective-permute-done | bytes 8736 | tf_op jit(solution)/shard_map/ppermute | solution.py:145
  19.3 11.1 %project.2 = (f32[3,1024,128]{2,1,0:T(8,128)}, bf16[96,64,128]{2,1,0:T(8,128)(2,1)}) custom-call(s32[48]{0:T(128)} %multiply_add_fusion.mat_idx, s32[48]{0:T(128)} %fusion.20.send_slot, bf16[32,96,128]{2,1,0:T(8,128)(2,1)} %copy-done.1, bf16[96,128]{1,0:T(8,128)(2,1)} %copy-done.8, bf16[96,128]{1,0:T(8,128)(2,1)} %copy-done.7, bf16[34,128]{1,0:T(8,128)(2,1)} %copy-done.11, ...), custom_call_target="tpu_custom_call" | custom-call | tf_op jit(solution)/shard_map/project/pallas_call | solution.py:310
  30.5 6.5 %all-to-all-start = ((bf16[16,6,64,128]{3,2,1,0:T(8,128)(2,1)}), bf16[16,6,64,128]{3,2,1,0:T(8,128)(2,1)S(1)}, u32[]{:S(2)}, u32[]{:S(2)}) async-start(bf16[16,6,64,128]{3,2,1,0:T(8,128)(2,1)} %bitcast.51), calls=%async_computation | async-start | bytes 3145728 | tf_op jit(solution)/shard_map/all_to_all | solution.py:304
  37.5 3.0 %collective-permute-start.5 = (f32[8,64,128]{2,1,0:T(8,128)S(1)}, f32[8,64,128]{2,1,0:T(8,128)S(1)}, u32[]{:S(2)}, u32[]{:S(2)}) collective-permute-start(f32[8,64,128]{2,1,0:T(8,128)S(1)} %broadcast_multiply_fusion), channel_id=1, source_target_pairs={{0,6},{2,4},{4,2},{6,0},{1,7},{3,5},{5,3},{7,1},{8,14},{10,12},{12... | collective-permute-start | bytes 786440 | tf_op jit(solution)/shard_map/ppermute | solution.py:214
  41.4 16.6 %all-to-all-done = bf16[16,6,64,128]{3,2,1,0:T(8,128)(2,1)S(1)} async-done(((bf16[16,6,64,128]{3,2,1,0:T(8,128)(2,1)}), bf16[16,6,64,128]{3,2,1,0:T(8,128)(2,1)S(1)}, u32[]{:S(2)}, u32[]{:S(2)}) %all-to-all-start) | async-done | bytes 1572896 | tf_op jit(solution)/shard_map/all_to_all | solution.py:304
  58.0 1.2 copy-done
  59.2 3.5 %combine.2 = (f32[16,64,128]{2,1,0:T(8,128)}, bf16[16,64,128]{2,1,0:T(8,128)(2,1)}) custom-call(s32[96]{0:T(128)} %add.233.table, bf16[96,64,128]{2,1,0:T(8,128)(2,1)} %bitcast.43), custom_call_target="tpu_custom_call" | custom-call | tf_op jit(solution)/shard_map/combine/pallas_call | solution.py:311
  62.7 2.2 collective-permute-start.4
  65.8 7.0 %collective-permute-done.4.other = bf16[16,64,128]{2,1,0:T(8,128)(2,1)S(1)} collective-permute-done((bf16[16,64,128]{2,1,0:T(8,128)(2,1)}, bf16[16,64,128]{2,1,0:T(8,128)(2,1)S(1)}, u32[]{:S(2)}, u32[]{:S(2)}) %collective-permute-start.4) | collective-permute-done | bytes 262176 | tf_op jit(solution)/shard_map/ppermute | solution.py:214
  73.5 3.4 %reply.2 = bf16[96,64,128]{2,1,0:T(8,128)(2,1)} custom-call(s32[96]{0:T(128)} %add.233.table, f32[16,64,128]{2,1,0:T(8,128)} %get-tuple-element.14.total, bf16[16,64,128]{2,1,0:T(8,128)(2,1)} %copy-done.4, f32[16,64,128]{2,1,0:T(8,128)} %pad_maximum_fusion.scaling), custom_call_target="tpu_custom_call" | custom-call | tf_op jit(solution)/shard_map/reply/pallas_call | solution.py:312
  76.9 27.7 %all_to_all.20 = bf16[16,6,64,128]{3,2,1,0:T(8,128)(2,1)} all-to-all(bf16[16,6,64,128]{3,2,1,0:T(8,128)(2,1)} %bitcast.47), channel_id=1, replica_groups=mesh['row'=4,'zh'=2,'zl'=2,'x'=2] {'row','zl','x'}, dimensions={0} | all-to-all | bytes 3145728 | tf_op jit(solution)/shard_map/all_to_all | solution.py:304
  104.6 8.6 %back.2.scaled = bf16[32,96,128]{2,1,0:T(8,128)(2,1)} custom-call(s32[48]{0:T(128)} %multiply_add_fusion.mat_idx, s32[48]{0:T(128)} %fusion.20.send_slot, bf16[96,64,128]{2,1,0:T(8,128)(2,1)} %bitcast.45, f32[3,1024,128]{2,1,0:T(8,128)} %get-tuple-element.16.pulled, bf16[32,96,128]{2,1,0:T(8,128)(2,1)} %grad.3, bf16[32,96,128]{2,1,0:T(8,128)(2,1)} %state.3, ...), custom_call_target="tpu_custom_call" | custom-call | tf_op jit(solution)/shard_map/back/pallas_call | solution.py:314
  113.9 1.3 collective-permute-start.7
  115.2 0.9 fusion.22
  116.2 3.0 %collective-permute-start.6 = (bf16[96,128]{1,0:T(8,128)(2,1)S(1)}, bf16[96,128]{1,0:T(8,128)(2,1)S(1)}, u32[]{:S(2)}, u32[]{:S(2)}) collective-permute-start(bf16[96,128]{1,0:T(8,128)(2,1)S(1)} %get-tuple-element.26), channel_id=1, source_target_pairs={{0,8},{8,16},{16,24},{1,9},{9,17},{17,25},{2,10},{10,18},{18,26},{... | collective-permute-start | bytes 73736 | tf_op jit(solution)/shard_map/ppermute | solution.py:140
  120.1 3.1 %collective-permute-start.8 = (bf16[34,128]{1,0:T(8,128)(2,1)S(1)}, bf16[34,128]{1,0:T(8,128)(2,1)S(1)}, u32[]{:S(2)}, u32[]{:S(2)}) collective-permute-start(bf16[34,128]{1,0:T(8,128)(2,1)S(1)} %pad_maximum_fusion.3), channel_id=1, source_target_pairs={{0,1},{1,2},{2,3},{3,4},{4,5},{5,6},{6,7},{8,9},{9,10},{10,11},{11... | collective-permute-start | bytes 26120 | tf_op jit(solution)/shard_map/ppermute | solution.py:144
  123.2 1.3 collective-permute-start.9
  124.6 4.3 %collective-permute-done.9.right = bf16[34,128]{1,0:T(8,128)(2,1)S(1)} collective-permute-done((bf16[34,128]{1,0:T(8,128)(2,1)S(1)}, bf16[34,128]{1,0:T(8,128)(2,1)S(1)}, u32[]{:S(2)}, u32[]{:S(2)}) %collective-permute-start.9) | collective-permute-done | bytes 8736 | tf_op jit(solution)/shard_map/ppermute | solution.py:145
  129.5 11.0 %project.3 = (f32[3,1024,128]{2,1,0:T(8,128)}, bf16[96,64,128]{2,1,0:T(8,128)(2,1)}) custom-call(s32[48]{0:T(128)} %multiply_add_fusion.mat_idx, s32[48]{0:T(128)} %fusion.20.send_slot, bf16[32,96,128]{2,1,0:T(8,128)(2,1)} %back.2.scaled, bf16[96,128]{1,0:T(8,128)(2,1)} %copy-done.10, bf16[96,128]{1,0:T(8,128)(2,1)} %copy-done.9, ...), custom_call_target="tpu_custom_call" | custom-call | tf_op jit(solution)/shard_map/project/pallas_call | solution.py:310
  140.6 29.3 %all_to_all.21 = bf16[16,6,64,128]{3,2,1,0:T(8,128)(2,1)} all-to-all(bf16[16,6,64,128]{3,2,1,0:T(8,128)(2,1)} %bitcast.52), channel_id=1, replica_groups=mesh['row'=4,'zh'=2,'zl'=2,'x'=2] {'row','zl','x'}, dimensions={0} | all-to-all | bytes 3145728 | tf_op jit(solution)/shard_map/all_to_all | solution.py:304
  169.9 3.5 %combine.3 = (f32[16,64,128]{2,1,0:T(8,128)}, bf16[16,64,128]{2,1,0:T(8,128)(2,1)}) custom-call(s32[96]{0:T(128)} %add.233.table, bf16[96,64,128]{2,1,0:T(8,128)(2,1)} %bitcast.46), custom_call_target="tpu_custom_call" | custom-call | tf_op jit(solution)/shard_map/combine/pallas_call | solution.py:311
  173.4 1.6 collective-permute-start.10
  174.9 9.0 %collective-permute-done.10.other = bf16[16,64,128]{2,1,0:T(8,128)(2,1)S(1)} collective-permute-done((bf16[16,64,128]{2,1,0:T(8,128)(2,1)}, bf16[16,64,128]{2,1,0:T(8,128)(2,1)S(1)}, u32[]{:S(2)}, u32[]{:S(2)}) %collective-permute-start.10) | collective-permute-done | bytes 262176 | tf_op jit(solution)/shard_map/ppermute | solution.py:214
  184.7 3.3 %reply.3 = bf16[96,64,128]{2,1,0:T(8,128)(2,1)} custom-call(s32[96]{0:T(128)} %add.233.table, f32[16,64,128]{2,1,0:T(8,128)} %get-tuple-element.18.total, bf16[16,64,128]{2,1,0:T(8,128)(2,1)} %copy-done.5, f32[16,64,128]{2,1,0:T(8,128)} %pad_maximum_fusion.scaling), custom_call_target="tpu_custom_call" | custom-call | tf_op jit(solution)/shard_map/reply/pallas_call | solution.py:312
  188.0 27.1 %all_to_all.22 = bf16[16,6,64,128]{3,2,1,0:T(8,128)(2,1)} all-to-all(bf16[16,6,64,128]{3,2,1,0:T(8,128)(2,1)} %bitcast.44), channel_id=1, replica_groups=mesh['row'=4,'zh'=2,'zl'=2,'x'=2] {'row','zl','x'}, dimensions={0} | all-to-all | bytes 3145728 | tf_op jit(solution)/shard_map/all_to_all | solution.py:304
  215.1 8.7 %back.3 = f32[32,96,128]{2,1,0:T(8,128)} custom-call(s32[48]{0:T(128)} %multiply_add_fusion.mat_idx, s32[48]{0:T(128)} %fusion.20.send_slot, bf16[96,64,128]{2,1,0:T(8,128)(2,1)} %bitcast.48, f32[3,1024,128]{2,1,0:T(8,128)} %get-tuple-element.20.pulled, bf16[32,96,128]{2,1,0:T(8,128)(2,1)} %grad.3, bf16[32,96,128]{2,1,0:T(8,128)(2,1)} %state.3, ...), custom_call_target="tpu_custom_call" | custom-call | tf_op jit(solution)/shard_map/back/pallas_call | solution.py:314
  (83 shorter events, 9.2 us)
Async XLA Ops:
  0.0 6.2 %copy-start.16 = (s32[1,3,16]{2,0,1:T(1,128)S(1)}, s32[1,3,16]{2,0,1:T(1,128)}, u32[]{:S(2)}) copy-start(s32[1,3,16]{2,0,1:T(1,128)} %param.15) | copy-start | bytes 580
  0.0 6.3 %copy-start.6 = (s32[4,24,16]{1,2,0:T(8,128)S(1)}, s32[4,24,16]{1,2,0:T(8,128)}, u32[]{:S(2)}) copy-start(s32[4,24,16]{1,2,0:T(8,128)} %param.14) | copy-start | bytes 18436
  0.0 6.5 %copy-start.15 = (s32[256]{0:T(256)S(1)}, s32[256]{0:T(256)}, u32[]{:S(2)}) copy-start(s32[256]{0:T(256)} %param.16) | copy-start | bytes 3076
  0.0 8.1 %copy-start.3 = (bf16[3,3,128,128]{3,2,1,0:T(8,128)(2,1)S(1)}, bf16[3,3,128,128]{3,2,1,0:T(8,128)(2,1)}, u32[]{:S(2)}) copy-start(bf16[3,3,128,128]{3,2,1,0:T(8,128)(2,1)} %param.11) | copy-start | bytes 884740
  1.7 17.0 %copy-start.1 = (bf16[32,96,128]{2,1,0:T(8,128)(2,1)}, bf16[32,96,128]{2,1,0:T(8,128)(2,1)S(1)}, u32[]{:S(2)}) copy-start(bf16[32,96,128]{2,1,0:T(8,128)(2,1)S(1)} %multiply_convert_fusion.scaled) | copy-start | bytes 2359300
  1.8 6.4 %collective-permute-start.1 = (bf16[96,128]{1,0:T(8,128)(2,1)S(1)}, bf16[96,128]{1,0:T(8,128)(2,1)S(1)}, u32[]{:S(2)}, u32[]{:S(2)}) collective-permute-start(bf16[96,128]{1,0:T(8,128)(2,1)S(1)} %get-tuple-element.29), channel_id=1, source_target_pairs={{8,0},{16,8},{24,16},{9,1},{17,9},{25,17},{10,2},{18,10},{26,18},{... | collective-permute-start | bytes 73736 | tf_op jit(solution)/shard_map/ppermute | solution.py:141
  3.1 5.2 %collective-permute-start = (bf16[96,128]{1,0:T(8,128)(2,1)S(1)}, bf16[96,128]{1,0:T(8,128)(2,1)S(1)}, u32[]{:S(2)}, u32[]{:S(2)}) collective-permute-start(bf16[96,128]{1,0:T(8,128)(2,1)S(1)} %get-tuple-element.30), channel_id=1, source_target_pairs={{0,8},{8,16},{16,24},{1,9},{9,17},{17,25},{2,10},{10,18},{18,26},{... | collective-permute-start | bytes 73736 | tf_op jit(solution)/shard_map/ppermute | solution.py:140
  8.2 10.6 %copy-start.7 = (bf16[96,128]{1,0:T(8,128)(2,1)}, bf16[96,128]{1,0:T(8,128)(2,1)S(1)}, u32[]{:S(2)}) copy-start(bf16[96,128]{1,0:T(8,128)(2,1)S(1)} %collective-permute-done.1.below) | copy-start | bytes 73732
  8.2 10.5 %copy-start.8 = (bf16[96,128]{1,0:T(8,128)(2,1)}, bf16[96,128]{1,0:T(8,128)(2,1)S(1)}, u32[]{:S(2)}) copy-start(bf16[96,128]{1,0:T(8,128)(2,1)S(1)} %collective-permute-done.above) | copy-start | bytes 73732
  8.3 7.7 %collective-permute-start.2 = (bf16[34,128]{1,0:T(8,128)(2,1)S(1)}, bf16[34,128]{1,0:T(8,128)(2,1)S(1)}, u32[]{:S(2)}, u32[]{:S(2)}) collective-permute-start(bf16[34,128]{1,0:T(8,128)(2,1)S(1)} %pad_maximum_fusion.1), channel_id=1, source_target_pairs={{0,1},{1,2},{2,3},{3,4},{4,5},{5,6},{6,7},{8,9},{9,10},{10,11},{11... | collective-permute-start | bytes 26120 | tf_op jit(solution)/shard_map/ppermute | solution.py:144
  13.2 5.6 %collective-permute-start.3 = (bf16[34,128]{1,0:T(8,128)(2,1)S(1)}, bf16[34,128]{1,0:T(8,128)(2,1)S(1)}, u32[]{:S(2)}, u32[]{:S(2)}) collective-permute-start(bf16[34,128]{1,0:T(8,128)(2,1)S(1)} %pad_maximum_fusion.2), channel_id=1, source_target_pairs={{1,0},{2,1},{3,2},{4,3},{5,4},{6,5},{7,6},{9,8},{10,9},{11,10},{12... | collective-permute-start | bytes 26120 | tf_op jit(solution)/shard_map/ppermute | solution.py:145
  16.0 2.8 %copy-start.11 = (bf16[34,128]{1,0:T(8,128)(2,1)}, bf16[34,128]{1,0:T(8,128)(2,1)S(1)}, u32[]{:S(2)}) copy-start(bf16[34,128]{1,0:T(8,128)(2,1)S(1)} %collective-permute-done.2.left) | copy-start | bytes 26116
  18.7 0.6 copy-start.13
  30.5 6.6 %copy-start.17 = (s32[8]{0:T(128)S(1)}, s32[8]{0:T(128)}, u32[]{:S(2)}) copy-start(s32[8]{0:T(128)} %param.17) | copy-start | bytes 100
  30.5 6.9 %copy-start.2 = (f32[8,64,128]{2,1,0:T(8,128)S(1)}, f32[8,64,128]{2,1,0:T(8,128)}, u32[]{:S(2)}) copy-start(f32[8,64,128]{2,1,0:T(8,128)} %param.13) | copy-start | bytes 786436
  30.5 27.5 %all-to-all-start = ((bf16[16,6,64,128]{3,2,1,0:T(8,128)(2,1)}), bf16[16,6,64,128]{3,2,1,0:T(8,128)(2,1)S(1)}, u32[]{:S(2)}, u32[]{:S(2)}) async-start(bf16[16,6,64,128]{3,2,1,0:T(8,128)(2,1)} %bitcast.51), calls=%async_computation | async-start | bytes 3145728 | tf_op jit(solution)/shard_map/all_to_all | solution.py:304
  37.5 27.4 %collective-permute-start.5 = (f32[8,64,128]{2,1,0:T(8,128)S(1)}, f32[8,64,128]{2,1,0:T(8,128)S(1)}, u32[]{:S(2)}, u32[]{:S(2)}) collective-permute-start(f32[8,64,128]{2,1,0:T(8,128)S(1)} %broadcast_multiply_fusion), channel_id=1, source_target_pairs={{0,6},{2,4},{4,2},{6,0},{1,7},{3,5},{5,3},{7,1},{8,14},{10,12},{12... | collective-permute-start | bytes 786440 | tf_op jit(solution)/shard_map/ppermute | solution.py:214
  58.0 1.2 copy-start
  62.7 10.1 %collective-permute-start.4 = (bf16[16,64,128]{2,1,0:T(8,128)(2,1)}, bf16[16,64,128]{2,1,0:T(8,128)(2,1)S(1)}, u32[]{:S(2)}, u32[]{:S(2)}) collective-permute-start(bf16[16,64,128]{2,1,0:T(8,128)(2,1)} %get-tuple-element.15), channel_id=1, source_target_pairs={{0,6},{2,4},{4,2},{6,0},{1,7},{3,5},{5,3},{7,1},{8,14},{10,12},{12... | collective-permute-start | bytes 786440 | tf_op jit(solution)/shard_map/ppermute | solution.py:214
  72.8 0.7 copy-start.4
  113.9 5.3 %collective-permute-start.7 = (bf16[96,128]{1,0:T(8,128)(2,1)S(1)}, bf16[96,128]{1,0:T(8,128)(2,1)S(1)}, u32[]{:S(2)}, u32[]{:S(2)}) collective-permute-start(bf16[96,128]{1,0:T(8,128)(2,1)S(1)} %get-tuple-element.25), channel_id=1, source_target_pairs={{8,0},{16,8},{24,16},{9,1},{17,9},{25,17},{10,2},{18,10},{26,18},{... | collective-permute-start | bytes 73736 | tf_op jit(solution)/shard_map/ppermute | solution.py:141
  116.2 3.9 %collective-permute-start.6 = (bf16[96,128]{1,0:T(8,128)(2,1)S(1)}, bf16[96,128]{1,0:T(8,128)(2,1)S(1)}, u32[]{:S(2)}, u32[]{:S(2)}) collective-permute-start(bf16[96,128]{1,0:T(8,128)(2,1)S(1)} %get-tuple-element.26), channel_id=1, source_target_pairs={{0,8},{8,16},{16,24},{1,9},{9,17},{17,25},{2,10},{10,18},{18,26},{... | collective-permute-start | bytes 73736 | tf_op jit(solution)/shard_map/ppermute | solution.py:140
  119.2 9.7 %copy-start.9 = (bf16[96,128]{1,0:T(8,128)(2,1)}, bf16[96,128]{1,0:T(8,128)(2,1)S(1)}, u32[]{:S(2)}) copy-start(bf16[96,128]{1,0:T(8,128)(2,1)S(1)} %collective-permute-done.7.below) | copy-start | bytes 73732
  120.0 8.9 %copy-start.10 = (bf16[96,128]{1,0:T(8,128)(2,1)}, bf16[96,128]{1,0:T(8,128)(2,1)S(1)}, u32[]{:S(2)}) copy-start(bf16[96,128]{1,0:T(8,128)(2,1)S(1)} %collective-permute-done.6.above) | copy-start | bytes 73732
  120.1 4.5 %collective-permute-start.8 = (bf16[34,128]{1,0:T(8,128)(2,1)S(1)}, bf16[34,128]{1,0:T(8,128)(2,1)S(1)}, u32[]{:S(2)}, u32[]{:S(2)}) collective-permute-start(bf16[34,128]{1,0:T(8,128)(2,1)S(1)} %pad_maximum_fusion.3), channel_id=1, source_target_pairs={{0,1},{1,2},{2,3},{3,4},{4,5},{5,6},{6,7},{8,9},{9,10},{10,11},{11... | collective-permute-start | bytes 26120 | tf_op jit(solution)/shard_map/ppermute | solution.py:144
  123.2 5.7 %collective-permute-start.9 = (bf16[34,128]{1,0:T(8,128)(2,1)S(1)}, bf16[34,128]{1,0:T(8,128)(2,1)S(1)}, u32[]{:S(2)}, u32[]{:S(2)}) collective-permute-start(bf16[34,128]{1,0:T(8,128)(2,1)S(1)} %pad_maximum_fusion.4), channel_id=1, source_target_pairs={{1,0},{2,1},{3,2},{4,3},{5,4},{6,5},{7,6},{9,8},{10,9},{11,10},{12... | collective-permute-start | bytes 26120 | tf_op jit(solution)/shard_map/ppermute | solution.py:145
  124.6 4.3 %copy-start.12 = (bf16[34,128]{1,0:T(8,128)(2,1)}, bf16[34,128]{1,0:T(8,128)(2,1)S(1)}, u32[]{:S(2)}) copy-start(bf16[34,128]{1,0:T(8,128)(2,1)S(1)} %collective-permute-done.8.left) | copy-start | bytes 26116
  128.9 0.6 copy-start.14
  173.4 10.6 %collective-permute-start.10 = (bf16[16,64,128]{2,1,0:T(8,128)(2,1)}, bf16[16,64,128]{2,1,0:T(8,128)(2,1)S(1)}, u32[]{:S(2)}, u32[]{:S(2)}) collective-permute-start(bf16[16,64,128]{2,1,0:T(8,128)(2,1)} %get-tuple-element.19), channel_id=1, source_target_pairs={{0,6},{2,4},{4,2},{6,0},{1,7},{3,5},{5,3},{7,1},{8,14},{10,12},{12... | collective-permute-start | bytes 786440 | tf_op jit(solution)/shard_map/ppermute | solution.py:214
  184.0 0.7 copy-start.5

commit v2 on v1

--- a/solution.py
+++ b/solution.py
@@ -14,6 +14,7 @@
 RING = 4
 
 relax_rate = 0.25
+LIM = dict(project=24 << 20, combine=8 << 20, reply=8 << 20, back=24 << 20)
 
 COL = ("zh", "zl", "x")
 GROUP = ("row", "zl", "x")
@@ -255,7 +256,7 @@
                 pltpu.VMEM((rows_dev + 2, cols_dev, 3 * chans), bf16),
             ],
         ),
-        name="project",
+        name="project", compiler_params=pltpu.CompilerParams(vmem_limit_bytes=LIM["project"]),
     )
     combine = pl.pallas_call(
         combine_kernel,
@@ -270,7 +271,7 @@
             out_specs=(whole((dense,) + block), whole((dense,) + block)),
             scratch_shapes=[pltpu.VMEM((dense + 1,) + block, f32)],
         ),
-        name="combine",
+        name="combine", compiler_params=pltpu.CompilerParams(vmem_limit_bytes=LIM["combine"]),
     )
     reply = pl.pallas_call(
         reply_kernel,
@@ -282,7 +283,7 @@
             out_specs=whole((slots,) + block),
             scratch_shapes=[pltpu.VMEM((dense + 1,) + block, bf16)],
         ),
-        name="reply",
+        name="reply", compiler_params=pltpu.CompilerParams(vmem_limit_bytes=LIM["reply"]),
     )
 
     def back(last):
@@ -296,7 +297,7 @@
                 out_specs=by_tile,
                 scratch_shapes=matrices + [pltpu.VMEM((HITS * bins, chans), bf16)],
             ),
-            name="back",
+            name="back", compiler_params=pltpu.CompilerParams(vmem_limit_bytes=LIM["back"]),
         )
 
     def across(value):

time: 225 us -> 231 us (1.027)
  Pallas kernels: 53.1 us -> 62.3 us
  local copies, waits for them, and re-layouts: 7.57 us -> 4.3 us
    pallas_call x2, Pallas kernels: 22.2 us -> 33.3 us  [on_device(): pulled, outgoing = project(mat_idx, send_slot, scaled, *halo, taps, rays)]
    pallas_call x2, Pallas kernels: 17.3 us -> 25.3 us  [on_device(): back(last)(mat_idx, send_slot, across(replies), pulled, grad, state, rays)]
    pallas_call x2, Pallas kernels: 6.67 us -> 1.55 us  [on_device(): replies = reply(table, total, exchange(low), scaling)]
    pallas_call x2, Pallas kernels: 7.04 us -> 2.23 us  [on_device(): total, low = combine(table, across(outgoing))]
  transfers between devices with their start and end apart: 12 -> 12, of which waited for: 6 -> 7; matrix products, arithmetic and copies ran while one was open for 3% -> 2% of each run, Pallas kernels for 2% -> 0%
where the time goes in v2:
time: 231 us
  blocking collectives  83.3 us (36%)
  Pallas kernels  62.3 us (27%)
  waiting for transfers between devices  41.5 us (18%)
  starting transfers between devices  32.6 us (14%)
  other arithmetic  6.1 us (3%)
  local copies, waits for them, and re-layouts  4.3 us (2%)
    all_to_all x3, blocking collectives, across(): lax.all_to_all(value, GROUP, split_axis=0, concat_axis=0, tiled=True)  83.3 us
    pallas_call x2, Pallas kernels, on_device(): pulled, outgoing = project(mat_idx, send_slot, scaled, *halo, taps, rays)  33.3 us
    pallas_call x2, Pallas kernels, on_device(): back(last)(mat_idx, send_slot, across(replies), pulled, grad, state, rays)  25.3 us
    ppermute x3, waiting for transfers between devices, exchange(): return lax.ppermute(value, ('zh', 'zl'), swap)  16.8 us
    all_to_all x1, waiting for transfers between devices, across(): lax.all_to_all(value, GROUP, split_axis=0, concat_axis=0, tiled=True)  15.5 us
    ppermute x2, waiting for transfers between devices, halo_of(): rights = lax.ppermute(first, COL, left)  8.27 us
    ppermute x2, starting transfers between devices, halo_of(): lefts = lax.ppermute(last, COL, right)  8.02 us
    all_to_all x1, starting transfers between devices, across(): lax.all_to_all(value, GROUP, split_axis=0, concat_axis=0, tiled=True)  7.1 us
  transfers between devices with their start and end apart: 12, of which 7 were waited for; matrix products, arithmetic and copies ran while one was open for 2% of the time, Pallas kernels for 0%

profile of v2, /device:TPU:0, one launch (start us, length us, event | category | flops | bytes accessed | tf_op | source)
XLA Modules:
  0.0 230.6 jit_solution(3675088594948076976)
XLA Ops:
  0.0 1.7 multiply_convert_fusion.scaled
  1.7 1.3 collective-permute-start.1
  3.0 3.0 %collective-permute-start = (bf16[96,128]{1,0:T(8,128)(2,1)S(1)}, bf16[96,128]{1,0:T(8,128)(2,1)S(1)}, u32[]{:S(2)}, u32[]{:S(2)}) collective-permute-start(bf16[96,128]{1,0:T(8,128)(2,1)S(1)} %get-tuple-element.30), channel_id=1, source_target_pairs={{0,8},{8,16},{16,24},{1,9},{9,17},{17,25},{2,10},{10,18},{18,26},{... | collective-permute-start | bytes 73736 | tf_op jit(solution)/shard_map/ppermute | solution.py:141
  7.7 4.9 %collective-permute-start.2 = (bf16[34,128]{1,0:T(8,128)(2,1)S(1)}, bf16[34,128]{1,0:T(8,128)(2,1)S(1)}, u32[]{:S(2)}, u32[]{:S(2)}) collective-permute-start(bf16[34,128]{1,0:T(8,128)(2,1)S(1)} %pad_maximum_fusion.1), channel_id=1, source_target_pairs={{0,1},{1,2},{2,3},{3,4},{4,5},{5,6},{6,7},{8,9},{9,10},{10,11},{11... | collective-permute-start | bytes 26120 | tf_op jit(solution)/shard_map/ppermute | solution.py:145
  12.6 1.3 collective-permute-start.3
  14.1 4.0 %collective-permute-done.3.right = bf16[34,128]{1,0:T(8,128)(2,1)S(1)} collective-permute-done((bf16[34,128]{1,0:T(8,128)(2,1)S(1)}, bf16[34,128]{1,0:T(8,128)(2,1)S(1)}, u32[]{:S(2)}, u32[]{:S(2)}) %collective-permute-start.3) | collective-permute-done | bytes 8736 | tf_op jit(solution)/shard_map/ppermute | solution.py:146
  18.1 2.2 copy-done
  20.3 16.7 %project.2 = (f32[3,1024,128]{2,1,0:T(8,128)S(1)}, bf16[96,64,128]{2,1,0:T(8,128)(2,1)S(1)}) custom-call(s32[48]{0:T(128)S(1)} %multiply_add_fusion.mat_idx, s32[48]{0:T(128)S(1)} %fusion.20.send_slot, bf16[32,96,128]{2,1,0:T(8,128)(2,1)S(1)} %multiply_convert_fusion.scaled, bf16[96,128]{1,0:T(8,128)(2,1)S(1)} %collective-permute-done.above, ...), custom_call_target="tpu_custom_call" | custom-call | tf_op jit(solution)/shard_map/project/pallas_call | solution.py:311
  37.0 1.1 copy-done.4
  38.1 7.1 %all-to-all-start = ((bf16[16,6,64,128]{3,2,1,0:T(8,128)(2,1)}), bf16[16,6,64,128]{3,2,1,0:T(8,128)(2,1)S(1)}, u32[]{:S(2)}, u32[]{:S(2)}) async-start(bf16[16,6,64,128]{3,2,1,0:T(8,128)(2,1)} %bitcast.51), calls=%async_computation | async-start | bytes 3145728 | tf_op jit(solution)/shard_map/all_to_all | solution.py:305
  45.6 1.7 broadcast_multiply_fusion
  47.4 2.9 %collective-permute-start.5 = (f32[8,64,128]{2,1,0:T(8,128)}, f32[8,64,128]{2,1,0:T(8,128)}, u32[]{:S(2)}, u32[]{:S(2)}) collective-permute-start(f32[8,64,128]{2,1,0:T(8,128)} %broadcast_multiply_fusion), channel_id=1, source_target_pairs={{0,6},{2,4},{4,2},{6,0},{1,7},{3,5},{5,3},{7,1},{8,14},{10,12},{12... | collective-permute-start | bytes 786440 | tf_op jit(solution)/shard_map/ppermute | solution.py:215
  50.7 15.5 %all-to-all-done = bf16[16,6,64,128]{3,2,1,0:T(8,128)(2,1)S(1)} async-done(((bf16[16,6,64,128]{3,2,1,0:T(8,128)(2,1)}), bf16[16,6,64,128]{3,2,1,0:T(8,128)(2,1)S(1)}, u32[]{:S(2)}, u32[]{:S(2)}) %all-to-all-start) | async-done | bytes 1572896 | tf_op jit(solution)/shard_map/all_to_all | solution.py:305
  66.2 1.1 combine.2
  67.3 2.3 collective-permute-start.4
  69.6 3.6 %collective-permute-done.5 = f32[8,64,128]{2,1,0:T(8,128)} collective-permute-done((f32[8,64,128]{2,1,0:T(8,128)}, f32[8,64,128]{2,1,0:T(8,128)}, u32[]{:S(2)}, u32[]{:S(2)}) %collective-permute-start.5) | collective-permute-done | bytes 262176 | tf_op jit(solution)/shard_map/ppermute | solution.py:215
  73.2 1.1 broadcast_select_fusion.1
  74.3 3.8 %collective-permute-done.4.other = bf16[16,64,128]{2,1,0:T(8,128)(2,1)S(1)} collective-permute-done((bf16[16,64,128]{2,1,0:T(8,128)(2,1)S(1)}, bf16[16,64,128]{2,1,0:T(8,128)(2,1)S(1)}, u32[]{:S(2)}, u32[]{:S(2)}) %collective-permute-start.4) | collective-permute-done | bytes 262176 | tf_op jit(solution)/shard_map/ppermute | solution.py:215
  79.0 29.3 %all_to_all.20 = bf16[16,6,64,128]{3,2,1,0:T(8,128)(2,1)S(1)} all-to-all(bf16[16,6,64,128]{3,2,1,0:T(8,128)(2,1)S(1)} %bitcast.47), channel_id=1, replica_groups=mesh['row'=4,'zh'=2,'zl'=2,'x'=2] {'row','zl','x'}, dimensions={0} | all-to-all | bytes 3145728 | tf_op jit(solution)/shard_map/all_to_all | solution.py:305
  108.3 12.3 %back.2.scaled = bf16[32,96,128]{2,1,0:T(8,128)(2,1)S(1)} custom-call(s32[48]{0:T(128)S(1)} %multiply_add_fusion.mat_idx, s32[48]{0:T(128)S(1)} %fusion.20.send_slot, bf16[96,64,128]{2,1,0:T(8,128)(2,1)S(1)} %bitcast.45, f32[3,1024,128]{2,1,0:T(8,128)S(1)} %get-tuple-element.16.pulled, bf16[32,96,128]{2,1,0:T(8,128)(2,1)S(1)} %copy-done.2, ...), custom_call_target="tpu_custom_call" | custom-call | tf_op jit(solution)/shard_map/back/pallas_call | solution.py:315
  120.6 1.3 collective-permute-start.7
  122.0 3.0 %collective-permute-start.6 = (bf16[96,128]{1,0:T(8,128)(2,1)S(1)}, bf16[96,128]{1,0:T(8,128)(2,1)S(1)}, u32[]{:S(2)}, u32[]{:S(2)}) collective-permute-start(bf16[96,128]{1,0:T(8,128)(2,1)S(1)} %get-tuple-element.26), channel_id=1, source_target_pairs={{0,8},{8,16},{16,24},{1,9},{9,17},{17,25},{2,10},{10,18},{18,26},{... | collective-permute-start | bytes 73736 | tf_op jit(solution)/shard_map/ppermute | solution.py:141
  125.9 3.1 %collective-permute-start.8 = (bf16[34,128]{1,0:T(8,128)(2,1)S(1)}, bf16[34,128]{1,0:T(8,128)(2,1)S(1)}, u32[]{:S(2)}, u32[]{:S(2)}) collective-permute-start(bf16[34,128]{1,0:T(8,128)(2,1)S(1)} %pad_maximum_fusion.3), channel_id=1, source_target_pairs={{0,1},{1,2},{2,3},{3,4},{4,5},{5,6},{6,7},{8,9},{9,10},{10,11},{11... | collective-permute-start | bytes 26120 | tf_op jit(solution)/shard_map/ppermute | solution.py:145
  129.1 1.3 collective-permute-start.9
  130.4 4.2 %collective-permute-done.9.right = bf16[34,128]{1,0:T(8,128)(2,1)S(1)} collective-permute-done((bf16[34,128]{1,0:T(8,128)(2,1)S(1)}, bf16[34,128]{1,0:T(8,128)(2,1)S(1)}, u32[]{:S(2)}, u32[]{:S(2)}) %collective-permute-start.9) | collective-permute-done | bytes 8736 | tf_op jit(solution)/shard_map/ppermute | solution.py:146
  134.7 16.7 %project.3 = (f32[3,1024,128]{2,1,0:T(8,128)S(1)}, bf16[96,64,128]{2,1,0:T(8,128)(2,1)S(1)}) custom-call(s32[48]{0:T(128)S(1)} %multiply_add_fusion.mat_idx, s32[48]{0:T(128)S(1)} %fusion.20.send_slot, bf16[32,96,128]{2,1,0:T(8,128)(2,1)S(1)} %back.2.scaled, bf16[96,128]{1,0:T(8,128)(2,1)S(1)} %collective-permute-done.6.above, ...), custom_call_target="tpu_custom_call" | custom-call | tf_op jit(solution)/shard_map/project/pallas_call | solution.py:311
  151.3 27.2 %all_to_all.21 = bf16[16,6,64,128]{3,2,1,0:T(8,128)(2,1)S(1)} all-to-all(bf16[16,6,64,128]{3,2,1,0:T(8,128)(2,1)S(1)} %bitcast.52), channel_id=1, replica_groups=mesh['row'=4,'zh'=2,'zl'=2,'x'=2] {'row','zl','x'}, dimensions={0} | all-to-all | bytes 3145728 | tf_op jit(solution)/shard_map/all_to_all | solution.py:305
  178.5 1.1 combine.3
  179.6 1.1 collective-permute-start.10
  180.7 9.4 %collective-permute-done.10.other = bf16[16,64,128]{2,1,0:T(8,128)(2,1)S(1)} collective-permute-done((bf16[16,64,128]{2,1,0:T(8,128)(2,1)S(1)}, bf16[16,64,128]{2,1,0:T(8,128)(2,1)S(1)}, u32[]{:S(2)}, u32[]{:S(2)}) %collective-permute-start.10) | collective-permute-done | bytes 262176 | tf_op jit(solution)/shard_map/ppermute | solution.py:215
  190.9 26.8 %all_to_all.22 = bf16[16,6,64,128]{3,2,1,0:T(8,128)(2,1)S(1)} all-to-all(bf16[16,6,64,128]{3,2,1,0:T(8,128)(2,1)S(1)} %bitcast.44), channel_id=1, replica_groups=mesh['row'=4,'zh'=2,'zl'=2,'x'=2] {'row','zl','x'}, dimensions={0} | all-to-all | bytes 3145728 | tf_op jit(solution)/shard_map/all_to_all | solution.py:305
  217.7 13.0 %back.3 = f32[32,96,128]{2,1,0:T(8,128)} custom-call(s32[48]{0:T(128)S(1)} %multiply_add_fusion.mat_idx, s32[48]{0:T(128)S(1)} %fusion.20.send_slot, bf16[96,64,128]{2,1,0:T(8,128)(2,1)S(1)} %bitcast.48, f32[3,1024,128]{2,1,0:T(8,128)S(1)} %get-tuple-element.20.pulled, bf16[32,96,128]{2,1,0:T(8,128)(2,1)S(1)} %copy-done.2, ...), custom_call_target="tpu_custom_call" | custom-call | tf_op jit(solution)/shard_map/back/pallas_call | solution.py:315
  (69 shorter events, 5.0 us)
Async XLA Ops:
  0.0 6.2 %copy-start.9 = (s32[1,3,16]{2,0,1:T(1,128)S(1)}, s32[1,3,16]{2,0,1:T(1,128)}, u32[]{:S(2)}) copy-start(s32[1,3,16]{2,0,1:T(1,128)} %param.15) | copy-start | bytes 580
  0.0 6.3 %copy-start.7 = (s32[4,24,16]{1,2,0:T(8,128)S(1)}, s32[4,24,16]{1,2,0:T(8,128)}, u32[]{:S(2)}) copy-start(s32[4,24,16]{1,2,0:T(8,128)} %param.14) | copy-start | bytes 18436
  0.0 6.5 %copy-start.8 = (s32[256]{0:T(256)S(1)}, s32[256]{0:T(256)}, u32[]{:S(2)}) copy-start(s32[256]{0:T(256)} %param.16) | copy-start | bytes 3076
  0.0 7.5 %copy-start.6 = (bf16[3,3,128,128]{3,2,1,0:T(8,128)(2,1)S(1)}, bf16[3,3,128,128]{3,2,1,0:T(8,128)(2,1)}, u32[]{:S(2)}) copy-start(bf16[3,3,128,128]{3,2,1,0:T(8,128)(2,1)} %param.11) | copy-start | bytes 884740
  1.7 5.9 %collective-permute-start.1 = (bf16[96,128]{1,0:T(8,128)(2,1)S(1)}, bf16[96,128]{1,0:T(8,128)(2,1)S(1)}, u32[]{:S(2)}, u32[]{:S(2)}) collective-permute-start(bf16[96,128]{1,0:T(8,128)(2,1)S(1)} %get-tuple-element.29), channel_id=1, source_target_pairs={{8,0},{16,8},{24,16},{9,1},{17,9},{25,17},{10,2},{18,10},{26,18},{... | collective-permute-start | bytes 73736 | tf_op jit(solution)/shard_map/ppermute | solution.py:142
  3.0 4.6 %collective-permute-start = (bf16[96,128]{1,0:T(8,128)(2,1)S(1)}, bf16[96,128]{1,0:T(8,128)(2,1)S(1)}, u32[]{:S(2)}, u32[]{:S(2)}) collective-permute-start(bf16[96,128]{1,0:T(8,128)(2,1)S(1)} %get-tuple-element.30), channel_id=1, source_target_pairs={{0,8},{8,16},{16,24},{1,9},{9,17},{17,25},{2,10},{10,18},{18,26},{... | collective-permute-start | bytes 73736 | tf_op jit(solution)/shard_map/ppermute | solution.py:141
  7.7 6.4 %collective-permute-start.2 = (bf16[34,128]{1,0:T(8,128)(2,1)S(1)}, bf16[34,128]{1,0:T(8,128)(2,1)S(1)}, u32[]{:S(2)}, u32[]{:S(2)}) collective-permute-start(bf16[34,128]{1,0:T(8,128)(2,1)S(1)} %pad_maximum_fusion.1), channel_id=1, source_target_pairs={{0,1},{1,2},{2,3},{3,4},{4,5},{5,6},{6,7},{8,9},{9,10},{10,11},{11... | collective-permute-start | bytes 26120 | tf_op jit(solution)/shard_map/ppermute | solution.py:145
  12.6 5.6 %collective-permute-start.3 = (bf16[34,128]{1,0:T(8,128)(2,1)S(1)}, bf16[34,128]{1,0:T(8,128)(2,1)S(1)}, u32[]{:S(2)}, u32[]{:S(2)}) collective-permute-start(bf16[34,128]{1,0:T(8,128)(2,1)S(1)} %pad_maximum_fusion.2), channel_id=1, source_target_pairs={{1,0},{2,1},{3,2},{4,3},{5,4},{6,5},{7,6},{9,8},{10,9},{11,10},{12... | collective-permute-start | bytes 26120 | tf_op jit(solution)/shard_map/ppermute | solution.py:146
  18.1 2.2 copy-start
  37.0 1.1 copy-start.4
  38.1 7.1 %copy-start.10 = (s32[8]{0:T(128)S(1)}, s32[8]{0:T(128)}, u32[]{:S(2)}) copy-start(s32[8]{0:T(128)} %param.17) | copy-start | bytes 100
  38.1 28.1 %all-to-all-start = ((bf16[16,6,64,128]{3,2,1,0:T(8,128)(2,1)}), bf16[16,6,64,128]{3,2,1,0:T(8,128)(2,1)S(1)}, u32[]{:S(2)}, u32[]{:S(2)}) async-start(bf16[16,6,64,128]{3,2,1,0:T(8,128)(2,1)} %bitcast.51), calls=%async_computation | async-start | bytes 3145728 | tf_op jit(solution)/shard_map/all_to_all | solution.py:305
  47.4 25.9 %collective-permute-start.5 = (f32[8,64,128]{2,1,0:T(8,128)}, f32[8,64,128]{2,1,0:T(8,128)}, u32[]{:S(2)}, u32[]{:S(2)}) collective-permute-start(f32[8,64,128]{2,1,0:T(8,128)} %broadcast_multiply_fusion), channel_id=1, source_target_pairs={{0,6},{2,4},{4,2},{6,0},{1,7},{3,5},{5,3},{7,1},{8,14},{10,12},{12... | collective-permute-start | bytes 786440 | tf_op jit(solution)/shard_map/ppermute | solution.py:215
  66.2 7.0 %copy-start.5 = (f32[8,64,128]{2,1,0:T(8,128)S(1)}, f32[8,64,128]{2,1,0:T(8,128)}, u32[]{:S(2)}) copy-start(f32[8,64,128]{2,1,0:T(8,128)} %param.13) | copy-start | bytes 786436
  67.3 10.9 %collective-permute-start.4 = (bf16[16,64,128]{2,1,0:T(8,128)(2,1)S(1)}, bf16[16,64,128]{2,1,0:T(8,128)(2,1)S(1)}, u32[]{:S(2)}, u32[]{:S(2)}) collective-permute-start(bf16[16,64,128]{2,1,0:T(8,128)(2,1)S(1)} %get-tuple-element.15), channel_id=1, source_target_pairs={{0,6},{2,4},{4,2},{6,0},{1,7},{3,5},{5,3},{7,1},{8,14},{10,12},{12... | collective-permute-start | bytes 786440 | tf_op jit(solution)/shard_map/ppermute | solution.py:215
  78.2 30.1 %copy-start.1 = (bf16[8,4,64,1024]{3,2,1,0:T(8,128)(2,1)S(1)}, bf16[8,4,64,1024]{3,2,1,0:T(8,128)(2,1)}, u32[]{:S(2)}) copy-start(bf16[8,4,64,1024]{3,2,1,0:T(8,128)(2,1)} %param.12) | copy-start | bytes 12582916
  78.9 29.4 %copy-start.2 = (bf16[32,96,128]{2,1,0:T(8,128)(2,1)S(1)}, bf16[32,96,128]{2,1,0:T(8,128)(2,1)}, u32[]{:S(2)}) copy-start(bf16[32,96,128]{2,1,0:T(8,128)(2,1)} %grad.3) | copy-start | bytes 2359300
  79.0 29.4 %copy-start.3 = (bf16[32,96,128]{2,1,0:T(8,128)(2,1)S(1)}, bf16[32,96,128]{2,1,0:T(8,128)(2,1)}, u32[]{:S(2)}) copy-start(bf16[32,96,128]{2,1,0:T(8,128)(2,1)} %state.3) | copy-start | bytes 2359300
  120.6 4.4 %collective-permute-start.7 = (bf16[96,128]{1,0:T(8,128)(2,1)S(1)}, bf16[96,128]{1,0:T(8,128)(2,1)S(1)}, u32[]{:S(2)}, u32[]{:S(2)}) collective-permute-start(bf16[96,128]{1,0:T(8,128)(2,1)S(1)} %get-tuple-element.25), channel_id=1, source_target_pairs={{8,0},{16,8},{24,16},{9,1},{17,9},{25,17},{10,2},{18,10},{26,18},{... | collective-permute-start | bytes 73736 | tf_op jit(solution)/shard_map/ppermute | solution.py:142
  122.0 3.9 %collective-permute-start.6 = (bf16[96,128]{1,0:T(8,128)(2,1)S(1)}, bf16[96,128]{1,0:T(8,128)(2,1)S(1)}, u32[]{:S(2)}, u32[]{:S(2)}) collective-permute-start(bf16[96,128]{1,0:T(8,128)(2,1)S(1)} %get-tuple-element.26), channel_id=1, source_target_pairs={{0,8},{8,16},{16,24},{1,9},{9,17},{17,25},{2,10},{10,18},{18,26},{... | collective-permute-start | bytes 73736 | tf_op jit(solution)/shard_map/ppermute | solution.py:141
  125.9 4.5 %collective-permute-start.8 = (bf16[34,128]{1,0:T(8,128)(2,1)S(1)}, bf16[34,128]{1,0:T(8,128)(2,1)S(1)}, u32[]{:S(2)}, u32[]{:S(2)}) collective-permute-start(bf16[34,128]{1,0:T(8,128)(2,1)S(1)} %pad_maximum_fusion.3), channel_id=1, source_target_pairs={{0,1},{1,2},{2,3},{3,4},{4,5},{5,6},{6,7},{8,9},{9,10},{10,11},{11... | collective-permute-start | bytes 26120 | tf_op jit(solution)/shard_map/ppermute | solution.py:145
  129.1 5.6 %collective-permute-start.9 = (bf16[34,128]{1,0:T(8,128)(2,1)S(1)}, bf16[34,128]{1,0:T(8,128)(2,1)S(1)}, u32[]{:S(2)}, u32[]{:S(2)}) collective-permute-start(bf16[34,128]{1,0:T(8,128)(2,1)S(1)} %pad_maximum_fusion.4), channel_id=1, source_target_pairs={{1,0},{2,1},{3,2},{4,3},{5,4},{6,5},{7,6},{9,8},{10,9},{11,10},{12... | collective-permute-start | bytes 26120 | tf_op jit(solution)/shard_map/ppermute | solution.py:146
  179.6 10.5 %collective-permute-start.10 = (bf16[16,64,128]{2,1,0:T(8,128)(2,1)S(1)}, bf16[16,64,128]{2,1,0:T(8,128)(2,1)S(1)}, u32[]{:S(2)}, u32[]{:S(2)}) collective-permute-start(bf16[16,64,128]{2,1,0:T(8,128)(2,1)S(1)} %get-tuple-element.19), channel_id=1, source_target_pairs={{0,6},{2,4},{4,2},{6,0},{1,7},{3,5},{5,3},{7,1},{8,14},{10,12},{12... | collective-permute-start | bytes 786440 | tf_op jit(solution)/shard_map/ppermute | solution.py:215

commit v3 on v1

v3 whole, which is shorter than its diff:
```python
import functools

import jax
import jax.numpy as jnp
from jax import lax
from jax.experimental import pallas as pl
from jax.experimental.pallas import tpu as pltpu
from jax.sharding import Mesh, PartitionSpec as P

PIX = 32
ANGLES = 8
HITS = 16
ITERS = 2
RING = 4
PARTS = 2

relax_rate = 0.25

COL = ("zh", "zl", "x")
GROUP = ("row", "zl", "x")

VMEM = pl.BlockSpec(memory_space=pltpu.VMEM)
SMEM = pl.BlockSpec(memory_space=pltpu.SMEM)
HBM = pl.BlockSpec(memory_space=pltpu.HBM)


def gather_kernel(mat_idx, rays, *refs):
    outs, sem = refs[:-1], refs[-1]
    part = outs[0].shape[1]

    def copy(q, h):
        source = rays.at[mat_idx[q], pl.ds(h * part, part)]
        return pltpu.make_async_copy(source, outs[h].at[q], sem.at[q, h])

    def begin(q, carry):
        for h in range(len(outs)):
            copy(q, h).start()
        return carry

    def finish(q, carry):
        for h in range(len(outs)):
            copy(q, h).wait()
        return carry

    pairs = outs[0].shape[0]
    lax.fori_loop(0, pairs, begin, 0)
    lax.fori_loop(0, pairs, finish, 0)


def project_tile(send_slot, matrices, low, out, t):
    hits = HITS
    part, tile_pix = matrices.shape[1:]
    matrix = matrices[pl.ds(t * hits, hits)].reshape(hits * part, tile_pix)
    value = jnp.dot(matrix, low, preferred_element_type=jnp.float32).astype(jnp.bfloat16)
    for k in range(hits):
        out[send_slot[t * hits + k]] = value[k * part : (k + 1) * part, :]


def conv_kernel(
    send_slot, scaled, above, below, left, right, taps, matrices,
    pulled, low, out, wide, cols3, *, tile_cols,
):
    rows, cols, chans = scaled.shape
    tile_pix = PIX * PIX
    half = PIX // 2
    f32, bf16 = jnp.float32, jnp.bfloat16
    wide[0, 8 : 8 + cols, :] = above[...].astype(f32)
    wide[rows + 1, 8 : 8 + cols, :] = below[...].astype(f32)
    wide[1 : rows + 1, 8 : 8 + cols, :] = scaled[...].astype(f32)
    lefts = left[...].astype(f32)
    rights = right[...].astype(f32)
    for r in range(rows + 2):
        wide[r, 7:8, :] = lefts[r : r + 1, :]
        wide[r, 8 + cols : 9 + cols, :] = rights[r : r + 1, :]
    for dc in range(3):
        value = wide[:, 7 + dc : 7 + dc + cols, :].astype(bf16)
        cols3[:, :, :, dc * chans : (dc + 1) * chans] = value.reshape(
            (rows + 2) // 2, 2, cols, chans
        )
    out[...] = jnp.zeros_like(out)

    def body(t, carry):
        r0 = (t // tile_cols) * half
        c0 = pl.multiple_of((t % tile_cols) * PIX, PIX)
        acc = None
        for dr in range(4):
            window = cols3[pl.ds(r0 + dr // 2, half), dr % 2, pl.ds(c0, PIX), :]
            term = jnp.dot(
                window.reshape(half * PIX, 3 * chans), taps[dr], preferred_element_type=f32
            )
            acc = term if acc is None else acc + term
        for odd in range(2):
            value = acc[:, odd * chans : (odd + 1) * chans].reshape(half, PIX, chans)
            pulled[t, :, odd] = value
            low[t, :, odd] = value.astype(bf16)
        project_tile(send_slot, matrices, low[t].reshape(tile_pix, chans), out, t)
        return carry

    lax.fori_loop(0, pulled.shape[0], body, 0)


def project_kernel(send_slot, low, matrices, out):
    tiles = low.shape[0]
    chans = low.shape[-1]
    out[...] = jnp.zeros_like(out)

    def body(t, carry):
        project_tile(send_slot, matrices, low[t].reshape(PIX * PIX, chans), out, t)
        return carry

    lax.fori_loop(0, tiles, body, 0)


def combine_kernel(table, recv, total, low, acc):
    acc[...] = jnp.zeros_like(acc)

    def body(j, carry):
        acc[table[j]] += recv[j].astype(jnp.float32)
        return carry

    lax.fori_loop(0, recv.shape[0], body, 0, unroll=8)
    total[...] = acc[: total.shape[0]]
    low[...] = acc[: total.shape[0]].astype(jnp.bfloat16)


def reply_kernel(table, total, other, scaling, out, held):
    n = total.shape[0]
    held[:n] = (scaling[...] * (total[...] + other[...].astype(jnp.float32))).astype(jnp.bfloat16)
    held[n] = jnp.zeros(held.shape[1:], jnp.bfloat16)

    def body(j, carry):
        out[j] = held[table[j]]
        return carry

    lax.fori_loop(0, out.shape[0], body, 0, unroll=8)


def back_tile(send_slot, returned, matrices, picked, t):
    part, tile_pix = matrices.shape[1:]
    for k in range(HITS):
        picked[k * part : (k + 1) * part, :] = returned[send_slot[t * HITS + k]]
    matrix = matrices[pl.ds(t * HITS, HITS)].reshape(HITS * part, tile_pix)
    return lax.dot_general(
        matrix, picked[...], (((0,), (0,)), ((), ())), preferred_element_type=jnp.float32
    )


def back_kernel(send_slot, returned, matrices, so_far, out, picked):
    tiles = so_far.shape[0]

    def body(t, carry):
        backed = back_tile(send_slot, returned, matrices, picked, t)
        out[t] = so_far[t] - relax_rate * backed.reshape(so_far.shape[1:])
        return carry

    lax.fori_loop(0, tiles, body, 0)


def finish_kernel(
    send_slot, returned, matrices, so_far, grad, state, *refs, tile_cols, last,
):
    outs, picked = refs[:-1], refs[-1]
    tiles = so_far.shape[0]
    cols, chans = grad.shape[1:]

    def body(t, carry):
        backed = back_tile(send_slot, returned, matrices, picked, t)
        change = so_far[t].reshape(backed.shape) - relax_rate * backed
        where = (
            pl.ds((t // tile_cols) * PIX, PIX),
            pl.ds(pl.multiple_of((t % tile_cols) * PIX, PIX), PIX),
        )
        adjoint = grad[where].astype(jnp.float32) + change.reshape(PIX, PIX, chans)
        if last:
            outs[0][where] = adjoint
        else:
            value = state[where].astype(jnp.float32)
            outs[0][where] = ((1.0 - value * value) * adjoint).astype(jnp.bfloat16)
        return carry

    lax.fori_loop(0, tiles, body, 0)


def halo_of(scaled):
    rows, cols, chans = scaled.shape
    nr = lax.axis_size("row")
    nc = lax.axis_size(COL)
    up = [(i, i + 1) for i in range(nr - 1)]
    down = [(b, a) for a, b in up]
    right = [(i, i + 1) for i in range(nc - 1)]
    left = [(b, a) for a, b in right]
    above = lax.ppermute(scaled[rows - 1], "row", up)
    below = lax.ppermute(scaled[0], "row", down)
    last = jnp.concatenate([above[cols - 1 :], scaled[:, cols - 1], below[cols - 1 :]], axis=0)
    first = jnp.concatenate([above[:1], scaled[:, 0], below[:1]], axis=0)
    lefts = lax.ppermute(last, COL, right)
    rights = lax.ppermute(first, COL, left)
    return above, below, lefts, rights


def on_device(state, grad, kernel, ray_matrix, ray_weight, hits, offsets, block_slot, angle_count):
    f32, bf16, i32 = jnp.float32, jnp.bfloat16, jnp.int32
    rows_dev, cols_dev, chans = state.shape
    angles, spots, bins, tile_pix = ray_matrix.shape
    nr = lax.axis_size("row")
    nx = lax.axis_size("x")
    nc = lax.axis_size(COL)
    devices = nr * nc
    row, zh, zl, x = (lax.axis_index(a) for a in ("row",) + COL)
    tile_rows = rows_dev // PIX
    tile_cols = cols_dev // PIX
    tiles = tile_rows * tile_cols
    pairs = tiles * HITS
    blk_dev = ray_weight.shape[0]
    blocks = blk_dev * devices
    blk_ang = blocks // ANGLES
    cap = 2 * max(2, (pairs + devices - 2) // devices + 1)
    cap = min(cap, pairs)
    peers = nr * 2 * nx
    slots = peers * cap
    dense = 2 * blk_dev
    part = bins // PARTS

    scaled = (
        (1.0 - jnp.square(state.astype(f32))) * grad.astype(f32)
    ).astype(bf16)
    halo = halo_of(scaled)

    everyone = hits.reshape(nr, tile_rows, nc, tile_cols, HITS).transpose(0, 2, 1, 3, 4)
    everyone = everyone.reshape(nr, 2, 2, nx, pairs)
    group = lax.dynamic_index_in_dim(everyone, zh, 1, keepdims=False).reshape(peers, pairs)
    storage = jnp.sum(
        jnp.where(group[:, :, None] == jnp.arange(blocks, dtype=i32), block_slot, 0), axis=2
    )
    owner = storage // blk_dev
    local = storage % blk_dev
    owner_z = (owner % nc) // nx
    owner_zh = owner_z // 2
    owner_zl = owner_z % 2
    side = jnp.where(owner_zh == zh, owner_zl, 1 - owner_zl)
    peer = ((owner // nc) * 2 + side) * nx + owner % nx
    place = owner_zh * blk_dev + local
    earlier = jnp.arange(pairs)[None, :] < jnp.arange(pairs)[:, None]
    ranking = jnp.sum(
        ((peer[:, :, None] == peer[:, None, :]) & earlier[None]).astype(i32), axis=2
    )
    me = (row * 2 + zl) * nx + x
    my_hits = lax.dynamic_index_in_dim(group, me, 0, keepdims=False)
    send_slot = lax.dynamic_index_in_dim(peer * cap + ranking, me, 0, keepdims=False)
    matched = (peer[:, None, :] == me) & (
        ranking[:, None, :] == jnp.arange(cap, dtype=i32)[None, :, None]
    )
    table = dense + jnp.sum(jnp.where(matched, place[:, None, :] - dense, 0), axis=2)
    table = table.reshape(slots)
    mat_idx = (my_hits // blk_ang) * spots + offsets.reshape(pairs)

    own_place = (row * nc + (zh * 2 + zl) * nx + x) * blk_dev + jnp.arange(blk_dev, dtype=i32)
    number = jnp.arange(blocks, dtype=i32)
    used = (
        (number % blk_ang).reshape(ANGLES, blk_ang) < angle_count[:, None]
    ).reshape(1, blocks)
    inuse = jnp.any((block_slot[None, :] == own_place[:, None]) & used, axis=1).astype(f32)
    own_scale = inuse[:, None, None] * ray_weight
    swap = [(z, RING - 1 - z) for z in range(RING)]

    def exchange(value):
        return lax.ppermute(value, ("zh", "zl"), swap)

    other_scale = exchange(own_scale)
    scaling = jnp.concatenate(
        [jnp.where(zh == 0, own_scale, other_scale), jnp.where(zh == 0, other_scale, own_scale)]
    )
    scalings = [scaling[:, h * part : (h + 1) * part] for h in range(PARTS)]
    taps = kernel[::-1, ::-1].transpose(0, 1, 3, 2).reshape(3, 3 * chans, chans)
    blank = jnp.zeros_like(taps[:1])
    taps = jnp.concatenate(
        [jnp.concatenate([taps, blank]), jnp.concatenate([blank, taps])], axis=2
    )
    rays = ray_matrix.reshape(angles * spots, bins, tile_pix)

    block = (part, chans)
    tiled = (tiles, PIX // 2, 2, PIX, chans)
    shape = jax.ShapeDtypeStruct
    slot_out = shape((slots,) + block, bf16)

    def limit(mib):
        return pltpu.CompilerParams(vmem_limit_bytes=mib << 20)

    gather = pl.pallas_call(
        gather_kernel,
        out_shape=[shape((pairs, part, tile_pix), bf16)] * PARTS,
        in_specs=[SMEM, HBM],
        out_specs=[VMEM] * PARTS,
        scratch_shapes=[pltpu.SemaphoreType.DMA((pairs, PARTS))],
        compiler_params=limit(8),
        name="gather",
    )
    conv = pl.pallas_call(
        functools.partial(conv_kernel, tile_cols=tile_cols),
        out_shape=(shape(tiled, f32), shape(tiled, bf16), slot_out),
        in_specs=[SMEM] + [VMEM] * 7,
        out_specs=(VMEM, VMEM, VMEM),
        scratch_shapes=[
            pltpu.VMEM((rows_dev + 2, cols_dev + 16, chans), f32),
            pltpu.VMEM(((rows_dev + 2) // 2, 2, cols_dev, 3 * chans), bf16),
        ],
        compiler_params=limit(20),
        name="conv",
    )
    project = pl.pallas_call(
        project_kernel,
        out_shape=slot_out,
        in_specs=[SMEM, VMEM, VMEM],
        out_specs=VMEM,
        compiler_params=limit(12),
        name="project",
    )
    combine = pl.pallas_call(
        combine_kernel,
        out_shape=(shape((dense,) + block, f32), shape((dense,) + block, bf16)),
        in_specs=[SMEM, VMEM],
        out_specs=(VMEM, VMEM),
        scratch_shapes=[pltpu.VMEM((dense + 1,) + block, f32)],
        compiler_params=limit(8),
        name="combine",
    )
    reply = pl.pallas_call(
        reply_kernel,
        out_shape=slot_out,
        in_specs=[SMEM, VMEM, VMEM, VMEM],
        out_specs=VMEM,
        scratch_shapes=[pltpu.VMEM((dense + 1,) + block, bf16)],
        compiler_params=limit(8),
        name="reply",
    )
    picked = pltpu.VMEM((HITS * part, chans), bf16)
    back = pl.pallas_call(
        back_kernel,
        out_shape=shape(tiled, f32),
        in_specs=[SMEM] + [VMEM] * 3,
        out_specs=VMEM,
        scratch_shapes=[picked],
        compiler_params=limit(16),
        name="back",
    )

    def finish(last):
        return pl.pallas_call(
            functools.partial(finish_kernel, tile_cols=tile_cols, last=last),
            out_shape=[shape(state.shape, f32 if last else bf16)],
            in_specs=[SMEM] + [VMEM] * 5,
            out_specs=[VMEM],
            scratch_shapes=[picked],
            compiler_params=limit(16),
            name="finish",
        )

    def across(value):
        value = value.reshape((peers, cap) + block)
        value = lax.all_to_all(value, GROUP, split_axis=0, concat_axis=0, tiled=True)
        return value.reshape((slots,) + block)

    mats = gather(mat_idx, rays)
    for turn in range(ITERS):
        if turn:
            halo = halo_of(scaled)
        pulled, low, first = conv(send_slot, scaled, *halo, taps, mats[0])
        sent = [first] + [project(send_slot, low, mats[h]) for h in range(1, PARTS)]
        replies = []
        for h in range(PARTS):
            total, mine = combine(table, across(sent[h]))
            replies.append(reply(table, total, exchange(mine), scalings[h]))
        so_far = pulled
        for h in range(PARTS - 1):
            so_far = back(send_slot, across(replies[h]), mats[h], so_far)
        last = turn == ITERS - 1
        (scaled,) = finish(last)(
            send_slot, across(replies[-1]), mats[-1], so_far, grad, state
        )
    return scaled


def solution(mesh):
    nr, nc = mesh.devices.shape
    fine = Mesh(mesh.devices.reshape(nr, 2, RING // 2, nc // RING), ("row",) + COL)
    image = P("row", COL, None)
    placed = (
        image,
        image,
        P(),
        P(),
        P(("row",) + COL, None, None),
        P(),
        image,
        P(),
        P(),
    )
    return jax.shard_map(
        on_device, mesh=fine, in_specs=placed, out_specs=image, check_vma=False
    )
```

time: 225 us -> 238 us (1.058)
  blocking collectives: 84.1 us -> 0 us
  starting transfers between devices: 32.5 us -> 70.1 us
  waiting for transfers between devices: 40.5 us -> 76.8 us
  local copies, waits for them, and re-layouts: 7.57 us -> 34.4 us
  Pallas kernels: 53.1 us -> 48 us
    all_to_all x3 -> x0, blocking collectives: 84.1 us -> none  [across(): lax.all_to_all(value, GROUP, split_axis=0, concat_axis=0, tiled=True)]
    all_to_all x1 -> x8, starting transfers between devices: 6.53 us -> 38.5 us  [across(): lax.all_to_all(value, GROUP, split_axis=0, concat_axis=0, tiled=True)]
    ppermute x3 -> x5, waiting for transfers between devices: 16 us -> 46.3 us  [exchange(): return lax.ppermute(value, ('zh', 'zl'), swap)]
    unnamed x41 -> x87, local copies, waits for them, and re-layouts: 3.91 us -> 33.6 us
    all_to_all x1 -> x8, waiting for transfers between devices: 16.6 us -> 25.5 us  [across(): lax.all_to_all(value, GROUP, split_axis=0, concat_axis=0, tiled=True)]
    ppermute x3 -> x5, starting transfers between devices: 6.73 us -> 12.1 us  [exchange(): return lax.ppermute(value, ('zh', 'zl'), swap)]
    pallas_call x8 -> x17, Pallas kernels: 53.1 us -> 48 us  [the longest x2 12.1 us: on_device(): pulled, low, first = conv(send_slot, scaled, *halo, taps, mats[0])]
    ppermute x2, waiting for transfers between devices: 7.07 us -> 4.22 us  [halo_of(): rights = lax.ppermute(first, COL, left)]
  transfers between devices with their start and end apart: 12 -> 21, of which waited for: 6 -> 11; matrix products, arithmetic and copies ran while one was open for 3% -> 2% of each run, Pallas kernels for 2% -> 12%
where the time goes in v3:
time: 238 us; the launch traced here: 236 us
  waiting for transfers between devices  76.8 us (32%)
  starting transfers between devices  70.1 us (29%)
  Pallas kernels  48 us (20%)
  local copies, waits for them, and re-layouts  34.4 us (14%)
  other arithmetic  6.09 us (3%)
    ppermute x5, waiting for transfers between devices, exchange(): return lax.ppermute(value, ('zh', 'zl'), swap)  46.3 us
    all_to_all x8, starting transfers between devices, across(): lax.all_to_all(value, GROUP, split_axis=0, concat_axis=0, tiled=True)  38.5 us
    unnamed x87, local copies, waits for them, and re-layouts  33.6 us
    all_to_all x8, waiting for transfers between devices, across(): lax.all_to_all(value, GROUP, split_axis=0, concat_axis=0, tiled=True)  25.5 us
    ppermute x5, starting transfers between devices, exchange(): return lax.ppermute(value, ('zh', 'zl'), swap)  12.1 us
    pallas_call x2, Pallas kernels, on_device(): pulled, low, first = conv(send_slot, scaled, *halo, taps, mats[0])  12.1 us
    pallas_call x1, Pallas kernels, on_device(): mats = gather(mat_idx, rays)  10.5 us
    ppermute x2, starting transfers between devices, halo_of(): lefts = lax.ppermute(last, COL, right)  8.2 us
  transfers between devices with their start and end apart: 21, of which 11 were waited for; matrix products, arithmetic and copies ran while one was open for 2% of the time, Pallas kernels for 12%

profile of v3, /device:TPU:0, one launch (start us, length us, event | category | flops | bytes accessed | tf_op | source)
XLA Modules:
  0.0 236.2 jit_solution(12884002419219767568)
XLA Ops:
  3.1 3.0 %collective-permute-start = (bf16[96,128]{1,0:T(8,128)(2,1)S(1)}, bf16[96,128]{1,0:T(8,128)(2,1)S(1)}, u32[]{:S(2)}, u32[]{:S(2)}) collective-permute-start(bf16[96,128]{1,0:T(8,128)(2,1)S(1)} %get-tuple-element.46), channel_id=1, source_target_pairs={{0,8},{8,16},{16,24},{1,9},{9,17},{17,25},{2,10},{10,18},{18,26},{... | collective-permute-start | bytes 73736 | tf_op jit(solution)/shard_map/ppermute | solution.py:192
  8.9 4.9 %collective-permute-start.2 = (bf16[34,128]{1,0:T(8,128)(2,1)S(1)}, bf16[34,128]{1,0:T(8,128)(2,1)S(1)}, u32[]{:S(2)}, u32[]{:S(2)}) collective-permute-start(bf16[34,128]{1,0:T(8,128)(2,1)S(1)} %pad_maximum_fusion.1), channel_id=1, source_target_pairs={{0,1},{1,2},{2,3},{3,4},{4,5},{5,6},{6,7},{8,9},{9,10},{10,11},{11... | collective-permute-start | bytes 26120 | tf_op jit(solution)/shard_map/ppermute | solution.py:196
  17.3 10.5 %gather.1 = (bf16[48,32,1024]{2,1,0:T(8,128)(2,1)S(1)}, bf16[48,32,1024]{2,1,0:T(8,128)(2,1)S(1)}) custom-call(s32[48]{0:T(128)S(1)} %multiply_add_fusion.mat_idx, bf16[32,64,1024]{2,1,0:T(8,128)(2,1)S(1)} %bitcast.47), custom_call_target="tpu_custom_call" | custom-call | tf_op jit(solution)/shard_map/gather/pallas_call | solution.py:363
  27.8 6.0 %conv.2 = (f32[3,16,2,32,128]{4,3,2,1,0:T(8,128)S(1)}, bf16[3,16,2,32,128]{4,3,2,1,0:T(8,128)(2,1)S(1)}, bf16[96,32,128]{2,1,0:T(8,128)(2,1)S(1)}) custom-call(s32[48]{0:T(128)S(1)} %fusion.24.send_slot, bf16[32,96,128]{2,1,0:T(8,128)(2,1)S(1)} %copy-done.16, bf16[96,128]{1,0:T(8,128)(2,1)S(1)} %collective-permute-done.above, ...), custom_call_target="tpu_custom_call" | custom-call | tf_op jit(solution)/shard_map/conv/pallas_call | solution.py:367
  36.8 6.2 %all-to-all-start.2 = ((bf16[16,6,32,128]{3,2,1,0:T(8,128)(2,1)}), bf16[16,6,32,128]{3,2,1,0:T(8,128)(2,1)}, u32[]{:S(2)}, u32[]{:S(2)}) async-start(bf16[16,6,32,128]{3,2,1,0:T(8,128)(2,1)} %bitcast.54), calls=%async_computation.2 | async-start | bytes 1572864 | tf_op jit(solution)/shard_map/all_to_all | solution.py:360
  47.2 7.8 %all-to-all-done.2 = bf16[16,6,32,128]{3,2,1,0:T(8,128)(2,1)} async-done(((bf16[16,6,32,128]{3,2,1,0:T(8,128)(2,1)}), bf16[16,6,32,128]{3,2,1,0:T(8,128)(2,1)}, u32[]{:S(2)}, u32[]{:S(2)}) %all-to-all-start.2) | async-done | bytes 786464 | tf_op jit(solution)/shard_map/all_to_all | solution.py:360
  55.0 4.3 %all-to-all-start = ((bf16[16,6,32,128]{3,2,1,0:T(8,128)(2,1)}), bf16[16,6,32,128]{3,2,1,0:T(8,128)(2,1)}, u32[]{:S(2)}, u32[]{:S(2)}) async-start(bf16[16,6,32,128]{3,2,1,0:T(8,128)(2,1)} %bitcast.48), calls=%async_computation | async-start | bytes 1572864 | tf_op jit(solution)/shard_map/all_to_all | solution.py:360
  60.3 4.1 %collective-permute-start.5 = (f32[8,64,128]{2,1,0:T(8,128)}, f32[8,64,128]{2,1,0:T(8,128)}, u32[]{:S(2)}, u32[]{:S(2)}) collective-permute-start(f32[8,64,128]{2,1,0:T(8,128)} %broadcast_multiply_fusion), channel_id=1, source_target_pairs={{0,6},{2,4},{4,2},{6,0},{1,7},{3,5},{5,3},{7,1},{8,14},{10,12},{12... | collective-permute-start | bytes 786440 | tf_op jit(solution)/shard_map/ppermute | solution.py:267
  66.5 12.9 %collective-permute-done.5 = f32[8,64,128]{2,1,0:T(8,128)} collective-permute-done((f32[8,64,128]{2,1,0:T(8,128)}, f32[8,64,128]{2,1,0:T(8,128)}, u32[]{:S(2)}, u32[]{:S(2)}) %collective-permute-start.5) | collective-permute-done | bytes 262176 | tf_op jit(solution)/shard_map/ppermute | solution.py:267
  83.9 4.3 %all-to-all-start.3 = ((bf16[16,6,32,128]{3,2,1,0:T(8,128)(2,1)}), bf16[16,6,32,128]{3,2,1,0:T(8,128)(2,1)}, u32[]{:S(2)}, u32[]{:S(2)}) async-start(bf16[16,6,32,128]{3,2,1,0:T(8,128)(2,1)} %bitcast.51), calls=%async_computation.3 | async-start | bytes 1572864 | tf_op jit(solution)/shard_map/all_to_all | solution.py:360
  89.8 2.8 %collective-permute-start.4 = (bf16[16,32,128]{2,1,0:T(8,128)(2,1)S(1)}, bf16[16,32,128]{2,1,0:T(8,128)(2,1)S(1)}, u32[]{:S(2)}, u32[]{:S(2)}) collective-permute-start(bf16[16,32,128]{2,1,0:T(8,128)(2,1)S(1)} %get-tuple-element.25), channel_id=1, source_target_pairs={{0,6},{2,4},{4,2},{6,0},{1,7},{3,5},{5,3},{7,1},{8,14},{10,12},{12... | collective-permute-start | bytes 393224 | tf_op jit(solution)/shard_map/ppermute | solution.py:267
  92.6 10.8 %collective-permute-done.4.other = bf16[16,32,128]{2,1,0:T(8,128)(2,1)S(1)} collective-permute-done((bf16[16,32,128]{2,1,0:T(8,128)(2,1)S(1)}, bf16[16,32,128]{2,1,0:T(8,128)(2,1)S(1)}, u32[]{:S(2)}, u32[]{:S(2)}) %collective-permute-start.4) | collective-permute-done | bytes 131104 | tf_op jit(solution)/shard_map/ppermute | solution.py:267
  105.1 4.3 %all-to-all-start.1 = ((bf16[16,6,32,128]{3,2,1,0:T(8,128)(2,1)}), bf16[16,6,32,128]{3,2,1,0:T(8,128)(2,1)}, u32[]{:S(2)}, u32[]{:S(2)}) async-start(bf16[16,6,32,128]{3,2,1,0:T(8,128)(2,1)} %bitcast.53), calls=%async_computation.1 | async-start | bytes 1572864 | tf_op jit(solution)/shard_map/all_to_all | solution.py:360
  112.7 2.7 %back.2.so_far = f32[3,16,2,32,128]{4,3,2,1,0:T(8,128)S(1)} custom-call(s32[48]{0:T(128)S(1)} %fusion.24.send_slot, bf16[96,32,128]{2,1,0:T(8,128)(2,1)} %bitcast.15.returned, bf16[48,32,1024]{2,1,0:T(8,128)(2,1)S(1)} %copy-done.1, f32[3,16,2,32,128]{4,3,2,1,0:T(8,128)S(1)} %copy-done.26), custom_call_target="tpu_custom_call" | custom-call | tf_op jit(solution)/shard_map/back/pallas_call | solution.py:375
  116.6 4.8 %all-to-all-done.1 = bf16[16,6,32,128]{3,2,1,0:T(8,128)(2,1)} async-done(((bf16[16,6,32,128]{3,2,1,0:T(8,128)(2,1)}), bf16[16,6,32,128]{3,2,1,0:T(8,128)(2,1)}, u32[]{:S(2)}, u32[]{:S(2)}) %all-to-all-start.1) | async-done | bytes 786464 | tf_op jit(solution)/shard_map/all_to_all | solution.py:360
  125.1 2.9 %finish.2.scaled = bf16[32,96,128]{2,1,0:T(8,128)(2,1)S(1)} custom-call(s32[48]{0:T(128)S(1)} %fusion.24.send_slot, bf16[96,32,128]{2,1,0:T(8,128)(2,1)} %bitcast.11.returned, bf16[48,32,1024]{2,1,0:T(8,128)(2,1)S(1)} %get-tuple-element.23.matrices, f32[3,16,2,32,128]{4,3,2,1,0:T(8,128)S(1)} %copy-done.13, bf16[32,96,128]{2,1,0:T(8,128)(2,1)S(1)} %copy-done.4, ...), custom_call_target="tpu_custom_call" | custom-call | tf_op jit(solution)/shard_map/finish/pallas_call | solution.py:377
  129.3 3.0 %collective-permute-start.7 = (bf16[96,128]{1,0:T(8,128)(2,1)S(1)}, bf16[96,128]{1,0:T(8,128)(2,1)S(1)}, u32[]{:S(2)}, u32[]{:S(2)}) collective-permute-start(bf16[96,128]{1,0:T(8,128)(2,1)S(1)} %get-tuple-element.42), channel_id=1, source_target_pairs={{0,8},{8,16},{16,24},{1,9},{9,17},{17,25},{2,10},{10,18},{18,26},{... | collective-permute-start | bytes 73736 | tf_op jit(solution)/shard_map/ppermute | solution.py:192
  133.2 3.3 %collective-permute-start.9 = (bf16[34,128]{1,0:T(8,128)(2,1)S(1)}, bf16[34,128]{1,0:T(8,128)(2,1)S(1)}, u32[]{:S(2)}, u32[]{:S(2)}) collective-permute-start(bf16[34,128]{1,0:T(8,128)(2,1)S(1)} %pad_maximum_fusion.3), channel_id=1, source_target_pairs={{0,1},{1,2},{2,3},{3,4},{4,5},{5,6},{6,7},{8,9},{9,10},{10,11},{11... | collective-permute-start | bytes 26120 | tf_op jit(solution)/shard_map/ppermute | solution.py:196
  137.9 4.2 %collective-permute-done.10.right = bf16[34,128]{1,0:T(8,128)(2,1)S(1)} collective-permute-done((bf16[34,128]{1,0:T(8,128)(2,1)S(1)}, bf16[34,128]{1,0:T(8,128)(2,1)S(1)}, u32[]{:S(2)}, u32[]{:S(2)}) %collective-permute-start.10) | collective-permute-done | bytes 8736 | tf_op jit(solution)/shard_map/ppermute | solution.py:197
  142.2 6.0 %conv.3 = (f32[3,16,2,32,128]{4,3,2,1,0:T(8,128)S(1)}, bf16[3,16,2,32,128]{4,3,2,1,0:T(8,128)(2,1)S(1)}, bf16[96,32,128]{2,1,0:T(8,128)(2,1)S(1)}) custom-call(s32[48]{0:T(128)S(1)} %fusion.24.send_slot, bf16[32,96,128]{2,1,0:T(8,128)(2,1)S(1)} %finish.2.scaled, bf16[96,128]{1,0:T(8,128)(2,1)S(1)} %collective-permute-done.7.above, ...), custom_call_target="tpu_custom_call" | custom-call | tf_op jit(solution)/shard_map/conv/pallas_call | solution.py:367
  151.1 6.6 %all-to-all-start.6 = ((bf16[16,6,32,128]{3,2,1,0:T(8,128)(2,1)}), bf16[16,6,32,128]{3,2,1,0:T(8,128)(2,1)}, u32[]{:S(2)}, u32[]{:S(2)}) async-start(bf16[16,6,32,128]{3,2,1,0:T(8,128)(2,1)} %bitcast.55), calls=%async_computation.6 | async-start | bytes 1572864 | tf_op jit(solution)/shard_map/all_to_all | solution.py:360
  161.7 8.0 %all-to-all-done.6 = bf16[16,6,32,128]{3,2,1,0:T(8,128)(2,1)} async-done(((bf16[16,6,32,128]{3,2,1,0:T(8,128)(2,1)}), bf16[16,6,32,128]{3,2,1,0:T(8,128)(2,1)}, u32[]{:S(2)}, u32[]{:S(2)}) %all-to-all-start.6) | async-done | bytes 786464 | tf_op jit(solution)/shard_map/all_to_all | solution.py:360
  169.7 4.3 %all-to-all-start.4 = ((bf16[16,6,32,128]{3,2,1,0:T(8,128)(2,1)}), bf16[16,6,32,128]{3,2,1,0:T(8,128)(2,1)}, u32[]{:S(2)}, u32[]{:S(2)}) async-start(bf16[16,6,32,128]{3,2,1,0:T(8,128)(2,1)} %bitcast.49), calls=%async_computation.4 | async-start | bytes 1572864 | tf_op jit(solution)/shard_map/all_to_all | solution.py:360
  175.6 2.2 collective-permute-start.12
  177.8 10.8 %collective-permute-done.12.other = bf16[16,32,128]{2,1,0:T(8,128)(2,1)S(1)} collective-permute-done((bf16[16,32,128]{2,1,0:T(8,128)(2,1)S(1)}, bf16[16,32,128]{2,1,0:T(8,128)(2,1)S(1)}, u32[]{:S(2)}, u32[]{:S(2)}) %collective-permute-start.12) | collective-permute-done | bytes 131104 | tf_op jit(solution)/shard_map/ppermute | solution.py:267
  191.3 4.3 %all-to-all-start.7 = ((bf16[16,6,32,128]{3,2,1,0:T(8,128)(2,1)}), bf16[16,6,32,128]{3,2,1,0:T(8,128)(2,1)}, u32[]{:S(2)}, u32[]{:S(2)}) async-start(bf16[16,6,32,128]{3,2,1,0:T(8,128)(2,1)} %bitcast.50), calls=%async_computation.7 | async-start | bytes 1572864 | tf_op jit(solution)/shard_map/all_to_all | solution.py:360
  197.2 2.9 %collective-permute-start.11 = (bf16[16,32,128]{2,1,0:T(8,128)(2,1)S(1)}, bf16[16,32,128]{2,1,0:T(8,128)(2,1)S(1)}, u32[]{:S(2)}, u32[]{:S(2)}) collective-permute-start(bf16[16,32,128]{2,1,0:T(8,128)(2,1)S(1)} %get-tuple-element.32), channel_id=1, source_target_pairs={{0,6},{2,4},{4,2},{6,0},{1,7},{3,5},{5,3},{7,1},{8,14},{10,12},{12... | collective-permute-start | bytes 393224 | tf_op jit(solution)/shard_map/ppermute | solution.py:267
  200.1 10.7 %collective-permute-done.11.other = bf16[16,32,128]{2,1,0:T(8,128)(2,1)S(1)} collective-permute-done((bf16[16,32,128]{2,1,0:T(8,128)(2,1)S(1)}, bf16[16,32,128]{2,1,0:T(8,128)(2,1)S(1)}, u32[]{:S(2)}, u32[]{:S(2)}) %collective-permute-start.11) | collective-permute-done | bytes 131104 | tf_op jit(solution)/shard_map/ppermute | solution.py:267
  212.4 4.3 %all-to-all-start.5 = ((bf16[16,6,32,128]{3,2,1,0:T(8,128)(2,1)}), bf16[16,6,32,128]{3,2,1,0:T(8,128)(2,1)}, u32[]{:S(2)}, u32[]{:S(2)}) async-start(bf16[16,6,32,128]{3,2,1,0:T(8,128)(2,1)} %bitcast.52), calls=%async_computation.5 | async-start | bytes 1572864 | tf_op jit(solution)/shard_map/all_to_all | solution.py:360
  220.0 2.7 %back.3.so_far = f32[3,16,2,32,128]{4,3,2,1,0:T(8,128)S(1)} custom-call(s32[48]{0:T(128)S(1)} %fusion.24.send_slot, bf16[96,32,128]{2,1,0:T(8,128)(2,1)} %bitcast.27.returned, bf16[48,32,1024]{2,1,0:T(8,128)(2,1)S(1)} %copy-done.3, f32[3,16,2,32,128]{4,3,2,1,0:T(8,128)S(1)} %copy-done.28), custom_call_target="tpu_custom_call" | custom-call | tf_op jit(solution)/shard_map/back/pallas_call | solution.py:375
  223.8 4.8 %all-to-all-done.5 = bf16[16,6,32,128]{3,2,1,0:T(8,128)(2,1)} async-done(((bf16[16,6,32,128]{3,2,1,0:T(8,128)(2,1)}), bf16[16,6,32,128]{3,2,1,0:T(8,128)(2,1)}, u32[]{:S(2)}, u32[]{:S(2)}) %all-to-all-start.5) | async-done | bytes 786464 | tf_op jit(solution)/shard_map/all_to_all | solution.py:360
  232.3 3.9 %finish.3 = f32[32,96,128]{2,1,0:T(8,128)} custom-call(s32[48]{0:T(128)S(1)} %fusion.24.send_slot, bf16[96,32,128]{2,1,0:T(8,128)(2,1)} %bitcast.23.returned, bf16[48,32,1024]{2,1,0:T(8,128)(2,1)S(1)} %get-tuple-element.23.matrices, f32[3,16,2,32,128]{4,3,2,1,0:T(8,128)S(1)} %copy-done.11, bf16[32,96,128]{2,1,0:T(8,128)(2,1)S(1)} %copy-done.5, ...), custom_call_target="tpu_custom_call" | custom-call | tf_op jit(solution)/shard_map/finish/pallas_call | solution.py:377
  (154 shorter events, 61.1 us)
Async XLA Ops:
  0.0 6.2 %copy-start.39 = (s32[1,3,16]{2,0,1:T(1,128)S(1)}, s32[1,3,16]{2,0,1:T(1,128)}, u32[]{:S(2)}) copy-start(s32[1,3,16]{2,0,1:T(1,128)} %param.15) | copy-start | bytes 580
  0.0 6.3 %copy-start.37 = (s32[4,24,16]{1,2,0:T(8,128)S(1)}, s32[4,24,16]{1,2,0:T(8,128)}, u32[]{:S(2)}) copy-start(s32[4,24,16]{1,2,0:T(8,128)} %param.14) | copy-start | bytes 18436
  0.0 6.5 %copy-start.38 = (s32[256]{0:T(256)S(1)}, s32[256]{0:T(256)}, u32[]{:S(2)}) copy-start(s32[256]{0:T(256)} %param.16) | copy-start | bytes 3076
  0.0 7.0 %copy-start.36 = (bf16[3,3,128,128]{3,2,1,0:T(8,128)(2,1)S(1)}, bf16[3,3,128,128]{3,2,1,0:T(8,128)(2,1)}, u32[]{:S(2)}) copy-start(bf16[3,3,128,128]{3,2,1,0:T(8,128)(2,1)} %param.11) | copy-start | bytes 884740
  1.7 13.3 %copy-start.15 = (bf16[32,96,128]{2,1,0:T(8,128)(2,1)}, bf16[32,96,128]{2,1,0:T(8,128)(2,1)S(1)}, u32[]{:S(2)}) copy-start(bf16[32,96,128]{2,1,0:T(8,128)(2,1)S(1)} %multiply_convert_fusion.scaled) | copy-start | bytes 2359300
  1.8 7.0 %collective-permute-start.1 = (bf16[96,128]{1,0:T(8,128)(2,1)S(1)}, bf16[96,128]{1,0:T(8,128)(2,1)S(1)}, u32[]{:S(2)}, u32[]{:S(2)}) collective-permute-start(bf16[96,128]{1,0:T(8,128)(2,1)S(1)} %get-tuple-element.45), channel_id=1, source_target_pairs={{8,0},{16,8},{24,16},{9,1},{17,9},{25,17},{10,2},{18,10},{26,18},{... | collective-permute-start | bytes 73736 | tf_op jit(solution)/shard_map/ppermute | solution.py:193
  3.1 5.8 %collective-permute-start = (bf16[96,128]{1,0:T(8,128)(2,1)S(1)}, bf16[96,128]{1,0:T(8,128)(2,1)S(1)}, u32[]{:S(2)}, u32[]{:S(2)}) collective-permute-start(bf16[96,128]{1,0:T(8,128)(2,1)S(1)} %get-tuple-element.46), channel_id=1, source_target_pairs={{0,8},{8,16},{16,24},{1,9},{9,17},{17,25},{2,10},{10,18},{18,26},{... | collective-permute-start | bytes 73736 | tf_op jit(solution)/shard_map/ppermute | solution.py:192
  8.9 18.9 %collective-permute-start.2 = (bf16[34,128]{1,0:T(8,128)(2,1)S(1)}, bf16[34,128]{1,0:T(8,128)(2,1)S(1)}, u32[]{:S(2)}, u32[]{:S(2)}) collective-permute-start(bf16[34,128]{1,0:T(8,128)(2,1)S(1)} %pad_maximum_fusion.1), channel_id=1, source_target_pairs={{0,1},{1,2},{2,3},{3,4},{4,5},{5,6},{6,7},{8,9},{9,10},{10,11},{11... | collective-permute-start | bytes 26120 | tf_op jit(solution)/shard_map/ppermute | solution.py:196
  13.8 14.0 %collective-permute-start.3 = (bf16[34,128]{1,0:T(8,128)(2,1)S(1)}, bf16[34,128]{1,0:T(8,128)(2,1)S(1)}, u32[]{:S(2)}, u32[]{:S(2)}) collective-permute-start(bf16[34,128]{1,0:T(8,128)(2,1)S(1)} %pad_maximum_fusion.2), channel_id=1, source_target_pairs={{1,0},{2,1},{3,2},{4,3},{5,4},{6,5},{7,6},{9,8},{10,9},{11,10},{12... | collective-permute-start | bytes 26120 | tf_op jit(solution)/shard_map/ppermute | solution.py:197
  17.3 10.5 %copy-start.8 = (bf16[4,384,256]{2,1,0:T(8,128)(2,1)S(1)}, bf16[4,384,256]{2,1,0:T(8,128)(2,1)}, u32[]{:S(2)}) copy-start(bf16[4,384,256]{2,1,0:T(8,128)(2,1)} %fusion.2.taps) | copy-start | bytes 2359300
  17.3 10.5 %copy-start.16 = (bf16[32,96,128]{2,1,0:T(8,128)(2,1)S(1)}, bf16[32,96,128]{2,1,0:T(8,128)(2,1)}, u32[]{:S(2)}) copy-start(bf16[32,96,128]{2,1,0:T(8,128)(2,1)} %copy-done.15) | copy-start | bytes 2359300
  36.8 6.2 %copy-start.40 = (s32[8]{0:T(128)S(1)}, s32[8]{0:T(128)}, u32[]{:S(2)}) copy-start(s32[8]{0:T(128)} %param.17) | copy-start | bytes 100
  36.8 18.2 %all-to-all-start.2 = ((bf16[16,6,32,128]{3,2,1,0:T(8,128)(2,1)}), bf16[16,6,32,128]{3,2,1,0:T(8,128)(2,1)}, u32[]{:S(2)}, u32[]{:S(2)}) async-start(bf16[16,6,32,128]{3,2,1,0:T(8,128)(2,1)} %bitcast.54), calls=%async_computation.2 | async-start | bytes 1572864 | tf_op jit(solution)/shard_map/all_to_all | solution.py:360
  47.2 12.3 %copy-start.35 = (f32[8,64,128]{2,1,0:T(8,128)S(1)}, f32[8,64,128]{2,1,0:T(8,128)}, u32[]{:S(2)}) copy-start(f32[8,64,128]{2,1,0:T(8,128)} %param.13) | copy-start | bytes 786436
  55.0 28.9 %all-to-all-start = ((bf16[16,6,32,128]{3,2,1,0:T(8,128)(2,1)}), bf16[16,6,32,128]{3,2,1,0:T(8,128)(2,1)}, u32[]{:S(2)}, u32[]{:S(2)}) async-start(bf16[16,6,32,128]{3,2,1,0:T(8,128)(2,1)} %bitcast.48), calls=%async_computation | async-start | bytes 1572864 | tf_op jit(solution)/shard_map/all_to_all | solution.py:360
  60.3 19.1 %collective-permute-start.5 = (f32[8,64,128]{2,1,0:T(8,128)}, f32[8,64,128]{2,1,0:T(8,128)}, u32[]{:S(2)}, u32[]{:S(2)}) collective-permute-start(f32[8,64,128]{2,1,0:T(8,128)} %broadcast_multiply_fusion), channel_id=1, source_target_pairs={{0,6},{2,4},{4,2},{6,0},{1,7},{3,5},{5,3},{7,1},{8,14},{10,12},{12... | collective-permute-start | bytes 786440 | tf_op jit(solution)/shard_map/ppermute | solution.py:267
  66.4 15.2 %collective-permute-start.6 = (bf16[16,32,128]{2,1,0:T(8,128)(2,1)S(1)}, bf16[16,32,128]{2,1,0:T(8,128)(2,1)S(1)}, u32[]{:S(2)}, u32[]{:S(2)}) collective-permute-start(bf16[16,32,128]{2,1,0:T(8,128)(2,1)S(1)} %get-tuple-element.28), channel_id=1, source_target_pairs={{0,6},{2,4},{4,2},{6,0},{1,7},{3,5},{5,3},{7,1},{8,14},{10,12},{12... | collective-permute-start | bytes 393224 | tf_op jit(solution)/shard_map/ppermute | solution.py:267
  83.9 21.2 %all-to-all-start.3 = ((bf16[16,6,32,128]{3,2,1,0:T(8,128)(2,1)}), bf16[16,6,32,128]{3,2,1,0:T(8,128)(2,1)}, u32[]{:S(2)}, u32[]{:S(2)}) async-start(bf16[16,6,32,128]{3,2,1,0:T(8,128)(2,1)} %bitcast.51), calls=%async_computation.3 | async-start | bytes 1572864 | tf_op jit(solution)/shard_map/all_to_all | solution.py:360
  89.8 13.7 %collective-permute-start.4 = (bf16[16,32,128]{2,1,0:T(8,128)(2,1)S(1)}, bf16[16,32,128]{2,1,0:T(8,128)(2,1)S(1)}, u32[]{:S(2)}, u32[]{:S(2)}) collective-permute-start(bf16[16,32,128]{2,1,0:T(8,128)(2,1)S(1)} %get-tuple-element.25), channel_id=1, source_target_pairs={{0,6},{2,4},{4,2},{6,0},{1,7},{3,5},{5,3},{7,1},{8,14},{10,12},{12... | collective-permute-start | bytes 393224 | tf_op jit(solution)/shard_map/ppermute | solution.py:267
  105.1 16.3 %all-to-all-start.1 = ((bf16[16,6,32,128]{3,2,1,0:T(8,128)(2,1)}), bf16[16,6,32,128]{3,2,1,0:T(8,128)(2,1)}, u32[]{:S(2)}, u32[]{:S(2)}) async-start(bf16[16,6,32,128]{3,2,1,0:T(8,128)(2,1)} %bitcast.53), calls=%async_computation.1 | async-start | bytes 1572864 | tf_op jit(solution)/shard_map/all_to_all | solution.py:360
  125.1 17.1 %copy-start.2 = (bf16[48,32,1024]{2,1,0:T(8,128)(2,1)S(1)}, bf16[48,32,1024]{2,1,0:T(8,128)(2,1)}, u32[]{:S(2)}) copy-start(bf16[48,32,1024]{2,1,0:T(8,128)(2,1)} %copy-done) | copy-start | bytes 9437188
  125.1 17.1 %copy-start.9 = (bf16[4,384,256]{2,1,0:T(8,128)(2,1)S(1)}, bf16[4,384,256]{2,1,0:T(8,128)(2,1)}, u32[]{:S(2)}) copy-start(bf16[4,384,256]{2,1,0:T(8,128)(2,1)} %fusion.2.taps) | copy-start | bytes 2359300
  128.0 4.4 %collective-permute-start.8 = (bf16[96,128]{1,0:T(8,128)(2,1)S(1)}, bf16[96,128]{1,0:T(8,128)(2,1)S(1)}, u32[]{:S(2)}, u32[]{:S(2)}) collective-permute-start(bf16[96,128]{1,0:T(8,128)(2,1)S(1)} %get-tuple-element.41), channel_id=1, source_target_pairs={{8,0},{16,8},{24,16},{9,1},{17,9},{25,17},{10,2},{18,10},{26,18},{... | collective-permute-start | bytes 73736 | tf_op jit(solution)/shard_map/ppermute | solution.py:193
  129.3 3.9 %collective-permute-start.7 = (bf16[96,128]{1,0:T(8,128)(2,1)S(1)}, bf16[96,128]{1,0:T(8,128)(2,1)S(1)}, u32[]{:S(2)}, u32[]{:S(2)}) collective-permute-start(bf16[96,128]{1,0:T(8,128)(2,1)S(1)} %get-tuple-element.42), channel_id=1, source_target_pairs={{0,8},{8,16},{16,24},{1,9},{9,17},{17,25},{2,10},{10,18},{18,26},{... | collective-permute-start | bytes 73736 | tf_op jit(solution)/shard_map/ppermute | solution.py:192
  133.2 4.7 %collective-permute-start.9 = (bf16[34,128]{1,0:T(8,128)(2,1)S(1)}, bf16[34,128]{1,0:T(8,128)(2,1)S(1)}, u32[]{:S(2)}, u32[]{:S(2)}) collective-permute-start(bf16[34,128]{1,0:T(8,128)(2,1)S(1)} %pad_maximum_fusion.3), channel_id=1, source_target_pairs={{0,1},{1,2},{2,3},{3,4},{4,5},{5,6},{6,7},{8,9},{9,10},{10,11},{11... | collective-permute-start | bytes 26120 | tf_op jit(solution)/shard_map/ppermute | solution.py:196
  136.6 5.6 %collective-permute-start.10 = (bf16[34,128]{1,0:T(8,128)(2,1)S(1)}, bf16[34,128]{1,0:T(8,128)(2,1)S(1)}, u32[]{:S(2)}, u32[]{:S(2)}) collective-permute-start(bf16[34,128]{1,0:T(8,128)(2,1)S(1)} %pad_maximum_fusion.4), channel_id=1, source_target_pairs={{1,0},{2,1},{3,2},{4,3},{5,4},{6,5},{7,6},{9,8},{10,9},{11,10},{12... | collective-permute-start | bytes 26120 | tf_op jit(solution)/shard_map/ppermute | solution.py:197
  151.1 18.6 %all-to-all-start.6 = ((bf16[16,6,32,128]{3,2,1,0:T(8,128)(2,1)}), bf16[16,6,32,128]{3,2,1,0:T(8,128)(2,1)}, u32[]{:S(2)}, u32[]{:S(2)}) async-start(bf16[16,6,32,128]{3,2,1,0:T(8,128)(2,1)} %bitcast.55), calls=%async_computation.6 | async-start | bytes 1572864 | tf_op jit(solution)/shard_map/all_to_all | solution.py:360
  169.7 21.6 %all-to-all-start.4 = ((bf16[16,6,32,128]{3,2,1,0:T(8,128)(2,1)}), bf16[16,6,32,128]{3,2,1,0:T(8,128)(2,1)}, u32[]{:S(2)}, u32[]{:S(2)}) async-start(bf16[16,6,32,128]{3,2,1,0:T(8,128)(2,1)} %bitcast.49), calls=%async_computation.4 | async-start | bytes 1572864 | tf_op jit(solution)/shard_map/all_to_all | solution.py:360
  175.6 13.0 %collective-permute-start.12 = (bf16[16,32,128]{2,1,0:T(8,128)(2,1)S(1)}, bf16[16,32,128]{2,1,0:T(8,128)(2,1)S(1)}, u32[]{:S(2)}, u32[]{:S(2)}) collective-permute-start(bf16[16,32,128]{2,1,0:T(8,128)(2,1)S(1)} %get-tuple-element.35), channel_id=1, source_target_pairs={{0,6},{2,4},{4,2},{6,0},{1,7},{3,5},{5,3},{7,1},{8,14},{10,12},{12... | collective-permute-start | bytes 393224 | tf_op jit(solution)/shard_map/ppermute | solution.py:267
  191.3 21.1 %all-to-all-start.7 = ((bf16[16,6,32,128]{3,2,1,0:T(8,128)(2,1)}), bf16[16,6,32,128]{3,2,1,0:T(8,128)(2,1)}, u32[]{:S(2)}, u32[]{:S(2)}) async-start(bf16[16,6,32,128]{3,2,1,0:T(8,128)(2,1)} %bitcast.50), calls=%async_computation.7 | async-start | bytes 1572864 | tf_op jit(solution)/shard_map/all_to_all | solution.py:360
  197.2 13.6 %collective-permute-start.11 = (bf16[16,32,128]{2,1,0:T(8,128)(2,1)S(1)}, bf16[16,32,128]{2,1,0:T(8,128)(2,1)S(1)}, u32[]{:S(2)}, u32[]{:S(2)}) collective-permute-start(bf16[16,32,128]{2,1,0:T(8,128)(2,1)S(1)} %get-tuple-element.32), channel_id=1, source_target_pairs={{0,6},{2,4},{4,2},{6,0},{1,7},{3,5},{5,3},{7,1},{8,14},{10,12},{12... | collective-permute-start | bytes 393224 | tf_op jit(solution)/shard_map/ppermute | solution.py:267
  212.4 16.3 %all-to-all-start.5 = ((bf16[16,6,32,128]{3,2,1,0:T(8,128)(2,1)}), bf16[16,6,32,128]{3,2,1,0:T(8,128)(2,1)}, u32[]{:S(2)}, u32[]{:S(2)}) async-start(bf16[16,6,32,128]{3,2,1,0:T(8,128)(2,1)} %bitcast.52), calls=%async_computation.5 | async-start | bytes 1572864 | tf_op jit(solution)/shard_map/all_to_all | solution.py:360
  (30 other events, 39.7 us)

commit v4 on v3

v4 whole, which is shorter than its diff:
```python
import functools

import jax
import jax.numpy as jnp
from jax import lax
from jax.experimental import pallas as pl
from jax.experimental.pallas import tpu as pltpu
from jax.sharding import Mesh, PartitionSpec as P

PIX = 32
ANGLES = 8
HITS = 16
ITERS = 2
RING = 4

relax_rate = 0.25

COL = ("zh", "zl", "x")
GROUP = ("row", "zl", "x")

VMEM = pl.BlockSpec(memory_space=pltpu.VMEM)
SMEM = pl.BlockSpec(memory_space=pltpu.SMEM)


def start_kernel(state, grad, scaled, top, bottom, left, right):
    value = state[...].astype(jnp.float32)
    value = (1.0 - value * value) * grad[...].astype(jnp.float32)
    emit_edges(value, scaled, top, bottom, left, right)


def emit_edges(value, scaled, top, bottom, left, right):
    rows, cols = value.shape[:2]
    scaled[...] = value.astype(jnp.bfloat16)
    top[...] = scaled[0]
    bottom[...] = scaled[rows - 1]
    left[...] = value[:, 0, :].astype(jnp.bfloat16)
    right[...] = value[:, cols - 1, :].astype(jnp.bfloat16)


def sides_kernel(above, below, left, right, first, last):
    rows = left.shape[0]
    cols = above.shape[0]
    f32 = jnp.float32
    for out, edge, at in ((first, left, 0), (last, right, cols - 1)):
        group = at // 16 * 16
        corner_a = above[group : group + 16, :].astype(f32)[at - group : at - group + 1, :]
        corner_b = below[group : group + 16, :].astype(f32)[at - group : at - group + 1, :]
        out[8 : 8 + rows, :] = edge[...].astype(f32)
        out[7:8, :] = corner_a
        out[8 + rows : 9 + rows, :] = corner_b


def load_matrices(mat_idx, rays, held, t):
    bins = rays.shape[1]
    for k in range(HITS):
        held[k * bins : (k + 1) * bins, :] = rays[mat_idx[t * HITS + k]]


def conv_kernel(
    mat_idx, send_slot, scaled, above, below, left, right, taps, rays,
    pulled, out, wide, cols3, held, *, tile_cols,
):
    rows, cols, chans = scaled.shape
    bins = rays.shape[1]
    half = PIX // 2
    f32, bf16 = jnp.float32, jnp.bfloat16
    wide[0, 8 : 8 + cols, :] = above[...].astype(f32)
    wide[rows + 1, 8 : 8 + cols, :] = below[...].astype(f32)
    wide[1 : rows + 1, 8 : 8 + cols, :] = scaled[...].astype(f32)
    for r in range(rows + 2):
        wide[r, 7:8, :] = left[7 + r : 8 + r, :]
        wide[r, 8 + cols : 9 + cols, :] = right[7 + r : 8 + r, :]
    for dc in range(3):
        value = wide[:, 7 + dc : 7 + dc + cols, :].astype(bf16)
        cols3[:, :, :, dc * chans : (dc + 1) * chans] = value.reshape(
            (rows + 2) // 2, 2, cols, chans
        )
    out[...] = jnp.zeros_like(out)

    def body(t, carry):
        r0 = (t // tile_cols) * half
        c0 = pl.multiple_of((t % tile_cols) * PIX, PIX)
        load_matrices(mat_idx, rays, held, t)
        acc = None
        for dr in range(4):
            window = cols3[pl.ds(r0 + dr // 2, half), dr % 2, pl.ds(c0, PIX), :]
            term = jnp.dot(
                window.reshape(half * PIX, 3 * chans), taps[dr], preferred_element_type=f32
            )
            acc = term if acc is None else acc + term
        for odd in range(2):
            value = acc[:, odd * chans : (odd + 1) * chans].reshape(half, PIX, chans)
            pulled[t, :, odd] = value
        low = pulled[t].reshape(PIX * PIX, chans).astype(bf16)
        value = jnp.dot(held[...], low, preferred_element_type=f32).astype(bf16)
        for k in range(HITS):
            out[send_slot[t * HITS + k]] = value[k * bins : (k + 1) * bins, :]
        return carry

    lax.fori_loop(0, pulled.shape[0], body, 0)


def combine_kernel(table, recv, total, low, acc):
    acc[...] = jnp.zeros_like(acc)

    def body(j, carry):
        acc[table[j]] += recv[j].astype(jnp.float32)
        return carry

    lax.fori_loop(0, recv.shape[0], body, 0, unroll=8)
    total[...] = acc[: total.shape[0]]
    low[...] = acc[: total.shape[0]].astype(jnp.bfloat16)


def reply_kernel(table, used, total, other, own_weight, other_weight, out, held):
    n = total.shape[0]
    own = own_weight.shape[0]
    place = used[n]
    for half, weight in enumerate((own_weight, other_weight)):
        first = jnp.where(half == 0, place, n - own - place)
        for b in range(own):
            d = first + b
            scale = used[d].astype(jnp.float32) * weight[b]
            value = total[d] + other[d].astype(jnp.float32)
            held[d] = (scale * value).astype(jnp.bfloat16)
    held[n] = jnp.zeros(held.shape[1:], jnp.bfloat16)

    def body(j, carry):
        out[j] = held[table[j]]
        return carry

    lax.fori_loop(0, out.shape[0], body, 0, unroll=8)


def finish_kernel(
    mat_idx, send_slot, returned, pulled, grad, state, rays, *refs, tile_cols, last,
):
    outs, (whole, picked, held) = refs[:-3], refs[-3:]
    tiles = pulled.shape[0]
    bins = rays.shape[1]
    chans = grad.shape[2]
    f32 = jnp.float32

    def body(t, carry):
        load_matrices(mat_idx, rays, held, t)
        for k in range(HITS):
            picked[k * bins : (k + 1) * bins, :] = returned[send_slot[t * HITS + k]]
        backed = lax.dot_general(
            held[...], picked[...], (((0,), (0,)), ((), ())), preferred_element_type=f32
        )
        change = pulled[t].reshape(backed.shape) - relax_rate * backed
        where = (
            pl.ds((t // tile_cols) * PIX, PIX),
            pl.ds(pl.multiple_of((t % tile_cols) * PIX, PIX), PIX),
        )
        adjoint = grad[where].astype(f32) + change.reshape(PIX, PIX, chans)
        if last:
            outs[0][where] = adjoint
        else:
            value = state[where].astype(f32)
            whole[where] = (1.0 - value * value) * adjoint
        return carry

    lax.fori_loop(0, tiles, body, 0)
    if not last:
        emit_edges(whole[...], *outs)


def on_device(state, grad, kernel, ray_matrix, ray_weight, hits, offsets, block_slot, angle_count):
    f32, bf16, i32 = jnp.float32, jnp.bfloat16, jnp.int32
    rows_dev, cols_dev, chans = state.shape
    angles, spots, bins, tile_pix = ray_matrix.shape
    nr = lax.axis_size("row")
    nx = lax.axis_size("x")
    nc = lax.axis_size(COL)
    devices = nr * nc
    row, zh, zl, x = (lax.axis_index(a) for a in ("row",) + COL)
    tile_rows = rows_dev // PIX
    tile_cols = cols_dev // PIX
    tiles = tile_rows * tile_cols
    pairs = tiles * HITS
    blk_dev = ray_weight.shape[0]
    blocks = blk_dev * devices
    blk_ang = blocks // ANGLES
    cap = 2 * max(2, (pairs + devices - 2) // devices + 1)
    cap = min(cap, pairs)
    peers = nr * 2 * nx
    slots = peers * cap
    dense = 2 * blk_dev
    swap = [(z, RING - 1 - z) for z in range(RING)]

    def exchange(value):
        return lax.ppermute(value, ("zh", "zl"), swap)

    other_weight = exchange(ray_weight)

    everyone = hits.reshape(nr, tile_rows, nc, tile_cols, HITS).transpose(0, 2, 1, 3, 4)
    everyone = everyone.reshape(nr, 2, 2, nx, pairs)
    group = lax.dynamic_index_in_dim(everyone, zh, 1, keepdims=False).reshape(peers, pairs)
    storage = jnp.sum(
        jnp.where(group[:, :, None] == jnp.arange(blocks, dtype=i32), block_slot, 0), axis=2
    )
    owner = storage // blk_dev
    local = storage % blk_dev
    owner_z = (owner % nc) // nx
    owner_zh = owner_z // 2
    owner_zl = owner_z % 2
    side = jnp.where(owner_zh == zh, owner_zl, 1 - owner_zl)
    peer = ((owner // nc) * 2 + side) * nx + owner % nx
    place = owner_zh * blk_dev + local
    earlier = jnp.arange(pairs)[None, :] < jnp.arange(pairs)[:, None]
    ranking = jnp.sum(
        ((peer[:, :, None] == peer[:, None, :]) & earlier[None]).astype(i32), axis=2
    )
    me = (row * 2 + zl) * nx + x
    my_hits = lax.dynamic_index_in_dim(group, me, 0, keepdims=False)
    send_slot = lax.dynamic_index_in_dim(peer * cap + ranking, me, 0, keepdims=False)
    matched = (peer[:, None, :] == me) & (
        ranking[:, None, :] == jnp.arange(cap, dtype=i32)[None, :, None]
    )
    table = dense + jnp.sum(jnp.where(matched, place[:, None, :] - dense, 0), axis=2)
    table = table.reshape(slots)
    mat_idx = (my_hits // blk_ang) * spots + offsets.reshape(pairs)

    my_z = zh * 2 + zl
    half = jnp.arange(dense, dtype=i32) // blk_dev
    dense_z = jnp.where(half == zh, my_z, RING - 1 - my_z)
    dense_place = (row * nc + dense_z * nx + x) * blk_dev + jnp.arange(dense, dtype=i32) % blk_dev
    number = jnp.arange(blocks, dtype=i32)
    active = (
        (number % blk_ang).reshape(ANGLES, blk_ang) < angle_count[:, None]
    ).reshape(1, blocks)
    used = jnp.any((block_slot[None, :] == dense_place[:, None]) & active, axis=1).astype(i32)
    used = jnp.concatenate([used, jnp.full((1,), zh * blk_dev, i32)])

    taps = kernel[::-1, ::-1].transpose(0, 1, 3, 2).reshape(3, 3 * chans, chans)
    blank = jnp.zeros_like(taps[:1])
    taps = jnp.concatenate(
        [jnp.concatenate([taps, blank]), jnp.concatenate([blank, taps])], axis=2
    )
    rays = ray_matrix.reshape(angles * spots, bins, tile_pix)

    block = (bins, chans)
    shape = jax.ShapeDtypeStruct
    slot_out = shape((slots,) + block, bf16)
    edges = (
        shape(state.shape, bf16),
        shape((cols_dev, chans), bf16),
        shape((cols_dev, chans), bf16),
        shape((rows_dev, chans), bf16),
        shape((rows_dev, chans), bf16),
    )

    def limit(mib):
        return pltpu.CompilerParams(vmem_limit_bytes=mib << 20)

    start = pl.pallas_call(
        start_kernel,
        out_shape=edges,
        in_specs=[VMEM] * 2,
        out_specs=(VMEM,) * 5,
        compiler_params=limit(8),
        name="start",
    )
    sides = pl.pallas_call(
        sides_kernel,
        out_shape=[shape((rows_dev + 16, chans), f32)] * 2,
        in_specs=[VMEM] * 4,
        out_specs=[VMEM] * 2,
        compiler_params=limit(4),
        name="sides",
    )
    held = pltpu.VMEM((HITS * bins, tile_pix), bf16)
    conv = pl.pallas_call(
        functools.partial(conv_kernel, tile_cols=tile_cols),
        out_shape=(shape((tiles, PIX // 2, 2, PIX, chans), f32), slot_out),
        in_specs=[SMEM] * 2 + [VMEM] * 7,
        out_specs=(VMEM, VMEM),
        scratch_shapes=[
            pltpu.VMEM((rows_dev + 2, cols_dev + 16, chans), f32),
            pltpu.VMEM(((rows_dev + 2) // 2, 2, cols_dev, 3 * chans), bf16),
            held,
        ],
        compiler_params=limit(20),
        name="conv",
    )
    combine = pl.pallas_call(
        combine_kernel,
        out_shape=(shape((dense,) + block, f32), shape((dense,) + block, bf16)),
        in_specs=[SMEM, VMEM],
        out_specs=(VMEM, VMEM),
        scratch_shapes=[pltpu.VMEM((dense + 1,) + block, f32)],
        compiler_params=limit(8),
        name="combine",
    )
    reply = pl.pallas_call(
        reply_kernel,
        out_shape=slot_out,
        in_specs=[SMEM] * 2 + [VMEM] * 4,
        out_specs=VMEM,
        scratch_shapes=[pltpu.VMEM((dense + 1,) + block, bf16)],
        compiler_params=limit(8),
        name="reply",
    )

    def finish(last):
        return pl.pallas_call(
            functools.partial(finish_kernel, tile_cols=tile_cols, last=last),
            out_shape=(shape(state.shape, f32),) if last else edges,
            in_specs=[SMEM] * 2 + [VMEM] * 5,
            out_specs=(VMEM,) * (1 if last else 5),
            scratch_shapes=[
                pltpu.VMEM((8, 128, 128) if last else state.shape, f32),
                pltpu.VMEM((HITS * bins, chans), bf16),
                held,
            ],
            compiler_params=limit(20),
            name="finish",
        )

    def across(value):
        value = value.reshape((peers, cap) + block)
        value = lax.all_to_all(value, GROUP, split_axis=0, concat_axis=0, tiled=True)
        return value.reshape((slots,) + block)

    up = [(i, i + 1) for i in range(nr - 1)]
    down = [(b, a) for a, b in up]
    rightward = [(i, i + 1) for i in range(nc - 1)]
    leftward = [(b, a) for a, b in rightward]

    def halo_of(top, bottom, left, right):
        above = lax.ppermute(bottom, "row", up)
        below = lax.ppermute(top, "row", down)
        first, last = sides(above, below, left, right)
        lefts = lax.ppermute(last, COL, rightward)
        rights = lax.ppermute(first, COL, leftward)
        return above, below, lefts, rights

    scaled, *rim = start(state, grad)
    halo = halo_of(*rim)
    for turn in range(ITERS):
        if turn:
            halo = halo_of(*rim)
        pulled, outgoing = conv(mat_idx, send_slot, scaled, *halo, taps, rays)
        if not turn:
            outgoing, table, used, other_weight = lax.optimization_barrier(
                (outgoing, table, used, other_weight)
            )
        total, mine = combine(table, across(outgoing))
        replies = reply(table, used, total, exchange(mine), ray_weight, other_weight)
        last = turn == ITERS - 1
        scaled, *rim = finish(last)(
            mat_idx, send_slot, across(replies), pulled, grad, state, rays
        )
    return scaled


def solution(mesh):
    nr, nc = mesh.devices.shape
    fine = Mesh(mesh.devices.reshape(nr, 2, RING // 2, nc // RING), ("row",) + COL)
    image = P("row", COL, None)
    placed = (
        image,
        image,
        P(),
        P(),
        P(("row",) + COL, None, None),
        P(),
        image,
        P(),
        P(),
    )
    return jax.shard_map(
        on_device, mesh=fine, in_specs=placed, out_specs=image, check_vma=False
    )
```

time: 238 us -> 195 us (0.82)
  blocking collectives: 0 us -> 106 us
  starting transfers between devices: 70.1 us -> 22.2 us
  waiting for transfers between devices: 76.8 us -> 30.6 us
  local copies, waits for them, and re-layouts: 34.4 us -> 5.31 us
  Pallas kernels: 48 us -> 28.2 us
  other arithmetic: 6.09 us -> 1.65 us
    all_to_all x0 -> x4, blocking collectives: none -> 106 us  [across(): lax.all_to_all(value, GROUP, split_axis=0, concat_axis=0, tiled=True)]
    all_to_all x8 -> x0, starting transfers between devices: 38.5 us -> none  [across(): lax.all_to_all(value, GROUP, split_axis=0, concat_axis=0, tiled=True)]
    unnamed x87 -> x25, local copies, waits for them, and re-layouts: 33.6 us -> 4.57 us
    ppermute x5 -> x3, waiting for transfers between devices: 46.3 us -> 18.4 us  [exchange(): return lax.ppermute(value, ('zh', 'zl'), swap)]
    all_to_all x8 -> x0, waiting for transfers between devices: 25.5 us -> none  [across(): lax.all_to_all(value, GROUP, split_axis=0, concat_axis=0, tiled=True)]
    pallas_call x17 -> x11, Pallas kernels: 48 us -> 28.2 us  [the longest x2 16.3 us: on_device(): pulled, outgoing = conv(mat_idx, send_slot, scaled, *halo, taps, rays)]
    ppermute x8, waiting for transfers between devices: 5.09 us -> 12.2 us  [the longest x2 8.38 us: halo_of(): rights = lax.ppermute(first, COL, leftward)]
    ppermute x8, starting transfers between devices: 19.4 us -> 14.6 us  [the longest x2 5.84 us: halo_of(): lefts = lax.ppermute(last, COL, rightward)]
  transfers between devices with their start and end apart: 21 -> 11, of which waited for: 11 -> 7; matrix products, arithmetic and copies ran while one was open for 2% -> 1% of each run, Pallas kernels for 12% -> 4%
where the time goes in v4:
time: 195 us; the launch traced here: 194 us
  blocking collectives  106 us (54%)
  waiting for transfers between devices  30.6 us (16%)
  Pallas kernels  28.2 us (14%)
  starting transfers between devices  22.2 us (11%)
  local copies, waits for them, and re-layouts  5.31 us (3%)
    all_to_all x4, blocking collectives, across(): lax.all_to_all(value, GROUP, split_axis=0, concat_axis=0, tiled=True)  106 us
    ppermute x3, waiting for transfers between devices, exchange(): return lax.ppermute(value, ('zh', 'zl'), swap)  18.4 us
    pallas_call x2, Pallas kernels, on_device(): pulled, outgoing = conv(mat_idx, send_slot, scaled, *halo, taps, rays)  16.3 us
    ppermute x2, waiting for transfers between devices, halo_of(): rights = lax.ppermute(first, COL, leftward)  8.38 us
    ppermute x3, starting transfers between devices, exchange(): return lax.ppermute(value, ('zh', 'zl'), swap)  7.56 us
    pallas_call x2, Pallas kernels, on_device(): finish(last)(mat_idx, send_slot, across(replies), pulled, grad, state, rays)  7.38 us
    ppermute x2, starting transfers between devices, halo_of(): lefts = lax.ppermute(last, COL, rightward)  5.84 us
    unnamed x25, local copies, waits for them, and re-layouts  4.57 us
  transfers between devices with their start and end apart: 11, of which 7 were waited for; matrix products, arithmetic and copies ran while one was open for 1% of the time, Pallas kernels for 4%

profile of v4, /device:TPU:0, one launch (start us, length us, event | category | flops | bytes accessed | tf_op | source)
XLA Modules:
  0.0 194.1 jit_solution(16864111339636986238)
XLA Ops:
  0.0 5.1 %collective-permute-start.4 = (f32[8,64,128]{2,1,0:T(8,128)}, f32[8,64,128]{2,1,0:T(8,128)S(1)}, u32[]{:S(2)}, u32[]{:S(2)}) collective-permute-start(f32[8,64,128]{2,1,0:T(8,128)} %own_weight.3), channel_id=1, source_target_pairs={{0,6},{2,4},{4,2},{6,0},{1,7},{3,5},{5,3},{7,1},{8,14},{10,12},{12... | collective-permute-start | bytes 786440 | tf_op jit(solution)/shard_map/ppermute | solution.py:193
  5.1 1.1 copy-done.2
  6.2 1.1 copy-done.4
  7.9 1.5 collective-permute-start
  9.4 1.3 collective-permute-start.1
  13.1 1.0 collective-permute-done.1.below
  14.1 3.4 %collective-permute-start.2 = (f32[48,128]{1,0:T(8,128)S(1)}, f32[48,128]{1,0:T(8,128)S(1)}, u32[]{:S(2)}, u32[]{:S(2)}) collective-permute-start(f32[48,128]{1,0:T(8,128)S(1)} %get-tuple-element.36), channel_id=1, source_target_pairs={{0,1},{1,2},{2,3},{3,4},{4,5},{5,6},{6,7},{8,9},{9,10},{10,11},{11... | collective-permute-start | bytes 73736 | tf_op jit(solution)/shard_map/ppermute | solution.py:335
  17.5 1.3 collective-permute-start.3
  19.0 4.2 %collective-permute-done.3.right = f32[48,128]{1,0:T(8,128)S(1)} collective-permute-done((f32[48,128]{1,0:T(8,128)S(1)}, f32[48,128]{1,0:T(8,128)S(1)}, u32[]{:S(2)}, u32[]{:S(2)}) %collective-permute-start.3) | collective-permute-done | bytes 24608 | tf_op jit(solution)/shard_map/ppermute | solution.py:336
  23.2 2.2 %copy-done = bf16[8,4,64,1024]{3,2,1,0:T(8,128)(2,1)S(1)} copy-done((bf16[8,4,64,1024]{3,2,1,0:T(8,128)(2,1)S(1)}, bf16[8,4,64,1024]{3,2,1,0:T(8,128)(2,1)}, u32[]{:S(2)}) %copy-start) | copy-done | bytes 4194328
  25.4 8.2 %conv.2 = (f32[3,16,2,32,128]{4,3,2,1,0:T(8,128)S(1)}, bf16[96,64,128]{2,1,0:T(8,128)(2,1)S(1)}) custom-call(s32[48]{0:T(128)S(1)} %multiply_add_fusion.mat_idx, s32[48]{0:T(128)S(1)} %fusion.28.send_slot, bf16[32,96,128]{2,1,0:T(8,128)(2,1)S(1)} %get-tuple-element.31.scaled, bf16[96,128]{1,0:T(8,128)(2,1)S(1)} %collective-permute-done.above, ...), custom_call_target="tpu_custom_call" | custom-call | tf_op jit(solution)/shard_map/conv/pallas_call | solution.py:344
  33.6 25.5 %all_to_all.20 = bf16[16,6,64,128]{3,2,1,0:T(8,128)(2,1)S(1)} all-to-all(bf16[16,6,64,128]{3,2,1,0:T(8,128)(2,1)S(1)} %bitcast.30), channel_id=1, replica_groups=mesh['row'=4,'zh'=2,'zl'=2,'x'=2] {'row','zl','x'}, dimensions={0} | all-to-all | bytes 3145728 | tf_op jit(solution)/shard_map/all_to_all | solution.py:323
  59.1 1.2 combine.2
  60.2 1.2 collective-permute-start.5
  61.4 9.2 %collective-permute-done.5.other = bf16[16,64,128]{2,1,0:T(8,128)(2,1)S(1)} collective-permute-done((bf16[16,64,128]{2,1,0:T(8,128)(2,1)S(1)}, bf16[16,64,128]{2,1,0:T(8,128)(2,1)S(1)}, u32[]{:S(2)}, u32[]{:S(2)}) %collective-permute-start.5) | collective-permute-done | bytes 262176 | tf_op jit(solution)/shard_map/ppermute | solution.py:193
  70.7 0.8 reply.2
  71.5 27.1 %all_to_all.21 = bf16[16,6,64,128]{3,2,1,0:T(8,128)(2,1)S(1)} all-to-all(bf16[16,6,64,128]{3,2,1,0:T(8,128)(2,1)S(1)} %bitcast.28), channel_id=1, replica_groups=mesh['row'=4,'zh'=2,'zl'=2,'x'=2] {'row','zl','x'}, dimensions={0} | all-to-all | bytes 3145728 | tf_op jit(solution)/shard_map/all_to_all | solution.py:323
  98.6 3.2 %finish.2 = (bf16[32,96,128]{2,1,0:T(8,128)(2,1)S(1)}, bf16[96,128]{1,0:T(8,128)(2,1)S(1)}, bf16[96,128]{1,0:T(8,128)(2,1)S(1)}, bf16[32,128]{1,0:T(8,128)(2,1)S(1)}, bf16[32,128]{1,0:T(8,128)(2,1)S(1)}) custom-call(s32[48]{0:T(128)S(1)} %multiply_add_fusion.mat_idx, s32[48]{0:T(128)S(1)} %fusion.28.send_slot, bf16[96,64,128]{2,1,0:T(8,128)(2,1)S(1)} %bitcast.24, ...), custom_call_target="tpu_custom_call" | custom-call | tf_op jit(solution)/shard_map/finish/pallas_call | solution.py:352
  101.7 2.2 %collective-permute-start.6 = (bf16[96,128]{1,0:T(8,128)(2,1)S(1)}, bf16[96,128]{1,0:T(8,128)(2,1)S(1)}, u32[]{:S(2)}, u32[]{:S(2)}) collective-permute-start(bf16[96,128]{1,0:T(8,128)(2,1)S(1)} %get-tuple-element.47), channel_id=1, source_target_pairs={{0,8},{8,16},{16,24},{1,9},{9,17},{17,25},{2,10},{10,18},{18,26},{... | collective-permute-start | bytes 73736 | tf_op jit(solution)/shard_map/ppermute | solution.py:332
  103.9 1.3 collective-permute-start.7
  105.2 2.6 %collective-permute-done.7.below = bf16[96,128]{1,0:T(8,128)(2,1)S(1)} collective-permute-done((bf16[96,128]{1,0:T(8,128)(2,1)S(1)}, bf16[96,128]{1,0:T(8,128)(2,1)S(1)}, u32[]{:S(2)}, u32[]{:S(2)}) %collective-permute-start.7) | collective-permute-done | bytes 24608 | tf_op jit(solution)/shard_map/ppermute | solution.py:333
  107.8 2.5 %collective-permute-start.8 = (f32[48,128]{1,0:T(8,128)S(1)}, f32[48,128]{1,0:T(8,128)S(1)}, u32[]{:S(2)}, u32[]{:S(2)}) collective-permute-start(f32[48,128]{1,0:T(8,128)S(1)} %get-tuple-element.51), channel_id=1, source_target_pairs={{0,1},{1,2},{2,3},{3,4},{4,5},{5,6},{6,7},{8,9},{9,10},{10,11},{11... | collective-permute-start | bytes 73736 | tf_op jit(solution)/shard_map/ppermute | solution.py:335
  110.3 1.3 collective-permute-start.9
  111.8 4.2 %collective-permute-done.9.right = f32[48,128]{1,0:T(8,128)S(1)} collective-permute-done((f32[48,128]{1,0:T(8,128)S(1)}, f32[48,128]{1,0:T(8,128)S(1)}, u32[]{:S(2)}, u32[]{:S(2)}) %collective-permute-start.9) | collective-permute-done | bytes 24608 | tf_op jit(solution)/shard_map/ppermute | solution.py:336
  116.0 8.2 %conv.3 = (f32[3,16,2,32,128]{4,3,2,1,0:T(8,128)S(1)}, bf16[96,64,128]{2,1,0:T(8,128)(2,1)S(1)}) custom-call(s32[48]{0:T(128)S(1)} %multiply_add_fusion.mat_idx, s32[48]{0:T(128)S(1)} %fusion.28.send_slot, bf16[32,96,128]{2,1,0:T(8,128)(2,1)S(1)} %get-tuple-element.46.scaled, bf16[96,128]{1,0:T(8,128)(2,1)S(1)} %collective-permute-done.6.above, ...), custom_call_target="tpu_custom_call" | custom-call | tf_op jit(solution)/shard_map/conv/pallas_call | solution.py:344
  124.2 26.4 %all_to_all.22 = bf16[16,6,64,128]{3,2,1,0:T(8,128)(2,1)S(1)} all-to-all(bf16[16,6,64,128]{3,2,1,0:T(8,128)(2,1)S(1)} %bitcast.31), channel_id=1, replica_groups=mesh['row'=4,'zh'=2,'zl'=2,'x'=2] {'row','zl','x'}, dimensions={0} | all-to-all | bytes 3145728 | tf_op jit(solution)/shard_map/all_to_all | solution.py:323
  150.6 1.2 combine.3
  151.8 1.3 collective-permute-start.10
  153.1 9.2 %collective-permute-done.10.other = bf16[16,64,128]{2,1,0:T(8,128)(2,1)S(1)} collective-permute-done((bf16[16,64,128]{2,1,0:T(8,128)(2,1)S(1)}, bf16[16,64,128]{2,1,0:T(8,128)(2,1)S(1)}, u32[]{:S(2)}, u32[]{:S(2)}) %collective-permute-start.10) | collective-permute-done | bytes 262176 | tf_op jit(solution)/shard_map/ppermute | solution.py:193
  162.2 0.8 reply.3
  163.1 26.8 %all_to_all.23 = bf16[16,6,64,128]{3,2,1,0:T(8,128)(2,1)S(1)} all-to-all(bf16[16,6,64,128]{3,2,1,0:T(8,128)(2,1)S(1)} %bitcast.27), channel_id=1, replica_groups=mesh['row'=4,'zh'=2,'zl'=2,'x'=2] {'row','zl','x'}, dimensions={0} | all-to-all | bytes 3145728 | tf_op jit(solution)/shard_map/all_to_all | solution.py:323
  189.8 4.2 %finish.3 = f32[32,96,128]{2,1,0:T(8,128)} custom-call(s32[48]{0:T(128)S(1)} %multiply_add_fusion.mat_idx, s32[48]{0:T(128)S(1)} %fusion.28.send_slot, bf16[96,64,128]{2,1,0:T(8,128)(2,1)S(1)} %bitcast.29, f32[3,16,2,32,128]{4,3,2,1,0:T(8,128)S(1)} %get-tuple-element.56.pulled, bf16[32,96,128]{2,1,0:T(8,128)(2,1)S(1)} %copy-done.5, ...), custom_call_target="tpu_custom_call" | custom-call | tf_op jit(solution)/shard_map/finish/pallas_call | solution.py:352
  (55 shorter events, 3.3 us)
Async XLA Ops:
  0.0 33.5 %collective-permute-start.4 = (f32[8,64,128]{2,1,0:T(8,128)}, f32[8,64,128]{2,1,0:T(8,128)S(1)}, u32[]{:S(2)}, u32[]{:S(2)}) collective-permute-start(f32[8,64,128]{2,1,0:T(8,128)} %own_weight.3), channel_id=1, source_target_pairs={{0,6},{2,4},{4,2},{6,0},{1,7},{3,5},{5,3},{7,1},{8,14},{10,12},{12... | collective-permute-start | bytes 786440 | tf_op jit(solution)/shard_map/ppermute | solution.py:193
  5.1 1.1 copy-start.2
  6.2 1.1 copy-start.4
  7.3 3.4 %copy-start.8 = (s32[4,24,16]{1,2,0:T(8,128)S(1)}, s32[4,24,16]{1,2,0:T(8,128)}, u32[]{:S(2)}) copy-start(s32[4,24,16]{1,2,0:T(8,128)} %param.14) | copy-start | bytes 18436
  7.3 3.6 %copy-start.9 = (s32[256]{0:T(256)S(1)}, s32[256]{0:T(256)}, u32[]{:S(2)}) copy-start(s32[256]{0:T(256)} %param.16) | copy-start | bytes 3076
  7.3 4.2 %copy-start.10 = (s32[1,3,16]{2,0,1:T(1,128)S(1)}, s32[1,3,16]{2,0,1:T(1,128)}, u32[]{:S(2)}) copy-start(s32[1,3,16]{2,0,1:T(1,128)} %param.15) | copy-start | bytes 580
  7.4 4.3 %copy-start.11 = (s32[8]{0:T(128)S(1)}, s32[8]{0:T(128)}, u32[]{:S(2)}) copy-start(s32[8]{0:T(128)} %param.17) | copy-start | bytes 100
  7.4 5.1 %copy-start.7 = (bf16[3,3,128,128]{3,2,1,0:T(8,128)(2,1)S(1)}, bf16[3,3,128,128]{3,2,1,0:T(8,128)(2,1)}, u32[]{:S(2)}) copy-start(bf16[3,3,128,128]{3,2,1,0:T(8,128)(2,1)} %param.11) | copy-start | bytes 884740
  7.9 5.2 %collective-permute-start = (bf16[96,128]{1,0:T(8,128)(2,1)S(1)}, bf16[96,128]{1,0:T(8,128)(2,1)S(1)}, u32[]{:S(2)}, u32[]{:S(2)}) collective-permute-start(bf16[96,128]{1,0:T(8,128)(2,1)S(1)} %get-tuple-element.32), channel_id=1, source_target_pairs={{0,8},{8,16},{16,24},{1,9},{9,17},{17,25},{2,10},{10,18},{18,26},{... | collective-permute-start | bytes 73736 | tf_op jit(solution)/shard_map/ppermute | solution.py:332
  9.4 4.7 %collective-permute-start.1 = (bf16[96,128]{1,0:T(8,128)(2,1)S(1)}, bf16[96,128]{1,0:T(8,128)(2,1)S(1)}, u32[]{:S(2)}, u32[]{:S(2)}) collective-permute-start(bf16[96,128]{1,0:T(8,128)(2,1)S(1)} %get-tuple-element.33), channel_id=1, source_target_pairs={{8,0},{16,8},{24,16},{9,1},{17,9},{25,17},{10,2},{18,10},{26,18},{... | collective-permute-start | bytes 73736 | tf_op jit(solution)/shard_map/ppermute | solution.py:333
  14.1 4.9 %collective-permute-start.2 = (f32[48,128]{1,0:T(8,128)S(1)}, f32[48,128]{1,0:T(8,128)S(1)}, u32[]{:S(2)}, u32[]{:S(2)}) collective-permute-start(f32[48,128]{1,0:T(8,128)S(1)} %get-tuple-element.36), channel_id=1, source_target_pairs={{0,1},{1,2},{2,3},{3,4},{4,5},{5,6},{6,7},{8,9},{9,10},{10,11},{11... | collective-permute-start | bytes 73736 | tf_op jit(solution)/shard_map/ppermute | solution.py:335
  17.5 5.7 %collective-permute-start.3 = (f32[48,128]{1,0:T(8,128)S(1)}, f32[48,128]{1,0:T(8,128)S(1)}, u32[]{:S(2)}, u32[]{:S(2)}) collective-permute-start(f32[48,128]{1,0:T(8,128)S(1)} %get-tuple-element.37), channel_id=1, source_target_pairs={{1,0},{2,1},{3,2},{4,3},{5,4},{6,5},{7,6},{9,8},{10,9},{11,10},{12... | collective-permute-start | bytes 73736 | tf_op jit(solution)/shard_map/ppermute | solution.py:336
  23.2 2.2 %copy-start = (bf16[8,4,64,1024]{3,2,1,0:T(8,128)(2,1)S(1)}, bf16[8,4,64,1024]{3,2,1,0:T(8,128)(2,1)}, u32[]{:S(2)}) copy-start(bf16[8,4,64,1024]{3,2,1,0:T(8,128)(2,1)} %param.12) | copy-start | bytes 12582916
  59.1 11.6 %copy-start.6 = (f32[8,64,128]{2,1,0:T(8,128)S(1)}, f32[8,64,128]{2,1,0:T(8,128)}, u32[]{:S(2)}) copy-start(f32[8,64,128]{2,1,0:T(8,128)} %own_weight.3) | copy-start | bytes 786436
  60.2 10.4 %collective-permute-start.5 = (bf16[16,64,128]{2,1,0:T(8,128)(2,1)S(1)}, bf16[16,64,128]{2,1,0:T(8,128)(2,1)S(1)}, u32[]{:S(2)}, u32[]{:S(2)}) collective-permute-start(bf16[16,64,128]{2,1,0:T(8,128)(2,1)S(1)} %get-tuple-element.43), channel_id=1, source_target_pairs={{0,6},{2,4},{4,2},{6,0},{1,7},{3,5},{5,3},{7,1},{8,14},{10,12},{12... | collective-permute-start | bytes 786440 | tf_op jit(solution)/shard_map/ppermute | solution.py:193
  70.7 27.9 %copy-start.1 = (bf16[8,4,64,1024]{3,2,1,0:T(8,128)(2,1)S(1)}, bf16[8,4,64,1024]{3,2,1,0:T(8,128)(2,1)}, u32[]{:S(2)}) copy-start(bf16[8,4,64,1024]{3,2,1,0:T(8,128)(2,1)} %param.12) | copy-start | bytes 12582916
  71.5 27.1 %copy-start.3 = (bf16[32,96,128]{2,1,0:T(8,128)(2,1)S(1)}, bf16[32,96,128]{2,1,0:T(8,128)(2,1)}, u32[]{:S(2)}) copy-start(bf16[32,96,128]{2,1,0:T(8,128)(2,1)} %state.5) | copy-start | bytes 2359300
  71.5 27.1 %copy-start.5 = (bf16[32,96,128]{2,1,0:T(8,128)(2,1)S(1)}, bf16[32,96,128]{2,1,0:T(8,128)(2,1)}, u32[]{:S(2)}) copy-start(bf16[32,96,128]{2,1,0:T(8,128)(2,1)} %grad.5) | copy-start | bytes 2359300
  101.7 3.5 %collective-permute-start.6 = (bf16[96,128]{1,0:T(8,128)(2,1)S(1)}, bf16[96,128]{1,0:T(8,128)(2,1)S(1)}, u32[]{:S(2)}, u32[]{:S(2)}) collective-permute-start(bf16[96,128]{1,0:T(8,128)(2,1)S(1)} %get-tuple-element.47), channel_id=1, source_target_pairs={{0,8},{8,16},{16,24},{1,9},{9,17},{17,25},{2,10},{10,18},{18,26},{... | collective-permute-start | bytes 73736 | tf_op jit(solution)/shard_map/ppermute | solution.py:332
  103.9 3.9 %collective-permute-start.7 = (bf16[96,128]{1,0:T(8,128)(2,1)S(1)}, bf16[96,128]{1,0:T(8,128)(2,1)S(1)}, u32[]{:S(2)}, u32[]{:S(2)}) collective-permute-start(bf16[96,128]{1,0:T(8,128)(2,1)S(1)} %get-tuple-element.48), channel_id=1, source_target_pairs={{8,0},{16,8},{24,16},{9,1},{17,9},{25,17},{10,2},{18,10},{26,18},{... | collective-permute-start | bytes 73736 | tf_op jit(solution)/shard_map/ppermute | solution.py:333
  107.8 4.0 %collective-permute-start.8 = (f32[48,128]{1,0:T(8,128)S(1)}, f32[48,128]{1,0:T(8,128)S(1)}, u32[]{:S(2)}, u32[]{:S(2)}) collective-permute-start(f32[48,128]{1,0:T(8,128)S(1)} %get-tuple-element.51), channel_id=1, source_target_pairs={{0,1},{1,2},{2,3},{3,4},{4,5},{5,6},{6,7},{8,9},{9,10},{10,11},{11... | collective-permute-start | bytes 73736 | tf_op jit(solution)/shard_map/ppermute | solution.py:335
  110.3 5.7 %collective-permute-start.9 = (f32[48,128]{1,0:T(8,128)S(1)}, f32[48,128]{1,0:T(8,128)S(1)}, u32[]{:S(2)}, u32[]{:S(2)}) collective-permute-start(f32[48,128]{1,0:T(8,128)S(1)} %get-tuple-element.52), channel_id=1, source_target_pairs={{1,0},{2,1},{3,2},{4,3},{5,4},{6,5},{7,6},{9,8},{10,9},{11,10},{12... | collective-permute-start | bytes 73736 | tf_op jit(solution)/shard_map/ppermute | solution.py:336
  151.8 10.4 %collective-permute-start.10 = (bf16[16,64,128]{2,1,0:T(8,128)(2,1)S(1)}, bf16[16,64,128]{2,1,0:T(8,128)(2,1)S(1)}, u32[]{:S(2)}, u32[]{:S(2)}) collective-permute-start(bf16[16,64,128]{2,1,0:T(8,128)(2,1)S(1)} %get-tuple-element.55), channel_id=1, source_target_pairs={{0,6},{2,4},{4,2},{6,0},{1,7},{3,5},{5,3},{7,1},{8,14},{10,12},{12... | collective-permute-start | bytes 786440 | tf_op jit(solution)/shard_map/ppermute | solution.py:193

commit v5 on v4

--- a/solution.py
+++ b/solution.py
@@ -22,10 +22,9 @@
 SMEM = pl.BlockSpec(memory_space=pltpu.SMEM)
 
 
-def start_kernel(state, grad, scaled, top, bottom, left, right):
+def start_kernel(state, grad, scaled):
     value = state[...].astype(jnp.float32)
-    value = (1.0 - value * value) * grad[...].astype(jnp.float32)
-    emit_edges(value, scaled, top, bottom, left, right)
+    scaled[...] = ((1.0 - value * value) * grad[...].astype(jnp.float32)).astype(jnp.bfloat16)
 
 
 def emit_edges(value, scaled, top, bottom, left, right):
@@ -50,54 +49,76 @@
         out[8 + rows : 9 + rows, :] = corner_b
 
 
-def load_matrices(mat_idx, rays, held, t):
+def matrices_of(mat_idx, rays, t):
+    return jnp.concatenate([rays[mat_idx[t * HITS + k]] for k in range(HITS)], axis=0)
+
+
+def forward_tile(mat_idx, send_slot, taps, rays, pulled, out, cols3, t, tile_cols):
+    chans = pulled.shape[-1]
     bins = rays.shape[1]
+    half = PIX // 2
+    r0, c0 = t // tile_cols * half, t % tile_cols * PIX
+    window = jnp.concatenate(
+        [
+            cols3[r0 + dr // 2 : r0 + dr // 2 + half, dr % 2, c0 : c0 + PIX, :].reshape(
+                half * PIX, 3 * chans
+            )
+            for dr in range(4)
+        ],
+        axis=1,
+    )
+    acc = jnp.dot(window, taps[...], preferred_element_type=jnp.float32)
+    for odd in range(2):
+        value = acc[:, odd * chans : (odd + 1) * chans].reshape(half, PIX, chans)
+        pulled[t, :, odd] = value
+    low = pulled[t].reshape(PIX * PIX, chans).astype(jnp.bfloat16)
+    value = jnp.dot(
+        matrices_of(mat_idx, rays, t), low, preferred_element_type=jnp.float32
+    ).astype(jnp.bfloat16)
     for k in range(HITS):
-        held[k * bins : (k + 1) * bins, :] = rays[mat_idx[t * HITS + k]]
-
-
-def conv_kernel(
-    mat_idx, send_slot, scaled, above, below, left, right, taps, rays,
-    pulled, out, wide, cols3, held, *, tile_cols,
+        out[send_slot[t * HITS + k]] = value[k * bins : (k + 1) * bins, :]
+
+
+def tiles_at(tiles, tile_cols, inner):
+    return [t for t in range(tiles) if (0 < t % tile_cols < tile_cols - 1) == inner]
+
+
+def inner_kernel(
+    mat_idx, send_slot, scaled, above, below, taps, rays, pulled, out, cols3, wide, *, tile_cols,
 ):
     rows, cols, chans = scaled.shape
-    bins = rays.shape[1]
-    half = PIX // 2
     f32, bf16 = jnp.float32, jnp.bfloat16
     wide[0, 8 : 8 + cols, :] = above[...].astype(f32)
     wide[rows + 1, 8 : 8 + cols, :] = below[...].astype(f32)
     wide[1 : rows + 1, 8 : 8 + cols, :] = scaled[...].astype(f32)
-    for r in range(rows + 2):
-        wide[r, 7:8, :] = left[7 + r : 8 + r, :]
-        wide[r, 8 + cols : 9 + cols, :] = right[7 + r : 8 + r, :]
+    wide[:, 0:8, :] = jnp.zeros((rows + 2, 8, chans), f32)
+    wide[:, 8 + cols :, :] = jnp.zeros((rows + 2, 8, chans), f32)
     for dc in range(3):
         value = wide[:, 7 + dc : 7 + dc + cols, :].astype(bf16)
         cols3[:, :, :, dc * chans : (dc + 1) * chans] = value.reshape(
             (rows + 2) // 2, 2, cols, chans
         )
     out[...] = jnp.zeros_like(out)
-
-    def body(t, carry):
-        r0 = (t // tile_cols) * half
-        c0 = pl.multiple_of((t % tile_cols) * PIX, PIX)
-        load_matrices(mat_idx, rays, held, t)
-        acc = None
-        for dr in range(4):
-            window = cols3[pl.ds(r0 + dr // 2, half), dr % 2, pl.ds(c0, PIX), :]
-            term = jnp.dot(
-                window.reshape(half * PIX, 3 * chans), taps[dr], preferred_element_type=f32
-            )
-            acc = term if acc is None else acc + term
-        for odd in range(2):
-            value = acc[:, odd * chans : (odd + 1) * chans].reshape(half, PIX, chans)
-            pulled[t, :, odd] = value
-        low = pulled[t].reshape(PIX * PIX, chans).astype(bf16)
-        value = jnp.dot(held[...], low, preferred_element_type=f32).astype(bf16)
-        for k in range(HITS):
-            out[send_slot[t * HITS + k]] = value[k * bins : (k + 1) * bins, :]
-        return carry
-
-    lax.fori_loop(0, pulled.shape[0], body, 0)
+    for t in tiles_at(pulled.shape[0], tile_cols, True):
+        forward_tile(mat_idx, send_slot, taps, rays, pulled, out, cols3, t, tile_cols)
+
+
+def outer_kernel(
+    mat_idx, send_slot, left, right, taps, rays, _pulled, _out, _cols3,
+    pulled, out, cols3, *, tile_cols,
+):
+    cols = cols3.shape[2]
+    chans = pulled.shape[-1]
+    group = 16
+    spot = lax.broadcasted_iota(jnp.int32, (group, chans), 0)
+    for edge, dc, first, at in ((left, 0, 0, 0), (right, 2, cols - group, group - 1)):
+        lanes = slice(dc * chans, (dc + 1) * chans)
+        for r in range(2 * cols3.shape[0]):
+            there = (r // 2, r % 2, slice(first, first + group), lanes)
+            value = jnp.where(spot == at, edge[7 + r : 8 + r, :], cols3[there].astype(jnp.float32))
+            cols3[there] = value.astype(jnp.bfloat16)
+    for t in tiles_at(pulled.shape[0], tile_cols, False):
+        forward_tile(mat_idx, send_slot, taps, rays, pulled, out, cols3, t, tile_cols)
 
 
 def combine_kernel(table, recv, total, low, acc):
@@ -135,34 +156,40 @@
 def finish_kernel(
     mat_idx, send_slot, returned, pulled, grad, state, rays, *refs, tile_cols, last,
 ):
-    outs, (whole, picked, held) = refs[:-3], refs[-3:]
+    outs, (whole, mark) = refs[:-2], refs[-2:]
     tiles = pulled.shape[0]
-    bins = rays.shape[1]
     chans = grad.shape[2]
     f32 = jnp.float32
 
-    def body(t, carry):
-        load_matrices(mat_idx, rays, held, t)
-        for k in range(HITS):
-            picked[k * bins : (k + 1) * bins, :] = returned[send_slot[t * HITS + k]]
+    def place(t):
+        r0, c0 = t // tile_cols * PIX, t % tile_cols * PIX
+        return slice(r0, r0 + PIX), slice(c0, c0 + PIX)
+
+    def leave(t):
+        where = place(t)
+        return pltpu.make_async_copy(whole.at[where], outs[0].at[where], mark.at[t])
+
+    for t in range(tiles):
+        picked = jnp.concatenate([returned[send_slot[t * HITS + k]] for k in range(HITS)], axis=0)
         backed = lax.dot_general(
-            held[...], picked[...], (((0,), (0,)), ((), ())), preferred_element_type=f32
-        )
+            picked,
+            matrices_of(mat_idx, rays, t),
+            (((0,), (0,)), ((), ())),
+            preferred_element_type=f32,
+        ).T
         change = pulled[t].reshape(backed.shape) - relax_rate * backed
-        where = (
-            pl.ds((t // tile_cols) * PIX, PIX),
-            pl.ds(pl.multiple_of((t % tile_cols) * PIX, PIX), PIX),
-        )
+        where = place(t)
         adjoint = grad[where].astype(f32) + change.reshape(PIX, PIX, chans)
         if last:
-            outs[0][where] = adjoint
+            whole[where] = adjoint
+            leave(t).start()
         else:
             value = state[where].astype(f32)
             whole[where] = (1.0 - value * value) * adjoint
-        return carry
-
-    lax.fori_loop(0, tiles, body, 0)
-    if not last:
+    if last:
+        for t in range(tiles):
+            leave(t).wait()
+    else:
         emit_edges(whole[...], *outs)
 
 
@@ -192,8 +219,6 @@
     def exchange(value):
         return lax.ppermute(value, ("zh", "zl"), swap)
 
-    other_weight = exchange(ray_weight)
-
     everyone = hits.reshape(nr, tile_rows, nc, tile_cols, HITS).transpose(0, 2, 1, 3, 4)
     everyone = everyone.reshape(nr, 2, 2, nx, pairs)
     group = lax.dynamic_index_in_dim(everyone, zh, 1, keepdims=False).reshape(peers, pairs)
@@ -237,7 +262,7 @@
     blank = jnp.zeros_like(taps[:1])
     taps = jnp.concatenate(
         [jnp.concatenate([taps, blank]), jnp.concatenate([blank, taps])], axis=2
-    )
+    ).reshape(4 * 3 * chans, 2 * chans)
     rays = ray_matrix.reshape(angles * spots, bins, tile_pix)
 
     block = (bins, chans)
@@ -256,9 +281,9 @@
 
     start = pl.pallas_call(
         start_kernel,
-        out_shape=edges,
+        out_shape=edges[0],
         in_specs=[VMEM] * 2,
-        out_specs=(VMEM,) * 5,
+        out_specs=VMEM,
         compiler_params=limit(8),
         name="start",
     )
@@ -270,19 +295,34 @@
         compiler_params=limit(4),
         name="sides",
     )
-    held = pltpu.VMEM((HITS * bins, tile_pix), bf16)
-    conv = pl.pallas_call(
-        functools.partial(conv_kernel, tile_cols=tile_cols),
-        out_shape=(shape((tiles, PIX // 2, 2, PIX, chans), f32), slot_out),
+    pulled_out = shape((tiles, PIX // 2, 2, PIX, chans), f32)
+    cols3_out = shape(((rows_dev + 2) // 2, 2, cols_dev, 3 * chans), bf16)
+    macs = tiles * tile_pix * chans * (9 * chans + HITS * bins)
+
+    def cost(share):
+        return pl.CostEstimate(
+            flops=2 * macs * share // tiles, bytes_accessed=rays.size * 2, transcendentals=0
+        )
+
+    inner = pl.pallas_call(
+        functools.partial(inner_kernel, tile_cols=tile_cols),
+        out_shape=(pulled_out, slot_out, cols3_out),
+        in_specs=[SMEM] * 2 + [VMEM] * 5,
+        out_specs=(VMEM,) * 3,
+        scratch_shapes=[pltpu.VMEM((rows_dev + 2, cols_dev + 16, chans), f32)],
+        compiler_params=limit(16),
+        cost_estimate=cost(len(tiles_at(tiles, tile_cols, True))),
+        name="inner",
+    )
+    outer = pl.pallas_call(
+        functools.partial(outer_kernel, tile_cols=tile_cols),
+        out_shape=(pulled_out, slot_out, cols3_out),
         in_specs=[SMEM] * 2 + [VMEM] * 7,
-        out_specs=(VMEM, VMEM),
-        scratch_shapes=[
-            pltpu.VMEM((rows_dev + 2, cols_dev + 16, chans), f32),
-            pltpu.VMEM(((rows_dev + 2) // 2, 2, cols_dev, 3 * chans), bf16),
-            held,
-        ],
-        compiler_params=limit(20),
-        name="conv",
+        out_specs=(VMEM,) * 3,
+        input_output_aliases={6: 0, 7: 1, 8: 2},
+        compiler_params=limit(16),
+        cost_estimate=cost(len(tiles_at(tiles, tile_cols, False))),
+        name="outer",
     )
     combine = pl.pallas_call(
         combine_kernel,
@@ -308,11 +348,10 @@
             functools.partial(finish_kernel, tile_cols=tile_cols, last=last),
             out_shape=(shape(state.shape, f32),) if last else edges,
             in_specs=[SMEM] * 2 + [VMEM] * 5,
-            out_specs=(VMEM,) * (1 if last else 5),
+            out_specs=(pl.BlockSpec(memory_space=pl.ANY),) if last else (VMEM,) * 5,
             scratch_shapes=[
-                pltpu.VMEM((8, 128, 128) if last else state.shape, f32),
-                pltpu.VMEM((HITS * bins, chans), bf16),
-                held,
+                pltpu.VMEM(state.shape, f32),
+                pltpu.SemaphoreType.DMA((tiles,)),
             ],
             compiler_params=limit(20),
             name="finish",
@@ -328,20 +367,29 @@
     rightward = [(i, i + 1) for i in range(nc - 1)]
     leftward = [(b, a) for a, b in rightward]
 
-    def halo_of(top, bottom, left, right):
+    def forward(scaled, top, bottom, left, right):
         above = lax.ppermute(bottom, "row", up)
         below = lax.ppermute(top, "row", down)
         first, last = sides(above, below, left, right)
         lefts = lax.ppermute(last, COL, rightward)
         rights = lax.ppermute(first, COL, leftward)
-        return above, below, lefts, rights
-
-    scaled, *rim = start(state, grad)
-    halo = halo_of(*rim)
+        parts = inner(mat_idx, send_slot, scaled, above, below, taps, rays)
+        return outer(mat_idx, send_slot, lefts, rights, taps, rays, *parts)[:2]
+
+    def scale(state, grad):
+        value = 1.0 - jnp.square(state.astype(f32))
+        return (value * grad.astype(f32)).astype(bf16)
+
+    other_weight = exchange(ray_weight)
+    scaled = start(state, grad)
+    rim = (
+        scale(state[0], grad[0]),
+        scale(state[rows_dev - 1], grad[rows_dev - 1]),
+        scale(state[:, 0], grad[:, 0]),
+        scale(state[:, cols_dev - 1], grad[:, cols_dev - 1]),
+    )
     for turn in range(ITERS):
-        if turn:
-            halo = halo_of(*rim)
-        pulled, outgoing = conv(mat_idx, send_slot, scaled, *halo, taps, rays)
+        pulled, outgoing = forward(scaled, *rim)
         if not turn:
             outgoing, table, used, other_weight = lax.optimization_barrier(
                 (outgoing, table, used, other_weight)

time: 195 us -> 186 us (0.954)
  waiting for transfers between devices: 30.6 us -> 23.2 us
  Pallas kernels: 28.2 us -> 21.7 us
  other arithmetic: 1.65 us -> 4.62 us
    ppermute x8, waiting for transfers between devices: 12.2 us -> 4.3 us  [the longest x2 2.63 us: forward(): below = lax.ppermute(top, 'row', down)]
    pallas_call x5 -> x7, Pallas kernels: 16.9 us -> 13.2 us  [the longest x2 7.46 us: forward(): return outer(mat_idx, send_slot, lefts, rights, taps, rays, *parts)[:2]]
    pallas_call x2, Pallas kernels: 7.38 us -> 4.49 us  [on_device(): finish(last)(mat_idx, send_slot, across(replies), pulled, grad, state, rays)]
    unnamed x25 -> x12, local copies, waits for them, and re-layouts: 4.57 us -> 4.21 us
  transfers between devices with their start and end apart: 11 -> 11, of which waited for: 7 -> 4; matrix products, arithmetic and copies ran while one was open for 1% -> 5% of each run, Pallas kernels for 4% -> 5%
where the time goes in v5:
time: 186 us
  blocking collectives  105 us (56%)
  starting transfers between devices  23.3 us (13%)
  waiting for transfers between devices  23.2 us (12%)
  Pallas kernels  21.7 us (12%)
  local copies, waits for them, and re-layouts  7.2 us (4%)
  other arithmetic  4.62 us (2%)
    all_to_all x4, blocking collectives, across(): lax.all_to_all(value, GROUP, split_axis=0, concat_axis=0, tiled=True)  105 us
    ppermute x3, waiting for transfers between devices, exchange(): return lax.ppermute(value, ('zh', 'zl'), swap)  18.9 us
    pallas_call x2, Pallas kernels, forward(): return outer(mat_idx, send_slot, lefts, rights, taps, rays, *parts)[:2]  7.46 us
    ppermute x3, starting transfers between devices, exchange(): return lax.ppermute(value, ('zh', 'zl'), swap)  7.1 us
    ppermute x2, starting transfers between devices, forward(): lefts = lax.ppermute(last, COL, rightward)  5.85 us
    pallas_call x2, Pallas kernels, forward(): parts = inner(mat_idx, send_slot, scaled, above, below, taps, rays)  5.47 us
    ppermute x2, starting transfers between devices, forward(): above = lax.ppermute(bottom, 'row', up)  5.18 us
    pallas_call x2, Pallas kernels, on_device(): finish(last)(mat_idx, send_slot, across(replies), pulled, grad, state, rays)  4.49 us
  transfers between devices with their start and end apart: 11, of which 4 were waited for; matrix products, arithmetic and copies ran while one was open for 5% of the time, Pallas kernels for 5%

profile of v5, /device:TPU:0, one launch (start us, length us, event | category | flops | bytes accessed | tf_op | source)
XLA Modules:
  0.0 185.7 jit_solution(6956749633912908063)
XLA Ops:
  0.0 0.9 fusion.5
  0.9 1.3 collective-permute-start.1
  2.2 3.0 %collective-permute-start = (bf16[96,128]{1,0:T(8,128)(2,1)S(1)}, bf16[96,128]{1,0:T(8,128)(2,1)S(1)}, u32[]{:S(2)}, u32[]{:S(2)}) collective-permute-start(bf16[96,128]{1,0:T(8,128)(2,1)S(1)} %get-tuple-element.62), channel_id=1, source_target_pairs={{0,8},{8,16},{16,24},{1,9},{9,17},{17,25},{2,10},{10,18},{18,26},{... | collective-permute-start | bytes 73736 | tf_op jit(solution)/shard_map/ppermute | solution.py:371
  5.3 5.1 %collective-permute-start.4 = (f32[8,64,128]{2,1,0:T(8,128)}, f32[8,64,128]{2,1,0:T(8,128)S(1)}, u32[]{:S(2)}, u32[]{:S(2)}) collective-permute-start(f32[8,64,128]{2,1,0:T(8,128)} %own_weight.3), channel_id=1, source_target_pairs={{0,6},{2,4},{4,2},{6,0},{1,7},{3,5},{5,3},{7,1},{8,14},{10,12},{12... | collective-permute-start | bytes 786440 | tf_op jit(solution)/shard_map/ppermute | solution.py:220
  10.4 0.9 fusion.34
  11.3 0.9 fusion.35
  13.2 1.2 select_reduce_fusion
  17.7 1.2 copy.31
  19.6 3.4 %collective-permute-start.2 = (f32[48,128]{1,0:T(8,128)S(1)}, f32[48,128]{1,0:T(8,128)S(1)}, u32[]{:S(2)}, u32[]{:S(2)}) collective-permute-start(f32[48,128]{1,0:T(8,128)S(1)} %get-tuple-element.32), channel_id=1, source_target_pairs={{0,1},{1,2},{2,3},{3,4},{4,5},{5,6},{6,7},{8,9},{9,10},{10,11},{11... | collective-permute-start | bytes 73736 | tf_op jit(solution)/shard_map/ppermute | solution.py:374
  23.0 1.3 collective-permute-start.3
  24.3 2.2 %copy-done = bf16[8,4,64,1024]{3,2,1,0:T(8,128)(2,1)S(1)} copy-done((bf16[8,4,64,1024]{3,2,1,0:T(8,128)(2,1)S(1)}, bf16[8,4,64,1024]{3,2,1,0:T(8,128)(2,1)}, u32[]{:S(2)}) %copy-start) | copy-done | bytes 4194328
  26.5 2.7 %inner.2 = (f32[3,16,2,32,128]{4,3,2,1,0:T(8,128)S(1)}, bf16[96,64,128]{2,1,0:T(8,128)(2,1)S(1)}, bf16[17,2,96,384]{3,2,1,0:T(8,128)(2,1)S(1)}) custom-call(s32[48]{0:T(128)S(1)} %multiply_add_fusion.mat_idx, s32[48]{0:T(128)S(1)} %fusion.32.send_slot, bf16[32,96,128]{2,1,0:T(8,128)(2,1)S(1)} %start.1.scaled, ...), custom_call_target="tpu_custom_call" | custom-call | flops 570425344 | bytes 4194304 | tf_op jit(solution)/shard_map/inner/pallas_call | solution.py:376
  29.2 3.7 %outer.2 = (f32[3,16,2,32,128]{4,3,2,1,0:T(8,128)S(1)}, bf16[96,64,128]{2,1,0:T(8,128)(2,1)S(1)}, bf16[17,2,96,384]{3,2,1,0:T(8,128)(2,1)S(1)}) custom-call(s32[48]{0:T(128)S(1)} %multiply_add_fusion.mat_idx, s32[48]{0:T(128)S(1)} %fusion.32.send_slot, ...), custom_call_target="tpu_custom_call", output_to_operand_aliasing={{0}: (6, {}), {1}: (7, {}), {2}: (8, {})} | custom-call | flops 1140850688 | bytes 4194304 | tf_op jit(solution)/shard_map/outer/pallas_call | solution.py:377
  33.0 25.4 %all_to_all.20 = bf16[16,6,64,128]{3,2,1,0:T(8,128)(2,1)S(1)} all-to-all(bf16[16,6,64,128]{3,2,1,0:T(8,128)(2,1)S(1)} %bitcast.45), channel_id=1, replica_groups=mesh['row'=4,'zh'=2,'zl'=2,'x'=2] {'row','zl','x'}, dimensions={0} | all-to-all | bytes 3145728 | tf_op jit(solution)/shard_map/all_to_all | solution.py:362
  58.3 1.2 combine.2
  60.2 9.7 %collective-permute-done.5.other = bf16[16,64,128]{2,1,0:T(8,128)(2,1)S(1)} collective-permute-done((bf16[16,64,128]{2,1,0:T(8,128)(2,1)S(1)}, bf16[16,64,128]{2,1,0:T(8,128)(2,1)S(1)}, u32[]{:S(2)}, u32[]{:S(2)}) %collective-permute-start.5) | collective-permute-done | bytes 262176 | tf_op jit(solution)/shard_map/ppermute | solution.py:220
  70.8 26.8 %all_to_all.21 = bf16[16,6,64,128]{3,2,1,0:T(8,128)(2,1)S(1)} all-to-all(bf16[16,6,64,128]{3,2,1,0:T(8,128)(2,1)S(1)} %bitcast.43), channel_id=1, replica_groups=mesh['row'=4,'zh'=2,'zl'=2,'x'=2] {'row','zl','x'}, dimensions={0} | all-to-all | bytes 3145728 | tf_op jit(solution)/shard_map/all_to_all | solution.py:362
  97.5 1.9 %finish.2 = (bf16[32,96,128]{2,1,0:T(8,128)(2,1)S(1)}, bf16[96,128]{1,0:T(8,128)(2,1)S(1)}, bf16[96,128]{1,0:T(8,128)(2,1)S(1)}, bf16[32,128]{1,0:T(8,128)(2,1)S(1)}, bf16[32,128]{1,0:T(8,128)(2,1)S(1)}) custom-call(s32[48]{0:T(128)S(1)} %multiply_add_fusion.mat_idx, s32[48]{0:T(128)S(1)} %fusion.32.send_slot, bf16[96,64,128]{2,1,0:T(8,128)(2,1)S(1)} %bitcast.39, ...), custom_call_target="tpu_custom_call" | custom-call | tf_op jit(solution)/shard_map/finish/pallas_call | solution.py:400
  99.4 2.1 %collective-permute-start.6 = (bf16[96,128]{1,0:T(8,128)(2,1)S(1)}, bf16[96,128]{1,0:T(8,128)(2,1)S(1)}, u32[]{:S(2)}, u32[]{:S(2)}) collective-permute-start(bf16[96,128]{1,0:T(8,128)(2,1)S(1)} %get-tuple-element.45), channel_id=1, source_target_pairs={{0,8},{8,16},{16,24},{1,9},{9,17},{17,25},{2,10},{10,18},{18,26},{... | collective-permute-start | bytes 73736 | tf_op jit(solution)/shard_map/ppermute | solution.py:371
  101.6 1.3 collective-permute-start.7
  102.9 2.6 %collective-permute-done.7.below = bf16[96,128]{1,0:T(8,128)(2,1)S(1)} collective-permute-done((bf16[96,128]{1,0:T(8,128)(2,1)S(1)}, bf16[96,128]{1,0:T(8,128)(2,1)S(1)}, u32[]{:S(2)}, u32[]{:S(2)}) %collective-permute-start.7) | collective-permute-done | bytes 24608 | tf_op jit(solution)/shard_map/ppermute | solution.py:372
  105.5 2.5 %collective-permute-start.8 = (f32[48,128]{1,0:T(8,128)S(1)}, f32[48,128]{1,0:T(8,128)S(1)}, u32[]{:S(2)}, u32[]{:S(2)}) collective-permute-start(f32[48,128]{1,0:T(8,128)S(1)} %get-tuple-element.49), channel_id=1, source_target_pairs={{0,1},{1,2},{2,3},{3,4},{4,5},{5,6},{6,7},{8,9},{9,10},{10,11},{11... | collective-permute-start | bytes 73736 | tf_op jit(solution)/shard_map/ppermute | solution.py:374
  108.0 1.3 collective-permute-start.9
  109.3 2.7 %inner.3 = (f32[3,16,2,32,128]{4,3,2,1,0:T(8,128)S(1)}, bf16[96,64,128]{2,1,0:T(8,128)(2,1)S(1)}, bf16[17,2,96,384]{3,2,1,0:T(8,128)(2,1)S(1)}) custom-call(s32[48]{0:T(128)S(1)} %multiply_add_fusion.mat_idx, s32[48]{0:T(128)S(1)} %fusion.32.send_slot, bf16[32,96,128]{2,1,0:T(8,128)(2,1)S(1)} %get-tuple-element.51.scaled, ...), custom_call_target="tpu_custom_call" | custom-call | flops 570425344 | bytes 4194304 | tf_op jit(solution)/shard_map/inner/pallas_call | solution.py:376
  112.0 1.7 collective-permute-done.9.right
  113.7 3.7 %outer.3 = (f32[3,16,2,32,128]{4,3,2,1,0:T(8,128)S(1)}, bf16[96,64,128]{2,1,0:T(8,128)(2,1)S(1)}, bf16[17,2,96,384]{3,2,1,0:T(8,128)(2,1)S(1)}) custom-call(s32[48]{0:T(128)S(1)} %multiply_add_fusion.mat_idx, s32[48]{0:T(128)S(1)} %fusion.32.send_slot, ...), custom_call_target="tpu_custom_call", output_to_operand_aliasing={{0}: (6, {}), {1}: (7, {}), {2}: (8, {})} | custom-call | flops 1140850688 | bytes 4194304 | tf_op jit(solution)/shard_map/outer/pallas_call | solution.py:377
  117.4 26.4 %all_to_all.22 = bf16[16,6,64,128]{3,2,1,0:T(8,128)(2,1)S(1)} all-to-all(bf16[16,6,64,128]{3,2,1,0:T(8,128)(2,1)S(1)} %bitcast.44), channel_id=1, replica_groups=mesh['row'=4,'zh'=2,'zl'=2,'x'=2] {'row','zl','x'}, dimensions={0} | all-to-all | bytes 3145728 | tf_op jit(solution)/shard_map/all_to_all | solution.py:362
  143.9 1.2 combine.3
  145.1 1.3 collective-permute-start.10
  146.4 9.1 %collective-permute-done.10.other = bf16[16,64,128]{2,1,0:T(8,128)(2,1)S(1)} collective-permute-done((bf16[16,64,128]{2,1,0:T(8,128)(2,1)S(1)}, bf16[16,64,128]{2,1,0:T(8,128)(2,1)S(1)}, u32[]{:S(2)}, u32[]{:S(2)}) %collective-permute-start.10) | collective-permute-done | bytes 262176 | tf_op jit(solution)/shard_map/ppermute | solution.py:220
  156.3 26.8 %all_to_all.23 = bf16[16,6,64,128]{3,2,1,0:T(8,128)(2,1)S(1)} all-to-all(bf16[16,6,64,128]{3,2,1,0:T(8,128)(2,1)S(1)} %bitcast.42), channel_id=1, replica_groups=mesh['row'=4,'zh'=2,'zl'=2,'x'=2] {'row','zl','x'}, dimensions={0} | all-to-all | bytes 3145728 | tf_op jit(solution)/shard_map/all_to_all | solution.py:362
  183.1 2.6 %finish.3 = f32[32,96,128]{2,1,0:T(8,128)} custom-call(s32[48]{0:T(128)S(1)} %multiply_add_fusion.mat_idx, s32[48]{0:T(128)S(1)} %fusion.32.send_slot, bf16[96,64,128]{2,1,0:T(8,128)(2,1)S(1)} %bitcast.46, f32[3,16,2,32,128]{4,3,2,1,0:T(8,128)S(1)} %get-tuple-element.58.pulled, bf16[32,96,128]{2,1,0:T(8,128)(2,1)S(1)} %copy-done.2, ...), custom_call_target="tpu_custom_call" | custom-call | tf_op jit(solution)/shard_map/finish/pallas_call | solution.py:400
  (47 shorter events, 7.2 us)
Async XLA Ops:
  0.0 19.1 %copy-start.2 = (bf16[32,96,128]{2,1,0:T(8,128)(2,1)S(1)}, bf16[32,96,128]{2,1,0:T(8,128)(2,1)}, u32[]{:S(2)}) copy-start(bf16[32,96,128]{2,1,0:T(8,128)(2,1)} %grad.5) | copy-start | bytes 2359300
  0.0 19.1 %copy-start.3 = (bf16[32,96,128]{2,1,0:T(8,128)(2,1)S(1)}, bf16[32,96,128]{2,1,0:T(8,128)(2,1)}, u32[]{:S(2)}) copy-start(bf16[32,96,128]{2,1,0:T(8,128)(2,1)} %state.5) | copy-start | bytes 2359300
  0.9 18.6 %collective-permute-start.1 = (bf16[96,128]{1,0:T(8,128)(2,1)S(1)}, bf16[96,128]{1,0:T(8,128)(2,1)S(1)}, u32[]{:S(2)}, u32[]{:S(2)}) collective-permute-start(bf16[96,128]{1,0:T(8,128)(2,1)S(1)} %get-tuple-element.61), channel_id=1, source_target_pairs={{8,0},{16,8},{24,16},{9,1},{17,9},{25,17},{10,2},{18,10},{26,18},{... | collective-permute-start | bytes 73736 | tf_op jit(solution)/shard_map/ppermute | solution.py:372
  2.2 17.3 %collective-permute-start = (bf16[96,128]{1,0:T(8,128)(2,1)S(1)}, bf16[96,128]{1,0:T(8,128)(2,1)S(1)}, u32[]{:S(2)}, u32[]{:S(2)}) collective-permute-start(bf16[96,128]{1,0:T(8,128)(2,1)S(1)} %get-tuple-element.62), channel_id=1, source_target_pairs={{0,8},{8,16},{16,24},{1,9},{9,17},{17,25},{2,10},{10,18},{18,26},{... | collective-permute-start | bytes 73736 | tf_op jit(solution)/shard_map/ppermute | solution.py:371
  5.3 27.7 %collective-permute-start.4 = (f32[8,64,128]{2,1,0:T(8,128)}, f32[8,64,128]{2,1,0:T(8,128)S(1)}, u32[]{:S(2)}, u32[]{:S(2)}) collective-permute-start(f32[8,64,128]{2,1,0:T(8,128)} %own_weight.3), channel_id=1, source_target_pairs={{0,6},{2,4},{4,2},{6,0},{1,7},{3,5},{5,3},{7,1},{8,14},{10,12},{12... | collective-permute-start | bytes 786440 | tf_op jit(solution)/shard_map/ppermute | solution.py:220
  19.6 9.6 %collective-permute-start.2 = (f32[48,128]{1,0:T(8,128)S(1)}, f32[48,128]{1,0:T(8,128)S(1)}, u32[]{:S(2)}, u32[]{:S(2)}) collective-permute-start(f32[48,128]{1,0:T(8,128)S(1)} %get-tuple-element.32), channel_id=1, source_target_pairs={{0,1},{1,2},{2,3},{3,4},{4,5},{5,6},{6,7},{8,9},{9,10},{10,11},{11... | collective-permute-start | bytes 73736 | tf_op jit(solution)/shard_map/ppermute | solution.py:374
  23.0 6.2 %collective-permute-start.3 = (f32[48,128]{1,0:T(8,128)S(1)}, f32[48,128]{1,0:T(8,128)S(1)}, u32[]{:S(2)}, u32[]{:S(2)}) collective-permute-start(f32[48,128]{1,0:T(8,128)S(1)} %get-tuple-element.33), channel_id=1, source_target_pairs={{1,0},{2,1},{3,2},{4,3},{5,4},{6,5},{7,6},{9,8},{10,9},{11,10},{12... | collective-permute-start | bytes 73736 | tf_op jit(solution)/shard_map/ppermute | solution.py:375
  24.3 2.2 %copy-start = (bf16[8,4,64,1024]{3,2,1,0:T(8,128)(2,1)S(1)}, bf16[8,4,64,1024]{3,2,1,0:T(8,128)(2,1)}, u32[]{:S(2)}) copy-start(bf16[8,4,64,1024]{3,2,1,0:T(8,128)(2,1)} %param.12) | copy-start | bytes 12582916
  26.5 2.8 %copy-start.1 = (bf16[8,4,64,1024]{3,2,1,0:T(8,128)(2,1)S(1)}, bf16[8,4,64,1024]{3,2,1,0:T(8,128)(2,1)}, u32[]{:S(2)}) copy-start(bf16[8,4,64,1024]{3,2,1,0:T(8,128)(2,1)} %param.12) | copy-start | bytes 12582916
  58.3 11.6 %copy-start.4 = (f32[8,64,128]{2,1,0:T(8,128)S(1)}, f32[8,64,128]{2,1,0:T(8,128)}, u32[]{:S(2)}) copy-start(f32[8,64,128]{2,1,0:T(8,128)} %own_weight.3) | copy-start | bytes 786436
  59.5 10.4 %collective-permute-start.5 = (bf16[16,64,128]{2,1,0:T(8,128)(2,1)S(1)}, bf16[16,64,128]{2,1,0:T(8,128)(2,1)S(1)}, u32[]{:S(2)}, u32[]{:S(2)}) collective-permute-start(bf16[16,64,128]{2,1,0:T(8,128)(2,1)S(1)} %get-tuple-element.42), channel_id=1, source_target_pairs={{0,6},{2,4},{4,2},{6,0},{1,7},{3,5},{5,3},{7,1},{8,14},{10,12},{12... | collective-permute-start | bytes 786440 | tf_op jit(solution)/shard_map/ppermute | solution.py:220
  99.4 3.5 %collective-permute-start.6 = (bf16[96,128]{1,0:T(8,128)(2,1)S(1)}, bf16[96,128]{1,0:T(8,128)(2,1)S(1)}, u32[]{:S(2)}, u32[]{:S(2)}) collective-permute-start(bf16[96,128]{1,0:T(8,128)(2,1)S(1)} %get-tuple-element.45), channel_id=1, source_target_pairs={{0,8},{8,16},{16,24},{1,9},{9,17},{17,25},{2,10},{10,18},{18,26},{... | collective-permute-start | bytes 73736 | tf_op jit(solution)/shard_map/ppermute | solution.py:371
  101.6 3.9 %collective-permute-start.7 = (bf16[96,128]{1,0:T(8,128)(2,1)S(1)}, bf16[96,128]{1,0:T(8,128)(2,1)S(1)}, u32[]{:S(2)}, u32[]{:S(2)}) collective-permute-start(bf16[96,128]{1,0:T(8,128)(2,1)S(1)} %get-tuple-element.46), channel_id=1, source_target_pairs={{8,0},{16,8},{24,16},{9,1},{17,9},{25,17},{10,2},{18,10},{26,18},{... | collective-permute-start | bytes 73736 | tf_op jit(solution)/shard_map/ppermute | solution.py:372
  105.5 6.5 %collective-permute-start.8 = (f32[48,128]{1,0:T(8,128)S(1)}, f32[48,128]{1,0:T(8,128)S(1)}, u32[]{:S(2)}, u32[]{:S(2)}) collective-permute-start(f32[48,128]{1,0:T(8,128)S(1)} %get-tuple-element.49), channel_id=1, source_target_pairs={{0,1},{1,2},{2,3},{3,4},{4,5},{5,6},{6,7},{8,9},{9,10},{10,11},{11... | collective-permute-start | bytes 73736 | tf_op jit(solution)/shard_map/ppermute | solution.py:374
  108.0 5.7 %collective-permute-start.9 = (f32[48,128]{1,0:T(8,128)S(1)}, f32[48,128]{1,0:T(8,128)S(1)}, u32[]{:S(2)}, u32[]{:S(2)}) collective-permute-start(f32[48,128]{1,0:T(8,128)S(1)} %get-tuple-element.50), channel_id=1, source_target_pairs={{1,0},{2,1},{3,2},{4,3},{5,4},{6,5},{7,6},{9,8},{10,9},{11,10},{12... | collective-permute-start | bytes 73736 | tf_op jit(solution)/shard_map/ppermute | solution.py:375
  145.1 10.4 %collective-permute-start.10 = (bf16[16,64,128]{2,1,0:T(8,128)(2,1)S(1)}, bf16[16,64,128]{2,1,0:T(8,128)(2,1)S(1)}, u32[]{:S(2)}, u32[]{:S(2)}) collective-permute-start(bf16[16,64,128]{2,1,0:T(8,128)(2,1)S(1)} %get-tuple-element.57), channel_id=1, source_target_pairs={{0,6},{2,4},{4,2},{6,0},{1,7},{3,5},{5,3},{7,1},{8,14},{10,12},{12... | collective-permute-start | bytes 786440 | tf_op jit(solution)/shard_map/ppermute | solution.py:220

commit v6 on v5

--- a/solution.py
+++ b/solution.py
@@ -20,11 +20,28 @@
 
 VMEM = pl.BlockSpec(memory_space=pltpu.VMEM)
 SMEM = pl.BlockSpec(memory_space=pltpu.SMEM)
-
-
-def start_kernel(state, grad, scaled):
-    value = state[...].astype(jnp.float32)
-    scaled[...] = ((1.0 - value * value) * grad[...].astype(jnp.float32)).astype(jnp.bfloat16)
+ANY = pl.BlockSpec(memory_space=pl.ANY)
+
+
+def start_kernel(state, grad, scaled, top, bottom, left, right, states, grads, whole, mark):
+    parts = mark.shape[1]
+    rows = states.shape[0] // parts
+
+    def load(a, p):
+        source, held = ((state, states), (grad, grads))[a]
+        where = pl.ds(p * rows, rows)
+        return pltpu.make_async_copy(source.at[where], held.at[where], mark.at[a, p])
+
+    for p in range(parts):
+        for a in range(2):
+            load(a, p).start()
+    for p in range(parts):
+        for a in range(2):
+            load(a, p).wait()
+        where = slice(p * rows, (p + 1) * rows)
+        value = states[where].astype(jnp.float32)
+        whole[where] = (1.0 - value * value) * grads[where].astype(jnp.float32)
+    emit_edges(whole[...], scaled, top, bottom, left, right)
 
 
 def emit_edges(value, scaled, top, bottom, left, right):
@@ -53,7 +70,9 @@
     return jnp.concatenate([rays[mat_idx[t * HITS + k]] for k in range(HITS)], axis=0)
 
 
-def forward_tile(mat_idx, send_slot, taps, rays, pulled, out, cols3, t, tile_cols):
+def forward_tile(
+    mat_idx, send_slot, taps, rays, pulled, out, cols3, t, tile_cols, waiting=()
+):
     chans = pulled.shape[-1]
     bins = rays.shape[1]
     half = PIX // 2
@@ -72,6 +91,8 @@
         value = acc[:, odd * chans : (odd + 1) * chans].reshape(half, PIX, chans)
         pulled[t, :, odd] = value
     low = pulled[t].reshape(PIX * PIX, chans).astype(jnp.bfloat16)
+    while waiting:
+        waiting.pop().wait()
     value = jnp.dot(
         matrices_of(mat_idx, rays, t), low, preferred_element_type=jnp.float32
     ).astype(jnp.bfloat16)
@@ -84,10 +105,29 @@
 
 
 def inner_kernel(
-    mat_idx, send_slot, scaled, above, below, taps, rays, pulled, out, cols3, wide, *, tile_cols,
+    mat_idx, send_slot, scaled, above, below, kernel, rays, pulled, out, cols3, taps, *refs,
+    tile_cols,
 ):
+    wide = refs[-1]
     rows, cols, chans = scaled.shape
     f32, bf16 = jnp.float32, jnp.bfloat16
+    load = None
+    if len(refs) > 1:
+        held, mark = refs[:2]
+        load = pltpu.make_async_copy(rays, held, mark.at[0])
+        load.start()
+        rays = held
+    blank = jnp.zeros((3 * chans, chans), bf16)
+    for dr in range(4):
+        base = dr * 3 * chans
+        for side in range(2):
+            lanes = slice(side * chans, (side + 1) * chans)
+            tap = dr - side
+            if not 0 <= tap < 3:
+                taps[base : base + 3 * chans, lanes] = blank
+                continue
+            for dc in range(3):
+                taps[base + dc * chans : base + (dc + 1) * chans, lanes] = kernel[2 - tap, 2 - dc].T
     wide[0, 8 : 8 + cols, :] = above[...].astype(f32)
     wide[rows + 1, 8 : 8 + cols, :] = below[...].astype(f32)
     wide[1 : rows + 1, 8 : 8 + cols, :] = scaled[...].astype(f32)
@@ -99,8 +139,11 @@
             (rows + 2) // 2, 2, cols, chans
         )
     out[...] = jnp.zeros_like(out)
+    waiting = [load] if load is not None else []
     for t in tiles_at(pulled.shape[0], tile_cols, True):
-        forward_tile(mat_idx, send_slot, taps, rays, pulled, out, cols3, t, tile_cols)
+        forward_tile(mat_idx, send_slot, taps, rays, pulled, out, cols3, t, tile_cols, waiting)
+    while waiting:
+        waiting.pop().wait()
 
 
 def outer_kernel(
@@ -258,11 +301,6 @@
     used = jnp.any((block_slot[None, :] == dense_place[:, None]) & active, axis=1).astype(i32)
     used = jnp.concatenate([used, jnp.full((1,), zh * blk_dev, i32)])
 
-    taps = kernel[::-1, ::-1].transpose(0, 1, 3, 2).reshape(3, 3 * chans, chans)
-    blank = jnp.zeros_like(taps[:1])
-    taps = jnp.concatenate(
-        [jnp.concatenate([taps, blank]), jnp.concatenate([blank, taps])], axis=2
-    ).reshape(4 * 3 * chans, 2 * chans)
     rays = ray_matrix.reshape(angles * spots, bins, tile_pix)
 
     block = (bins, chans)
@@ -281,9 +319,15 @@
 
     start = pl.pallas_call(
         start_kernel,
-        out_shape=edges[0],
-        in_specs=[VMEM] * 2,
-        out_specs=VMEM,
+        out_shape=edges,
+        in_specs=[ANY] * 2,
+        out_specs=(VMEM,) * 5,
+        scratch_shapes=[
+            pltpu.VMEM(state.shape, bf16),
+            pltpu.VMEM(state.shape, bf16),
+            pltpu.VMEM(state.shape, f32),
+            pltpu.SemaphoreType.DMA((2, 4)),
+        ],
         compiler_params=limit(8),
         name="start",
     )
@@ -304,16 +348,22 @@
             flops=2 * macs * share // tiles, bytes_accessed=rays.size * 2, transcendentals=0
         )
 
-    inner = pl.pallas_call(
-        functools.partial(inner_kernel, tile_cols=tile_cols),
-        out_shape=(pulled_out, slot_out, cols3_out),
-        in_specs=[SMEM] * 2 + [VMEM] * 5,
-        out_specs=(VMEM,) * 3,
-        scratch_shapes=[pltpu.VMEM((rows_dev + 2, cols_dev + 16, chans), f32)],
-        compiler_params=limit(16),
-        cost_estimate=cost(len(tiles_at(tiles, tile_cols, True))),
-        name="inner",
-    )
+    taps_out = shape((4 * 3 * chans, 2 * chans), bf16)
+
+    def inner(early):
+        held = (shape(rays.shape, bf16),) if early else ()
+        mark = [pltpu.SemaphoreType.DMA((1,))] if early else []
+        return pl.pallas_call(
+            functools.partial(inner_kernel, tile_cols=tile_cols),
+            out_shape=(pulled_out, slot_out, cols3_out, taps_out) + held,
+            in_specs=[SMEM] * 2 + [VMEM] * 4 + [ANY if early else VMEM],
+            out_specs=(VMEM,) * (4 + len(held)),
+            scratch_shapes=mark + [pltpu.VMEM((rows_dev + 2, cols_dev + 16, chans), f32)],
+            compiler_params=limit(16),
+            cost_estimate=cost(len(tiles_at(tiles, tile_cols, True))),
+            name="inner",
+        )
+
     outer = pl.pallas_call(
         functools.partial(outer_kernel, tile_cols=tile_cols),
         out_shape=(pulled_out, slot_out, cols3_out),
@@ -367,33 +417,29 @@
     rightward = [(i, i + 1) for i in range(nc - 1)]
     leftward = [(b, a) for a, b in rightward]
 
-    def forward(scaled, top, bottom, left, right):
+    def apart(value):
+        return pltpu.with_memory_space_constraint(value, pltpu.HBM)
+
+    def forward(early, scaled, top, bottom, left, right):
         above = lax.ppermute(bottom, "row", up)
         below = lax.ppermute(top, "row", down)
         first, last = sides(above, below, left, right)
         lefts = lax.ppermute(last, COL, rightward)
         rights = lax.ppermute(first, COL, leftward)
-        parts = inner(mat_idx, send_slot, scaled, above, below, taps, rays)
-        return outer(mat_idx, send_slot, lefts, rights, taps, rays, *parts)[:2]
-
-    def scale(state, grad):
-        value = 1.0 - jnp.square(state.astype(f32))
-        return (value * grad.astype(f32)).astype(bf16)
-
-    other_weight = exchange(ray_weight)
-    scaled = start(state, grad)
-    rim = (
-        scale(state[0], grad[0]),
-        scale(state[rows_dev - 1], grad[rows_dev - 1]),
-        scale(state[:, 0], grad[:, 0]),
-        scale(state[:, cols_dev - 1], grad[:, cols_dev - 1]),
-    )
+        *parts, taps = inner(early)(
+            mat_idx, send_slot, scaled, above, below, kernel, apart(rays) if early else rays
+        )[: 4 + early]
+        near = rays
+        if early:
+            near, taps = taps, parts.pop()
+        return outer(mat_idx, send_slot, lefts, rights, taps, near, *parts)[:2]
+
+    scaled, *rim = start(apart(state), apart(grad))
     for turn in range(ITERS):
-        pulled, outgoing = forward(scaled, *rim)
+        pulled, outgoing = forward(turn == 0, scaled, *rim)
         if not turn:
-            outgoing, table, used, other_weight = lax.optimization_barrier(
-                (outgoing, table, used, other_weight)
-            )
+            outgoing, weight = lax.optimization_barrier((outgoing, ray_weight))
+            other_weight = exchange(weight)
         total, mine = combine(table, across(outgoing))
         replies = reply(table, used, total, exchange(mine), ray_weight, other_weight)
         last = turn == ITERS - 1

time: 186 us -> 190 us (1.022)
  blocking collectives: 105 us -> 81.1 us
  waiting for transfers between devices: 23.2 us -> 38.5 us
  starting transfers between devices: 23.3 us -> 36.6 us
  Pallas kernels: 21.7 us -> 26.9 us
  other arithmetic: 4.62 us -> 1.59 us
  local copies, waits for them, and re-layouts: 7.2 us -> 4.54 us
    all_to_all x4 -> x3, blocking collectives: 105 us -> 81.1 us  [across(): lax.all_to_all(value, GROUP, split_axis=0, concat_axis=0, tiled=True)]
    all_to_all x0 -> x1, waiting for transfers between devices: none -> 16.4 us  [across(): lax.all_to_all(value, GROUP, split_axis=0, concat_axis=0, tiled=True)]
    all_to_all x0 -> x1, starting transfers between devices: none -> 7.06 us  [across(): lax.all_to_all(value, GROUP, split_axis=0, concat_axis=0, tiled=True)]
    ppermute x3, starting transfers between devices: 7.1 us -> 14 us  [exchange(): return lax.ppermute(value, ('zh', 'zl'), swap)]
    pallas_call x5, Pallas kernels: 13.2 us -> 17 us  [the longest x2 7.83 us: forward(): inner(early)]
    ppermute x3, waiting for transfers between devices: 18.9 us -> 15.6 us  [exchange(): return lax.ppermute(value, ('zh', 'zl'), swap)]
    ppermute x2, waiting for transfers between devices: 2.63 us -> 5.1 us  [forward(): below = lax.ppermute(top, 'row', down)]
    unnamed x12 -> x27, local copies, waits for them, and re-layouts: 4.21 us -> 4.03 us
  transfers between devices with their start and end apart: 11 -> 12, of which waited for: 4 -> 6; matrix products, arithmetic and copies ran while one was open for 5% -> 1% of each run, Pallas kernels for 5% -> 5%
where the time goes in v6:
time: 190 us
  blocking collectives  81.1 us (43%)
  waiting for transfers between devices  38.5 us (20%)
  starting transfers between devices  36.6 us (19%)
  Pallas kernels  26.9 us (14%)
  local copies, waits for them, and re-layouts  4.54 us (2%)
    all_to_all x3, blocking collectives, across(): lax.all_to_all(value, GROUP, split_axis=0, concat_axis=0, tiled=True)  81.1 us
    all_to_all x1, waiting for transfers between devices, across(): lax.all_to_all(value, GROUP, split_axis=0, concat_axis=0, tiled=True)  16.4 us
    ppermute x3, waiting for transfers between devices, exchange(): return lax.ppermute(value, ('zh', 'zl'), swap)  15.6 us
    ppermute x3, starting transfers between devices, exchange(): return lax.ppermute(value, ('zh', 'zl'), swap)  14 us
    pallas_call x2, Pallas kernels, forward(): inner(early)  7.83 us
    pallas_call x2, Pallas kernels, forward(): return outer(mat_idx, send_slot, lefts, rights, taps, near, *parts)[:2]  7.41 us
    all_to_all x1, starting transfers between devices, across(): lax.all_to_all(value, GROUP, split_axis=0, concat_axis=0, tiled=True)  7.06 us
    ppermute x2, starting transfers between devices, forward(): lefts = lax.ppermute(last, COL, rightward)  5.84 us
  transfers between devices with their start and end apart: 12, of which 6 were waited for; matrix products, arithmetic and copies ran while one was open for 1% of the time, Pallas kernels for 5%

profile of v6, /device:TPU:0, one launch (start us, length us, event | category | flops | bytes accessed | tf_op | source)
XLA Modules:
  0.0 189.6 jit_solution(1397736596850809551)
XLA Ops:
  0.0 1.8 start.1
  1.8 2.4 %collective-permute-start = (bf16[96,128]{1,0:T(8,128)(2,1)S(1)}, bf16[96,128]{1,0:T(8,128)(2,1)S(1)}, u32[]{:S(2)}, u32[]{:S(2)}) collective-permute-start(bf16[96,128]{1,0:T(8,128)(2,1)S(1)} %get-tuple-element.38), channel_id=1, source_target_pairs={{0,8},{8,16},{16,24},{1,9},{9,17},{17,25},{2,10},{10,18},{18,26},{... | collective-permute-start | bytes 73736 | tf_op jit(solution)/shard_map/ppermute | solution.py:424
  4.2 1.3 collective-permute-start.1
  6.9 2.5 %collective-permute-done.1.below = bf16[96,128]{1,0:T(8,128)(2,1)S(1)} collective-permute-done((bf16[96,128]{1,0:T(8,128)(2,1)S(1)}, bf16[96,128]{1,0:T(8,128)(2,1)S(1)}, u32[]{:S(2)}, u32[]{:S(2)}) %collective-permute-start.1) | collective-permute-done | bytes 24608 | tf_op jit(solution)/shard_map/ppermute | solution.py:425
  9.4 3.4 %collective-permute-start.2 = (f32[48,128]{1,0:T(8,128)S(1)}, f32[48,128]{1,0:T(8,128)S(1)}, u32[]{:S(2)}, u32[]{:S(2)}) collective-permute-start(f32[48,128]{1,0:T(8,128)S(1)} %get-tuple-element.42), channel_id=1, source_target_pairs={{0,1},{1,2},{2,3},{3,4},{4,5},{5,6},{6,7},{8,9},{9,10},{10,11},{11... | collective-permute-start | bytes 73736 | tf_op jit(solution)/shard_map/ppermute | solution.py:427
  12.8 1.3 collective-permute-start.3
  14.1 4.8 %inner.2 = (f32[3,16,2,32,128]{4,3,2,1,0:T(8,128)S(1)}, bf16[96,64,128]{2,1,0:T(8,128)(2,1)S(1)}, bf16[17,2,96,384]{3,2,1,0:T(8,128)(2,1)S(1)}, bf16[1536,256]{1,0:T(8,128)(2,1)S(1)}, bf16[32,64,1024]{2,1,0:T(8,128)(2,1)S(1)}) custom-call(s32[48]{0:T(128)S(1)} %multiply_add_fusion.mat_idx, s32[48]{0:T(128)S(1)} %fusion.25.send_slot, ...), custom_call_target="tpu_custom_call" | custom-call | flops 570425344 | bytes 4194304 | tf_op jit(solution)/shard_map/inner/pallas_call | solution.py:429
  19.0 3.7 %outer.2 = (f32[3,16,2,32,128]{4,3,2,1,0:T(8,128)S(1)}, bf16[96,64,128]{2,1,0:T(8,128)(2,1)S(1)}, bf16[17,2,96,384]{3,2,1,0:T(8,128)(2,1)S(1)}) custom-call(s32[48]{0:T(128)S(1)} %multiply_add_fusion.mat_idx, s32[48]{0:T(128)S(1)} %fusion.25.send_slot, ...), custom_call_target="tpu_custom_call", output_to_operand_aliasing={{0}: (6, {}), {1}: (7, {}), {2}: (8, {})} | custom-call | flops 1140850688 | bytes 4194304 | tf_op jit(solution)/shard_map/outer/pallas_call | solution.py:435
  23.9 7.1 %all-to-all-start = ((bf16[16,6,64,128]{3,2,1,0:T(8,128)(2,1)}), bf16[16,6,64,128]{3,2,1,0:T(8,128)(2,1)S(1)}, u32[]{:S(2)}, u32[]{:S(2)}) async-start(bf16[16,6,64,128]{3,2,1,0:T(8,128)(2,1)} %bitcast.27), calls=%async_computation | async-start | bytes 3145728 | tf_op jit(solution)/shard_map/all_to_all | solution.py:412
  31.5 4.0 %collective-permute-start.5 = (f32[8,64,128]{2,1,0:T(8,128)}, f32[8,64,128]{2,1,0:T(8,128)}, u32[]{:S(2)}, u32[]{:S(2)}) collective-permute-start(f32[8,64,128]{2,1,0:T(8,128)} %own_weight.3), channel_id=1, source_target_pairs={{0,6},{2,4},{4,2},{6,0},{1,7},{3,5},{5,3},{7,1},{8,14},{10,12},{12... | collective-permute-start | bytes 786440 | tf_op jit(solution)/shard_map/ppermute | solution.py:263
  35.5 16.4 %all-to-all-done = bf16[16,6,64,128]{3,2,1,0:T(8,128)(2,1)S(1)} async-done(((bf16[16,6,64,128]{3,2,1,0:T(8,128)(2,1)}), bf16[16,6,64,128]{3,2,1,0:T(8,128)(2,1)S(1)}, u32[]{:S(2)}, u32[]{:S(2)}) %all-to-all-start) | async-done | bytes 1572896 | tf_op jit(solution)/shard_map/all_to_all | solution.py:412
  51.9 1.9 combine.2
  54.5 8.6 %collective-permute-start.4 = (bf16[16,64,128]{2,1,0:T(8,128)(2,1)}, bf16[16,64,128]{2,1,0:T(8,128)(2,1)S(1)}, u32[]{:S(2)}, u32[]{:S(2)}) collective-permute-start(bf16[16,64,128]{2,1,0:T(8,128)(2,1)} %get-tuple-element.53), channel_id=1, source_target_pairs={{0,6},{2,4},{4,2},{6,0},{1,7},{3,5},{5,3},{7,1},{8,14},{10,12},{12... | collective-permute-start | bytes 786440 | tf_op jit(solution)/shard_map/ppermute | solution.py:263
  63.4 6.6 %collective-permute-done.4.other = bf16[16,64,128]{2,1,0:T(8,128)(2,1)S(1)} collective-permute-done((bf16[16,64,128]{2,1,0:T(8,128)(2,1)}, bf16[16,64,128]{2,1,0:T(8,128)(2,1)S(1)}, u32[]{:S(2)}, u32[]{:S(2)}) %collective-permute-start.4) | collective-permute-done | bytes 262176 | tf_op jit(solution)/shard_map/ppermute | solution.py:263
  72.0 1.4 reply.2
  73.4 26.2 %all_to_all.20 = bf16[16,6,64,128]{3,2,1,0:T(8,128)(2,1)S(1)} all-to-all(bf16[16,6,64,128]{3,2,1,0:T(8,128)(2,1)S(1)} %bitcast.26), channel_id=1, replica_groups=mesh['row'=4,'zh'=2,'zl'=2,'x'=2] {'row','zl','x'}, dimensions={0} | all-to-all | bytes 3145728 | tf_op jit(solution)/shard_map/all_to_all | solution.py:412
  99.7 1.8 finish.2
  101.4 2.1 %collective-permute-start.6 = (bf16[96,128]{1,0:T(8,128)(2,1)S(1)}, bf16[96,128]{1,0:T(8,128)(2,1)S(1)}, u32[]{:S(2)}, u32[]{:S(2)}) collective-permute-start(bf16[96,128]{1,0:T(8,128)(2,1)S(1)} %get-tuple-element.56), channel_id=1, source_target_pairs={{0,8},{8,16},{16,24},{1,9},{9,17},{17,25},{2,10},{10,18},{18,26},{... | collective-permute-start | bytes 73736 | tf_op jit(solution)/shard_map/ppermute | solution.py:424
  103.6 1.3 collective-permute-start.7
  104.9 2.6 %collective-permute-done.7.below = bf16[96,128]{1,0:T(8,128)(2,1)S(1)} collective-permute-done((bf16[96,128]{1,0:T(8,128)(2,1)S(1)}, bf16[96,128]{1,0:T(8,128)(2,1)S(1)}, u32[]{:S(2)}, u32[]{:S(2)}) %collective-permute-start.7) | collective-permute-done | bytes 24608 | tf_op jit(solution)/shard_map/ppermute | solution.py:425
  107.5 2.5 %collective-permute-start.8 = (f32[48,128]{1,0:T(8,128)S(1)}, f32[48,128]{1,0:T(8,128)S(1)}, u32[]{:S(2)}, u32[]{:S(2)}) collective-permute-start(f32[48,128]{1,0:T(8,128)S(1)} %get-tuple-element.60), channel_id=1, source_target_pairs={{0,1},{1,2},{2,3},{3,4},{4,5},{5,6},{6,7},{8,9},{9,10},{10,11},{11... | collective-permute-start | bytes 73736 | tf_op jit(solution)/shard_map/ppermute | solution.py:427
  110.0 1.3 collective-permute-start.9
  111.3 3.0 %inner.3 = (f32[3,16,2,32,128]{4,3,2,1,0:T(8,128)S(1)}, bf16[96,64,128]{2,1,0:T(8,128)(2,1)S(1)}, bf16[17,2,96,384]{3,2,1,0:T(8,128)(2,1)S(1)}, bf16[1536,256]{1,0:T(8,128)(2,1)S(1)}) custom-call(s32[48]{0:T(128)S(1)} %multiply_add_fusion.mat_idx, s32[48]{0:T(128)S(1)} %fusion.25.send_slot, bf16[32,96,128]{2,1,0:T(8,128)(2,1)S(1)} %get-tuple-element.62.scaled, ...), custom_call_target="tpu_custom_call" | custom-call | flops 570425344 | bytes 4194304 | tf_op jit(solution)/shard_map/inner/pallas_call | solution.py:429
  114.3 1.4 collective-permute-done.9.right
  115.7 3.7 %outer.3 = (f32[3,16,2,32,128]{4,3,2,1,0:T(8,128)S(1)}, bf16[96,64,128]{2,1,0:T(8,128)(2,1)S(1)}, bf16[17,2,96,384]{3,2,1,0:T(8,128)(2,1)S(1)}) custom-call(s32[48]{0:T(128)S(1)} %multiply_add_fusion.mat_idx, s32[48]{0:T(128)S(1)} %fusion.25.send_slot, ...), custom_call_target="tpu_custom_call", output_to_operand_aliasing={{0}: (6, {}), {1}: (7, {}), {2}: (8, {})} | custom-call | flops 1140850688 | bytes 4194304 | tf_op jit(solution)/shard_map/outer/pallas_call | solution.py:435
  119.4 28.1 %all_to_all.21 = bf16[16,6,64,128]{3,2,1,0:T(8,128)(2,1)S(1)} all-to-all(bf16[16,6,64,128]{3,2,1,0:T(8,128)(2,1)S(1)} %bitcast.28), channel_id=1, replica_groups=mesh['row'=4,'zh'=2,'zl'=2,'x'=2] {'row','zl','x'}, dimensions={0} | all-to-all | bytes 3145728 | tf_op jit(solution)/shard_map/all_to_all | solution.py:412
  147.5 1.2 combine.3
  148.7 1.4 collective-permute-start.10
  150.1 9.0 %collective-permute-done.10.other = bf16[16,64,128]{2,1,0:T(8,128)(2,1)S(1)} collective-permute-done((bf16[16,64,128]{2,1,0:T(8,128)(2,1)S(1)}, bf16[16,64,128]{2,1,0:T(8,128)(2,1)S(1)}, u32[]{:S(2)}, u32[]{:S(2)}) %collective-permute-start.10) | collective-permute-done | bytes 262176 | tf_op jit(solution)/shard_map/ppermute | solution.py:263
  159.1 1.2 reply.3
  160.3 26.8 %all_to_all.22 = bf16[16,6,64,128]{3,2,1,0:T(8,128)(2,1)S(1)} all-to-all(bf16[16,6,64,128]{3,2,1,0:T(8,128)(2,1)S(1)} %bitcast.25), channel_id=1, replica_groups=mesh['row'=4,'zh'=2,'zl'=2,'x'=2] {'row','zl','x'}, dimensions={0} | all-to-all | bytes 3145728 | tf_op jit(solution)/shard_map/all_to_all | solution.py:412
  187.1 2.5 %finish.3 = f32[32,96,128]{2,1,0:T(8,128)} custom-call(s32[48]{0:T(128)S(1)} %multiply_add_fusion.mat_idx, s32[48]{0:T(128)S(1)} %fusion.25.send_slot, bf16[96,64,128]{2,1,0:T(8,128)(2,1)S(1)} %bitcast.29, f32[3,16,2,32,128]{4,3,2,1,0:T(8,128)S(1)} %get-tuple-element.70.pulled, bf16[32,96,128]{2,1,0:T(8,128)(2,1)S(1)} %copy-done.2, ...), custom_call_target="tpu_custom_call" | custom-call | tf_op jit(solution)/shard_map/finish/pallas_call | solution.py:446
  (57 shorter events, 6.2 us)
Async XLA Ops:
  0.0 5.5 %copy-start.11 = (s32[1,3,16]{2,0,1:T(1,128)S(1)}, s32[1,3,16]{2,0,1:T(1,128)}, u32[]{:S(2)}) copy-start(s32[1,3,16]{2,0,1:T(1,128)} %param.15) | copy-start | bytes 580
  0.0 5.6 %copy-start.9 = (s32[4,24,16]{1,2,0:T(8,128)S(1)}, s32[4,24,16]{1,2,0:T(8,128)}, u32[]{:S(2)}) copy-start(s32[4,24,16]{1,2,0:T(8,128)} %param.14) | copy-start | bytes 18436
  0.0 5.8 %copy-start.10 = (s32[256]{0:T(256)S(1)}, s32[256]{0:T(256)}, u32[]{:S(2)}) copy-start(s32[256]{0:T(256)} %param.16) | copy-start | bytes 3076
  0.0 14.1 %copy-start.4 = (bf16[3,3,128,128]{3,2,1,0:T(8,128)(2,1)S(1)}, bf16[3,3,128,128]{3,2,1,0:T(8,128)(2,1)}, u32[]{:S(2)}) copy-start(bf16[3,3,128,128]{3,2,1,0:T(8,128)(2,1)} %kernel.3) | copy-start | bytes 884740
  1.8 5.2 %collective-permute-start = (bf16[96,128]{1,0:T(8,128)(2,1)S(1)}, bf16[96,128]{1,0:T(8,128)(2,1)S(1)}, u32[]{:S(2)}, u32[]{:S(2)}) collective-permute-start(bf16[96,128]{1,0:T(8,128)(2,1)S(1)} %get-tuple-element.38), channel_id=1, source_target_pairs={{0,8},{8,16},{16,24},{1,9},{9,17},{17,25},{2,10},{10,18},{18,26},{... | collective-permute-start | bytes 73736 | tf_op jit(solution)/shard_map/ppermute | solution.py:424
  4.2 5.2 %collective-permute-start.1 = (bf16[96,128]{1,0:T(8,128)(2,1)S(1)}, bf16[96,128]{1,0:T(8,128)(2,1)S(1)}, u32[]{:S(2)}, u32[]{:S(2)}) collective-permute-start(bf16[96,128]{1,0:T(8,128)(2,1)S(1)} %get-tuple-element.39), channel_id=1, source_target_pairs={{8,0},{16,8},{24,16},{9,1},{17,9},{25,17},{10,2},{18,10},{26,18},{... | collective-permute-start | bytes 73736 | tf_op jit(solution)/shard_map/ppermute | solution.py:425
  9.4 9.6 %collective-permute-start.2 = (f32[48,128]{1,0:T(8,128)S(1)}, f32[48,128]{1,0:T(8,128)S(1)}, u32[]{:S(2)}, u32[]{:S(2)}) collective-permute-start(f32[48,128]{1,0:T(8,128)S(1)} %get-tuple-element.42), channel_id=1, source_target_pairs={{0,1},{1,2},{2,3},{3,4},{4,5},{5,6},{6,7},{8,9},{9,10},{10,11},{11... | collective-permute-start | bytes 73736 | tf_op jit(solution)/shard_map/ppermute | solution.py:427
  12.8 6.2 %collective-permute-start.3 = (f32[48,128]{1,0:T(8,128)S(1)}, f32[48,128]{1,0:T(8,128)S(1)}, u32[]{:S(2)}, u32[]{:S(2)}) collective-permute-start(f32[48,128]{1,0:T(8,128)S(1)} %get-tuple-element.43), channel_id=1, source_target_pairs={{1,0},{2,1},{3,2},{4,3},{5,4},{6,5},{7,6},{9,8},{10,9},{11,10},{12... | collective-permute-start | bytes 73736 | tf_op jit(solution)/shard_map/ppermute | solution.py:428
  22.7 1.1 copy-start.3
  23.9 7.1 %copy-start.12 = (s32[8]{0:T(128)S(1)}, s32[8]{0:T(128)}, u32[]{:S(2)}) copy-start(s32[8]{0:T(128)} %param.17) | copy-start | bytes 100
  23.9 28.0 %all-to-all-start = ((bf16[16,6,64,128]{3,2,1,0:T(8,128)(2,1)}), bf16[16,6,64,128]{3,2,1,0:T(8,128)(2,1)S(1)}, u32[]{:S(2)}, u32[]{:S(2)}) async-start(bf16[16,6,64,128]{3,2,1,0:T(8,128)(2,1)} %bitcast.27), calls=%async_computation | async-start | bytes 3145728 | tf_op jit(solution)/shard_map/all_to_all | solution.py:412
  31.5 31.9 %collective-permute-start.5 = (f32[8,64,128]{2,1,0:T(8,128)}, f32[8,64,128]{2,1,0:T(8,128)}, u32[]{:S(2)}, u32[]{:S(2)}) collective-permute-start(f32[8,64,128]{2,1,0:T(8,128)} %own_weight.3), channel_id=1, source_target_pairs={{0,6},{2,4},{4,2},{6,0},{1,7},{3,5},{5,3},{7,1},{8,14},{10,12},{12... | collective-permute-start | bytes 786440 | tf_op jit(solution)/shard_map/ppermute | solution.py:263
  53.7 0.8 copy-start.7
  54.5 15.5 %collective-permute-start.4 = (bf16[16,64,128]{2,1,0:T(8,128)(2,1)}, bf16[16,64,128]{2,1,0:T(8,128)(2,1)S(1)}, u32[]{:S(2)}, u32[]{:S(2)}) collective-permute-start(bf16[16,64,128]{2,1,0:T(8,128)(2,1)} %get-tuple-element.53), channel_id=1, source_target_pairs={{0,6},{2,4},{4,2},{6,0},{1,7},{3,5},{5,3},{7,1},{8,14},{10,12},{12... | collective-permute-start | bytes 786440 | tf_op jit(solution)/shard_map/ppermute | solution.py:263
  70.0 1.0 copy-start.5
  71.0 1.0 copy-start.8
  72.0 27.6 %copy-start = (bf16[8,4,64,1024]{3,2,1,0:T(8,128)(2,1)S(1)}, bf16[8,4,64,1024]{3,2,1,0:T(8,128)(2,1)}, u32[]{:S(2)}) copy-start(bf16[8,4,64,1024]{3,2,1,0:T(8,128)(2,1)} %param.12) | copy-start | bytes 12582916
  73.4 26.3 %copy-start.1 = (bf16[32,96,128]{2,1,0:T(8,128)(2,1)S(1)}, bf16[32,96,128]{2,1,0:T(8,128)(2,1)}, u32[]{:S(2)}) copy-start(bf16[32,96,128]{2,1,0:T(8,128)(2,1)} %state.5) | copy-start | bytes 2359300
  73.4 26.2 %copy-start.2 = (bf16[32,96,128]{2,1,0:T(8,128)(2,1)S(1)}, bf16[32,96,128]{2,1,0:T(8,128)(2,1)}, u32[]{:S(2)}) copy-start(bf16[32,96,128]{2,1,0:T(8,128)(2,1)} %grad.5) | copy-start | bytes 2359300
  101.4 3.5 %collective-permute-start.6 = (bf16[96,128]{1,0:T(8,128)(2,1)S(1)}, bf16[96,128]{1,0:T(8,128)(2,1)S(1)}, u32[]{:S(2)}, u32[]{:S(2)}) collective-permute-start(bf16[96,128]{1,0:T(8,128)(2,1)S(1)} %get-tuple-element.56), channel_id=1, source_target_pairs={{0,8},{8,16},{16,24},{1,9},{9,17},{17,25},{2,10},{10,18},{18,26},{... | collective-permute-start | bytes 73736 | tf_op jit(solution)/shard_map/ppermute | solution.py:424
  103.6 3.9 %collective-permute-start.7 = (bf16[96,128]{1,0:T(8,128)(2,1)S(1)}, bf16[96,128]{1,0:T(8,128)(2,1)S(1)}, u32[]{:S(2)}, u32[]{:S(2)}) collective-permute-start(bf16[96,128]{1,0:T(8,128)(2,1)S(1)} %get-tuple-element.57), channel_id=1, source_target_pairs={{8,0},{16,8},{24,16},{9,1},{17,9},{25,17},{10,2},{18,10},{26,18},{... | collective-permute-start | bytes 73736 | tf_op jit(solution)/shard_map/ppermute | solution.py:425
  107.5 6.8 %collective-permute-start.8 = (f32[48,128]{1,0:T(8,128)S(1)}, f32[48,128]{1,0:T(8,128)S(1)}, u32[]{:S(2)}, u32[]{:S(2)}) collective-permute-start(f32[48,128]{1,0:T(8,128)S(1)} %get-tuple-element.60), channel_id=1, source_target_pairs={{0,1},{1,2},{2,3},{3,4},{4,5},{5,6},{6,7},{8,9},{9,10},{10,11},{11... | collective-permute-start | bytes 73736 | tf_op jit(solution)/shard_map/ppermute | solution.py:427
  110.0 5.7 %collective-permute-start.9 = (f32[48,128]{1,0:T(8,128)S(1)}, f32[48,128]{1,0:T(8,128)S(1)}, u32[]{:S(2)}, u32[]{:S(2)}) collective-permute-start(f32[48,128]{1,0:T(8,128)S(1)} %get-tuple-element.61), channel_id=1, source_target_pairs={{1,0},{2,1},{3,2},{4,3},{5,4},{6,5},{7,6},{9,8},{10,9},{11,10},{12... | collective-permute-start | bytes 73736 | tf_op jit(solution)/shard_map/ppermute | solution.py:428
  147.5 11.6 %copy-start.6 = (f32[8,64,128]{2,1,0:T(8,128)S(1)}, f32[8,64,128]{2,1,0:T(8,128)}, u32[]{:S(2)}) copy-start(f32[8,64,128]{2,1,0:T(8,128)} %own_weight.3) | copy-start | bytes 786436
  148.7 10.4 %collective-permute-start.10 = (bf16[16,64,128]{2,1,0:T(8,128)(2,1)S(1)}, bf16[16,64,128]{2,1,0:T(8,128)(2,1)S(1)}, u32[]{:S(2)}, u32[]{:S(2)}) collective-permute-start(bf16[16,64,128]{2,1,0:T(8,128)(2,1)S(1)} %get-tuple-element.69), channel_id=1, source_target_pairs={{0,6},{2,4},{4,2},{6,0},{1,7},{3,5},{5,3},{7,1},{8,14},{10,12},{12... | collective-permute-start | bytes 786440 | tf_op jit(solution)/shard_map/ppermute | solution.py:263

commit v7 on v6

--- a/solution.py
+++ b/solution.py
@@ -424,22 +424,28 @@
         above = lax.ppermute(bottom, "row", up)
         below = lax.ppermute(top, "row", down)
         first, last = sides(above, below, left, right)
+        if early:
+            last, weight = lax.optimization_barrier((last, ray_weight))
         lefts = lax.ppermute(last, COL, rightward)
         rights = lax.ppermute(first, COL, leftward)
+        other_weight = exchange(weight) if early else None
         *parts, taps = inner(early)(
             mat_idx, send_slot, scaled, above, below, kernel, apart(rays) if early else rays
         )[: 4 + early]
         near = rays
         if early:
             near, taps = taps, parts.pop()
-        return outer(mat_idx, send_slot, lefts, rights, taps, near, *parts)[:2]
+        pulled, outgoing, _ = outer(mat_idx, send_slot, lefts, rights, taps, near, *parts)
+        return pulled, outgoing, other_weight
 
     scaled, *rim = start(apart(state), apart(grad))
     for turn in range(ITERS):
-        pulled, outgoing = forward(turn == 0, scaled, *rim)
+        pulled, outgoing, swapped = forward(turn == 0, scaled, *rim)
         if not turn:
-            outgoing, weight = lax.optimization_barrier((outgoing, ray_weight))
-            other_weight = exchange(weight)
+            other_weight = swapped
+            outgoing, table, used, other_weight = lax.optimization_barrier(
+                (outgoing, table, used, other_weight)
+            )
         total, mine = combine(table, across(outgoing))
         replies = reply(table, used, total, exchange(mine), ray_weight, other_weight)
         last = turn == ITERS - 1

time: 190 us -> 182 us (0.958)
  blocking collectives: 81.1 us -> 108 us
  waiting for transfers between devices: 38.5 us -> 23.3 us
  starting transfers between devices: 36.6 us -> 22.5 us
  local copies, waits for them, and re-layouts: 4.54 us -> 0.62 us
    all_to_all x3 -> x4, blocking collectives: 81.1 us -> 108 us  [across(): lax.all_to_all(value, GROUP, split_axis=0, concat_axis=0, tiled=True)]
    all_to_all x1 -> x0, waiting for transfers between devices: 16.4 us -> none  [across(): lax.all_to_all(value, GROUP, split_axis=0, concat_axis=0, tiled=True)]
    all_to_all x1 -> x0, starting transfers between devices: 7.06 us -> none  [across(): lax.all_to_all(value, GROUP, split_axis=0, concat_axis=0, tiled=True)]
    ppermute x3, starting transfers between devices: 14 us -> 6.93 us  [exchange(): return lax.ppermute(value, ('zh', 'zl'), swap)]
    unnamed x27 -> x19, local copies, waits for them, and re-layouts: 4.03 us -> 0.11 us
    ppermute x3, waiting for transfers between devices: 15.6 us -> 17.6 us  [exchange(): return lax.ppermute(value, ('zh', 'zl'), swap)]
  transfers between devices with their start and end apart: 12 -> 11, of which waited for: 6 -> 5; matrix products, arithmetic and copies ran while one was open for 1% -> 1% of each run, Pallas kernels for 5% -> 6%
where the time goes in v7:
time: 182 us
  blocking collectives  108 us (59%)
  Pallas kernels  25.5 us (14%)
  waiting for transfers between devices  23.3 us (13%)
  starting transfers between devices  22.5 us (12%)
    all_to_all x4, blocking collectives, across(): lax.all_to_all(value, GROUP, split_axis=0, concat_axis=0, tiled=True)  108 us
    ppermute x3, waiting for transfers between devices, exchange(): return lax.ppermute(value, ('zh', 'zl'), swap)  17.6 us
    pallas_call x2, Pallas kernels, forward(): inner(early)  7.9 us
    pallas_call x2, Pallas kernels, forward(): outer(mat_idx, send_slot, lefts, rights, taps, near, *parts)  7.42 us
    ppermute x3, starting transfers between devices, exchange(): return lax.ppermute(value, ('zh', 'zl'), swap)  6.93 us
    ppermute x2, starting transfers between devices, forward(): lefts = lax.ppermute(last, COL, rightward)  5.85 us
    ppermute x2, starting transfers between devices, forward(): above = lax.ppermute(bottom, 'row', up)  4.57 us
    pallas_call x2, Pallas kernels, on_device(): finish(last)(mat_idx, send_slot, across(replies), pulled, grad, state, rays)  4.46 us
  transfers between devices with their start and end apart: 11, of which 5 were waited for; matrix products, arithmetic and copies ran while one was open for 1% of the time, Pallas kernels for 6%

profile of v7, /device:TPU:0, one launch (start us, length us, event | category | flops | bytes accessed | tf_op | source)
XLA Modules:
  0.0 181.7 jit_solution(7491140808228791704)
XLA Ops:
  0.0 1.8 start.1
  1.8 2.4 %collective-permute-start = (bf16[96,128]{1,0:T(8,128)(2,1)S(1)}, bf16[96,128]{1,0:T(8,128)(2,1)S(1)}, u32[]{:S(2)}, u32[]{:S(2)}) collective-permute-start(bf16[96,128]{1,0:T(8,128)(2,1)S(1)} %get-tuple-element.42), channel_id=1, source_target_pairs={{0,8},{8,16},{16,24},{1,9},{9,17},{17,25},{2,10},{10,18},{18,26},{... | collective-permute-start | bytes 73736 | tf_op jit(solution)/shard_map/ppermute | solution.py:424
  4.2 1.3 collective-permute-start.1
  5.8 0.5 select_reduce_fusion
  7.8 1.7 collective-permute-done.1.below
  9.5 3.7 %collective-permute-start.4 = (f32[8,64,128]{2,1,0:T(8,128)S(1)}, f32[8,64,128]{2,1,0:T(8,128)S(1)}, u32[]{:S(2)}, u32[]{:S(2)}) collective-permute-start(f32[8,64,128]{2,1,0:T(8,128)S(1)} %copy-done.4), channel_id=1, source_target_pairs={{0,6},{2,4},{4,2},{6,0},{1,7},{3,5},{5,3},{7,1},{8,14},{10,12},{12... | collective-permute-start | bytes 786440 | tf_op jit(solution)/shard_map/ppermute | solution.py:263
  13.2 3.4 %collective-permute-start.2 = (f32[48,128]{1,0:T(8,128)S(1)}, f32[48,128]{1,0:T(8,128)S(1)}, u32[]{:S(2)}, u32[]{:S(2)}) collective-permute-start(f32[48,128]{1,0:T(8,128)S(1)} %get-tuple-element.47), channel_id=1, source_target_pairs={{0,1},{1,2},{2,3},{3,4},{4,5},{5,6},{6,7},{8,9},{9,10},{10,11},{11... | collective-permute-start | bytes 73736 | tf_op jit(solution)/shard_map/ppermute | solution.py:429
  16.6 1.3 collective-permute-start.3
  17.9 4.9 %inner.2 = (f32[3,16,2,32,128]{4,3,2,1,0:T(8,128)S(1)}, bf16[96,64,128]{2,1,0:T(8,128)(2,1)S(1)}, bf16[17,2,96,384]{3,2,1,0:T(8,128)(2,1)S(1)}, bf16[1536,256]{1,0:T(8,128)(2,1)S(1)}, bf16[32,64,1024]{2,1,0:T(8,128)(2,1)S(1)}) custom-call(s32[48]{0:T(128)S(1)} %multiply_add_fusion.mat_idx, s32[48]{0:T(128)S(1)} %fusion.25.send_slot, ...), custom_call_target="tpu_custom_call" | custom-call | flops 570425344 | bytes 4194304 | tf_op jit(solution)/shard_map/inner/pallas_call | solution.py:432
  22.8 3.7 %outer.2 = (f32[3,16,2,32,128]{4,3,2,1,0:T(8,128)S(1)}, bf16[96,64,128]{2,1,0:T(8,128)(2,1)S(1)}, bf16[17,2,96,384]{3,2,1,0:T(8,128)(2,1)S(1)}) custom-call(s32[48]{0:T(128)S(1)} %multiply_add_fusion.mat_idx, s32[48]{0:T(128)S(1)} %fusion.25.send_slot, ...), custom_call_target="tpu_custom_call", output_to_operand_aliasing={{0}: (6, {}), {1}: (7, {}), {2}: (8, {})} | custom-call | flops 1140850688 | bytes 4194304 | tf_op jit(solution)/shard_map/outer/pallas_call | solution.py:438
  26.5 27.1 %all_to_all.20 = bf16[16,6,64,128]{3,2,1,0:T(8,128)(2,1)S(1)} all-to-all(bf16[16,6,64,128]{3,2,1,0:T(8,128)(2,1)S(1)} %bitcast.27), channel_id=1, replica_groups=mesh['row'=4,'zh'=2,'zl'=2,'x'=2] {'row','zl','x'}, dimensions={0} | all-to-all | bytes 3145728 | tf_op jit(solution)/shard_map/all_to_all | solution.py:412
  53.6 1.2 combine.2
  54.8 1.9 %collective-permute-start.5 = (bf16[16,64,128]{2,1,0:T(8,128)(2,1)S(1)}, bf16[16,64,128]{2,1,0:T(8,128)(2,1)S(1)}, u32[]{:S(2)}, u32[]{:S(2)}) collective-permute-start(bf16[16,64,128]{2,1,0:T(8,128)(2,1)S(1)} %get-tuple-element.61), channel_id=1, source_target_pairs={{0,6},{2,4},{4,2},{6,0},{1,7},{3,5},{5,3},{7,1},{8,14},{10,12},{12... | collective-permute-start | bytes 786440 | tf_op jit(solution)/shard_map/ppermute | solution.py:263
  56.6 8.6 %collective-permute-done.5.other = bf16[16,64,128]{2,1,0:T(8,128)(2,1)S(1)} collective-permute-done((bf16[16,64,128]{2,1,0:T(8,128)(2,1)S(1)}, bf16[16,64,128]{2,1,0:T(8,128)(2,1)S(1)}, u32[]{:S(2)}, u32[]{:S(2)}) %collective-permute-start.5) | collective-permute-done | bytes 262176 | tf_op jit(solution)/shard_map/ppermute | solution.py:263
  65.2 0.8 reply.2
  66.0 27.1 %all_to_all.21 = bf16[16,6,64,128]{3,2,1,0:T(8,128)(2,1)S(1)} all-to-all(bf16[16,6,64,128]{3,2,1,0:T(8,128)(2,1)S(1)} %bitcast.26), channel_id=1, replica_groups=mesh['row'=4,'zh'=2,'zl'=2,'x'=2] {'row','zl','x'}, dimensions={0} | all-to-all | bytes 3145728 | tf_op jit(solution)/shard_map/all_to_all | solution.py:412
  93.1 1.9 %finish.2 = (bf16[32,96,128]{2,1,0:T(8,128)(2,1)S(1)}, bf16[96,128]{1,0:T(8,128)(2,1)S(1)}, bf16[96,128]{1,0:T(8,128)(2,1)S(1)}, bf16[32,128]{1,0:T(8,128)(2,1)S(1)}, bf16[32,128]{1,0:T(8,128)(2,1)S(1)}) custom-call(s32[48]{0:T(128)S(1)} %multiply_add_fusion.mat_idx, s32[48]{0:T(128)S(1)} %fusion.25.send_slot, bf16[96,64,128]{2,1,0:T(8,128)(2,1)S(1)} %bitcast.22, ...), custom_call_target="tpu_custom_call" | custom-call | tf_op jit(solution)/shard_map/finish/pallas_call | solution.py:452
  95.0 2.2 %collective-permute-start.6 = (bf16[96,128]{1,0:T(8,128)(2,1)S(1)}, bf16[96,128]{1,0:T(8,128)(2,1)S(1)}, u32[]{:S(2)}, u32[]{:S(2)}) collective-permute-start(bf16[96,128]{1,0:T(8,128)(2,1)S(1)} %get-tuple-element.64), channel_id=1, source_target_pairs={{0,8},{8,16},{16,24},{1,9},{9,17},{17,25},{2,10},{10,18},{18,26},{... | collective-permute-start | bytes 73736 | tf_op jit(solution)/shard_map/ppermute | solution.py:424
  97.1 1.3 collective-permute-start.7
  98.5 2.6 %collective-permute-done.7.below = bf16[96,128]{1,0:T(8,128)(2,1)S(1)} collective-permute-done((bf16[96,128]{1,0:T(8,128)(2,1)S(1)}, bf16[96,128]{1,0:T(8,128)(2,1)S(1)}, u32[]{:S(2)}, u32[]{:S(2)}) %collective-permute-start.7) | collective-permute-done | bytes 24608 | tf_op jit(solution)/shard_map/ppermute | solution.py:425
  101.1 2.5 %collective-permute-start.8 = (f32[48,128]{1,0:T(8,128)S(1)}, f32[48,128]{1,0:T(8,128)S(1)}, u32[]{:S(2)}, u32[]{:S(2)}) collective-permute-start(f32[48,128]{1,0:T(8,128)S(1)} %get-tuple-element.68), channel_id=1, source_target_pairs={{0,1},{1,2},{2,3},{3,4},{4,5},{5,6},{6,7},{8,9},{9,10},{10,11},{11... | collective-permute-start | bytes 73736 | tf_op jit(solution)/shard_map/ppermute | solution.py:429
  103.5 1.3 collective-permute-start.9
  104.8 3.0 %inner.3 = (f32[3,16,2,32,128]{4,3,2,1,0:T(8,128)S(1)}, bf16[96,64,128]{2,1,0:T(8,128)(2,1)S(1)}, bf16[17,2,96,384]{3,2,1,0:T(8,128)(2,1)S(1)}, bf16[1536,256]{1,0:T(8,128)(2,1)S(1)}) custom-call(s32[48]{0:T(128)S(1)} %multiply_add_fusion.mat_idx, s32[48]{0:T(128)S(1)} %fusion.25.send_slot, bf16[32,96,128]{2,1,0:T(8,128)(2,1)S(1)} %get-tuple-element.70.scaled, ...), custom_call_target="tpu_custom_call" | custom-call | flops 570425344 | bytes 4194304 | tf_op jit(solution)/shard_map/inner/pallas_call | solution.py:432
  107.9 1.4 collective-permute-done.9.right
  109.3 3.7 %outer.3 = (f32[3,16,2,32,128]{4,3,2,1,0:T(8,128)S(1)}, bf16[96,64,128]{2,1,0:T(8,128)(2,1)S(1)}, bf16[17,2,96,384]{3,2,1,0:T(8,128)(2,1)S(1)}) custom-call(s32[48]{0:T(128)S(1)} %multiply_add_fusion.mat_idx, s32[48]{0:T(128)S(1)} %fusion.25.send_slot, ...), custom_call_target="tpu_custom_call", output_to_operand_aliasing={{0}: (6, {}), {1}: (7, {}), {2}: (8, {})} | custom-call | flops 1140850688 | bytes 4194304 | tf_op jit(solution)/shard_map/outer/pallas_call | solution.py:438
  113.0 26.9 %all_to_all.22 = bf16[16,6,64,128]{3,2,1,0:T(8,128)(2,1)S(1)} all-to-all(bf16[16,6,64,128]{3,2,1,0:T(8,128)(2,1)S(1)} %bitcast.28), channel_id=1, replica_groups=mesh['row'=4,'zh'=2,'zl'=2,'x'=2] {'row','zl','x'}, dimensions={0} | all-to-all | bytes 3145728 | tf_op jit(solution)/shard_map/all_to_all | solution.py:412
  139.9 1.2 combine.3
  141.1 1.4 collective-permute-start.10
  142.5 9.0 %collective-permute-done.10.other = bf16[16,64,128]{2,1,0:T(8,128)(2,1)S(1)} collective-permute-done((bf16[16,64,128]{2,1,0:T(8,128)(2,1)S(1)}, bf16[16,64,128]{2,1,0:T(8,128)(2,1)S(1)}, u32[]{:S(2)}, u32[]{:S(2)}) %collective-permute-start.10) | collective-permute-done | bytes 262176 | tf_op jit(solution)/shard_map/ppermute | solution.py:263
  151.5 0.8 reply.3
  152.3 26.8 %all_to_all.23 = bf16[16,6,64,128]{3,2,1,0:T(8,128)(2,1)S(1)} all-to-all(bf16[16,6,64,128]{3,2,1,0:T(8,128)(2,1)S(1)} %bitcast.25), channel_id=1, replica_groups=mesh['row'=4,'zh'=2,'zl'=2,'x'=2] {'row','zl','x'}, dimensions={0} | all-to-all | bytes 3145728 | tf_op jit(solution)/shard_map/all_to_all | solution.py:412
  179.1 2.6 %finish.3 = f32[32,96,128]{2,1,0:T(8,128)} custom-call(s32[48]{0:T(128)S(1)} %multiply_add_fusion.mat_idx, s32[48]{0:T(128)S(1)} %fusion.25.send_slot, bf16[96,64,128]{2,1,0:T(8,128)(2,1)S(1)} %bitcast.29, f32[3,16,2,32,128]{4,3,2,1,0:T(8,128)S(1)} %get-tuple-element.78.pulled, bf16[32,96,128]{2,1,0:T(8,128)(2,1)S(1)} %copy-done.2, ...), custom_call_target="tpu_custom_call" | custom-call | tf_op jit(solution)/shard_map/finish/pallas_call | solution.py:452
  (48 shorter events, 1.7 us)
Async XLA Ops:
  0.0 5.6 %copy-start.5 = (s32[4,24,16]{1,2,0:T(8,128)S(1)}, s32[4,24,16]{1,2,0:T(8,128)}, u32[]{:S(2)}) copy-start(s32[4,24,16]{1,2,0:T(8,128)} %param.14) | copy-start | bytes 18436
  0.0 5.8 %copy-start.6 = (s32[256]{0:T(256)S(1)}, s32[256]{0:T(256)}, u32[]{:S(2)}) copy-start(s32[256]{0:T(256)} %param.16) | copy-start | bytes 3076
  0.0 6.4 %copy-start.7 = (s32[1,3,16]{2,0,1:T(1,128)S(1)}, s32[1,3,16]{2,0,1:T(1,128)}, u32[]{:S(2)}) copy-start(s32[1,3,16]{2,0,1:T(1,128)} %param.15) | copy-start | bytes 580
  0.0 7.2 %copy-start.8 = (s32[8]{0:T(128)S(1)}, s32[8]{0:T(128)}, u32[]{:S(2)}) copy-start(s32[8]{0:T(128)} %param.17) | copy-start | bytes 100
  0.0 9.4 %copy-start.4 = (f32[8,64,128]{2,1,0:T(8,128)S(1)}, f32[8,64,128]{2,1,0:T(8,128)}, u32[]{:S(2)}) copy-start(f32[8,64,128]{2,1,0:T(8,128)} %own_weight.3) | copy-start | bytes 786436
  0.0 17.9 %copy-start.3 = (bf16[3,3,128,128]{3,2,1,0:T(8,128)(2,1)S(1)}, bf16[3,3,128,128]{3,2,1,0:T(8,128)(2,1)}, u32[]{:S(2)}) copy-start(bf16[3,3,128,128]{3,2,1,0:T(8,128)(2,1)} %kernel.3) | copy-start | bytes 884740
  1.8 6.0 %collective-permute-start = (bf16[96,128]{1,0:T(8,128)(2,1)S(1)}, bf16[96,128]{1,0:T(8,128)(2,1)S(1)}, u32[]{:S(2)}, u32[]{:S(2)}) collective-permute-start(bf16[96,128]{1,0:T(8,128)(2,1)S(1)} %get-tuple-element.42), channel_id=1, source_target_pairs={{0,8},{8,16},{16,24},{1,9},{9,17},{17,25},{2,10},{10,18},{18,26},{... | collective-permute-start | bytes 73736 | tf_op jit(solution)/shard_map/ppermute | solution.py:424
  4.2 5.2 %collective-permute-start.1 = (bf16[96,128]{1,0:T(8,128)(2,1)S(1)}, bf16[96,128]{1,0:T(8,128)(2,1)S(1)}, u32[]{:S(2)}, u32[]{:S(2)}) collective-permute-start(bf16[96,128]{1,0:T(8,128)(2,1)S(1)} %get-tuple-element.43), channel_id=1, source_target_pairs={{8,0},{16,8},{24,16},{9,1},{17,9},{25,17},{10,2},{18,10},{26,18},{... | collective-permute-start | bytes 73736 | tf_op jit(solution)/shard_map/ppermute | solution.py:425
  9.5 17.1 %collective-permute-start.4 = (f32[8,64,128]{2,1,0:T(8,128)S(1)}, f32[8,64,128]{2,1,0:T(8,128)S(1)}, u32[]{:S(2)}, u32[]{:S(2)}) collective-permute-start(f32[8,64,128]{2,1,0:T(8,128)S(1)} %copy-done.4), channel_id=1, source_target_pairs={{0,6},{2,4},{4,2},{6,0},{1,7},{3,5},{5,3},{7,1},{8,14},{10,12},{12... | collective-permute-start | bytes 786440 | tf_op jit(solution)/shard_map/ppermute | solution.py:263
  13.2 9.6 %collective-permute-start.2 = (f32[48,128]{1,0:T(8,128)S(1)}, f32[48,128]{1,0:T(8,128)S(1)}, u32[]{:S(2)}, u32[]{:S(2)}) collective-permute-start(f32[48,128]{1,0:T(8,128)S(1)} %get-tuple-element.47), channel_id=1, source_target_pairs={{0,1},{1,2},{2,3},{3,4},{4,5},{5,6},{6,7},{8,9},{9,10},{10,11},{11... | collective-permute-start | bytes 73736 | tf_op jit(solution)/shard_map/ppermute | solution.py:429
  16.6 6.2 %collective-permute-start.3 = (f32[48,128]{1,0:T(8,128)S(1)}, f32[48,128]{1,0:T(8,128)S(1)}, u32[]{:S(2)}, u32[]{:S(2)}) collective-permute-start(f32[48,128]{1,0:T(8,128)S(1)} %get-tuple-element.48), channel_id=1, source_target_pairs={{1,0},{2,1},{3,2},{4,3},{5,4},{6,5},{7,6},{9,8},{10,9},{11,10},{12... | collective-permute-start | bytes 73736 | tf_op jit(solution)/shard_map/ppermute | solution.py:430
  54.8 10.4 %collective-permute-start.5 = (bf16[16,64,128]{2,1,0:T(8,128)(2,1)S(1)}, bf16[16,64,128]{2,1,0:T(8,128)(2,1)S(1)}, u32[]{:S(2)}, u32[]{:S(2)}) collective-permute-start(bf16[16,64,128]{2,1,0:T(8,128)(2,1)S(1)} %get-tuple-element.61), channel_id=1, source_target_pairs={{0,6},{2,4},{4,2},{6,0},{1,7},{3,5},{5,3},{7,1},{8,14},{10,12},{12... | collective-permute-start | bytes 786440 | tf_op jit(solution)/shard_map/ppermute | solution.py:263
  65.2 27.9 %copy-start = (bf16[8,4,64,1024]{3,2,1,0:T(8,128)(2,1)S(1)}, bf16[8,4,64,1024]{3,2,1,0:T(8,128)(2,1)}, u32[]{:S(2)}) copy-start(bf16[8,4,64,1024]{3,2,1,0:T(8,128)(2,1)} %param.12) | copy-start | bytes 12582916
  66.0 27.1 %copy-start.1 = (bf16[32,96,128]{2,1,0:T(8,128)(2,1)S(1)}, bf16[32,96,128]{2,1,0:T(8,128)(2,1)}, u32[]{:S(2)}) copy-start(bf16[32,96,128]{2,1,0:T(8,128)(2,1)} %state.5) | copy-start | bytes 2359300
  66.0 27.1 %copy-start.2 = (bf16[32,96,128]{2,1,0:T(8,128)(2,1)S(1)}, bf16[32,96,128]{2,1,0:T(8,128)(2,1)}, u32[]{:S(2)}) copy-start(bf16[32,96,128]{2,1,0:T(8,128)(2,1)} %grad.5) | copy-start | bytes 2359300
  95.0 3.5 %collective-permute-start.6 = (bf16[96,128]{1,0:T(8,128)(2,1)S(1)}, bf16[96,128]{1,0:T(8,128)(2,1)S(1)}, u32[]{:S(2)}, u32[]{:S(2)}) collective-permute-start(bf16[96,128]{1,0:T(8,128)(2,1)S(1)} %get-tuple-element.64), channel_id=1, source_target_pairs={{0,8},{8,16},{16,24},{1,9},{9,17},{17,25},{2,10},{10,18},{18,26},{... | collective-permute-start | bytes 73736 | tf_op jit(solution)/shard_map/ppermute | solution.py:424
  97.1 3.9 %collective-permute-start.7 = (bf16[96,128]{1,0:T(8,128)(2,1)S(1)}, bf16[96,128]{1,0:T(8,128)(2,1)S(1)}, u32[]{:S(2)}, u32[]{:S(2)}) collective-permute-start(bf16[96,128]{1,0:T(8,128)(2,1)S(1)} %get-tuple-element.65), channel_id=1, source_target_pairs={{8,0},{16,8},{24,16},{9,1},{17,9},{25,17},{10,2},{18,10},{26,18},{... | collective-permute-start | bytes 73736 | tf_op jit(solution)/shard_map/ppermute | solution.py:425
  101.1 6.8 %collective-permute-start.8 = (f32[48,128]{1,0:T(8,128)S(1)}, f32[48,128]{1,0:T(8,128)S(1)}, u32[]{:S(2)}, u32[]{:S(2)}) collective-permute-start(f32[48,128]{1,0:T(8,128)S(1)} %get-tuple-element.68), channel_id=1, source_target_pairs={{0,1},{1,2},{2,3},{3,4},{4,5},{5,6},{6,7},{8,9},{9,10},{10,11},{11... | collective-permute-start | bytes 73736 | tf_op jit(solution)/shard_map/ppermute | solution.py:429
  103.5 5.7 %collective-permute-start.9 = (f32[48,128]{1,0:T(8,128)S(1)}, f32[48,128]{1,0:T(8,128)S(1)}, u32[]{:S(2)}, u32[]{:S(2)}) collective-permute-start(f32[48,128]{1,0:T(8,128)S(1)} %get-tuple-element.69), channel_id=1, source_target_pairs={{1,0},{2,1},{3,2},{4,3},{5,4},{6,5},{7,6},{9,8},{10,9},{11,10},{12... | collective-permute-start | bytes 73736 | tf_op jit(solution)/shard_map/ppermute | solution.py:430
  141.1 10.4 %collective-permute-start.10 = (bf16[16,64,128]{2,1,0:T(8,128)(2,1)S(1)}, bf16[16,64,128]{2,1,0:T(8,128)(2,1)S(1)}, u32[]{:S(2)}, u32[]{:S(2)}) collective-permute-start(bf16[16,64,128]{2,1,0:T(8,128)(2,1)S(1)} %get-tuple-element.77), channel_id=1, source_target_pairs={{0,6},{2,4},{4,2},{6,0},{1,7},{3,5},{5,3},{7,1},{8,14},{10,12},{12... | collective-permute-start | bytes 786440 | tf_op jit(solution)/shard_map/ppermute | solution.py:263

commit v8 on v7

--- a/solution.py
+++ b/solution.py
@@ -23,7 +23,7 @@
 ANY = pl.BlockSpec(memory_space=pl.ANY)
 
 
-def start_kernel(state, grad, scaled, top, bottom, left, right, states, grads, whole, mark):
+def start_kernel(odd, state, grad, scaled, row_a, row_b, col_a, col_b, states, grads, whole, mark):
     parts = mark.shape[1]
     rows = states.shape[0] // parts
 
@@ -41,29 +41,41 @@
         where = slice(p * rows, (p + 1) * rows)
         value = states[where].astype(jnp.float32)
         whole[where] = (1.0 - value * value) * grads[where].astype(jnp.float32)
-    emit_edges(whole[...], scaled, top, bottom, left, right)
-
-
-def emit_edges(value, scaled, top, bottom, left, right):
+    emit_edges(whole[...], odd, scaled, row_a, row_b, col_a, col_b)
+
+
+def pick(flag, yes, no):
+    return jnp.where(flag == 1, yes, no)
+
+
+def emit_edges(value, odd, scaled, row_a, row_b, col_a, col_b):
     rows, cols = value.shape[:2]
     scaled[...] = value.astype(jnp.bfloat16)
-    top[...] = scaled[0]
-    bottom[...] = scaled[rows - 1]
-    left[...] = value[:, 0, :].astype(jnp.bfloat16)
-    right[...] = value[:, cols - 1, :].astype(jnp.bfloat16)
-
-
-def sides_kernel(above, below, left, right, first, last):
-    rows = left.shape[0]
-    cols = above.shape[0]
+    row_a[...] = pick(odd[0], value[0], value[rows - 1]).astype(jnp.bfloat16)
+    row_b[...] = pick(odd[0], value[rows - 1], value[0]).astype(jnp.bfloat16)
+    left, right = value[:, 0, :], value[:, cols - 1, :]
+    col_a[...] = pick(odd[1], left, right)
+    col_b[...] = pick(odd[1], right, left)
+
+
+def sides_kernel(odd, near_a, near_b, col_a, col_b, out_a, out_b):
+    rows = col_a.shape[0]
+    cols = near_a.shape[0]
     f32 = jnp.float32
-    for out, edge, at in ((first, left, 0), (last, right, cols - 1)):
-        group = at // 16 * 16
-        corner_a = above[group : group + 16, :].astype(f32)[at - group : at - group + 1, :]
-        corner_b = below[group : group + 16, :].astype(f32)[at - group : at - group + 1, :]
-        out[8 : 8 + rows, :] = edge[...].astype(f32)
-        out[7:8, :] = corner_a
-        out[8 + rows : 9 + rows, :] = corner_b
+
+    def ends(ref):
+        low = ref[0:16, :].astype(f32)[0:1, :]
+        high = ref[cols - 16 : cols, :].astype(f32)[15:16, :]
+        return low, high
+
+    a, b = ends(near_a), ends(near_b)
+    above = [pick(odd[0], a[i], b[i]) for i in range(2)]
+    below = [pick(odd[0], b[i], a[i]) for i in range(2)]
+    for out, edge, order in ((out_a, col_a, (0, 1)), (out_b, col_b, (1, 0))):
+        yes, no = order
+        out[8 : 8 + rows, :] = edge[...]
+        out[7:8, :] = pick(odd[1], above[yes], above[no])
+        out[8 + rows : 9 + rows, :] = pick(odd[1], below[yes], below[no])
 
 
 def matrices_of(mat_idx, rays, t):
@@ -105,17 +117,20 @@
 
 
 def inner_kernel(
-    mat_idx, send_slot, scaled, above, below, kernel, rays, pulled, out, cols3, taps, *refs,
-    tile_cols,
+    odd, mat_idx, send_slot, scaled, near_a, near_b, kernel, rays,
+    pulled, out, cols3, taps, *refs, tile_cols,
 ):
     wide = refs[-1]
     rows, cols, chans = scaled.shape
     f32, bf16 = jnp.float32, jnp.bfloat16
-    load = None
+    waiting = []
     if len(refs) > 1:
         held, mark = refs[:2]
-        load = pltpu.make_async_copy(rays, held, mark.at[0])
-        load.start()
+        count = rays.shape[0] // mark.shape[0]
+        for i in range(mark.shape[0]):
+            where = pl.ds(i * count, count)
+            waiting.append(pltpu.make_async_copy(rays.at[where], held.at[where], mark.at[i]))
+            waiting[-1].start()
         rays = held
     blank = jnp.zeros((3 * chans, chans), bf16)
     for dr in range(4):
@@ -128,8 +143,9 @@
                 continue
             for dc in range(3):
                 taps[base + dc * chans : base + (dc + 1) * chans, lanes] = kernel[2 - tap, 2 - dc].T
-    wide[0, 8 : 8 + cols, :] = above[...].astype(f32)
-    wide[rows + 1, 8 : 8 + cols, :] = below[...].astype(f32)
+    a, b = near_a[...].astype(f32), near_b[...].astype(f32)
+    wide[0, 8 : 8 + cols, :] = pick(odd[0], a, b)
+    wide[rows + 1, 8 : 8 + cols, :] = pick(odd[0], b, a)
     wide[1 : rows + 1, 8 : 8 + cols, :] = scaled[...].astype(f32)
     wide[:, 0:8, :] = jnp.zeros((rows + 2, 8, chans), f32)
     wide[:, 8 + cols :, :] = jnp.zeros((rows + 2, 8, chans), f32)
@@ -139,7 +155,6 @@
             (rows + 2) // 2, 2, cols, chans
         )
     out[...] = jnp.zeros_like(out)
-    waiting = [load] if load is not None else []
     for t in tiles_at(pulled.shape[0], tile_cols, True):
         forward_tile(mat_idx, send_slot, taps, rays, pulled, out, cols3, t, tile_cols, waiting)
     while waiting:
@@ -147,13 +162,15 @@
 
 
 def outer_kernel(
-    mat_idx, send_slot, left, right, taps, rays, _pulled, _out, _cols3,
+    odd, mat_idx, send_slot, near_a, near_b, taps, rays, _pulled, _out, _cols3,
     pulled, out, cols3, *, tile_cols,
 ):
     cols = cols3.shape[2]
     chans = pulled.shape[-1]
     group = 16
     spot = lax.broadcasted_iota(jnp.int32, (group, chans), 0)
+    a, b = near_a[...], near_b[...]
+    left, right = pick(odd[1], a, b), pick(odd[1], b, a)
     for edge, dc, first, at in ((left, 0, 0, 0), (right, 2, cols - group, group - 1)):
         lanes = slice(dc * chans, (dc + 1) * chans)
         for r in range(2 * cols3.shape[0]):
@@ -197,7 +214,7 @@
 
 
 def finish_kernel(
-    mat_idx, send_slot, returned, pulled, grad, state, rays, *refs, tile_cols, last,
+    odd, mat_idx, send_slot, returned, pulled, grad, state, rays, *refs, tile_cols, last,
 ):
     outs, (whole, mark) = refs[:-2], refs[-2:]
     tiles = pulled.shape[0]
@@ -233,7 +250,7 @@
         for t in range(tiles):
             leave(t).wait()
     else:
-        emit_edges(whole[...], *outs)
+        emit_edges(whole[...], odd, *outs)
 
 
 def on_device(state, grad, kernel, ray_matrix, ray_weight, hits, offsets, block_slot, angle_count):
@@ -257,10 +274,9 @@
     peers = nr * 2 * nx
     slots = peers * cap
     dense = 2 * blk_dev
-    swap = [(z, RING - 1 - z) for z in range(RING)]
 
     def exchange(value):
-        return lax.ppermute(value, ("zh", "zl"), swap)
+        return lax.ppermute(value, "zh", [(0, 1), (1, 0)])
 
     everyone = hits.reshape(nr, tile_rows, nc, tile_cols, HITS).transpose(0, 2, 1, 3, 4)
     everyone = everyone.reshape(nr, 2, 2, nx, pairs)
@@ -273,8 +289,7 @@
     owner_z = (owner % nc) // nx
     owner_zh = owner_z // 2
     owner_zl = owner_z % 2
-    side = jnp.where(owner_zh == zh, owner_zl, 1 - owner_zl)
-    peer = ((owner // nc) * 2 + side) * nx + owner % nx
+    peer = ((owner // nc) * 2 + owner_zl) * nx + owner % nx
     place = owner_zh * blk_dev + local
     earlier = jnp.arange(pairs)[None, :] < jnp.arange(pairs)[:, None]
     ranking = jnp.sum(
@@ -290,9 +305,7 @@
     table = table.reshape(slots)
     mat_idx = (my_hits // blk_ang) * spots + offsets.reshape(pairs)
 
-    my_z = zh * 2 + zl
-    half = jnp.arange(dense, dtype=i32) // blk_dev
-    dense_z = jnp.where(half == zh, my_z, RING - 1 - my_z)
+    dense_z = jnp.arange(dense, dtype=i32) // blk_dev * 2 + zl
     dense_place = (row * nc + dense_z * nx + x) * blk_dev + jnp.arange(dense, dtype=i32) % blk_dev
     number = jnp.arange(blocks, dtype=i32)
     active = (
@@ -310,9 +323,10 @@
         shape(state.shape, bf16),
         shape((cols_dev, chans), bf16),
         shape((cols_dev, chans), bf16),
-        shape((rows_dev, chans), bf16),
-        shape((rows_dev, chans), bf16),
-    )
+        shape((rows_dev, chans), f32),
+        shape((rows_dev, chans), f32),
+    )
+    odd = jnp.stack([row % 2, (zh * (RING // 2) * nx + zl * nx + x) % 2])
 
     def limit(mib):
         return pltpu.CompilerParams(vmem_limit_bytes=mib << 20)
@@ -320,7 +334,7 @@
     start = pl.pallas_call(
         start_kernel,
         out_shape=edges,
-        in_specs=[ANY] * 2,
+        in_specs=[SMEM] + [ANY] * 2,
         out_specs=(VMEM,) * 5,
         scratch_shapes=[
             pltpu.VMEM(state.shape, bf16),
@@ -334,7 +348,7 @@
     sides = pl.pallas_call(
         sides_kernel,
         out_shape=[shape((rows_dev + 16, chans), f32)] * 2,
-        in_specs=[VMEM] * 4,
+        in_specs=[SMEM] + [VMEM] * 4,
         out_specs=[VMEM] * 2,
         compiler_params=limit(4),
         name="sides",
@@ -352,11 +366,11 @@
 
     def inner(early):
         held = (shape(rays.shape, bf16),) if early else ()
-        mark = [pltpu.SemaphoreType.DMA((1,))] if early else []
+        mark = [pltpu.SemaphoreType.DMA((angles,))] if early else []
         return pl.pallas_call(
             functools.partial(inner_kernel, tile_cols=tile_cols),
             out_shape=(pulled_out, slot_out, cols3_out, taps_out) + held,
-            in_specs=[SMEM] * 2 + [VMEM] * 4 + [ANY if early else VMEM],
+            in_specs=[SMEM] * 3 + [VMEM] * 4 + [ANY if early else VMEM],
             out_specs=(VMEM,) * (4 + len(held)),
             scratch_shapes=mark + [pltpu.VMEM((rows_dev + 2, cols_dev + 16, chans), f32)],
             compiler_params=limit(16),
@@ -367,9 +381,9 @@
     outer = pl.pallas_call(
         functools.partial(outer_kernel, tile_cols=tile_cols),
         out_shape=(pulled_out, slot_out, cols3_out),
-        in_specs=[SMEM] * 2 + [VMEM] * 7,
+        in_specs=[SMEM] * 3 + [VMEM] * 7,
         out_specs=(VMEM,) * 3,
-        input_output_aliases={6: 0, 7: 1, 8: 2},
+        input_output_aliases={7: 0, 8: 1, 9: 2},
         compiler_params=limit(16),
         cost_estimate=cost(len(tiles_at(tiles, tile_cols, False))),
         name="outer",
@@ -397,7 +411,7 @@
         return pl.pallas_call(
             functools.partial(finish_kernel, tile_cols=tile_cols, last=last),
             out_shape=(shape(state.shape, f32),) if last else edges,
-            in_specs=[SMEM] * 2 + [VMEM] * 5,
+            in_specs=[SMEM] * 3 + [VMEM] * 5,
             out_specs=(pl.BlockSpec(memory_space=pl.ANY),) if last else (VMEM,) * 5,
             scratch_shapes=[
                 pltpu.VMEM(state.shape, f32),
@@ -412,33 +426,33 @@
         value = lax.all_to_all(value, GROUP, split_axis=0, concat_axis=0, tiled=True)
         return value.reshape((slots,) + block)
 
-    up = [(i, i + 1) for i in range(nr - 1)]
-    down = [(b, a) for a, b in up]
-    rightward = [(i, i + 1) for i in range(nc - 1)]
-    leftward = [(b, a) for a, b in rightward]
+    def swaps(value_a, value_b, axis):
+        count = lax.axis_size(axis)
+        even = [(i, i ^ 1) for i in range(count)]
+        uneven = [(i, ((i + 1) ^ 1) - 1) for i in range(1, count - 1)]
+        return lax.ppermute(value_a, axis, even), lax.ppermute(value_b, axis, uneven)
 
     def apart(value):
         return pltpu.with_memory_space_constraint(value, pltpu.HBM)
 
-    def forward(early, scaled, top, bottom, left, right):
-        above = lax.ppermute(bottom, "row", up)
-        below = lax.ppermute(top, "row", down)
-        first, last = sides(above, below, left, right)
+    def forward(early, scaled, row_a, row_b, col_a, col_b):
+        above = swaps(row_a, row_b, "row")
+        side_a, side_b = sides(odd, *above, col_a, col_b)
+        other_weight = None
         if early:
-            last, weight = lax.optimization_barrier((last, ray_weight))
-        lefts = lax.ppermute(last, COL, rightward)
-        rights = lax.ppermute(first, COL, leftward)
-        other_weight = exchange(weight) if early else None
+            side_b, weight = lax.optimization_barrier((side_b, ray_weight))
+            other_weight = exchange(weight)
+        beside = swaps(side_a, side_b, COL)
         *parts, taps = inner(early)(
-            mat_idx, send_slot, scaled, above, below, kernel, apart(rays) if early else rays
+            odd, mat_idx, send_slot, scaled, *above, kernel, apart(rays) if early else rays
         )[: 4 + early]
         near = rays
         if early:
             near, taps = taps, parts.pop()
-        pulled, outgoing, _ = outer(mat_idx, send_slot, lefts, rights, taps, near, *parts)
+        pulled, outgoing, _ = outer(odd, mat_idx, send_slot, *beside, taps, near, *parts)
         return pulled, outgoing, other_weight
 
-    scaled, *rim = start(apart(state), apart(grad))
+    scaled, *rim = start(odd, apart(state), apart(grad))
     for turn in range(ITERS):
         pulled, outgoing, swapped = forward(turn == 0, scaled, *rim)
         if not turn:
@@ -450,7 +464,7 @@
         replies = reply(table, used, total, exchange(mine), ray_weight, other_weight)
         last = turn == ITERS - 1
         scaled, *rim = finish(last)(
-            mat_idx, send_slot, across(replies), pulled, grad, state, rays
+            odd, mat_idx, send_slot, across(replies), pulled, grad, state, rays
         )
     return scaled
 

time: 182 us -> 179 us (0.984)
  starting transfers between devices: 22.5 us -> 17.2 us
  waiting for transfers between devices: 23.3 us -> 26.1 us
  blocking collectives: 108 us -> 106 us
    ppermute x11, starting transfers between devices: 22.5 us -> 17.2 us  [the longest x3 8 us: exchange(): return lax.ppermute(value, 'zh', [(0, 1), (1, 0)])]
    ppermute x11, waiting for transfers between devices: 23.3 us -> 26.1 us  [the longest x3 25.8 us: exchange(): return lax.ppermute(value, 'zh', [(0, 1), (1, 0)])]
    all_to_all x4, blocking collectives: 108 us -> 106 us  [across(): lax.all_to_all(value, GROUP, split_axis=0, concat_axis=0, tiled=True)]
  transfers between devices with their start and end apart: 11 -> 11, of which waited for: 5 -> 3; matrix products, arithmetic and copies ran while one was open for 1% -> 1% of each run, Pallas kernels for 6% -> 6%
where the time goes in v8:
time: 179 us; the launch traced here: 178 us
  blocking collectives  106 us (59%)
  Pallas kernels  26.7 us (15%)
  waiting for transfers between devices  26.1 us (15%)
  starting transfers between devices  17.2 us (10%)
    all_to_all x4, blocking collectives, across(): lax.all_to_all(value, GROUP, split_axis=0, concat_axis=0, tiled=True)  106 us
    ppermute x3, waiting for transfers between devices, exchange(): return lax.ppermute(value, 'zh', [(0, 1), (1, 0)])  25.8 us
    ppermute x3, starting transfers between devices, exchange(): return lax.ppermute(value, 'zh', [(0, 1), (1, 0)])  8 us
    pallas_call x2, Pallas kernels, forward(): inner(early)  7.52 us
    pallas_call x2, Pallas kernels, forward(): outer(odd, mat_idx, send_slot, *beside, taps, near, *parts)  7.44 us
    ppermute x4, starting transfers between devices, swaps(): lax.ppermute(value_a, axis, even)  6.63 us
    pallas_call x2, Pallas kernels, on_device(): finish(last)  4.46 us
  transfers between devices with their start and end apart: 11, of which 3 were waited for; matrix products, arithmetic and copies ran while one was open for 1% of the time, Pallas kernels for 6%

profile of v8, /device:TPU:0, one launch (start us, length us, event | category | flops | bytes accessed | tf_op | source)
XLA Modules:
  0.0 178.4 jit_solution(13111468418571850230)
XLA Ops:
  0.1 2.2 %start.1 = (bf16[32,96,128]{2,1,0:T(8,128)(2,1)S(1)}, bf16[96,128]{1,0:T(8,128)(2,1)S(1)}, bf16[96,128]{1,0:T(8,128)(2,1)S(1)}, f32[32,128]{1,0:T(8,128)S(1)}, f32[32,128]{1,0:T(8,128)S(1)}) custom-call(s32[2]{0:T(128)S(1)} %pad_add_fusion.odd, bf16[32,96,128]{2,1,0:T(8,128)(2,1)} %state.5, bf16[32,96,128]{2,1,0:T(8,128)(2,1)} %grad.5), custom_call_target="tpu_custom_call" | custom-call | tf_op jit(solution)/shard_map/start/pallas_call | solution.py:455
  2.4 0.6 collective-permute-start
  2.9 0.7 collective-permute-start.1
  3.8 0.5 select_reduce_fusion
  4.5 0.5 convert_reduce_fusion
  5.8 0.6 sides.2
  6.4 3.7 %collective-permute-start.4 = (f32[8,64,128]{2,1,0:T(8,128)S(1)}, f32[8,64,128]{2,1,0:T(8,128)S(1)}, u32[]{:S(2)}, u32[]{:S(2)}) collective-permute-start(f32[8,64,128]{2,1,0:T(8,128)S(1)} %copy-done.4), channel_id=1, source_target_pairs={{0,4},{4,0},{1,5},{5,1},{2,6},{6,2},{3,7},{7,3},{8,12},{12,8},{9,1... | collective-permute-start | bytes 786440 | tf_op jit(solution)/shard_map/ppermute | solution.py:279
  10.1 0.7 collective-permute-start.3
  10.8 4.3 %collective-permute-start.2 = (f32[48,128]{1,0:T(8,128)S(1)}, f32[48,128]{1,0:T(8,128)S(1)}, u32[]{:S(2)}, u32[]{:S(2)}) collective-permute-start(f32[48,128]{1,0:T(8,128)S(1)} %get-tuple-element.46), channel_id=1, source_target_pairs={{0,1},{1,0},{2,3},{3,2},{4,5},{5,4},{6,7},{7,6},{8,9},{9,8},{10,11... | collective-permute-start | bytes 73736 | tf_op jit(solution)/shard_map/ppermute | solution.py:433
  15.1 4.5 %inner.2 = (f32[3,16,2,32,128]{4,3,2,1,0:T(8,128)S(1)}, bf16[96,64,128]{2,1,0:T(8,128)(2,1)S(1)}, bf16[17,2,96,384]{3,2,1,0:T(8,128)(2,1)S(1)}, bf16[1536,256]{1,0:T(8,128)(2,1)S(1)}, bf16[32,64,1024]{2,1,0:T(8,128)(2,1)S(1)}) custom-call(s32[2]{0:T(128)S(1)} %pad_add_fusion.odd, s32[48]{0:T(128)S(1)} %multiply_add_fusion.mat_idx, s32[48]{0:T(128)S(1)} %fusion.28.send_slot, ...), custom_call_target="tpu_custom_call" | custom-call | flops 570425344 | bytes 4194304 | tf_op jit(solution)/shard_map/inner/pallas_call | solution.py:446
  19.7 3.7 %outer.2 = (f32[3,16,2,32,128]{4,3,2,1,0:T(8,128)S(1)}, bf16[96,64,128]{2,1,0:T(8,128)(2,1)S(1)}, bf16[17,2,96,384]{3,2,1,0:T(8,128)(2,1)S(1)}) custom-call(s32[2]{0:T(128)S(1)} %pad_add_fusion.odd, s32[48]{0:T(128)S(1)} %multiply_add_fusion.mat_idx, s32[48]{0:T(128)S(1)} %fusion.28.send_slot, ...), custom_call_target="tpu_custom_call", output_to_operand_aliasing={{0}: (7, {}), {1}: (8, {}), {2}: (9, {})} | custom-call | flops 1140850688 | bytes 4194304 | tf_op jit(solution)/shard_map/outer/pallas_call | solution.py:452
  23.4 27.9 %all_to_all.20 = bf16[16,6,64,128]{3,2,1,0:T(8,128)(2,1)S(1)} all-to-all(bf16[16,6,64,128]{3,2,1,0:T(8,128)(2,1)S(1)} %bitcast.29), channel_id=1, replica_groups=mesh['row'=4,'zh'=2,'zl'=2,'x'=2] {'row','zl','x'}, dimensions={0} | all-to-all | bytes 3145728 | tf_op jit(solution)/shard_map/all_to_all | solution.py:426
  51.3 1.2 combine.2
  52.5 2.8 %collective-permute-start.5 = (bf16[16,64,128]{2,1,0:T(8,128)(2,1)S(1)}, bf16[16,64,128]{2,1,0:T(8,128)(2,1)S(1)}, u32[]{:S(2)}, u32[]{:S(2)}) collective-permute-start(bf16[16,64,128]{2,1,0:T(8,128)(2,1)S(1)} %get-tuple-element.61), channel_id=1, source_target_pairs={{0,4},{4,0},{1,5},{5,1},{2,6},{6,2},{3,7},{7,3},{8,12},{12,8},{9,1... | collective-permute-start | bytes 786440 | tf_op jit(solution)/shard_map/ppermute | solution.py:279
  55.3 12.3 %collective-permute-done.5.other = bf16[16,64,128]{2,1,0:T(8,128)(2,1)S(1)} collective-permute-done((bf16[16,64,128]{2,1,0:T(8,128)(2,1)S(1)}, bf16[16,64,128]{2,1,0:T(8,128)(2,1)S(1)}, u32[]{:S(2)}, u32[]{:S(2)}) %collective-permute-start.5) | collective-permute-done | bytes 262176 | tf_op jit(solution)/shard_map/ppermute | solution.py:279
  67.6 0.8 reply.2
  68.4 23.4 %all_to_all.21 = bf16[16,6,64,128]{3,2,1,0:T(8,128)(2,1)S(1)} all-to-all(bf16[16,6,64,128]{3,2,1,0:T(8,128)(2,1)S(1)} %bitcast.28), channel_id=1, replica_groups=mesh['row'=4,'zh'=2,'zl'=2,'x'=2] {'row','zl','x'}, dimensions={0} | all-to-all | bytes 3145728 | tf_op jit(solution)/shard_map/all_to_all | solution.py:426
  91.9 1.9 %finish.2 = (bf16[32,96,128]{2,1,0:T(8,128)(2,1)S(1)}, bf16[96,128]{1,0:T(8,128)(2,1)S(1)}, bf16[96,128]{1,0:T(8,128)(2,1)S(1)}, f32[32,128]{1,0:T(8,128)S(1)}, f32[32,128]{1,0:T(8,128)S(1)}) custom-call(s32[2]{0:T(128)S(1)} %pad_add_fusion.odd, s32[48]{0:T(128)S(1)} %multiply_add_fusion.mat_idx, s32[48]{0:T(128)S(1)} %fusion.28.send_slot, ...), custom_call_target="tpu_custom_call" | custom-call | tf_op jit(solution)/shard_map/finish/pallas_call | solution.py:466
  93.8 0.3 collective-permute-start.6
  94.1 0.7 collective-permute-start.7
  95.0 0.6 sides.3
  95.6 1.4 collective-permute-start.8
  97.0 0.7 collective-permute-start.9
  97.6 3.0 %inner.3 = (f32[3,16,2,32,128]{4,3,2,1,0:T(8,128)S(1)}, bf16[96,64,128]{2,1,0:T(8,128)(2,1)S(1)}, bf16[17,2,96,384]{3,2,1,0:T(8,128)(2,1)S(1)}, bf16[1536,256]{1,0:T(8,128)(2,1)S(1)}) custom-call(s32[2]{0:T(128)S(1)} %pad_add_fusion.odd, s32[48]{0:T(128)S(1)} %multiply_add_fusion.mat_idx, s32[48]{0:T(128)S(1)} %fusion.28.send_slot, ...), custom_call_target="tpu_custom_call" | custom-call | flops 570425344 | bytes 4194304 | tf_op jit(solution)/shard_map/inner/pallas_call | solution.py:446
  100.7 3.7 %outer.3 = (f32[3,16,2,32,128]{4,3,2,1,0:T(8,128)S(1)}, bf16[96,64,128]{2,1,0:T(8,128)(2,1)S(1)}, bf16[17,2,96,384]{3,2,1,0:T(8,128)(2,1)S(1)}) custom-call(s32[2]{0:T(128)S(1)} %pad_add_fusion.odd, s32[48]{0:T(128)S(1)} %multiply_add_fusion.mat_idx, s32[48]{0:T(128)S(1)} %fusion.28.send_slot, ...), custom_call_target="tpu_custom_call", output_to_operand_aliasing={{0}: (7, {}), {1}: (8, {}), {2}: (9, {})} | custom-call | flops 1140850688 | bytes 4194304 | tf_op jit(solution)/shard_map/outer/pallas_call | solution.py:452
  104.4 31.3 %all_to_all.22 = bf16[16,6,64,128]{3,2,1,0:T(8,128)(2,1)S(1)} all-to-all(bf16[16,6,64,128]{3,2,1,0:T(8,128)(2,1)S(1)} %bitcast.30), channel_id=1, replica_groups=mesh['row'=4,'zh'=2,'zl'=2,'x'=2] {'row','zl','x'}, dimensions={0} | all-to-all | bytes 3145728 | tf_op jit(solution)/shard_map/all_to_all | solution.py:426
  135.7 1.2 combine.3
  136.9 1.5 collective-permute-start.10
  138.4 13.4 %collective-permute-done.10.other = bf16[16,64,128]{2,1,0:T(8,128)(2,1)S(1)} collective-permute-done((bf16[16,64,128]{2,1,0:T(8,128)(2,1)S(1)}, bf16[16,64,128]{2,1,0:T(8,128)(2,1)S(1)}, u32[]{:S(2)}, u32[]{:S(2)}) %collective-permute-start.10) | collective-permute-done | bytes 262176 | tf_op jit(solution)/shard_map/ppermute | solution.py:279
  151.9 0.8 reply.3
  152.7 23.2 %all_to_all.23 = bf16[16,6,64,128]{3,2,1,0:T(8,128)(2,1)S(1)} all-to-all(bf16[16,6,64,128]{3,2,1,0:T(8,128)(2,1)S(1)} %bitcast.27), channel_id=1, replica_groups=mesh['row'=4,'zh'=2,'zl'=2,'x'=2] {'row','zl','x'}, dimensions={0} | all-to-all | bytes 3145728 | tf_op jit(solution)/shard_map/all_to_all | solution.py:426
  175.8 2.6 %finish.3 = f32[32,96,128]{2,1,0:T(8,128)} custom-call(s32[2]{0:T(128)S(1)} %pad_add_fusion.odd, s32[48]{0:T(128)S(1)} %multiply_add_fusion.mat_idx, s32[48]{0:T(128)S(1)} %fusion.28.send_slot, bf16[96,64,128]{2,1,0:T(8,128)(2,1)S(1)} %bitcast.31, f32[3,16,2,32,128]{4,3,2,1,0:T(8,128)S(1)} %get-tuple-element.78.pulled, bf16[32,96,128]{2,1,0:T(8,128)(2,1)S(1)} %copy-done.2, ...), custom_call_target="tpu_custom_call" | custom-call | tf_op jit(solution)/shard_map/finish/pallas_call | solution.py:466
  (49 shorter events, 1.6 us)
Async XLA Ops:
  0.0 3.6 %copy-start.5 = (s32[4,24,16]{1,2,0:T(8,128)S(1)}, s32[4,24,16]{1,2,0:T(8,128)}, u32[]{:S(2)}) copy-start(s32[4,24,16]{1,2,0:T(8,128)} %param.14) | copy-start | bytes 18436
  0.0 3.8 %copy-start.6 = (s32[256]{0:T(256)S(1)}, s32[256]{0:T(256)}, u32[]{:S(2)}) copy-start(s32[256]{0:T(256)} %param.16) | copy-start | bytes 3076
  0.0 4.4 %copy-start.7 = (s32[1,3,16]{2,0,1:T(1,128)S(1)}, s32[1,3,16]{2,0,1:T(1,128)}, u32[]{:S(2)}) copy-start(s32[1,3,16]{2,0,1:T(1,128)} %param.15) | copy-start | bytes 580
  0.0 5.2 %copy-start.8 = (s32[8]{0:T(128)S(1)}, s32[8]{0:T(128)}, u32[]{:S(2)}) copy-start(s32[8]{0:T(128)} %param.17) | copy-start | bytes 100
  0.0 6.4 %copy-start.4 = (f32[8,64,128]{2,1,0:T(8,128)S(1)}, f32[8,64,128]{2,1,0:T(8,128)}, u32[]{:S(2)}) copy-start(f32[8,64,128]{2,1,0:T(8,128)} %own_weight.3) | copy-start | bytes 786436
  0.0 15.1 %copy-start.3 = (bf16[3,3,128,128]{3,2,1,0:T(8,128)(2,1)S(1)}, bf16[3,3,128,128]{3,2,1,0:T(8,128)(2,1)}, u32[]{:S(2)}) copy-start(bf16[3,3,128,128]{3,2,1,0:T(8,128)(2,1)} %kernel.3) | copy-start | bytes 884740
  2.4 3.4 %collective-permute-start = (bf16[96,128]{1,0:T(8,128)(2,1)S(1)}, bf16[96,128]{1,0:T(8,128)(2,1)S(1)}, u32[]{:S(2)}, u32[]{:S(2)}) collective-permute-start(bf16[96,128]{1,0:T(8,128)(2,1)S(1)} %get-tuple-element.42), channel_id=1, source_target_pairs={{0,8},{8,0},{16,24},{24,16},{1,9},{9,1},{17,25},{25,17},{2,10},{10... | collective-permute-start | bytes 73736 | tf_op jit(solution)/shard_map/ppermute | solution.py:433
  2.9 2.9 %collective-permute-start.1 = (bf16[96,128]{1,0:T(8,128)(2,1)S(1)}, bf16[96,128]{1,0:T(8,128)(2,1)S(1)}, u32[]{:S(2)}, u32[]{:S(2)}) collective-permute-start(bf16[96,128]{1,0:T(8,128)(2,1)S(1)} %get-tuple-element.43), channel_id=1, source_target_pairs={{8,16},{16,8},{9,17},{17,9},{10,18},{18,10},{11,19},{19,11},{12,20... | collective-permute-start | bytes 73736 | tf_op jit(solution)/shard_map/ppermute | solution.py:433
  6.4 17.0 %collective-permute-start.4 = (f32[8,64,128]{2,1,0:T(8,128)S(1)}, f32[8,64,128]{2,1,0:T(8,128)S(1)}, u32[]{:S(2)}, u32[]{:S(2)}) collective-permute-start(f32[8,64,128]{2,1,0:T(8,128)S(1)} %copy-done.4), channel_id=1, source_target_pairs={{0,4},{4,0},{1,5},{5,1},{2,6},{6,2},{3,7},{7,3},{8,12},{12,8},{9,1... | collective-permute-start | bytes 786440 | tf_op jit(solution)/shard_map/ppermute | solution.py:279
  10.1 9.5 %collective-permute-start.3 = (f32[48,128]{1,0:T(8,128)S(1)}, f32[48,128]{1,0:T(8,128)S(1)}, u32[]{:S(2)}, u32[]{:S(2)}) collective-permute-start(f32[48,128]{1,0:T(8,128)S(1)} %get-tuple-element.48), channel_id=1, source_target_pairs={{1,2},{2,1},{3,4},{4,3},{5,6},{6,5},{9,10},{10,9},{11,12},{12,11},... | collective-permute-start | bytes 73736 | tf_op jit(solution)/shard_map/ppermute | solution.py:433
  10.8 8.9 %collective-permute-start.2 = (f32[48,128]{1,0:T(8,128)S(1)}, f32[48,128]{1,0:T(8,128)S(1)}, u32[]{:S(2)}, u32[]{:S(2)}) collective-permute-start(f32[48,128]{1,0:T(8,128)S(1)} %get-tuple-element.46), channel_id=1, source_target_pairs={{0,1},{1,0},{2,3},{3,2},{4,5},{5,4},{6,7},{7,6},{8,9},{9,8},{10,11... | collective-permute-start | bytes 73736 | tf_op jit(solution)/shard_map/ppermute | solution.py:433
  52.5 15.1 %collective-permute-start.5 = (bf16[16,64,128]{2,1,0:T(8,128)(2,1)S(1)}, bf16[16,64,128]{2,1,0:T(8,128)(2,1)S(1)}, u32[]{:S(2)}, u32[]{:S(2)}) collective-permute-start(bf16[16,64,128]{2,1,0:T(8,128)(2,1)S(1)} %get-tuple-element.61), channel_id=1, source_target_pairs={{0,4},{4,0},{1,5},{5,1},{2,6},{6,2},{3,7},{7,3},{8,12},{12,8},{9,1... | collective-permute-start | bytes 786440 | tf_op jit(solution)/shard_map/ppermute | solution.py:279
  67.6 24.3 %copy-start = (bf16[8,4,64,1024]{3,2,1,0:T(8,128)(2,1)S(1)}, bf16[8,4,64,1024]{3,2,1,0:T(8,128)(2,1)}, u32[]{:S(2)}) copy-start(bf16[8,4,64,1024]{3,2,1,0:T(8,128)(2,1)} %param.12) | copy-start | bytes 12582916
  68.4 23.5 %copy-start.1 = (bf16[32,96,128]{2,1,0:T(8,128)(2,1)S(1)}, bf16[32,96,128]{2,1,0:T(8,128)(2,1)}, u32[]{:S(2)}) copy-start(bf16[32,96,128]{2,1,0:T(8,128)(2,1)} %state.5) | copy-start | bytes 2359300
  68.4 23.5 %copy-start.2 = (bf16[32,96,128]{2,1,0:T(8,128)(2,1)S(1)}, bf16[32,96,128]{2,1,0:T(8,128)(2,1)}, u32[]{:S(2)}) copy-start(bf16[32,96,128]{2,1,0:T(8,128)(2,1)} %grad.5) | copy-start | bytes 2359300
  93.8 1.3 collective-permute-start.6
  94.1 0.9 collective-permute-start.7
  95.6 5.1 %collective-permute-start.8 = (f32[48,128]{1,0:T(8,128)S(1)}, f32[48,128]{1,0:T(8,128)S(1)}, u32[]{:S(2)}, u32[]{:S(2)}) collective-permute-start(f32[48,128]{1,0:T(8,128)S(1)} %get-tuple-element.68), channel_id=1, source_target_pairs={{0,1},{1,0},{2,3},{3,2},{4,5},{5,4},{6,7},{7,6},{8,9},{9,8},{10,11... | collective-permute-start | bytes 73736 | tf_op jit(solution)/shard_map/ppermute | solution.py:433
  97.0 3.7 %collective-permute-start.9 = (f32[48,128]{1,0:T(8,128)S(1)}, f32[48,128]{1,0:T(8,128)S(1)}, u32[]{:S(2)}, u32[]{:S(2)}) collective-permute-start(f32[48,128]{1,0:T(8,128)S(1)} %get-tuple-element.69), channel_id=1, source_target_pairs={{1,2},{2,1},{3,4},{4,3},{5,6},{6,5},{9,10},{10,9},{11,12},{12,11},... | collective-permute-start | bytes 73736 | tf_op jit(solution)/shard_map/ppermute | solution.py:433
  136.9 15.0 %collective-permute-start.10 = (bf16[16,64,128]{2,1,0:T(8,128)(2,1)S(1)}, bf16[16,64,128]{2,1,0:T(8,128)(2,1)S(1)}, u32[]{:S(2)}, u32[]{:S(2)}) collective-permute-start(bf16[16,64,128]{2,1,0:T(8,128)(2,1)S(1)} %get-tuple-element.77), channel_id=1, source_target_pairs={{0,4},{4,0},{1,5},{5,1},{2,6},{6,2},{3,7},{7,3},{8,12},{12,8},{9,1... | collective-permute-start | bytes 786440 | tf_op jit(solution)/shard_map/ppermute | solution.py:279

commit v9 on v8

--- a/solution.py
+++ b/solution.py
@@ -181,16 +181,20 @@
         forward_tile(mat_idx, send_slot, taps, rays, pulled, out, cols3, t, tile_cols)
 
 
-def combine_kernel(table, recv, total, low, acc):
-    acc[...] = jnp.zeros_like(acc)
+def combine_kernel(table, recv, total, low, acc_a, acc_b):
+    acc_a[...] = jnp.zeros_like(acc_a)
+    acc_b[...] = jnp.zeros_like(acc_b)
 
     def body(j, carry):
-        acc[table[j]] += recv[j].astype(jnp.float32)
+        acc_a[table[2 * j]] += recv[2 * j].astype(jnp.float32)
+        acc_b[table[2 * j + 1]] += recv[2 * j + 1].astype(jnp.float32)
         return carry
 
-    lax.fori_loop(0, recv.shape[0], body, 0, unroll=8)
-    total[...] = acc[: total.shape[0]]
-    low[...] = acc[: total.shape[0]].astype(jnp.bfloat16)
+    lax.fori_loop(0, recv.shape[0] // 2, body, 0, unroll=4)
+    n = total.shape[0]
+    value = acc_a[:n] + acc_b[:n]
+    total[...] = value
+    low[...] = value.astype(jnp.bfloat16)
 
 
 def reply_kernel(table, used, total, other, own_weight, other_weight, out, held):
@@ -366,7 +370,7 @@
 
     def inner(early):
         held = (shape(rays.shape, bf16),) if early else ()
-        mark = [pltpu.SemaphoreType.DMA((angles,))] if early else []
+        mark = [pltpu.SemaphoreType.DMA((angles * spots,))] if early else []
         return pl.pallas_call(
             functools.partial(inner_kernel, tile_cols=tile_cols),
             out_shape=(pulled_out, slot_out, cols3_out, taps_out) + held,
@@ -393,7 +397,7 @@
         out_shape=(shape((dense,) + block, f32), shape((dense,) + block, bf16)),
         in_specs=[SMEM, VMEM],
         out_specs=(VMEM, VMEM),
-        scratch_shapes=[pltpu.VMEM((dense + 1,) + block, f32)],
+        scratch_shapes=[pltpu.VMEM((dense + 1,) + block, f32)] * 2,
         compiler_params=limit(8),
         name="combine",
     )
@@ -438,11 +442,12 @@
     def forward(early, scaled, row_a, row_b, col_a, col_b):
         above = swaps(row_a, row_b, "row")
         side_a, side_b = sides(odd, *above, col_a, col_b)
+        beside = swaps(side_a, side_b, COL)
         other_weight = None
         if early:
-            side_b, weight = lax.optimization_barrier((side_b, ray_weight))
+            arrived, weight = lax.optimization_barrier((beside[0], ray_weight))
+            beside = (arrived, beside[1])
             other_weight = exchange(weight)
-        beside = swaps(side_a, side_b, COL)
         *parts, taps = inner(early)(
             odd, mat_idx, send_slot, scaled, *above, kernel, apart(rays) if early else rays
         )[: 4 + early]

time: 179 us -> 182 us (1.017)
  waiting for transfers between devices: 26.1 us -> 29.9 us
    ppermute x3, waiting for transfers between devices: 25.8 us -> 28 us  [exchange(): return lax.ppermute(value, 'zh', [(0, 1), (1, 0)])]
  transfers between devices with their start and end apart: 11 -> 11, of which waited for: 3 -> 5; matrix products, arithmetic and copies ran while one was open for 1% -> 1% of each run, Pallas kernels for 6% -> 6%
where the time goes in v9:
time: 182 us
  blocking collectives  107 us (59%)
  waiting for transfers between devices  29.9 us (16%)
  Pallas kernels  27 us (15%)
  starting transfers between devices  15.5 us (9%)
    all_to_all x4, blocking collectives, across(): lax.all_to_all(value, GROUP, split_axis=0, concat_axis=0, tiled=True)  107 us
    ppermute x3, waiting for transfers between devices, exchange(): return lax.ppermute(value, 'zh', [(0, 1), (1, 0)])  28 us
    pallas_call x2, Pallas kernels, forward(): inner(early)  8.06 us
    ppermute x3, starting transfers between devices, exchange(): return lax.ppermute(value, 'zh', [(0, 1), (1, 0)])  8.05 us
    pallas_call x2, Pallas kernels, forward(): outer(odd, mat_idx, send_slot, *beside, taps, near, *parts)  7.44 us
    ppermute x4, starting transfers between devices, swaps(): lax.ppermute(value_a, axis, even)  4.85 us
    pallas_call x2, Pallas kernels, on_device(): finish(last)  4.46 us
  transfers between devices with their start and end apart: 11, of which 5 were waited for; matrix products, arithmetic and copies ran while one was open for 1% of the time, Pallas kernels for 6%

profile of v9, /device:TPU:0, one launch (start us, length us, event | category | flops | bytes accessed | tf_op | source)
XLA Modules:
  0.0 181.9 jit_solution(12258080188861445932)
XLA Ops:
  0.1 2.2 %start.1 = (bf16[32,96,128]{2,1,0:T(8,128)(2,1)S(1)}, bf16[96,128]{1,0:T(8,128)(2,1)S(1)}, bf16[96,128]{1,0:T(8,128)(2,1)S(1)}, f32[32,128]{1,0:T(8,128)S(1)}, f32[32,128]{1,0:T(8,128)S(1)}) custom-call(s32[2]{0:T(128)S(1)} %pad_add_fusion.odd, bf16[32,96,128]{2,1,0:T(8,128)(2,1)} %state.5, bf16[32,96,128]{2,1,0:T(8,128)(2,1)} %grad.5), custom_call_target="tpu_custom_call" | custom-call | tf_op jit(solution)/shard_map/start/pallas_call | solution.py:460
  2.4 0.6 collective-permute-start
  2.9 0.7 collective-permute-start.1
  3.8 0.5 select_reduce_fusion
  5.6 0.6 sides.2
  6.2 2.6 %collective-permute-start.2 = (f32[48,128]{1,0:T(8,128)S(1)}, f32[48,128]{1,0:T(8,128)S(1)}, u32[]{:S(2)}, u32[]{:S(2)}) collective-permute-start(f32[48,128]{1,0:T(8,128)S(1)} %get-tuple-element.46), channel_id=1, source_target_pairs={{0,1},{1,0},{2,3},{3,2},{4,5},{5,4},{6,7},{7,6},{8,9},{9,8},{10,11... | collective-permute-start | bytes 73736 | tf_op jit(solution)/shard_map/ppermute | solution.py:437
  8.9 1.6 collective-permute-done.2.near_a
  10.6 3.1 %collective-permute-start.4 = (f32[8,64,128]{2,1,0:T(8,128)S(1)}, f32[8,64,128]{2,1,0:T(8,128)S(1)}, u32[]{:S(2)}, u32[]{:S(2)}) collective-permute-start(f32[8,64,128]{2,1,0:T(8,128)S(1)} %copy-done.4), channel_id=1, source_target_pairs={{0,4},{4,0},{1,5},{5,1},{2,6},{6,2},{3,7},{7,3},{8,12},{12,8},{9,1... | collective-permute-start | bytes 786440 | tf_op jit(solution)/shard_map/ppermute | solution.py:283
  13.8 0.7 collective-permute-start.3
  14.4 5.0 %inner.2 = (f32[3,16,2,32,128]{4,3,2,1,0:T(8,128)S(1)}, bf16[96,64,128]{2,1,0:T(8,128)(2,1)S(1)}, bf16[17,2,96,384]{3,2,1,0:T(8,128)(2,1)S(1)}, bf16[1536,256]{1,0:T(8,128)(2,1)S(1)}, bf16[32,64,1024]{2,1,0:T(8,128)(2,1)S(1)}) custom-call(s32[2]{0:T(128)S(1)} %pad_add_fusion.odd, s32[48]{0:T(128)S(1)} %multiply_add_fusion.mat_idx, s32[48]{0:T(128)S(1)} %fusion.28.send_slot, ...), custom_call_target="tpu_custom_call" | custom-call | flops 570425344 | bytes 4194304 | tf_op jit(solution)/shard_map/inner/pallas_call | solution.py:451
  19.5 3.7 %outer.2 = (f32[3,16,2,32,128]{4,3,2,1,0:T(8,128)S(1)}, bf16[96,64,128]{2,1,0:T(8,128)(2,1)S(1)}, bf16[17,2,96,384]{3,2,1,0:T(8,128)(2,1)S(1)}) custom-call(s32[2]{0:T(128)S(1)} %pad_add_fusion.odd, s32[48]{0:T(128)S(1)} %multiply_add_fusion.mat_idx, s32[48]{0:T(128)S(1)} %fusion.28.send_slot, ...), custom_call_target="tpu_custom_call", output_to_operand_aliasing={{0}: (7, {}), {1}: (8, {}), {2}: (9, {})} | custom-call | flops 1140850688 | bytes 4194304 | tf_op jit(solution)/shard_map/outer/pallas_call | solution.py:457
  23.2 2.2 %collective-permute-done.4.other_weight = f32[8,64,128]{2,1,0:T(8,128)S(1)} collective-permute-done((f32[8,64,128]{2,1,0:T(8,128)S(1)}, f32[8,64,128]{2,1,0:T(8,128)S(1)}, u32[]{:S(2)}, u32[]{:S(2)}) %collective-permute-start.4) | collective-permute-done | bytes 262176 | tf_op jit(solution)/shard_map/ppermute | solution.py:283
  25.4 29.0 %all_to_all.20 = bf16[16,6,64,128]{3,2,1,0:T(8,128)(2,1)S(1)} all-to-all(bf16[16,6,64,128]{3,2,1,0:T(8,128)(2,1)S(1)} %bitcast.30), channel_id=1, replica_groups=mesh['row'=4,'zh'=2,'zl'=2,'x'=2] {'row','zl','x'}, dimensions={0} | all-to-all | bytes 3145728 | tf_op jit(solution)/shard_map/all_to_all | solution.py:430
  54.3 1.0 combine.2
  55.4 3.4 %collective-permute-start.5 = (bf16[16,64,128]{2,1,0:T(8,128)(2,1)S(1)}, bf16[16,64,128]{2,1,0:T(8,128)(2,1)S(1)}, u32[]{:S(2)}, u32[]{:S(2)}) collective-permute-start(bf16[16,64,128]{2,1,0:T(8,128)(2,1)S(1)} %get-tuple-element.61), channel_id=1, source_target_pairs={{0,4},{4,0},{1,5},{5,1},{2,6},{6,2},{3,7},{7,3},{8,12},{12,8},{9,1... | collective-permute-start | bytes 786440 | tf_op jit(solution)/shard_map/ppermute | solution.py:283
  58.8 12.4 %collective-permute-done.5.other = bf16[16,64,128]{2,1,0:T(8,128)(2,1)S(1)} collective-permute-done((bf16[16,64,128]{2,1,0:T(8,128)(2,1)S(1)}, bf16[16,64,128]{2,1,0:T(8,128)(2,1)S(1)}, u32[]{:S(2)}, u32[]{:S(2)}) %collective-permute-start.5) | collective-permute-done | bytes 262176 | tf_op jit(solution)/shard_map/ppermute | solution.py:283
  71.1 0.8 reply.2
  71.9 23.4 %all_to_all.21 = bf16[16,6,64,128]{3,2,1,0:T(8,128)(2,1)S(1)} all-to-all(bf16[16,6,64,128]{3,2,1,0:T(8,128)(2,1)S(1)} %bitcast.28), channel_id=1, replica_groups=mesh['row'=4,'zh'=2,'zl'=2,'x'=2] {'row','zl','x'}, dimensions={0} | all-to-all | bytes 3145728 | tf_op jit(solution)/shard_map/all_to_all | solution.py:430
  95.4 1.9 %finish.2 = (bf16[32,96,128]{2,1,0:T(8,128)(2,1)S(1)}, bf16[96,128]{1,0:T(8,128)(2,1)S(1)}, bf16[96,128]{1,0:T(8,128)(2,1)S(1)}, f32[32,128]{1,0:T(8,128)S(1)}, f32[32,128]{1,0:T(8,128)S(1)}) custom-call(s32[2]{0:T(128)S(1)} %pad_add_fusion.odd, s32[48]{0:T(128)S(1)} %multiply_add_fusion.mat_idx, s32[48]{0:T(128)S(1)} %fusion.28.send_slot, ...), custom_call_target="tpu_custom_call" | custom-call | tf_op jit(solution)/shard_map/finish/pallas_call | solution.py:471
  97.6 0.7 collective-permute-start.7
  98.5 0.6 sides.3
  99.1 1.4 collective-permute-start.8
  100.5 0.7 collective-permute-start.9
  101.1 3.0 %inner.3 = (f32[3,16,2,32,128]{4,3,2,1,0:T(8,128)S(1)}, bf16[96,64,128]{2,1,0:T(8,128)(2,1)S(1)}, bf16[17,2,96,384]{3,2,1,0:T(8,128)(2,1)S(1)}, bf16[1536,256]{1,0:T(8,128)(2,1)S(1)}) custom-call(s32[2]{0:T(128)S(1)} %pad_add_fusion.odd, s32[48]{0:T(128)S(1)} %multiply_add_fusion.mat_idx, s32[48]{0:T(128)S(1)} %fusion.28.send_slot, ...), custom_call_target="tpu_custom_call" | custom-call | flops 570425344 | bytes 4194304 | tf_op jit(solution)/shard_map/inner/pallas_call | solution.py:451
  104.2 3.7 %outer.3 = (f32[3,16,2,32,128]{4,3,2,1,0:T(8,128)S(1)}, bf16[96,64,128]{2,1,0:T(8,128)(2,1)S(1)}, bf16[17,2,96,384]{3,2,1,0:T(8,128)(2,1)S(1)}) custom-call(s32[2]{0:T(128)S(1)} %pad_add_fusion.odd, s32[48]{0:T(128)S(1)} %multiply_add_fusion.mat_idx, s32[48]{0:T(128)S(1)} %fusion.28.send_slot, ...), custom_call_target="tpu_custom_call", output_to_operand_aliasing={{0}: (7, {}), {1}: (8, {}), {2}: (9, {})} | custom-call | flops 1140850688 | bytes 4194304 | tf_op jit(solution)/shard_map/outer/pallas_call | solution.py:457
  107.9 31.3 %all_to_all.22 = bf16[16,6,64,128]{3,2,1,0:T(8,128)(2,1)S(1)} all-to-all(bf16[16,6,64,128]{3,2,1,0:T(8,128)(2,1)S(1)} %bitcast.29), channel_id=1, replica_groups=mesh['row'=4,'zh'=2,'zl'=2,'x'=2] {'row','zl','x'}, dimensions={0} | all-to-all | bytes 3145728 | tf_op jit(solution)/shard_map/all_to_all | solution.py:430
  139.2 1.0 combine.3
  140.3 1.5 collective-permute-start.10
  141.8 13.5 %collective-permute-done.10.other = bf16[16,64,128]{2,1,0:T(8,128)(2,1)S(1)} collective-permute-done((bf16[16,64,128]{2,1,0:T(8,128)(2,1)S(1)}, bf16[16,64,128]{2,1,0:T(8,128)(2,1)S(1)}, u32[]{:S(2)}, u32[]{:S(2)}) %collective-permute-start.10) | collective-permute-done | bytes 262176 | tf_op jit(solution)/shard_map/ppermute | solution.py:283
  155.3 0.8 reply.3
  156.1 23.2 %all_to_all.23 = bf16[16,6,64,128]{3,2,1,0:T(8,128)(2,1)S(1)} all-to-all(bf16[16,6,64,128]{3,2,1,0:T(8,128)(2,1)S(1)} %bitcast.27), channel_id=1, replica_groups=mesh['row'=4,'zh'=2,'zl'=2,'x'=2] {'row','zl','x'}, dimensions={0} | all-to-all | bytes 3145728 | tf_op jit(solution)/shard_map/all_to_all | solution.py:430
  179.3 2.6 %finish.3 = f32[32,96,128]{2,1,0:T(8,128)} custom-call(s32[2]{0:T(128)S(1)} %pad_add_fusion.odd, s32[48]{0:T(128)S(1)} %multiply_add_fusion.mat_idx, s32[48]{0:T(128)S(1)} %fusion.28.send_slot, bf16[96,64,128]{2,1,0:T(8,128)(2,1)S(1)} %bitcast.31, f32[3,16,2,32,128]{4,3,2,1,0:T(8,128)S(1)} %get-tuple-element.78.pulled, bf16[32,96,128]{2,1,0:T(8,128)(2,1)S(1)} %copy-done.2, ...), custom_call_target="tpu_custom_call" | custom-call | tf_op jit(solution)/shard_map/finish/pallas_call | solution.py:471
  (49 shorter events, 2.4 us)
Async XLA Ops:
  0.0 3.6 %copy-start.5 = (s32[4,24,16]{1,2,0:T(8,128)S(1)}, s32[4,24,16]{1,2,0:T(8,128)}, u32[]{:S(2)}) copy-start(s32[4,24,16]{1,2,0:T(8,128)} %param.14) | copy-start | bytes 18436
  0.0 3.8 %copy-start.6 = (s32[256]{0:T(256)S(1)}, s32[256]{0:T(256)}, u32[]{:S(2)}) copy-start(s32[256]{0:T(256)} %param.16) | copy-start | bytes 3076
  0.0 4.4 %copy-start.7 = (s32[1,3,16]{2,0,1:T(1,128)S(1)}, s32[1,3,16]{2,0,1:T(1,128)}, u32[]{:S(2)}) copy-start(s32[1,3,16]{2,0,1:T(1,128)} %param.15) | copy-start | bytes 580
  0.0 5.2 %copy-start.8 = (s32[8]{0:T(128)S(1)}, s32[8]{0:T(128)}, u32[]{:S(2)}) copy-start(s32[8]{0:T(128)} %param.17) | copy-start | bytes 100
  0.0 10.5 %copy-start.4 = (f32[8,64,128]{2,1,0:T(8,128)S(1)}, f32[8,64,128]{2,1,0:T(8,128)}, u32[]{:S(2)}) copy-start(f32[8,64,128]{2,1,0:T(8,128)} %own_weight.3) | copy-start | bytes 786436
  0.0 14.4 %copy-start.3 = (bf16[3,3,128,128]{3,2,1,0:T(8,128)(2,1)S(1)}, bf16[3,3,128,128]{3,2,1,0:T(8,128)(2,1)}, u32[]{:S(2)}) copy-start(bf16[3,3,128,128]{3,2,1,0:T(8,128)(2,1)} %kernel.3) | copy-start | bytes 884740
  2.4 3.2 %collective-permute-start = (bf16[96,128]{1,0:T(8,128)(2,1)S(1)}, bf16[96,128]{1,0:T(8,128)(2,1)S(1)}, u32[]{:S(2)}, u32[]{:S(2)}) collective-permute-start(bf16[96,128]{1,0:T(8,128)(2,1)S(1)} %get-tuple-element.42), channel_id=1, source_target_pairs={{0,8},{8,0},{16,24},{24,16},{1,9},{9,1},{17,25},{25,17},{2,10},{10... | collective-permute-start | bytes 73736 | tf_op jit(solution)/shard_map/ppermute | solution.py:437
  2.9 2.7 %collective-permute-start.1 = (bf16[96,128]{1,0:T(8,128)(2,1)S(1)}, bf16[96,128]{1,0:T(8,128)(2,1)S(1)}, u32[]{:S(2)}, u32[]{:S(2)}) collective-permute-start(bf16[96,128]{1,0:T(8,128)(2,1)S(1)} %get-tuple-element.43), channel_id=1, source_target_pairs={{8,16},{16,8},{9,17},{17,9},{10,18},{18,10},{11,19},{19,11},{12,20... | collective-permute-start | bytes 73736 | tf_op jit(solution)/shard_map/ppermute | solution.py:437
  6.2 4.4 %collective-permute-start.2 = (f32[48,128]{1,0:T(8,128)S(1)}, f32[48,128]{1,0:T(8,128)S(1)}, u32[]{:S(2)}, u32[]{:S(2)}) collective-permute-start(f32[48,128]{1,0:T(8,128)S(1)} %get-tuple-element.46), channel_id=1, source_target_pairs={{0,1},{1,0},{2,3},{3,2},{4,5},{5,4},{6,7},{7,6},{8,9},{9,8},{10,11... | collective-permute-start | bytes 73736 | tf_op jit(solution)/shard_map/ppermute | solution.py:437
  10.6 14.8 %collective-permute-start.4 = (f32[8,64,128]{2,1,0:T(8,128)S(1)}, f32[8,64,128]{2,1,0:T(8,128)S(1)}, u32[]{:S(2)}, u32[]{:S(2)}) collective-permute-start(f32[8,64,128]{2,1,0:T(8,128)S(1)} %copy-done.4), channel_id=1, source_target_pairs={{0,4},{4,0},{1,5},{5,1},{2,6},{6,2},{3,7},{7,3},{8,12},{12,8},{9,1... | collective-permute-start | bytes 786440 | tf_op jit(solution)/shard_map/ppermute | solution.py:283
  13.8 5.7 %collective-permute-start.3 = (f32[48,128]{1,0:T(8,128)S(1)}, f32[48,128]{1,0:T(8,128)S(1)}, u32[]{:S(2)}, u32[]{:S(2)}) collective-permute-start(f32[48,128]{1,0:T(8,128)S(1)} %get-tuple-element.48), channel_id=1, source_target_pairs={{1,2},{2,1},{3,4},{4,3},{5,6},{6,5},{9,10},{10,9},{11,12},{12,11},... | collective-permute-start | bytes 73736 | tf_op jit(solution)/shard_map/ppermute | solution.py:437
  55.4 15.7 %collective-permute-start.5 = (bf16[16,64,128]{2,1,0:T(8,128)(2,1)S(1)}, bf16[16,64,128]{2,1,0:T(8,128)(2,1)S(1)}, u32[]{:S(2)}, u32[]{:S(2)}) collective-permute-start(bf16[16,64,128]{2,1,0:T(8,128)(2,1)S(1)} %get-tuple-element.61), channel_id=1, source_target_pairs={{0,4},{4,0},{1,5},{5,1},{2,6},{6,2},{3,7},{7,3},{8,12},{12,8},{9,1... | collective-permute-start | bytes 786440 | tf_op jit(solution)/shard_map/ppermute | solution.py:283
  71.1 24.3 %copy-start = (bf16[8,4,64,1024]{3,2,1,0:T(8,128)(2,1)S(1)}, bf16[8,4,64,1024]{3,2,1,0:T(8,128)(2,1)}, u32[]{:S(2)}) copy-start(bf16[8,4,64,1024]{3,2,1,0:T(8,128)(2,1)} %param.12) | copy-start | bytes 12582916
  71.9 23.5 %copy-start.1 = (bf16[32,96,128]{2,1,0:T(8,128)(2,1)S(1)}, bf16[32,96,128]{2,1,0:T(8,128)(2,1)}, u32[]{:S(2)}) copy-start(bf16[32,96,128]{2,1,0:T(8,128)(2,1)} %state.5) | copy-start | bytes 2359300
  71.9 23.5 %copy-start.2 = (bf16[32,96,128]{2,1,0:T(8,128)(2,1)S(1)}, bf16[32,96,128]{2,1,0:T(8,128)(2,1)}, u32[]{:S(2)}) copy-start(bf16[32,96,128]{2,1,0:T(8,128)(2,1)} %grad.5) | copy-start | bytes 2359300
  97.3 1.3 collective-permute-start.6
  97.6 0.9 collective-permute-start.7
  99.1 5.1 %collective-permute-start.8 = (f32[48,128]{1,0:T(8,128)S(1)}, f32[48,128]{1,0:T(8,128)S(1)}, u32[]{:S(2)}, u32[]{:S(2)}) collective-permute-start(f32[48,128]{1,0:T(8,128)S(1)} %get-tuple-element.68), channel_id=1, source_target_pairs={{0,1},{1,0},{2,3},{3,2},{4,5},{5,4},{6,7},{7,6},{8,9},{9,8},{10,11... | collective-permute-start | bytes 73736 | tf_op jit(solution)/shard_map/ppermute | solution.py:437
  100.5 3.7 %collective-permute-start.9 = (f32[48,128]{1,0:T(8,128)S(1)}, f32[48,128]{1,0:T(8,128)S(1)}, u32[]{:S(2)}, u32[]{:S(2)}) collective-permute-start(f32[48,128]{1,0:T(8,128)S(1)} %get-tuple-element.69), channel_id=1, source_target_pairs={{1,2},{2,1},{3,4},{4,3},{5,6},{6,5},{9,10},{10,9},{11,12},{12,11},... | collective-permute-start | bytes 73736 | tf_op jit(solution)/shard_map/ppermute | solution.py:437
  140.3 15.0 %collective-permute-start.10 = (bf16[16,64,128]{2,1,0:T(8,128)(2,1)S(1)}, bf16[16,64,128]{2,1,0:T(8,128)(2,1)S(1)}, u32[]{:S(2)}, u32[]{:S(2)}) collective-permute-start(bf16[16,64,128]{2,1,0:T(8,128)(2,1)S(1)} %get-tuple-element.77), channel_id=1, source_target_pairs={{0,4},{4,0},{1,5},{5,1},{2,6},{6,2},{3,7},{7,3},{8,12},{12,8},{9,1... | collective-permute-start | bytes 786440 | tf_op jit(solution)/shard_map/ppermute | solution.py:283

commit v10 on v9

--- a/solution.py
+++ b/solution.py
@@ -82,9 +82,7 @@
     return jnp.concatenate([rays[mat_idx[t * HITS + k]] for k in range(HITS)], axis=0)
 
 
-def forward_tile(
-    mat_idx, send_slot, taps, rays, pulled, out, cols3, t, tile_cols, waiting=()
-):
+def forward_tile(mat_idx, send_slot, taps, rays, pulled, out, cols3, t, tile_cols):
     chans = pulled.shape[-1]
     bins = rays.shape[1]
     half = PIX // 2
@@ -103,8 +101,6 @@
         value = acc[:, odd * chans : (odd + 1) * chans].reshape(half, PIX, chans)
         pulled[t, :, odd] = value
     low = pulled[t].reshape(PIX * PIX, chans).astype(jnp.bfloat16)
-    while waiting:
-        waiting.pop().wait()
     value = jnp.dot(
         matrices_of(mat_idx, rays, t), low, preferred_element_type=jnp.float32
     ).astype(jnp.bfloat16)
@@ -118,20 +114,10 @@
 
 def inner_kernel(
     odd, mat_idx, send_slot, scaled, near_a, near_b, kernel, rays,
-    pulled, out, cols3, taps, *refs, tile_cols,
+    pulled, out, cols3, taps, wide, *, tile_cols,
 ):
-    wide = refs[-1]
     rows, cols, chans = scaled.shape
     f32, bf16 = jnp.float32, jnp.bfloat16
-    waiting = []
-    if len(refs) > 1:
-        held, mark = refs[:2]
-        count = rays.shape[0] // mark.shape[0]
-        for i in range(mark.shape[0]):
-            where = pl.ds(i * count, count)
-            waiting.append(pltpu.make_async_copy(rays.at[where], held.at[where], mark.at[i]))
-            waiting[-1].start()
-        rays = held
     blank = jnp.zeros((3 * chans, chans), bf16)
     for dr in range(4):
         base = dr * 3 * chans
@@ -156,9 +142,7 @@
         )
     out[...] = jnp.zeros_like(out)
     for t in tiles_at(pulled.shape[0], tile_cols, True):
-        forward_tile(mat_idx, send_slot, taps, rays, pulled, out, cols3, t, tile_cols, waiting)
-    while waiting:
-        waiting.pop().wait()
+        forward_tile(mat_idx, send_slot, taps, rays, pulled, out, cols3, t, tile_cols)
 
 
 def outer_kernel(
@@ -205,7 +189,7 @@
         first = jnp.where(half == 0, place, n - own - place)
         for b in range(own):
             d = first + b
-            scale = used[d].astype(jnp.float32) * weight[b]
+            scale = used[d].astype(jnp.float32) * weight[b].astype(jnp.float32)
             value = total[d] + other[d].astype(jnp.float32)
             held[d] = (scale * value).astype(jnp.bfloat16)
     held[n] = jnp.zeros(held.shape[1:], jnp.bfloat16)
@@ -355,6 +339,9 @@
         in_specs=[SMEM] + [VMEM] * 4,
         out_specs=[VMEM] * 2,
         compiler_params=limit(4),
+        cost_estimate=pl.CostEstimate(
+            flops=4 * rays.size * 512, bytes_accessed=rays.size * 2, transcendentals=0
+        ),
         name="sides",
     )
     pulled_out = shape((tiles, PIX // 2, 2, PIX, chans), f32)
@@ -368,20 +355,16 @@
 
     taps_out = shape((4 * 3 * chans, 2 * chans), bf16)
 
-    def inner(early):
-        held = (shape(rays.shape, bf16),) if early else ()
-        mark = [pltpu.SemaphoreType.DMA((angles * spots,))] if early else []
-        return pl.pallas_call(
-            functools.partial(inner_kernel, tile_cols=tile_cols),
-            out_shape=(pulled_out, slot_out, cols3_out, taps_out) + held,
-            in_specs=[SMEM] * 3 + [VMEM] * 4 + [ANY if early else VMEM],
-            out_specs=(VMEM,) * (4 + len(held)),
-            scratch_shapes=mark + [pltpu.VMEM((rows_dev + 2, cols_dev + 16, chans), f32)],
-            compiler_params=limit(16),
-            cost_estimate=cost(len(tiles_at(tiles, tile_cols, True))),
-            name="inner",
-        )
-
+    inner = pl.pallas_call(
+        functools.partial(inner_kernel, tile_cols=tile_cols),
+        out_shape=(pulled_out, slot_out, cols3_out, taps_out),
+        in_specs=[SMEM] * 3 + [VMEM] * 5,
+        out_specs=(VMEM,) * 4,
+        scratch_shapes=[pltpu.VMEM((rows_dev + 2, cols_dev + 16, chans), f32)],
+        compiler_params=limit(16),
+        cost_estimate=cost(len(tiles_at(tiles, tile_cols, True))),
+        name="inner",
+    )
     outer = pl.pallas_call(
         functools.partial(outer_kernel, tile_cols=tile_cols),
         out_shape=(pulled_out, slot_out, cols3_out),
@@ -442,19 +425,13 @@
     def forward(early, scaled, row_a, row_b, col_a, col_b):
         above = swaps(row_a, row_b, "row")
         side_a, side_b = sides(odd, *above, col_a, col_b)
-        beside = swaps(side_a, side_b, COL)
         other_weight = None
         if early:
-            arrived, weight = lax.optimization_barrier((beside[0], ray_weight))
-            beside = (arrived, beside[1])
+            side_b, weight = lax.optimization_barrier((side_b, ray_weight.astype(bf16)))
             other_weight = exchange(weight)
-        *parts, taps = inner(early)(
-            odd, mat_idx, send_slot, scaled, *above, kernel, apart(rays) if early else rays
-        )[: 4 + early]
-        near = rays
-        if early:
-            near, taps = taps, parts.pop()
-        pulled, outgoing, _ = outer(odd, mat_idx, send_slot, *beside, taps, near, *parts)
+        beside = swaps(side_a, side_b, COL)
+        *parts, taps = inner(odd, mat_idx, send_slot, scaled, *above, kernel, rays)
+        pulled, outgoing, _ = outer(odd, mat_idx, send_slot, *beside, taps, rays, *parts)
         return pulled, outgoing, other_weight
 
     scaled, *rim = start(odd, apart(state), apart(grad))

time: 182 us -> 175 us (0.962)
  blocking collectives: 107 us -> 103 us
  Pallas kernels: 27 us -> 25 us
    ppermute x3, starting transfers between devices: 8.05 us -> 3.63 us  [exchange(): return lax.ppermute(value, 'zh', [(0, 1), (1, 0)])]
    all_to_all x4, blocking collectives: 107 us -> 103 us  [across(): lax.all_to_all(value, GROUP, split_axis=0, concat_axis=0, tiled=True)]
    ppermute x4, starting transfers between devices: 4.85 us -> 7.64 us  [swaps(): lax.ppermute(value_a, axis, even)]
    pallas_call x4, Pallas kernels: 15.5 us -> 13.5 us  [the longest x2 7.44 us: forward(): outer(odd, mat_idx, send_slot, *beside, taps, rays, *parts)]
  transfers between devices with their start and end apart: 11 -> 11, of which waited for: 5 -> 3; matrix products, arithmetic and copies ran while one was open for 1% -> 1% of each run, Pallas kernels for 6% -> 6%
where the time goes in v10:
time: 175 us; the launch traced here: 174 us
  blocking collectives  103 us (59%)
  waiting for transfers between devices  29.3 us (17%)
  Pallas kernels  25 us (14%)
  starting transfers between devices  14 us (8%)
    all_to_all x4, blocking collectives, across(): lax.all_to_all(value, GROUP, split_axis=0, concat_axis=0, tiled=True)  103 us
    ppermute x3, waiting for transfers between devices, exchange(): return lax.ppermute(value, 'zh', [(0, 1), (1, 0)])  29 us
    ppermute x4, starting transfers between devices, swaps(): lax.ppermute(value_a, axis, even)  7.64 us
    pallas_call x2, Pallas kernels, forward(): outer(odd, mat_idx, send_slot, *beside, taps, rays, *parts)  7.44 us
    pallas_call x2, Pallas kernels, forward(): *parts, taps = inner(odd, mat_idx, send_slot, scaled, *above, kernel, rays)  6.06 us
    pallas_call x2, Pallas kernels, on_device(): finish(last)  4.46 us
    ppermute x3, starting transfers between devices, exchange(): return lax.ppermute(value, 'zh', [(0, 1), (1, 0)])  3.63 us
  transfers between devices with their start and end apart: 11, of which 3 were waited for; matrix products, arithmetic and copies ran while one was open for 1% of the time, Pallas kernels for 6%

profile of v10, /device:TPU:0, one launch (start us, length us, event | category | flops | bytes accessed | tf_op | source)
XLA Modules:
  0.0 174.3 jit_solution(15889773846132388316)
XLA Ops:
  0.1 2.2 %start.1 = (bf16[32,96,128]{2,1,0:T(8,128)(2,1)S(1)}, bf16[96,128]{1,0:T(8,128)(2,1)S(1)}, bf16[96,128]{1,0:T(8,128)(2,1)S(1)}, f32[32,128]{1,0:T(8,128)S(1)}, f32[32,128]{1,0:T(8,128)S(1)}) custom-call(s32[2]{0:T(128)S(1)} %pad_add_fusion.odd, bf16[32,96,128]{2,1,0:T(8,128)(2,1)} %state.5, bf16[32,96,128]{2,1,0:T(8,128)(2,1)} %grad.5), custom_call_target="tpu_custom_call" | custom-call | tf_op jit(solution)/shard_map/start/pallas_call | solution.py:437
  2.4 0.6 collective-permute-start
  2.9 0.7 collective-permute-start.1
  3.8 0.5 select_reduce_fusion
  4.9 0.5 convert_reduce_fusion
  6.0 0.6 sides.2
  6.5 0.8 collective-permute-start.3
  7.3 5.4 %collective-permute-start.2 = (f32[48,128]{1,0:T(8,128)S(1)}, f32[48,128]{1,0:T(8,128)S(1)}, u32[]{:S(2)}, u32[]{:S(2)}) collective-permute-start(f32[48,128]{1,0:T(8,128)S(1)} %get-tuple-element.45), channel_id=1, source_target_pairs={{0,1},{1,0},{2,3},{3,2},{4,5},{5,4},{6,7},{7,6},{8,9},{9,8},{10,11... | collective-permute-start | bytes 73736 | tf_op jit(solution)/shard_map/ppermute | solution.py:420
  12.7 2.6 %collective-permute-start.4 = (bf16[8,64,128]{2,1,0:T(8,128)(2,1)S(1)}, bf16[8,64,128]{2,1,0:T(8,128)(2,1)S(1)}, u32[]{:S(2)}, u32[]{:S(2)}) collective-permute-start(bf16[8,64,128]{2,1,0:T(8,128)(2,1)S(1)} %convert_element_type.10), channel_id=1, source_target_pairs={{0,4},{4,0},{1,5},{5,1},{2,6},{6,2},{3,7},{7,3},{8,12},{12,8},{9,1... | collective-permute-start | bytes 393224 | tf_op jit(solution)/shard_map/ppermute | solution.py:267
  15.3 3.0 %inner.2 = (f32[3,16,2,32,128]{4,3,2,1,0:T(8,128)S(1)}, bf16[96,64,128]{2,1,0:T(8,128)(2,1)S(1)}, bf16[17,2,96,384]{3,2,1,0:T(8,128)(2,1)S(1)}, bf16[1536,256]{1,0:T(8,128)(2,1)S(1)}) custom-call(s32[2]{0:T(128)S(1)} %pad_add_fusion.odd, s32[48]{0:T(128)S(1)} %multiply_add_fusion.mat_idx, s32[48]{0:T(128)S(1)} %fusion.28.send_slot, ...), custom_call_target="tpu_custom_call" | custom-call | flops 570425344 | bytes 4194304 | tf_op jit(solution)/shard_map/inner/pallas_call | solution.py:433
  18.3 3.7 %outer.2 = (f32[3,16,2,32,128]{4,3,2,1,0:T(8,128)S(1)}, bf16[96,64,128]{2,1,0:T(8,128)(2,1)S(1)}, bf16[17,2,96,384]{3,2,1,0:T(8,128)(2,1)S(1)}) custom-call(s32[2]{0:T(128)S(1)} %pad_add_fusion.odd, s32[48]{0:T(128)S(1)} %multiply_add_fusion.mat_idx, s32[48]{0:T(128)S(1)} %fusion.28.send_slot, ...), custom_call_target="tpu_custom_call", output_to_operand_aliasing={{0}: (7, {}), {1}: (8, {}), {2}: (9, {})} | custom-call | flops 1140850688 | bytes 4194304 | tf_op jit(solution)/shard_map/outer/pallas_call | solution.py:434
  22.1 26.3 %all_to_all.20 = bf16[16,6,64,128]{3,2,1,0:T(8,128)(2,1)S(1)} all-to-all(bf16[16,6,64,128]{3,2,1,0:T(8,128)(2,1)S(1)} %bitcast.30), channel_id=1, replica_groups=mesh['row'=4,'zh'=2,'zl'=2,'x'=2] {'row','zl','x'}, dimensions={0} | all-to-all | bytes 3145728 | tf_op jit(solution)/shard_map/all_to_all | solution.py:413
  48.4 1.0 combine.2
  49.4 0.6 collective-permute-start.5
  50.0 14.4 %collective-permute-done.5.other = bf16[16,64,128]{2,1,0:T(8,128)(2,1)S(1)} collective-permute-done((bf16[16,64,128]{2,1,0:T(8,128)(2,1)S(1)}, bf16[16,64,128]{2,1,0:T(8,128)(2,1)S(1)}, u32[]{:S(2)}, u32[]{:S(2)}) %collective-permute-start.5) | collective-permute-done | bytes 262176 | tf_op jit(solution)/shard_map/ppermute | solution.py:267
  64.5 0.8 reply.2
  65.3 23.3 %all_to_all.21 = bf16[16,6,64,128]{3,2,1,0:T(8,128)(2,1)S(1)} all-to-all(bf16[16,6,64,128]{3,2,1,0:T(8,128)(2,1)S(1)} %bitcast.29), channel_id=1, replica_groups=mesh['row'=4,'zh'=2,'zl'=2,'x'=2] {'row','zl','x'}, dimensions={0} | all-to-all | bytes 3145728 | tf_op jit(solution)/shard_map/all_to_all | solution.py:413
  88.6 1.9 %finish.2 = (bf16[32,96,128]{2,1,0:T(8,128)(2,1)S(1)}, bf16[96,128]{1,0:T(8,128)(2,1)S(1)}, bf16[96,128]{1,0:T(8,128)(2,1)S(1)}, f32[32,128]{1,0:T(8,128)S(1)}, f32[32,128]{1,0:T(8,128)S(1)}) custom-call(s32[2]{0:T(128)S(1)} %pad_add_fusion.odd, s32[48]{0:T(128)S(1)} %multiply_add_fusion.mat_idx, s32[48]{0:T(128)S(1)} %fusion.28.send_slot, ...), custom_call_target="tpu_custom_call" | custom-call | tf_op jit(solution)/shard_map/finish/pallas_call | solution.py:448
  90.5 0.3 collective-permute-start.6
  90.8 0.7 collective-permute-start.7
  91.8 0.6 sides.3
  92.3 1.4 collective-permute-start.8
  93.7 0.7 collective-permute-start.9
  94.4 3.0 %inner.3 = (f32[3,16,2,32,128]{4,3,2,1,0:T(8,128)S(1)}, bf16[96,64,128]{2,1,0:T(8,128)(2,1)S(1)}, bf16[17,2,96,384]{3,2,1,0:T(8,128)(2,1)S(1)}, bf16[1536,256]{1,0:T(8,128)(2,1)S(1)}) custom-call(s32[2]{0:T(128)S(1)} %pad_add_fusion.odd, s32[48]{0:T(128)S(1)} %multiply_add_fusion.mat_idx, s32[48]{0:T(128)S(1)} %fusion.28.send_slot, ...), custom_call_target="tpu_custom_call" | custom-call | flops 570425344 | bytes 4194304 | tf_op jit(solution)/shard_map/inner/pallas_call | solution.py:433
  97.4 3.7 %outer.3 = (f32[3,16,2,32,128]{4,3,2,1,0:T(8,128)S(1)}, bf16[96,64,128]{2,1,0:T(8,128)(2,1)S(1)}, bf16[17,2,96,384]{3,2,1,0:T(8,128)(2,1)S(1)}) custom-call(s32[2]{0:T(128)S(1)} %pad_add_fusion.odd, s32[48]{0:T(128)S(1)} %multiply_add_fusion.mat_idx, s32[48]{0:T(128)S(1)} %fusion.28.send_slot, ...), custom_call_target="tpu_custom_call", output_to_operand_aliasing={{0}: (7, {}), {1}: (8, {}), {2}: (9, {})} | custom-call | flops 1140850688 | bytes 4194304 | tf_op jit(solution)/shard_map/outer/pallas_call | solution.py:434
  101.2 30.5 %all_to_all.22 = bf16[16,6,64,128]{3,2,1,0:T(8,128)(2,1)S(1)} all-to-all(bf16[16,6,64,128]{3,2,1,0:T(8,128)(2,1)S(1)} %bitcast.31), channel_id=1, replica_groups=mesh['row'=4,'zh'=2,'zl'=2,'x'=2] {'row','zl','x'}, dimensions={0} | all-to-all | bytes 3145728 | tf_op jit(solution)/shard_map/all_to_all | solution.py:413
  131.7 1.0 combine.3
  132.7 0.4 collective-permute-start.10
  133.2 14.6 %collective-permute-done.10.other = bf16[16,64,128]{2,1,0:T(8,128)(2,1)S(1)} collective-permute-done((bf16[16,64,128]{2,1,0:T(8,128)(2,1)S(1)}, bf16[16,64,128]{2,1,0:T(8,128)(2,1)S(1)}, u32[]{:S(2)}, u32[]{:S(2)}) %collective-permute-start.10) | collective-permute-done | bytes 262176 | tf_op jit(solution)/shard_map/ppermute | solution.py:267
  147.8 0.8 reply.3
  148.6 23.2 %all_to_all.23 = bf16[16,6,64,128]{3,2,1,0:T(8,128)(2,1)S(1)} all-to-all(bf16[16,6,64,128]{3,2,1,0:T(8,128)(2,1)S(1)} %bitcast.26), channel_id=1, replica_groups=mesh['row'=4,'zh'=2,'zl'=2,'x'=2] {'row','zl','x'}, dimensions={0} | all-to-all | bytes 3145728 | tf_op jit(solution)/shard_map/all_to_all | solution.py:413
  171.8 2.6 %finish.3 = f32[32,96,128]{2,1,0:T(8,128)} custom-call(s32[2]{0:T(128)S(1)} %pad_add_fusion.odd, s32[48]{0:T(128)S(1)} %multiply_add_fusion.mat_idx, s32[48]{0:T(128)S(1)} %fusion.28.send_slot, bf16[96,64,128]{2,1,0:T(8,128)(2,1)S(1)} %bitcast.32, f32[3,16,2,32,128]{4,3,2,1,0:T(8,128)S(1)} %get-tuple-element.76.pulled, bf16[32,96,128]{2,1,0:T(8,128)(2,1)S(1)} %copy-done.2, ...), custom_call_target="tpu_custom_call" | custom-call | tf_op jit(solution)/shard_map/finish/pallas_call | solution.py:448
  (50 shorter events, 1.6 us)
Async XLA Ops:
  0.0 3.6 %copy-start.5 = (s32[4,24,16]{1,2,0:T(8,128)S(1)}, s32[4,24,16]{1,2,0:T(8,128)}, u32[]{:S(2)}) copy-start(s32[4,24,16]{1,2,0:T(8,128)} %param.14) | copy-start | bytes 18436
  0.0 3.8 %copy-start.6 = (s32[256]{0:T(256)S(1)}, s32[256]{0:T(256)}, u32[]{:S(2)}) copy-start(s32[256]{0:T(256)} %param.16) | copy-start | bytes 3076
  0.0 4.4 %copy-start.7 = (s32[1,3,16]{2,0,1:T(1,128)S(1)}, s32[1,3,16]{2,0,1:T(1,128)}, u32[]{:S(2)}) copy-start(s32[1,3,16]{2,0,1:T(1,128)} %param.15) | copy-start | bytes 580
  0.0 4.5 %copy-start.8 = (s32[8]{0:T(128)S(1)}, s32[8]{0:T(128)}, u32[]{:S(2)}) copy-start(s32[8]{0:T(128)} %param.17) | copy-start | bytes 100
  0.0 5.9 %copy-start.3 = (f32[8,64,128]{2,1,0:T(8,128)S(1)}, f32[8,64,128]{2,1,0:T(8,128)}, u32[]{:S(2)}) copy-start(f32[8,64,128]{2,1,0:T(8,128)} %own_weight.3) | copy-start | bytes 786436
  2.4 3.6 %collective-permute-start = (bf16[96,128]{1,0:T(8,128)(2,1)S(1)}, bf16[96,128]{1,0:T(8,128)(2,1)S(1)}, u32[]{:S(2)}, u32[]{:S(2)}) collective-permute-start(bf16[96,128]{1,0:T(8,128)(2,1)S(1)} %get-tuple-element.41), channel_id=1, source_target_pairs={{0,8},{8,0},{16,24},{24,16},{1,9},{9,1},{17,25},{25,17},{2,10},{10... | collective-permute-start | bytes 73736 | tf_op jit(solution)/shard_map/ppermute | solution.py:420
  2.9 3.0 %collective-permute-start.1 = (bf16[96,128]{1,0:T(8,128)(2,1)S(1)}, bf16[96,128]{1,0:T(8,128)(2,1)S(1)}, u32[]{:S(2)}, u32[]{:S(2)}) collective-permute-start(bf16[96,128]{1,0:T(8,128)(2,1)S(1)} %get-tuple-element.42), channel_id=1, source_target_pairs={{8,16},{16,8},{9,17},{17,9},{10,18},{18,10},{11,19},{19,11},{12,20... | collective-permute-start | bytes 73736 | tf_op jit(solution)/shard_map/ppermute | solution.py:420
  5.9 9.3 %copy-start = (bf16[8,4,64,1024]{3,2,1,0:T(8,128)(2,1)S(1)}, bf16[8,4,64,1024]{3,2,1,0:T(8,128)(2,1)}, u32[]{:S(2)}) copy-start(bf16[8,4,64,1024]{3,2,1,0:T(8,128)(2,1)} %param.12) | copy-start | bytes 12582916
  5.9 9.3 %copy-start.4 = (bf16[3,3,128,128]{3,2,1,0:T(8,128)(2,1)S(1)}, bf16[3,3,128,128]{3,2,1,0:T(8,128)(2,1)}, u32[]{:S(2)}) copy-start(bf16[3,3,128,128]{3,2,1,0:T(8,128)(2,1)} %kernel.3) | copy-start | bytes 884740
  6.5 11.8 %collective-permute-start.3 = (f32[48,128]{1,0:T(8,128)S(1)}, f32[48,128]{1,0:T(8,128)S(1)}, u32[]{:S(2)}, u32[]{:S(2)}) collective-permute-start(f32[48,128]{1,0:T(8,128)S(1)} %get-tuple-element.47), channel_id=1, source_target_pairs={{1,2},{2,1},{3,4},{4,3},{5,6},{6,5},{9,10},{10,9},{11,12},{12,11},... | collective-permute-start | bytes 73736 | tf_op jit(solution)/shard_map/ppermute | solution.py:420
  7.3 11.0 %collective-permute-start.2 = (f32[48,128]{1,0:T(8,128)S(1)}, f32[48,128]{1,0:T(8,128)S(1)}, u32[]{:S(2)}, u32[]{:S(2)}) collective-permute-start(f32[48,128]{1,0:T(8,128)S(1)} %get-tuple-element.45), channel_id=1, source_target_pairs={{0,1},{1,0},{2,3},{3,2},{4,5},{5,4},{6,7},{7,6},{8,9},{9,8},{10,11... | collective-permute-start | bytes 73736 | tf_op jit(solution)/shard_map/ppermute | solution.py:420
  12.7 9.4 %collective-permute-start.4 = (bf16[8,64,128]{2,1,0:T(8,128)(2,1)S(1)}, bf16[8,64,128]{2,1,0:T(8,128)(2,1)S(1)}, u32[]{:S(2)}, u32[]{:S(2)}) collective-permute-start(bf16[8,64,128]{2,1,0:T(8,128)(2,1)S(1)} %convert_element_type.10), channel_id=1, source_target_pairs={{0,4},{4,0},{1,5},{5,1},{2,6},{6,2},{3,7},{7,3},{8,12},{12,8},{9,1... | collective-permute-start | bytes 393224 | tf_op jit(solution)/shard_map/ppermute | solution.py:267
  49.4 15.0 %collective-permute-start.5 = (bf16[16,64,128]{2,1,0:T(8,128)(2,1)S(1)}, bf16[16,64,128]{2,1,0:T(8,128)(2,1)S(1)}, u32[]{:S(2)}, u32[]{:S(2)}) collective-permute-start(bf16[16,64,128]{2,1,0:T(8,128)(2,1)S(1)} %get-tuple-element.59), channel_id=1, source_target_pairs={{0,4},{4,0},{1,5},{5,1},{2,6},{6,2},{3,7},{7,3},{8,12},{12,8},{9,1... | collective-permute-start | bytes 786440 | tf_op jit(solution)/shard_map/ppermute | solution.py:267
  65.3 23.3 %copy-start.1 = (bf16[32,96,128]{2,1,0:T(8,128)(2,1)S(1)}, bf16[32,96,128]{2,1,0:T(8,128)(2,1)}, u32[]{:S(2)}) copy-start(bf16[32,96,128]{2,1,0:T(8,128)(2,1)} %state.5) | copy-start | bytes 2359300
  65.3 23.3 %copy-start.2 = (bf16[32,96,128]{2,1,0:T(8,128)(2,1)S(1)}, bf16[32,96,128]{2,1,0:T(8,128)(2,1)}, u32[]{:S(2)}) copy-start(bf16[32,96,128]{2,1,0:T(8,128)(2,1)} %grad.5) | copy-start | bytes 2359300
  90.5 1.3 collective-permute-start.6
  90.8 0.9 collective-permute-start.7
  92.3 5.1 %collective-permute-start.8 = (f32[48,128]{1,0:T(8,128)S(1)}, f32[48,128]{1,0:T(8,128)S(1)}, u32[]{:S(2)}, u32[]{:S(2)}) collective-permute-start(f32[48,128]{1,0:T(8,128)S(1)} %get-tuple-element.66), channel_id=1, source_target_pairs={{0,1},{1,0},{2,3},{3,2},{4,5},{5,4},{6,7},{7,6},{8,9},{9,8},{10,11... | collective-permute-start | bytes 73736 | tf_op jit(solution)/shard_map/ppermute | solution.py:420
  93.7 3.7 %collective-permute-start.9 = (f32[48,128]{1,0:T(8,128)S(1)}, f32[48,128]{1,0:T(8,128)S(1)}, u32[]{:S(2)}, u32[]{:S(2)}) collective-permute-start(f32[48,128]{1,0:T(8,128)S(1)} %get-tuple-element.67), channel_id=1, source_target_pairs={{1,2},{2,1},{3,4},{4,3},{5,6},{6,5},{9,10},{10,9},{11,12},{12,11},... | collective-permute-start | bytes 73736 | tf_op jit(solution)/shard_map/ppermute | solution.py:420
  132.7 15.0 %collective-permute-start.10 = (bf16[16,64,128]{2,1,0:T(8,128)(2,1)S(1)}, bf16[16,64,128]{2,1,0:T(8,128)(2,1)S(1)}, u32[]{:S(2)}, u32[]{:S(2)}) collective-permute-start(bf16[16,64,128]{2,1,0:T(8,128)(2,1)S(1)} %get-tuple-element.75), channel_id=1, source_target_pairs={{0,4},{4,0},{1,5},{5,1},{2,6},{6,2},{3,7},{7,3},{8,12},{12,8},{9,1... | collective-permute-start | bytes 786440 | tf_op jit(solution)/shard_map/ppermute | solution.py:267

commit v11 on v10

--- a/solution.py
+++ b/solution.py
@@ -49,10 +49,15 @@
 
 
 def emit_edges(value, odd, scaled, row_a, row_b, col_a, col_b):
-    rows, cols = value.shape[:2]
-    scaled[...] = value.astype(jnp.bfloat16)
+    rows = value.shape[0]
     row_a[...] = pick(odd[0], value[0], value[rows - 1]).astype(jnp.bfloat16)
     row_b[...] = pick(odd[0], value[rows - 1], value[0]).astype(jnp.bfloat16)
+    emit_sides(value, odd, scaled, col_a, col_b)
+
+
+def emit_sides(value, odd, scaled, col_a, col_b):
+    cols = value.shape[1]
+    scaled[...] = value.astype(jnp.bfloat16)
     left, right = value[:, 0, :], value[:, cols - 1, :]
     col_a[...] = pick(odd[1], left, right)
     col_b[...] = pick(odd[1], right, left)
@@ -201,6 +206,42 @@
     lax.fori_loop(0, out.shape[0], body, 0, unroll=8)
 
 
+def rim_kernel(
+    odd, mat_idx, send_slot, returned, pulled, grad, state, rays, row_a, row_b, *, tile_cols,
+):
+    tiles = pulled.shape[0]
+    rows, cols, chans = grad.shape
+    tile_pix = rays.shape[2]
+    f32 = jnp.float32
+    lanes = 128
+    edges = ((0, 0, slice(0, lanes)), (rows - 1, PIX - 1, slice(tile_pix - lanes, tile_pix)))
+    for t in range(tiles):
+        c0 = t % tile_cols * PIX
+        picked = jnp.concatenate([returned[send_slot[t * HITS + k]] for k in range(HITS)], axis=0)
+        for which, (row, line, part) in enumerate(edges):
+            if not 0 <= row - t // tile_cols * PIX < PIX:
+                continue
+            matrix = jnp.concatenate(
+                [rays[mat_idx[t * HITS + k], :, part] for k in range(HITS)], axis=0
+            )
+            backed = lax.dot_general(
+                picked, matrix, (((0,), (0,)), ((), ())), preferred_element_type=f32
+            ).T
+            backed = backed[:PIX] if which == 0 else backed[lanes - PIX :]
+            change = pulled[t, line // 2, line % 2] - relax_rate * backed
+            adjoint = grad[row, c0 : c0 + PIX, :].astype(f32) + change
+            value = state[row, c0 : c0 + PIX, :].astype(f32)
+            value = ((1.0 - value * value) * adjoint).astype(jnp.bfloat16)
+
+            @pl.when(odd[0] == which)
+            def _():
+                row_b[c0 : c0 + PIX, :] = value
+
+            @pl.when(odd[0] != which)
+            def _():
+                row_a[c0 : c0 + PIX, :] = value
+
+
 def finish_kernel(
     odd, mat_idx, send_slot, returned, pulled, grad, state, rays, *refs, tile_cols, last,
 ):
@@ -238,7 +279,7 @@
         for t in range(tiles):
             leave(t).wait()
     else:
-        emit_edges(whole[...], odd, *outs)
+        emit_sides(whole[...], odd, *outs)
 
 
 def on_device(state, grad, kernel, ray_matrix, ray_weight, hits, offsets, block_slot, angle_count):
@@ -293,15 +334,6 @@
     table = table.reshape(slots)
     mat_idx = (my_hits // blk_ang) * spots + offsets.reshape(pairs)
 
-    dense_z = jnp.arange(dense, dtype=i32) // blk_dev * 2 + zl
-    dense_place = (row * nc + dense_z * nx + x) * blk_dev + jnp.arange(dense, dtype=i32) % blk_dev
-    number = jnp.arange(blocks, dtype=i32)
-    active = (
-        (number % blk_ang).reshape(ANGLES, blk_ang) < angle_count[:, None]
-    ).reshape(1, blocks)
-    used = jnp.any((block_slot[None, :] == dense_place[:, None]) & active, axis=1).astype(i32)
-    used = jnp.concatenate([used, jnp.full((1,), zh * blk_dev, i32)])
-
     rays = ray_matrix.reshape(angles * spots, bins, tile_pix)
 
     block = (bins, chans)
@@ -397,16 +429,38 @@
     def finish(last):
         return pl.pallas_call(
             functools.partial(finish_kernel, tile_cols=tile_cols, last=last),
-            out_shape=(shape(state.shape, f32),) if last else edges,
+            out_shape=(shape(state.shape, f32),) if last else edges[:1] + edges[3:],
             in_specs=[SMEM] * 3 + [VMEM] * 5,
-            out_specs=(pl.BlockSpec(memory_space=pl.ANY),) if last else (VMEM,) * 5,
+            out_specs=(ANY,) if last else (VMEM,) * 3,
             scratch_shapes=[
                 pltpu.VMEM(state.shape, f32),
                 pltpu.SemaphoreType.DMA((tiles,)),
             ],
             compiler_params=limit(20),
+            cost_estimate=cost(tiles),
             name="finish",
         )
+
+    rim_of = pl.pallas_call(
+        functools.partial(rim_kernel, tile_cols=tile_cols),
+        out_shape=edges[1:3],
+        in_specs=[SMEM] * 3 + [VMEM] * 5,
+        out_specs=(VMEM,) * 2,
+        compiler_params=limit(16),
+        name="rim",
+    )
+
+    dense_z = jnp.arange(dense, dtype=i32) // blk_dev * 2 + zl
+    dense_place = (row * nc + dense_z * nx + x) * blk_dev + jnp.arange(dense, dtype=i32) % blk_dev
+    own_first = jnp.full((1,), zh * blk_dev, i32)
+
+    def in_use(counts, dense_place, own_first):
+        number = jnp.arange(blocks, dtype=i32)
+        active = (
+            (number % blk_ang).reshape(ANGLES, blk_ang) < counts[:, None]
+        ).reshape(1, blocks)
+        used = jnp.any((block_slot[None, :] == dense_place[:, None]) & active, axis=1).astype(i32)
+        return jnp.concatenate([used, own_first])
 
     def across(value):
         value = value.reshape((peers, cap) + block)
@@ -439,15 +493,19 @@
         pulled, outgoing, swapped = forward(turn == 0, scaled, *rim)
         if not turn:
             other_weight = swapped
-            outgoing, table, used, other_weight = lax.optimization_barrier(
-                (outgoing, table, used, other_weight)
+            outgoing, table, other_weight, dense_place, own_first = lax.optimization_barrier(
+                (outgoing, table, other_weight, dense_place, own_first)
             )
         total, mine = combine(table, across(outgoing))
+        if not turn:
+            mine, *own = lax.optimization_barrier((mine, angle_count, dense_place, own_first))
+            used = in_use(*own)
         replies = reply(table, used, total, exchange(mine), ray_weight, other_weight)
         last = turn == ITERS - 1
-        scaled, *rim = finish(last)(
-            odd, mat_idx, send_slot, across(replies), pulled, grad, state, rays
-        )
+        given = (odd, mat_idx, send_slot, across(replies), pulled, grad, state, rays)
+        scaled, *sides_of = finish(last)(*given)
+        if not last:
+            rim = (*rim_of(*given), *sides_of)
     return scaled
 
 

time: 175 us -> 176 us (level)
  Pallas kernels: 25 us -> 27.5 us
    pallas_call x2 -> x3, Pallas kernels: 4.46 us -> 6.94 us  [the longest x2 4.48 us: on_device(): scaled, *sides_of = finish(last)(*given)]
  transfers between devices with their start and end apart: 11 -> 11, of which waited for: 3 -> 2; matrix products, arithmetic and copies ran while one was open for 1% -> 1% of each run, Pallas kernels for 6% -> 7%
where the time goes in v11:
time: 176 us; the launch traced here: 175 us
  blocking collectives  102 us (58%)
  waiting for transfers between devices  28.6 us (16%)
  Pallas kernels  27.5 us (16%)
  starting transfers between devices  14.1 us (8%)
    all_to_all x4, blocking collectives, across(): lax.all_to_all(value, GROUP, split_axis=0, concat_axis=0, tiled=True)  102 us
    ppermute x3, waiting for transfers between devices, exchange(): return lax.ppermute(value, 'zh', [(0, 1), (1, 0)])  28.6 us
    pallas_call x2, Pallas kernels, forward(): outer(odd, mat_idx, send_slot, *beside, taps, rays, *parts)  7.44 us
    ppermute x4, starting transfers between devices, swaps(): lax.ppermute(value_a, axis, even)  7.44 us
    pallas_call x2, Pallas kernels, forward(): *parts, taps = inner(odd, mat_idx, send_slot, scaled, *above, kernel, rays)  6.06 us
    pallas_call x2, Pallas kernels, on_device(): scaled, *sides_of = finish(last)(*given)  4.48 us
    ppermute x3, starting transfers between devices, exchange(): return lax.ppermute(value, 'zh', [(0, 1), (1, 0)])  3.76 us
  transfers between devices with their start and end apart: 11, of which 2 were waited for; matrix products, arithmetic and copies ran while one was open for 1% of the time, Pallas kernels for 7%

profile of v11, /device:TPU:0, one launch (start us, length us, event | category | flops | bytes accessed | tf_op | source)
XLA Modules:
  0.0 175.3 jit_solution(4661367558518548612)
XLA Ops:
  0.1 2.2 %start.1 = (bf16[32,96,128]{2,1,0:T(8,128)(2,1)S(1)}, bf16[96,128]{1,0:T(8,128)(2,1)S(1)}, bf16[96,128]{1,0:T(8,128)(2,1)S(1)}, f32[32,128]{1,0:T(8,128)S(1)}, f32[32,128]{1,0:T(8,128)S(1)}) custom-call(s32[2]{0:T(128)S(1)} %pad_add_fusion.odd, bf16[32,96,128]{2,1,0:T(8,128)(2,1)} %state.7, bf16[32,96,128]{2,1,0:T(8,128)(2,1)} %grad.7), custom_call_target="tpu_custom_call" | custom-call | tf_op jit(solution)/shard_map/start/pallas_call | solution.py:491
  2.3 0.6 collective-permute-start
  2.9 0.7 collective-permute-start.1
  3.8 0.5 select_reduce_fusion
  4.5 0.5 convert_reduce_fusion
  5.5 0.6 sides.2
  6.1 0.8 collective-permute-start.3
  6.9 5.4 %collective-permute-start.2 = (f32[48,128]{1,0:T(8,128)S(1)}, f32[48,128]{1,0:T(8,128)S(1)}, u32[]{:S(2)}, u32[]{:S(2)}) collective-permute-start(f32[48,128]{1,0:T(8,128)S(1)} %get-tuple-element.50), channel_id=1, source_target_pairs={{0,1},{1,0},{2,3},{3,2},{4,5},{5,4},{6,7},{7,6},{8,9},{9,8},{10,11... | collective-permute-start | bytes 73736 | tf_op jit(solution)/shard_map/ppermute | solution.py:474
  12.2 2.6 %collective-permute-start.4 = (bf16[8,64,128]{2,1,0:T(8,128)(2,1)S(1)}, bf16[8,64,128]{2,1,0:T(8,128)(2,1)S(1)}, u32[]{:S(2)}, u32[]{:S(2)}) collective-permute-start(bf16[8,64,128]{2,1,0:T(8,128)(2,1)S(1)} %convert_element_type.10), channel_id=1, source_target_pairs={{0,4},{4,0},{1,5},{5,1},{2,6},{6,2},{3,7},{7,3},{8,12},{12,8},{9,1... | collective-permute-start | bytes 393224 | tf_op jit(solution)/shard_map/ppermute | solution.py:308
  14.8 3.0 %inner.2 = (f32[3,16,2,32,128]{4,3,2,1,0:T(8,128)S(1)}, bf16[96,64,128]{2,1,0:T(8,128)(2,1)S(1)}, bf16[17,2,96,384]{3,2,1,0:T(8,128)(2,1)S(1)}, bf16[1536,256]{1,0:T(8,128)(2,1)S(1)}) custom-call(s32[2]{0:T(128)S(1)} %pad_add_fusion.odd, s32[48]{0:T(128)S(1)} %multiply_add_fusion.mat_idx, s32[48]{0:T(128)S(1)} %fusion.28.send_slot, ...), custom_call_target="tpu_custom_call" | custom-call | flops 570425344 | bytes 4194304 | tf_op jit(solution)/shard_map/inner/pallas_call | solution.py:487
  17.9 3.7 %outer.2 = (f32[3,16,2,32,128]{4,3,2,1,0:T(8,128)S(1)}, bf16[96,64,128]{2,1,0:T(8,128)(2,1)S(1)}, bf16[17,2,96,384]{3,2,1,0:T(8,128)(2,1)S(1)}) custom-call(s32[2]{0:T(128)S(1)} %pad_add_fusion.odd, s32[48]{0:T(128)S(1)} %multiply_add_fusion.mat_idx, s32[48]{0:T(128)S(1)} %fusion.28.send_slot, ...), custom_call_target="tpu_custom_call", output_to_operand_aliasing={{0}: (7, {}), {1}: (8, {}), {2}: (9, {})} | custom-call | flops 1140850688 | bytes 4194304 | tf_op jit(solution)/shard_map/outer/pallas_call | solution.py:488
  21.6 26.8 %all_to_all.20 = bf16[16,6,64,128]{3,2,1,0:T(8,128)(2,1)S(1)} all-to-all(bf16[16,6,64,128]{3,2,1,0:T(8,128)(2,1)S(1)} %bitcast.32), channel_id=1, replica_groups=mesh['row'=4,'zh'=2,'zl'=2,'x'=2] {'row','zl','x'}, dimensions={0} | all-to-all | bytes 3145728 | tf_op jit(solution)/shard_map/all_to_all | solution.py:467
  48.4 1.0 combine.2
  49.6 0.5 collective-permute-start.5
  50.4 14.2 %collective-permute-done.5.other = bf16[16,64,128]{2,1,0:T(8,128)(2,1)S(1)} collective-permute-done((bf16[16,64,128]{2,1,0:T(8,128)(2,1)S(1)}, bf16[16,64,128]{2,1,0:T(8,128)(2,1)S(1)}, u32[]{:S(2)}, u32[]{:S(2)}) %collective-permute-start.5) | collective-permute-done | bytes 262176 | tf_op jit(solution)/shard_map/ppermute | solution.py:308
  64.6 0.8 reply.2
  65.4 23.4 %all_to_all.21 = bf16[16,6,64,128]{3,2,1,0:T(8,128)(2,1)S(1)} all-to-all(bf16[16,6,64,128]{3,2,1,0:T(8,128)(2,1)S(1)} %bitcast.31), channel_id=1, replica_groups=mesh['row'=4,'zh'=2,'zl'=2,'x'=2] {'row','zl','x'}, dimensions={0} | all-to-all | bytes 3145728 | tf_op jit(solution)/shard_map/all_to_all | solution.py:467
  88.8 2.5 %rim.1 = (bf16[96,128]{1,0:T(8,128)(2,1)S(1)}, bf16[96,128]{1,0:T(8,128)(2,1)S(1)}) custom-call(s32[2]{0:T(128)S(1)} %pad_add_fusion.odd, s32[48]{0:T(128)S(1)} %multiply_add_fusion.mat_idx, s32[48]{0:T(128)S(1)} %fusion.28.send_slot, bf16[96,64,128]{2,1,0:T(8,128)(2,1)S(1)} %bitcast.26, f32[3,16,2,32,128]{4,3,2,1,0:T(8,128)S(1)} %get-tuple-element.71.pulled, ...), custom_call_target="tpu_custom_call" | custom-call | tf_op jit(solution)/shard_map/rim/pallas_call | solution.py:508
  91.6 0.7 collective-permute-start.7
  92.3 1.9 %finish.2 = (bf16[32,96,128]{2,1,0:T(8,128)(2,1)S(1)}, f32[32,128]{1,0:T(8,128)S(1)}, f32[32,128]{1,0:T(8,128)S(1)}) custom-call(s32[2]{0:T(128)S(1)} %pad_add_fusion.odd, s32[48]{0:T(128)S(1)} %multiply_add_fusion.mat_idx, s32[48]{0:T(128)S(1)} %fusion.28.send_slot, bf16[96,64,128]{2,1,0:T(8,128)(2,1)S(1)} %bitcast.27, ...), custom_call_target="tpu_custom_call" | custom-call | flops 1711276032 | bytes 4194304 | tf_op jit(solution)/shard_map/finish/pallas_call | solution.py:506
  94.2 0.6 sides.3
  94.8 1.1 collective-permute-start.8
  95.9 0.8 collective-permute-start.9
  96.8 3.0 %inner.3 = (f32[3,16,2,32,128]{4,3,2,1,0:T(8,128)S(1)}, bf16[96,64,128]{2,1,0:T(8,128)(2,1)S(1)}, bf16[17,2,96,384]{3,2,1,0:T(8,128)(2,1)S(1)}, bf16[1536,256]{1,0:T(8,128)(2,1)S(1)}) custom-call(s32[2]{0:T(128)S(1)} %pad_add_fusion.odd, s32[48]{0:T(128)S(1)} %multiply_add_fusion.mat_idx, s32[48]{0:T(128)S(1)} %fusion.28.send_slot, ...), custom_call_target="tpu_custom_call" | custom-call | flops 570425344 | bytes 4194304 | tf_op jit(solution)/shard_map/inner/pallas_call | solution.py:487
  99.8 3.7 %outer.3 = (f32[3,16,2,32,128]{4,3,2,1,0:T(8,128)S(1)}, bf16[96,64,128]{2,1,0:T(8,128)(2,1)S(1)}, bf16[17,2,96,384]{3,2,1,0:T(8,128)(2,1)S(1)}) custom-call(s32[2]{0:T(128)S(1)} %pad_add_fusion.odd, s32[48]{0:T(128)S(1)} %multiply_add_fusion.mat_idx, s32[48]{0:T(128)S(1)} %fusion.28.send_slot, ...), custom_call_target="tpu_custom_call", output_to_operand_aliasing={{0}: (7, {}), {1}: (8, {}), {2}: (9, {})} | custom-call | flops 1140850688 | bytes 4194304 | tf_op jit(solution)/shard_map/outer/pallas_call | solution.py:488
  103.6 28.9 %all_to_all.22 = bf16[16,6,64,128]{3,2,1,0:T(8,128)(2,1)S(1)} all-to-all(bf16[16,6,64,128]{3,2,1,0:T(8,128)(2,1)S(1)} %bitcast.33), channel_id=1, replica_groups=mesh['row'=4,'zh'=2,'zl'=2,'x'=2] {'row','zl','x'}, dimensions={0} | all-to-all | bytes 3145728 | tf_op jit(solution)/shard_map/all_to_all | solution.py:467
  132.5 1.0 combine.3
  133.6 0.6 collective-permute-start.10
  134.2 14.4 %collective-permute-done.10.other = bf16[16,64,128]{2,1,0:T(8,128)(2,1)S(1)} collective-permute-done((bf16[16,64,128]{2,1,0:T(8,128)(2,1)S(1)}, bf16[16,64,128]{2,1,0:T(8,128)(2,1)S(1)}, u32[]{:S(2)}, u32[]{:S(2)}) %collective-permute-start.10) | collective-permute-done | bytes 262176 | tf_op jit(solution)/shard_map/ppermute | solution.py:308
  148.6 0.8 reply.3
  149.4 23.2 %all_to_all.23 = bf16[16,6,64,128]{3,2,1,0:T(8,128)(2,1)S(1)} all-to-all(bf16[16,6,64,128]{3,2,1,0:T(8,128)(2,1)S(1)} %bitcast.28), channel_id=1, replica_groups=mesh['row'=4,'zh'=2,'zl'=2,'x'=2] {'row','zl','x'}, dimensions={0} | all-to-all | bytes 3145728 | tf_op jit(solution)/shard_map/all_to_all | solution.py:467
  172.6 2.6 %finish.3 = f32[32,96,128]{2,1,0:T(8,128)} custom-call(s32[2]{0:T(128)S(1)} %pad_add_fusion.odd, s32[48]{0:T(128)S(1)} %multiply_add_fusion.mat_idx, s32[48]{0:T(128)S(1)} %fusion.28.send_slot, bf16[96,64,128]{2,1,0:T(8,128)(2,1)S(1)} %bitcast.34, f32[3,16,2,32,128]{4,3,2,1,0:T(8,128)S(1)} %get-tuple-element.86.pulled, bf16[32,96,128]{2,1,0:T(8,128)(2,1)S(1)} %copy-done.3, ...), custom_call_target="tpu_custom_call" | custom-call | flops 1711276032 | bytes 4194304 | tf_op jit(solution)/shard_map/finish/pallas_call | solution.py:506
  (53 shorter events, 1.7 us)
Async XLA Ops:
  0.0 3.6 %copy-start.6 = (s32[4,24,16]{1,2,0:T(8,128)S(1)}, s32[4,24,16]{1,2,0:T(8,128)}, u32[]{:S(2)}) copy-start(s32[4,24,16]{1,2,0:T(8,128)} %param.14) | copy-start | bytes 18436
  0.0 3.8 %copy-start.7 = (s32[256]{0:T(256)S(1)}, s32[256]{0:T(256)}, u32[]{:S(2)}) copy-start(s32[256]{0:T(256)} %param.16) | copy-start | bytes 3076
  0.0 4.4 %copy-start.8 = (s32[1,3,16]{2,0,1:T(1,128)S(1)}, s32[1,3,16]{2,0,1:T(1,128)}, u32[]{:S(2)}) copy-start(s32[1,3,16]{2,0,1:T(1,128)} %param.15) | copy-start | bytes 580
  0.0 5.4 %copy-start.4 = (f32[8,64,128]{2,1,0:T(8,128)S(1)}, f32[8,64,128]{2,1,0:T(8,128)}, u32[]{:S(2)}) copy-start(f32[8,64,128]{2,1,0:T(8,128)} %own_weight.3) | copy-start | bytes 786436
  2.3 3.1 %collective-permute-start = (bf16[96,128]{1,0:T(8,128)(2,1)S(1)}, bf16[96,128]{1,0:T(8,128)(2,1)S(1)}, u32[]{:S(2)}, u32[]{:S(2)}) collective-permute-start(bf16[96,128]{1,0:T(8,128)(2,1)S(1)} %get-tuple-element.46), channel_id=1, source_target_pairs={{0,8},{8,0},{16,24},{24,16},{1,9},{9,1},{17,25},{25,17},{2,10},{10... | collective-permute-start | bytes 73736 | tf_op jit(solution)/shard_map/ppermute | solution.py:474
  2.9 2.6 %collective-permute-start.1 = (bf16[96,128]{1,0:T(8,128)(2,1)S(1)}, bf16[96,128]{1,0:T(8,128)(2,1)S(1)}, u32[]{:S(2)}, u32[]{:S(2)}) collective-permute-start(bf16[96,128]{1,0:T(8,128)(2,1)S(1)} %get-tuple-element.47), channel_id=1, source_target_pairs={{8,16},{16,8},{9,17},{17,9},{10,18},{18,10},{11,19},{19,11},{12,20... | collective-permute-start | bytes 73736 | tf_op jit(solution)/shard_map/ppermute | solution.py:474
  5.5 9.3 %copy-start = (bf16[8,4,64,1024]{3,2,1,0:T(8,128)(2,1)S(1)}, bf16[8,4,64,1024]{3,2,1,0:T(8,128)(2,1)}, u32[]{:S(2)}) copy-start(bf16[8,4,64,1024]{3,2,1,0:T(8,128)(2,1)} %param.12) | copy-start | bytes 12582916
  5.5 9.3 %copy-start.5 = (bf16[3,3,128,128]{3,2,1,0:T(8,128)(2,1)S(1)}, bf16[3,3,128,128]{3,2,1,0:T(8,128)(2,1)}, u32[]{:S(2)}) copy-start(bf16[3,3,128,128]{3,2,1,0:T(8,128)(2,1)} %kernel.3) | copy-start | bytes 884740
  6.1 11.8 %collective-permute-start.3 = (f32[48,128]{1,0:T(8,128)S(1)}, f32[48,128]{1,0:T(8,128)S(1)}, u32[]{:S(2)}, u32[]{:S(2)}) collective-permute-start(f32[48,128]{1,0:T(8,128)S(1)} %get-tuple-element.52), channel_id=1, source_target_pairs={{1,2},{2,1},{3,4},{4,3},{5,6},{6,5},{9,10},{10,9},{11,12},{12,11},... | collective-permute-start | bytes 73736 | tf_op jit(solution)/shard_map/ppermute | solution.py:474
  6.9 11.0 %collective-permute-start.2 = (f32[48,128]{1,0:T(8,128)S(1)}, f32[48,128]{1,0:T(8,128)S(1)}, u32[]{:S(2)}, u32[]{:S(2)}) collective-permute-start(f32[48,128]{1,0:T(8,128)S(1)} %get-tuple-element.50), channel_id=1, source_target_pairs={{0,1},{1,0},{2,3},{3,2},{4,5},{5,4},{6,7},{7,6},{8,9},{9,8},{10,11... | collective-permute-start | bytes 73736 | tf_op jit(solution)/shard_map/ppermute | solution.py:474
  12.2 9.4 %collective-permute-start.4 = (bf16[8,64,128]{2,1,0:T(8,128)(2,1)S(1)}, bf16[8,64,128]{2,1,0:T(8,128)(2,1)S(1)}, u32[]{:S(2)}, u32[]{:S(2)}) collective-permute-start(bf16[8,64,128]{2,1,0:T(8,128)(2,1)S(1)} %convert_element_type.10), channel_id=1, source_target_pairs={{0,4},{4,0},{1,5},{5,1},{2,6},{6,2},{3,7},{7,3},{8,12},{12,8},{9,1... | collective-permute-start | bytes 393224 | tf_op jit(solution)/shard_map/ppermute | solution.py:308
  48.4 1.1 copy-start.9
  49.6 15.0 %collective-permute-start.5 = (bf16[16,64,128]{2,1,0:T(8,128)(2,1)S(1)}, bf16[16,64,128]{2,1,0:T(8,128)(2,1)S(1)}, u32[]{:S(2)}, u32[]{:S(2)}) collective-permute-start(bf16[16,64,128]{2,1,0:T(8,128)(2,1)S(1)} %get-tuple-element.69), channel_id=1, source_target_pairs={{0,4},{4,0},{1,5},{5,1},{2,6},{6,2},{3,7},{7,3},{8,12},{12,8},{9,1... | collective-permute-start | bytes 786440 | tf_op jit(solution)/shard_map/ppermute | solution.py:308
  64.6 24.3 %copy-start.1 = (bf16[8,4,64,1024]{3,2,1,0:T(8,128)(2,1)S(1)}, bf16[8,4,64,1024]{3,2,1,0:T(8,128)(2,1)}, u32[]{:S(2)}) copy-start(bf16[8,4,64,1024]{3,2,1,0:T(8,128)(2,1)} %param.12) | copy-start | bytes 12582916
  65.4 23.5 %copy-start.2 = (bf16[32,96,128]{2,1,0:T(8,128)(2,1)S(1)}, bf16[32,96,128]{2,1,0:T(8,128)(2,1)}, u32[]{:S(2)}) copy-start(bf16[32,96,128]{2,1,0:T(8,128)(2,1)} %state.7) | copy-start | bytes 2359300
  65.4 23.5 %copy-start.3 = (bf16[32,96,128]{2,1,0:T(8,128)(2,1)S(1)}, bf16[32,96,128]{2,1,0:T(8,128)(2,1)}, u32[]{:S(2)}) copy-start(bf16[32,96,128]{2,1,0:T(8,128)(2,1)} %grad.7) | copy-start | bytes 2359300
  91.3 2.9 %collective-permute-start.6 = (bf16[96,128]{1,0:T(8,128)(2,1)S(1)}, bf16[96,128]{1,0:T(8,128)(2,1)S(1)}, u32[]{:S(2)}, u32[]{:S(2)}) collective-permute-start(bf16[96,128]{1,0:T(8,128)(2,1)S(1)} %get-tuple-element.72), channel_id=1, source_target_pairs={{0,8},{8,0},{16,24},{24,16},{1,9},{9,1},{17,25},{25,17},{2,10},{10... | collective-permute-start | bytes 73736 | tf_op jit(solution)/shard_map/ppermute | solution.py:474
  91.6 2.6 %collective-permute-start.7 = (bf16[96,128]{1,0:T(8,128)(2,1)S(1)}, bf16[96,128]{1,0:T(8,128)(2,1)S(1)}, u32[]{:S(2)}, u32[]{:S(2)}) collective-permute-start(bf16[96,128]{1,0:T(8,128)(2,1)S(1)} %get-tuple-element.73), channel_id=1, source_target_pairs={{8,16},{16,8},{9,17},{17,9},{10,18},{18,10},{11,19},{19,11},{12,20... | collective-permute-start | bytes 73736 | tf_op jit(solution)/shard_map/ppermute | solution.py:474
  94.8 5.0 %collective-permute-start.8 = (f32[48,128]{1,0:T(8,128)S(1)}, f32[48,128]{1,0:T(8,128)S(1)}, u32[]{:S(2)}, u32[]{:S(2)}) collective-permute-start(f32[48,128]{1,0:T(8,128)S(1)} %get-tuple-element.76), channel_id=1, source_target_pairs={{0,1},{1,0},{2,3},{3,2},{4,5},{5,4},{6,7},{7,6},{8,9},{9,8},{10,11... | collective-permute-start | bytes 73736 | tf_op jit(solution)/shard_map/ppermute | solution.py:474
  95.9 3.9 %collective-permute-start.9 = (f32[48,128]{1,0:T(8,128)S(1)}, f32[48,128]{1,0:T(8,128)S(1)}, u32[]{:S(2)}, u32[]{:S(2)}) collective-permute-start(f32[48,128]{1,0:T(8,128)S(1)} %get-tuple-element.77), channel_id=1, source_target_pairs={{1,2},{2,1},{3,4},{4,3},{5,6},{6,5},{9,10},{10,9},{11,12},{12,11},... | collective-permute-start | bytes 73736 | tf_op jit(solution)/shard_map/ppermute | solution.py:474
  133.6 15.0 %collective-permute-start.10 = (bf16[16,64,128]{2,1,0:T(8,128)(2,1)S(1)}, bf16[16,64,128]{2,1,0:T(8,128)(2,1)S(1)}, u32[]{:S(2)}, u32[]{:S(2)}) collective-permute-start(bf16[16,64,128]{2,1,0:T(8,128)(2,1)S(1)} %get-tuple-element.85), channel_id=1, source_target_pairs={{0,4},{4,0},{1,5},{5,1},{2,6},{6,2},{3,7},{7,3},{8,12},{12,8},{9,1... | collective-permute-start | bytes 786440 | tf_op jit(solution)/shard_map/ppermute | solution.py:308

commit v12 on v10

--- a/solution.py
+++ b/solution.py
@@ -112,13 +112,23 @@
     return [t for t in range(tiles) if (0 < t % tile_cols < tile_cols - 1) == inner]
 
 
-def inner_kernel(
-    odd, mat_idx, send_slot, scaled, near_a, near_b, kernel, rays,
-    pulled, out, cols3, taps, wide, *, tile_cols,
-):
-    rows, cols, chans = scaled.shape
+def spread(rows, wide, cols3, first):
+    count, cols, chans = rows.shape
     f32, bf16 = jnp.float32, jnp.bfloat16
-    blank = jnp.zeros((3 * chans, chans), bf16)
+    blank = jnp.zeros((count, 8, chans), f32)
+    wide[:, 0:8, :] = blank
+    wide[:, 8 + cols : 16 + cols, :] = blank
+    wide[:, 8 : 8 + cols, :] = rows.astype(f32)
+    for dc in range(3):
+        lanes = slice(dc * chans, (dc + 1) * chans)
+        value = wide[:, 7 + dc : 7 + dc + cols, :].astype(bf16)
+        for r in range(count):
+            cols3[(first + r) // 2, (first + r) % 2, :, lanes] = value[r]
+
+
+def centre_kernel(scaled, kernel, out, cols3, taps, wide):
+    chans = scaled.shape[2]
+    blank = jnp.zeros((3 * chans, chans), jnp.bfloat16)
     for dr in range(4):
         base = dr * 3 * chans
         for side in range(2):
@@ -129,18 +139,18 @@
                 continue
             for dc in range(3):
                 taps[base + dc * chans : base + (dc + 1) * chans, lanes] = kernel[2 - tap, 2 - dc].T
-    a, b = near_a[...].astype(f32), near_b[...].astype(f32)
-    wide[0, 8 : 8 + cols, :] = pick(odd[0], a, b)
-    wide[rows + 1, 8 : 8 + cols, :] = pick(odd[0], b, a)
-    wide[1 : rows + 1, 8 : 8 + cols, :] = scaled[...].astype(f32)
-    wide[:, 0:8, :] = jnp.zeros((rows + 2, 8, chans), f32)
-    wide[:, 8 + cols :, :] = jnp.zeros((rows + 2, 8, chans), f32)
-    for dc in range(3):
-        value = wide[:, 7 + dc : 7 + dc + cols, :].astype(bf16)
-        cols3[:, :, :, dc * chans : (dc + 1) * chans] = value.reshape(
-            (rows + 2) // 2, 2, cols, chans
-        )
+    spread(scaled[...], wide, cols3, 1)
     out[...] = jnp.zeros_like(out)
+
+
+def inner_kernel(
+    odd, mat_idx, send_slot, near_a, near_b, taps, rays, _out, _cols3,
+    pulled, out, cols3, wide, *, tile_cols,
+):
+    a, b = near_a[...], near_b[...]
+    last = 2 * cols3.shape[0] - 1
+    spread(pick(odd[0], a, b)[None], wide, cols3, 0)
+    spread(pick(odd[0], b, a)[None], wide, cols3, last)
     for t in tiles_at(pulled.shape[0], tile_cols, True):
         forward_tile(mat_idx, send_slot, taps, rays, pulled, out, cols3, t, tile_cols)
 
@@ -293,15 +303,6 @@
     table = table.reshape(slots)
     mat_idx = (my_hits // blk_ang) * spots + offsets.reshape(pairs)
 
-    dense_z = jnp.arange(dense, dtype=i32) // blk_dev * 2 + zl
-    dense_place = (row * nc + dense_z * nx + x) * blk_dev + jnp.arange(dense, dtype=i32) % blk_dev
-    number = jnp.arange(blocks, dtype=i32)
-    active = (
-        (number % blk_ang).reshape(ANGLES, blk_ang) < angle_count[:, None]
-    ).reshape(1, blocks)
-    used = jnp.any((block_slot[None, :] == dense_place[:, None]) & active, axis=1).astype(i32)
-    used = jnp.concatenate([used, jnp.full((1,), zh * blk_dev, i32)])
-
     rays = ray_matrix.reshape(angles * spots, bins, tile_pix)
 
     block = (bins, chans)
@@ -355,13 +356,24 @@
 
     taps_out = shape((4 * 3 * chans, 2 * chans), bf16)
 
+    centre = pl.pallas_call(
+        centre_kernel,
+        out_shape=(slot_out, cols3_out, taps_out),
+        in_specs=[VMEM] * 2,
+        out_specs=(VMEM,) * 3,
+        scratch_shapes=[pltpu.VMEM((rows_dev, cols_dev + 16, chans), f32)],
+        compiler_params=limit(12),
+        cost_estimate=cost(1),
+        name="centre",
+    )
     inner = pl.pallas_call(
         functools.partial(inner_kernel, tile_cols=tile_cols),
-        out_shape=(pulled_out, slot_out, cols3_out, taps_out),
-        in_specs=[SMEM] * 3 + [VMEM] * 5,
-        out_specs=(VMEM,) * 4,
-        scratch_shapes=[pltpu.VMEM((rows_dev + 2, cols_dev + 16, chans), f32)],
-        compiler_params=limit(16),
+        out_shape=(pulled_out, slot_out, cols3_out),
+        in_specs=[SMEM] * 3 + [VMEM] * 6,
+        out_specs=(VMEM,) * 3,
+        scratch_shapes=[pltpu.VMEM((1, cols_dev + 16, chans), f32)],
+        input_output_aliases={7: 1, 8: 2},
+        compiler_params=limit(12),
         cost_estimate=cost(len(tiles_at(tiles, tile_cols, True))),
         name="inner",
     )
@@ -399,14 +411,27 @@
             functools.partial(finish_kernel, tile_cols=tile_cols, last=last),
             out_shape=(shape(state.shape, f32),) if last else edges,
             in_specs=[SMEM] * 3 + [VMEM] * 5,
-            out_specs=(pl.BlockSpec(memory_space=pl.ANY),) if last else (VMEM,) * 5,
+            out_specs=(ANY,) if last else (VMEM,) * 5,
             scratch_shapes=[
                 pltpu.VMEM(state.shape, f32),
                 pltpu.SemaphoreType.DMA((tiles,)),
             ],
             compiler_params=limit(20),
+            cost_estimate=cost(tiles),
             name="finish",
         )
+
+    dense_z = jnp.arange(dense, dtype=i32) // blk_dev * 2 + zl
+    dense_place = (row * nc + dense_z * nx + x) * blk_dev + jnp.arange(dense, dtype=i32) % blk_dev
+    own_first = jnp.full((1,), zh * blk_dev, i32)
+
+    def in_use(counts, dense_place, own_first):
+        number = jnp.arange(blocks, dtype=i32)
+        active = (
+            (number % blk_ang).reshape(ANGLES, blk_ang) < counts[:, None]
+        ).reshape(1, blocks)
+        used = jnp.any((block_slot[None, :] == dense_place[:, None]) & active, axis=1).astype(i32)
+        return jnp.concatenate([used, own_first])
 
     def across(value):
         value = value.reshape((peers, cap) + block)
@@ -427,10 +452,13 @@
         side_a, side_b = sides(odd, *above, col_a, col_b)
         other_weight = None
         if early:
-            side_b, weight = lax.optimization_barrier((side_b, ray_weight.astype(bf16)))
+            side_b, weight, scaled = lax.optimization_barrier(
+                (side_b, ray_weight.astype(bf16), scaled)
+            )
             other_weight = exchange(weight)
         beside = swaps(side_a, side_b, COL)
-        *parts, taps = inner(odd, mat_idx, send_slot, scaled, *above, kernel, rays)
+        outgoing, cols3, taps = centre(scaled, kernel)
+        parts = inner(odd, mat_idx, send_slot, *above, taps, rays, outgoing, cols3)
         pulled, outgoing, _ = outer(odd, mat_idx, send_slot, *beside, taps, rays, *parts)
         return pulled, outgoing, other_weight
 
@@ -439,10 +467,13 @@
         pulled, outgoing, swapped = forward(turn == 0, scaled, *rim)
         if not turn:
             other_weight = swapped
-            outgoing, table, used, other_weight = lax.optimization_barrier(
-                (outgoing, table, used, other_weight)
+            outgoing, table, other_weight, dense_place, own_first = lax.optimization_barrier(
+                (outgoing, table, other_weight, dense_place, own_first)
             )
         total, mine = combine(table, across(outgoing))
+        if not turn:
+            mine, *own = lax.optimization_barrier((mine, angle_count, dense_place, own_first))
+            used = in_use(*own)
         replies = reply(table, used, total, exchange(mine), ray_weight, other_weight)
         last = turn == ITERS - 1
         scaled, *rim = finish(last)(

time: 175 us -> 175 us (level)
    pallas_call x2 -> x4, Pallas kernels: 6.06 us -> 6.59 us  [the longest x2 4.96 us: forward(): parts = inner(odd, mat_idx, send_slot, *above, taps, rays, outgoing, cols3)]
  transfers between devices with their start and end apart: 11 -> 11, of which waited for: 3 -> 2; matrix products, arithmetic and copies ran while one was open for 1% -> 1% of each run, Pallas kernels for 6% -> 6%
where the time goes in v12:
time: 175 us
  blocking collectives  104 us (59%)
  waiting for transfers between devices  29 us (17%)
  Pallas kernels  25.5 us (15%)
  starting transfers between devices  13.7 us (8%)
    all_to_all x4, blocking collectives, across(): lax.all_to_all(value, GROUP, split_axis=0, concat_axis=0, tiled=True)  104 us
    ppermute x3, waiting for transfers between devices, exchange(): return lax.ppermute(value, 'zh', [(0, 1), (1, 0)])  29 us
    pallas_call x2, Pallas kernels, forward(): outer(odd, mat_idx, send_slot, *beside, taps, rays, *parts)  7.45 us
    ppermute x4, starting transfers between devices, swaps(): lax.ppermute(value_a, axis, even)  7.43 us
    pallas_call x2, Pallas kernels, forward(): parts = inner(odd, mat_idx, send_slot, *above, taps, rays, outgoing, cols3)  4.96 us
    pallas_call x2, Pallas kernels, on_device(): finish(last)  4.48 us
  transfers between devices with their start and end apart: 11, of which 2 were waited for; matrix products, arithmetic and copies ran while one was open for 1% of the time, Pallas kernels for 6%

profile of v12, /device:TPU:0, one launch (start us, length us, event | category | flops | bytes accessed | tf_op | source)
XLA Modules:
  0.0 175.0 jit_solution(16047569440564139882)
XLA Ops:
  0.1 2.2 %start.1 = (bf16[32,96,128]{2,1,0:T(8,128)(2,1)S(1)}, bf16[96,128]{1,0:T(8,128)(2,1)S(1)}, bf16[96,128]{1,0:T(8,128)(2,1)S(1)}, f32[32,128]{1,0:T(8,128)S(1)}, f32[32,128]{1,0:T(8,128)S(1)}) custom-call(s32[2]{0:T(128)S(1)} %pad_add_fusion.odd, bf16[32,96,128]{2,1,0:T(8,128)(2,1)} %state.5, bf16[32,96,128]{2,1,0:T(8,128)(2,1)} %grad.5), custom_call_target="tpu_custom_call" | custom-call | tf_op jit(solution)/shard_map/start/pallas_call | solution.py:465
  2.3 0.6 collective-permute-start
  2.9 0.7 collective-permute-start.1
  3.8 0.5 select_reduce_fusion
  4.5 0.5 convert_reduce_fusion
  5.5 0.6 sides.2
  6.1 0.8 collective-permute-start.3
  6.9 5.4 %collective-permute-start.2 = (f32[48,128]{1,0:T(8,128)S(1)}, f32[48,128]{1,0:T(8,128)S(1)}, u32[]{:S(2)}, u32[]{:S(2)}) collective-permute-start(f32[48,128]{1,0:T(8,128)S(1)} %get-tuple-element.55), channel_id=1, source_target_pairs={{0,1},{1,0},{2,3},{3,2},{4,5},{5,4},{6,7},{7,6},{8,9},{9,8},{10,11... | collective-permute-start | bytes 73736 | tf_op jit(solution)/shard_map/ppermute | solution.py:445
  12.2 2.6 %collective-permute-start.4 = (bf16[8,64,128]{2,1,0:T(8,128)(2,1)S(1)}, bf16[8,64,128]{2,1,0:T(8,128)(2,1)S(1)}, u32[]{:S(2)}, u32[]{:S(2)}) collective-permute-start(bf16[8,64,128]{2,1,0:T(8,128)(2,1)S(1)} %convert_element_type.10), channel_id=1, source_target_pairs={{0,4},{4,0},{1,5},{5,1},{2,6},{6,2},{3,7},{7,3},{8,12},{12,8},{9,1... | collective-permute-start | bytes 393224 | tf_op jit(solution)/shard_map/ppermute | solution.py:277
  14.8 0.8 centre.2
  15.6 2.5 %inner.2 = (f32[3,16,2,32,128]{4,3,2,1,0:T(8,128)S(1)}, bf16[96,64,128]{2,1,0:T(8,128)(2,1)S(1)}, bf16[17,2,96,384]{3,2,1,0:T(8,128)(2,1)S(1)}) custom-call(s32[2]{0:T(128)S(1)} %pad_add_fusion.odd, s32[48]{0:T(128)S(1)} %multiply_add_fusion.mat_idx, s32[48]{0:T(128)S(1)} %fusion.28.send_slot, ...), custom_call_target="tpu_custom_call", output_to_operand_aliasing={{1}: (7, {}), {2}: (8, {})} | custom-call | flops 570425344 | bytes 4194304 | tf_op jit(solution)/shard_map/inner/pallas_call | solution.py:461
  18.2 3.7 %outer.2 = (f32[3,16,2,32,128]{4,3,2,1,0:T(8,128)S(1)}, bf16[96,64,128]{2,1,0:T(8,128)(2,1)S(1)}, bf16[17,2,96,384]{3,2,1,0:T(8,128)(2,1)S(1)}) custom-call(s32[2]{0:T(128)S(1)} %pad_add_fusion.odd, s32[48]{0:T(128)S(1)} %multiply_add_fusion.mat_idx, s32[48]{0:T(128)S(1)} %fusion.28.send_slot, ...), custom_call_target="tpu_custom_call", output_to_operand_aliasing={{0}: (7, {}), {1}: (8, {}), {2}: (9, {})} | custom-call | flops 1140850688 | bytes 4194304 | tf_op jit(solution)/shard_map/outer/pallas_call | solution.py:462
  21.9 26.8 %all_to_all.20 = bf16[16,6,64,128]{3,2,1,0:T(8,128)(2,1)S(1)} all-to-all(bf16[16,6,64,128]{3,2,1,0:T(8,128)(2,1)S(1)} %bitcast.26), channel_id=1, replica_groups=mesh['row'=4,'zh'=2,'zl'=2,'x'=2] {'row','zl','x'}, dimensions={0} | all-to-all | bytes 3145728 | tf_op jit(solution)/shard_map/all_to_all | solution.py:438
  48.7 1.0 combine.2
  49.9 0.5 collective-permute-start.5
  50.7 14.2 %collective-permute-done.5.other = bf16[16,64,128]{2,1,0:T(8,128)(2,1)S(1)} collective-permute-done((bf16[16,64,128]{2,1,0:T(8,128)(2,1)S(1)}, bf16[16,64,128]{2,1,0:T(8,128)(2,1)S(1)}, u32[]{:S(2)}, u32[]{:S(2)}) %collective-permute-start.5) | collective-permute-done | bytes 262176 | tf_op jit(solution)/shard_map/ppermute | solution.py:277
  64.9 0.8 reply.2
  65.7 23.4 %all_to_all.21 = bf16[16,6,64,128]{3,2,1,0:T(8,128)(2,1)S(1)} all-to-all(bf16[16,6,64,128]{3,2,1,0:T(8,128)(2,1)S(1)} %bitcast.31), channel_id=1, replica_groups=mesh['row'=4,'zh'=2,'zl'=2,'x'=2] {'row','zl','x'}, dimensions={0} | all-to-all | bytes 3145728 | tf_op jit(solution)/shard_map/all_to_all | solution.py:438
  89.1 1.9 %finish.2 = (bf16[32,96,128]{2,1,0:T(8,128)(2,1)S(1)}, bf16[96,128]{1,0:T(8,128)(2,1)S(1)}, bf16[96,128]{1,0:T(8,128)(2,1)S(1)}, f32[32,128]{1,0:T(8,128)S(1)}, f32[32,128]{1,0:T(8,128)S(1)}) custom-call(s32[2]{0:T(128)S(1)} %pad_add_fusion.odd, s32[48]{0:T(128)S(1)} %multiply_add_fusion.mat_idx, s32[48]{0:T(128)S(1)} %fusion.28.send_slot, ...), custom_call_target="tpu_custom_call" | custom-call | flops 1711276032 | bytes 4194304 | tf_op jit(solution)/shard_map/finish/pallas_call | solution.py:479
  91.4 0.7 collective-permute-start.7
  92.0 0.8 centre.3
  92.9 0.6 sides.3
  93.4 1.1 collective-permute-start.8
  94.6 0.8 collective-permute-start.9
  95.4 2.5 %inner.3 = (f32[3,16,2,32,128]{4,3,2,1,0:T(8,128)S(1)}, bf16[96,64,128]{2,1,0:T(8,128)(2,1)S(1)}, bf16[17,2,96,384]{3,2,1,0:T(8,128)(2,1)S(1)}) custom-call(s32[2]{0:T(128)S(1)} %pad_add_fusion.odd, s32[48]{0:T(128)S(1)} %multiply_add_fusion.mat_idx, s32[48]{0:T(128)S(1)} %fusion.28.send_slot, ...), custom_call_target="tpu_custom_call", output_to_operand_aliasing={{1}: (7, {}), {2}: (8, {})} | custom-call | flops 570425344 | bytes 4194304 | tf_op jit(solution)/shard_map/inner/pallas_call | solution.py:461
  97.9 3.7 %outer.3 = (f32[3,16,2,32,128]{4,3,2,1,0:T(8,128)S(1)}, bf16[96,64,128]{2,1,0:T(8,128)(2,1)S(1)}, bf16[17,2,96,384]{3,2,1,0:T(8,128)(2,1)S(1)}) custom-call(s32[2]{0:T(128)S(1)} %pad_add_fusion.odd, s32[48]{0:T(128)S(1)} %multiply_add_fusion.mat_idx, s32[48]{0:T(128)S(1)} %fusion.28.send_slot, ...), custom_call_target="tpu_custom_call", output_to_operand_aliasing={{0}: (7, {}), {1}: (8, {}), {2}: (9, {})} | custom-call | flops 1140850688 | bytes 4194304 | tf_op jit(solution)/shard_map/outer/pallas_call | solution.py:462
  101.6 30.6 %all_to_all.22 = bf16[16,6,64,128]{3,2,1,0:T(8,128)(2,1)S(1)} all-to-all(bf16[16,6,64,128]{3,2,1,0:T(8,128)(2,1)S(1)} %bitcast.25), channel_id=1, replica_groups=mesh['row'=4,'zh'=2,'zl'=2,'x'=2] {'row','zl','x'}, dimensions={0} | all-to-all | bytes 3145728 | tf_op jit(solution)/shard_map/all_to_all | solution.py:438
  132.2 1.0 combine.3
  133.5 14.8 %collective-permute-done.10.other = bf16[16,64,128]{2,1,0:T(8,128)(2,1)S(1)} collective-permute-done((bf16[16,64,128]{2,1,0:T(8,128)(2,1)S(1)}, bf16[16,64,128]{2,1,0:T(8,128)(2,1)S(1)}, u32[]{:S(2)}, u32[]{:S(2)}) %collective-permute-start.10) | collective-permute-done | bytes 262176 | tf_op jit(solution)/shard_map/ppermute | solution.py:277
  148.3 0.8 reply.3
  149.1 23.2 %all_to_all.23 = bf16[16,6,64,128]{3,2,1,0:T(8,128)(2,1)S(1)} all-to-all(bf16[16,6,64,128]{3,2,1,0:T(8,128)(2,1)S(1)} %bitcast.28), channel_id=1, replica_groups=mesh['row'=4,'zh'=2,'zl'=2,'x'=2] {'row','zl','x'}, dimensions={0} | all-to-all | bytes 3145728 | tf_op jit(solution)/shard_map/all_to_all | solution.py:438
  172.3 2.6 %finish.3 = f32[32,96,128]{2,1,0:T(8,128)} custom-call(s32[2]{0:T(128)S(1)} %pad_add_fusion.odd, s32[48]{0:T(128)S(1)} %multiply_add_fusion.mat_idx, s32[48]{0:T(128)S(1)} %fusion.28.send_slot, bf16[96,64,128]{2,1,0:T(8,128)(2,1)S(1)} %bitcast.32, f32[3,16,2,32,128]{4,3,2,1,0:T(8,128)S(1)} %get-tuple-element.96.pulled, bf16[32,96,128]{2,1,0:T(8,128)(2,1)S(1)} %copy-done.3, ...), custom_call_target="tpu_custom_call" | custom-call | flops 1711276032 | bytes 4194304 | tf_op jit(solution)/shard_map/finish/pallas_call | solution.py:479
  (54 shorter events, 1.9 us)
Async XLA Ops:
  0.0 3.6 %copy-start.6 = (s32[4,24,16]{1,2,0:T(8,128)S(1)}, s32[4,24,16]{1,2,0:T(8,128)}, u32[]{:S(2)}) copy-start(s32[4,24,16]{1,2,0:T(8,128)} %param.14) | copy-start | bytes 18436
  0.0 3.8 %copy-start.7 = (s32[256]{0:T(256)S(1)}, s32[256]{0:T(256)}, u32[]{:S(2)}) copy-start(s32[256]{0:T(256)} %param.16) | copy-start | bytes 3076
  0.0 4.4 %copy-start.8 = (s32[1,3,16]{2,0,1:T(1,128)S(1)}, s32[1,3,16]{2,0,1:T(1,128)}, u32[]{:S(2)}) copy-start(s32[1,3,16]{2,0,1:T(1,128)} %param.15) | copy-start | bytes 580
  0.0 5.4 %copy-start.4 = (f32[8,64,128]{2,1,0:T(8,128)S(1)}, f32[8,64,128]{2,1,0:T(8,128)}, u32[]{:S(2)}) copy-start(f32[8,64,128]{2,1,0:T(8,128)} %own_weight.3) | copy-start | bytes 786436
  2.3 3.1 %collective-permute-start = (bf16[96,128]{1,0:T(8,128)(2,1)S(1)}, bf16[96,128]{1,0:T(8,128)(2,1)S(1)}, u32[]{:S(2)}, u32[]{:S(2)}) collective-permute-start(bf16[96,128]{1,0:T(8,128)(2,1)S(1)} %get-tuple-element.51), channel_id=1, source_target_pairs={{0,8},{8,0},{16,24},{24,16},{1,9},{9,1},{17,25},{25,17},{2,10},{10... | collective-permute-start | bytes 73736 | tf_op jit(solution)/shard_map/ppermute | solution.py:445
  2.9 2.6 %collective-permute-start.1 = (bf16[96,128]{1,0:T(8,128)(2,1)S(1)}, bf16[96,128]{1,0:T(8,128)(2,1)S(1)}, u32[]{:S(2)}, u32[]{:S(2)}) collective-permute-start(bf16[96,128]{1,0:T(8,128)(2,1)S(1)} %get-tuple-element.52), channel_id=1, source_target_pairs={{8,16},{16,8},{9,17},{17,9},{10,18},{18,10},{11,19},{19,11},{12,20... | collective-permute-start | bytes 73736 | tf_op jit(solution)/shard_map/ppermute | solution.py:445
  5.5 9.3 %copy-start.5 = (bf16[3,3,128,128]{3,2,1,0:T(8,128)(2,1)S(1)}, bf16[3,3,128,128]{3,2,1,0:T(8,128)(2,1)}, u32[]{:S(2)}) copy-start(bf16[3,3,128,128]{3,2,1,0:T(8,128)(2,1)} %kernel.3) | copy-start | bytes 884740
  5.5 10.1 %copy-start = (bf16[8,4,64,1024]{3,2,1,0:T(8,128)(2,1)S(1)}, bf16[8,4,64,1024]{3,2,1,0:T(8,128)(2,1)}, u32[]{:S(2)}) copy-start(bf16[8,4,64,1024]{3,2,1,0:T(8,128)(2,1)} %param.12) | copy-start | bytes 12582916
  6.1 12.1 %collective-permute-start.3 = (f32[48,128]{1,0:T(8,128)S(1)}, f32[48,128]{1,0:T(8,128)S(1)}, u32[]{:S(2)}, u32[]{:S(2)}) collective-permute-start(f32[48,128]{1,0:T(8,128)S(1)} %get-tuple-element.58), channel_id=1, source_target_pairs={{1,2},{2,1},{3,4},{4,3},{5,6},{6,5},{9,10},{10,9},{11,12},{12,11},... | collective-permute-start | bytes 73736 | tf_op jit(solution)/shard_map/ppermute | solution.py:445
  6.9 11.3 %collective-permute-start.2 = (f32[48,128]{1,0:T(8,128)S(1)}, f32[48,128]{1,0:T(8,128)S(1)}, u32[]{:S(2)}, u32[]{:S(2)}) collective-permute-start(f32[48,128]{1,0:T(8,128)S(1)} %get-tuple-element.55), channel_id=1, source_target_pairs={{0,1},{1,0},{2,3},{3,2},{4,5},{5,4},{6,7},{7,6},{8,9},{9,8},{10,11... | collective-permute-start | bytes 73736 | tf_op jit(solution)/shard_map/ppermute | solution.py:445
  12.2 9.7 %collective-permute-start.4 = (bf16[8,64,128]{2,1,0:T(8,128)(2,1)S(1)}, bf16[8,64,128]{2,1,0:T(8,128)(2,1)S(1)}, u32[]{:S(2)}, u32[]{:S(2)}) collective-permute-start(bf16[8,64,128]{2,1,0:T(8,128)(2,1)S(1)} %convert_element_type.10), channel_id=1, source_target_pairs={{0,4},{4,0},{1,5},{5,1},{2,6},{6,2},{3,7},{7,3},{8,12},{12,8},{9,1... | collective-permute-start | bytes 393224 | tf_op jit(solution)/shard_map/ppermute | solution.py:277
  48.7 1.0 copy-start.9
  49.9 15.0 %collective-permute-start.5 = (bf16[16,64,128]{2,1,0:T(8,128)(2,1)S(1)}, bf16[16,64,128]{2,1,0:T(8,128)(2,1)S(1)}, u32[]{:S(2)}, u32[]{:S(2)}) collective-permute-start(bf16[16,64,128]{2,1,0:T(8,128)(2,1)S(1)} %get-tuple-element.77), channel_id=1, source_target_pairs={{0,4},{4,0},{1,5},{5,1},{2,6},{6,2},{3,7},{7,3},{8,12},{12,8},{9,1... | collective-permute-start | bytes 786440 | tf_op jit(solution)/shard_map/ppermute | solution.py:277
  64.9 24.3 %copy-start.1 = (bf16[8,4,64,1024]{3,2,1,0:T(8,128)(2,1)S(1)}, bf16[8,4,64,1024]{3,2,1,0:T(8,128)(2,1)}, u32[]{:S(2)}) copy-start(bf16[8,4,64,1024]{3,2,1,0:T(8,128)(2,1)} %param.12) | copy-start | bytes 12582916
  65.7 23.5 %copy-start.2 = (bf16[32,96,128]{2,1,0:T(8,128)(2,1)S(1)}, bf16[32,96,128]{2,1,0:T(8,128)(2,1)}, u32[]{:S(2)}) copy-start(bf16[32,96,128]{2,1,0:T(8,128)(2,1)} %state.5) | copy-start | bytes 2359300
  65.7 23.5 %copy-start.3 = (bf16[32,96,128]{2,1,0:T(8,128)(2,1)S(1)}, bf16[32,96,128]{2,1,0:T(8,128)(2,1)}, u32[]{:S(2)}) copy-start(bf16[32,96,128]{2,1,0:T(8,128)(2,1)} %grad.5) | copy-start | bytes 2359300
  91.0 1.8 %collective-permute-start.6 = (bf16[96,128]{1,0:T(8,128)(2,1)S(1)}, bf16[96,128]{1,0:T(8,128)(2,1)S(1)}, u32[]{:S(2)}, u32[]{:S(2)}) collective-permute-start(bf16[96,128]{1,0:T(8,128)(2,1)S(1)} %get-tuple-element.80), channel_id=1, source_target_pairs={{0,8},{8,0},{16,24},{24,16},{1,9},{9,1},{17,25},{25,17},{2,10},{10... | collective-permute-start | bytes 73736 | tf_op jit(solution)/shard_map/ppermute | solution.py:445
  91.4 1.5 collective-permute-start.7
  93.4 4.5 %collective-permute-start.8 = (f32[48,128]{1,0:T(8,128)S(1)}, f32[48,128]{1,0:T(8,128)S(1)}, u32[]{:S(2)}, u32[]{:S(2)}) collective-permute-start(f32[48,128]{1,0:T(8,128)S(1)} %get-tuple-element.84), channel_id=1, source_target_pairs={{0,1},{1,0},{2,3},{3,2},{4,5},{5,4},{6,7},{7,6},{8,9},{9,8},{10,11... | collective-permute-start | bytes 73736 | tf_op jit(solution)/shard_map/ppermute | solution.py:445
  94.6 3.3 %collective-permute-start.9 = (f32[48,128]{1,0:T(8,128)S(1)}, f32[48,128]{1,0:T(8,128)S(1)}, u32[]{:S(2)}, u32[]{:S(2)}) collective-permute-start(f32[48,128]{1,0:T(8,128)S(1)} %get-tuple-element.85), channel_id=1, source_target_pairs={{1,2},{2,1},{3,4},{4,3},{5,6},{6,5},{9,10},{10,9},{11,12},{12,11},... | collective-permute-start | bytes 73736 | tf_op jit(solution)/shard_map/ppermute | solution.py:445
  133.3 15.0 %collective-permute-start.10 = (bf16[16,64,128]{2,1,0:T(8,128)(2,1)S(1)}, bf16[16,64,128]{2,1,0:T(8,128)(2,1)S(1)}, u32[]{:S(2)}, u32[]{:S(2)}) collective-permute-start(bf16[16,64,128]{2,1,0:T(8,128)(2,1)S(1)} %get-tuple-element.95), channel_id=1, source_target_pairs={{0,4},{4,0},{1,5},{5,1},{2,6},{6,2},{3,7},{7,3},{8,12},{12,8},{9,1... | collective-permute-start | bytes 786440 | tf_op jit(solution)/shard_map/ppermute | solution.py:277

commit v13 on v10

--- a/solution.py
+++ b/solution.py
@@ -23,7 +23,7 @@
 ANY = pl.BlockSpec(memory_space=pl.ANY)
 
 
-def start_kernel(odd, state, grad, scaled, row_a, row_b, col_a, col_b, states, grads, whole, mark):
+def start_kernel(state, grad, scaled, row_a, row_b, col_a, col_b, states, grads, whole, mark):
     parts = mark.shape[1]
     rows = states.shape[0] // parts
 
@@ -41,24 +41,30 @@
         where = slice(p * rows, (p + 1) * rows)
         value = states[where].astype(jnp.float32)
         whole[where] = (1.0 - value * value) * grads[where].astype(jnp.float32)
-    emit_edges(whole[...], odd, scaled, row_a, row_b, col_a, col_b)
-
-
-def pick(flag, yes, no):
-    return jnp.where(flag == 1, yes, no)
-
-
-def emit_edges(value, odd, scaled, row_a, row_b, col_a, col_b):
+    emit_edges(whole[...], scaled, row_a, row_b, col_a, col_b)
+
+
+def parity(dim):
+    if dim == 0:
+        return lax.axis_index("row") % 2
+    return (lax.axis_index("zl") * lax.axis_size("x") + lax.axis_index("x")) % 2
+
+
+def pick(dim, yes, no):
+    return jnp.where(parity(dim) == 1, yes, no)
+
+
+def emit_edges(value, scaled, row_a, row_b, col_a, col_b):
     rows, cols = value.shape[:2]
     scaled[...] = value.astype(jnp.bfloat16)
-    row_a[...] = pick(odd[0], value[0], value[rows - 1]).astype(jnp.bfloat16)
-    row_b[...] = pick(odd[0], value[rows - 1], value[0]).astype(jnp.bfloat16)
+    row_a[...] = pick(0, value[0], value[rows - 1]).astype(jnp.bfloat16)
+    row_b[...] = pick(0, value[rows - 1], value[0]).astype(jnp.bfloat16)
     left, right = value[:, 0, :], value[:, cols - 1, :]
-    col_a[...] = pick(odd[1], left, right)
-    col_b[...] = pick(odd[1], right, left)
-
-
-def sides_kernel(odd, near_a, near_b, col_a, col_b, out_a, out_b):
+    col_a[...] = pick(1, left, right)
+    col_b[...] = pick(1, right, left)
+
+
+def sides_kernel(near_a, near_b, col_a, col_b, out_a, out_b):
     rows = col_a.shape[0]
     cols = near_a.shape[0]
     f32 = jnp.float32
@@ -69,22 +75,23 @@
         return low, high
 
     a, b = ends(near_a), ends(near_b)
-    above = [pick(odd[0], a[i], b[i]) for i in range(2)]
-    below = [pick(odd[0], b[i], a[i]) for i in range(2)]
+    above = [pick(0, a[i], b[i]) for i in range(2)]
+    below = [pick(0, b[i], a[i]) for i in range(2)]
     for out, edge, order in ((out_a, col_a, (0, 1)), (out_b, col_b, (1, 0))):
         yes, no = order
         out[8 : 8 + rows, :] = edge[...]
-        out[7:8, :] = pick(odd[1], above[yes], above[no])
-        out[8 + rows : 9 + rows, :] = pick(odd[1], below[yes], below[no])
-
-
-def matrices_of(mat_idx, rays, t):
-    return jnp.concatenate([rays[mat_idx[t * HITS + k]] for k in range(HITS)], axis=0)
-
-
-def forward_tile(mat_idx, send_slot, taps, rays, pulled, out, cols3, t, tile_cols):
+        out[7:8, :] = pick(1, above[yes], above[no])
+        out[8 + rows : 9 + rows, :] = pick(1, below[yes], below[no])
+
+
+def matrices_of(routes, rays, t):
+    return jnp.concatenate([rays[routes[t * HITS + k]] for k in range(HITS)], axis=0)
+
+
+def forward_tile(routes, taps, rays, pulled, out, cols3, t, tile_cols):
     chans = pulled.shape[-1]
     bins = rays.shape[1]
+    slot = pulled.shape[0] * HITS
     half = PIX // 2
     r0, c0 = t // tile_cols * half, t % tile_cols * PIX
     window = jnp.concatenate(
@@ -102,10 +109,10 @@
         pulled[t, :, odd] = value
     low = pulled[t].reshape(PIX * PIX, chans).astype(jnp.bfloat16)
     value = jnp.dot(
-        matrices_of(mat_idx, rays, t), low, preferred_element_type=jnp.float32
+        matrices_of(routes, rays, t), low, preferred_element_type=jnp.float32
     ).astype(jnp.bfloat16)
     for k in range(HITS):
-        out[send_slot[t * HITS + k]] = value[k * bins : (k + 1) * bins, :]
+        out[routes[slot + t * HITS + k]] = value[k * bins : (k + 1) * bins, :]
 
 
 def tiles_at(tiles, tile_cols, inner):
@@ -113,7 +120,7 @@
 
 
 def inner_kernel(
-    odd, mat_idx, send_slot, scaled, near_a, near_b, kernel, rays,
+    routes, scaled, near_a, near_b, kernel, rays,
     pulled, out, cols3, taps, wide, *, tile_cols,
 ):
     rows, cols, chans = scaled.shape
@@ -130,8 +137,8 @@
             for dc in range(3):
                 taps[base + dc * chans : base + (dc + 1) * chans, lanes] = kernel[2 - tap, 2 - dc].T
     a, b = near_a[...].astype(f32), near_b[...].astype(f32)
-    wide[0, 8 : 8 + cols, :] = pick(odd[0], a, b)
-    wide[rows + 1, 8 : 8 + cols, :] = pick(odd[0], b, a)
+    wide[0, 8 : 8 + cols, :] = pick(0, a, b)
+    wide[rows + 1, 8 : 8 + cols, :] = pick(0, b, a)
     wide[1 : rows + 1, 8 : 8 + cols, :] = scaled[...].astype(f32)
     wide[:, 0:8, :] = jnp.zeros((rows + 2, 8, chans), f32)
     wide[:, 8 + cols :, :] = jnp.zeros((rows + 2, 8, chans), f32)
@@ -142,11 +149,11 @@
         )
     out[...] = jnp.zeros_like(out)
     for t in tiles_at(pulled.shape[0], tile_cols, True):
-        forward_tile(mat_idx, send_slot, taps, rays, pulled, out, cols3, t, tile_cols)
+        forward_tile(routes, taps, rays, pulled, out, cols3, t, tile_cols)
 
 
 def outer_kernel(
-    odd, mat_idx, send_slot, near_a, near_b, taps, rays, _pulled, _out, _cols3,
+    routes, near_a, near_b, taps, rays, _pulled, _out, _cols3,
     pulled, out, cols3, *, tile_cols,
 ):
     cols = cols3.shape[2]
@@ -154,7 +161,7 @@
     group = 16
     spot = lax.broadcasted_iota(jnp.int32, (group, chans), 0)
     a, b = near_a[...], near_b[...]
-    left, right = pick(odd[1], a, b), pick(odd[1], b, a)
+    left, right = pick(1, a, b), pick(1, b, a)
     for edge, dc, first, at in ((left, 0, 0, 0), (right, 2, cols - group, group - 1)):
         lanes = slice(dc * chans, (dc + 1) * chans)
         for r in range(2 * cols3.shape[0]):
@@ -162,7 +169,7 @@
             value = jnp.where(spot == at, edge[7 + r : 8 + r, :], cols3[there].astype(jnp.float32))
             cols3[there] = value.astype(jnp.bfloat16)
     for t in tiles_at(pulled.shape[0], tile_cols, False):
-        forward_tile(mat_idx, send_slot, taps, rays, pulled, out, cols3, t, tile_cols)
+        forward_tile(routes, taps, rays, pulled, out, cols3, t, tile_cols)
 
 
 def combine_kernel(table, recv, total, low, acc_a, acc_b):
@@ -202,10 +209,11 @@
 
 
 def finish_kernel(
-    odd, mat_idx, send_slot, returned, pulled, grad, state, rays, *refs, tile_cols, last,
+    routes, returned, pulled, grad, state, rays, *refs, tile_cols, last,
 ):
     outs, (whole, mark) = refs[:-2], refs[-2:]
     tiles = pulled.shape[0]
+    slot = tiles * HITS
     chans = grad.shape[2]
     f32 = jnp.float32
 
@@ -218,10 +226,10 @@
         return pltpu.make_async_copy(whole.at[where], outs[0].at[where], mark.at[t])
 
     for t in range(tiles):
-        picked = jnp.concatenate([returned[send_slot[t * HITS + k]] for k in range(HITS)], axis=0)
+        picked = jnp.concatenate([returned[routes[slot + t * HITS + k]] for k in range(HITS)], axis=0)
         backed = lax.dot_general(
             picked,
-            matrices_of(mat_idx, rays, t),
+            matrices_of(routes, rays, t),
             (((0,), (0,)), ((), ())),
             preferred_element_type=f32,
         ).T
@@ -238,7 +246,7 @@
         for t in range(tiles):
             leave(t).wait()
     else:
-        emit_edges(whole[...], odd, *outs)
+        emit_edges(whole[...], *outs)
 
 
 def on_device(state, grad, kernel, ray_matrix, ray_weight, hits, offsets, block_slot, angle_count):
@@ -292,6 +300,7 @@
     table = dense + jnp.sum(jnp.where(matched, place[:, None, :] - dense, 0), axis=2)
     table = table.reshape(slots)
     mat_idx = (my_hits // blk_ang) * spots + offsets.reshape(pairs)
+    routes = jnp.concatenate([mat_idx, send_slot])
 
     dense_z = jnp.arange(dense, dtype=i32) // blk_dev * 2 + zl
     dense_place = (row * nc + dense_z * nx + x) * blk_dev + jnp.arange(dense, dtype=i32) % blk_dev
@@ -314,7 +323,6 @@
         shape((rows_dev, chans), f32),
         shape((rows_dev, chans), f32),
     )
-    odd = jnp.stack([row % 2, (zh * (RING // 2) * nx + zl * nx + x) % 2])
 
     def limit(mib):
         return pltpu.CompilerParams(vmem_limit_bytes=mib << 20)
@@ -322,7 +330,7 @@
     start = pl.pallas_call(
         start_kernel,
         out_shape=edges,
-        in_specs=[SMEM] + [ANY] * 2,
+        in_specs=[ANY] * 2,
         out_specs=(VMEM,) * 5,
         scratch_shapes=[
             pltpu.VMEM(state.shape, bf16),
@@ -336,7 +344,7 @@
     sides = pl.pallas_call(
         sides_kernel,
         out_shape=[shape((rows_dev + 16, chans), f32)] * 2,
-        in_specs=[SMEM] + [VMEM] * 4,
+        in_specs=[VMEM] * 4,
         out_specs=[VMEM] * 2,
         compiler_params=limit(4),
         cost_estimate=pl.CostEstimate(
@@ -358,7 +366,7 @@
     inner = pl.pallas_call(
         functools.partial(inner_kernel, tile_cols=tile_cols),
         out_shape=(pulled_out, slot_out, cols3_out, taps_out),
-        in_specs=[SMEM] * 3 + [VMEM] * 5,
+        in_specs=[SMEM] + [VMEM] * 5,
         out_specs=(VMEM,) * 4,
         scratch_shapes=[pltpu.VMEM((rows_dev + 2, cols_dev + 16, chans), f32)],
         compiler_params=limit(16),
@@ -368,9 +376,9 @@
     outer = pl.pallas_call(
         functools.partial(outer_kernel, tile_cols=tile_cols),
         out_shape=(pulled_out, slot_out, cols3_out),
-        in_specs=[SMEM] * 3 + [VMEM] * 7,
+        in_specs=[SMEM] + [VMEM] * 7,
         out_specs=(VMEM,) * 3,
-        input_output_aliases={7: 0, 8: 1, 9: 2},
+        input_output_aliases={5: 0, 6: 1, 7: 2},
         compiler_params=limit(16),
         cost_estimate=cost(len(tiles_at(tiles, tile_cols, False))),
         name="outer",
@@ -398,7 +406,7 @@
         return pl.pallas_call(
             functools.partial(finish_kernel, tile_cols=tile_cols, last=last),
             out_shape=(shape(state.shape, f32),) if last else edges,
-            in_specs=[SMEM] * 3 + [VMEM] * 5,
+            in_specs=[SMEM] + [VMEM] * 5,
             out_specs=(pl.BlockSpec(memory_space=pl.ANY),) if last else (VMEM,) * 5,
             scratch_shapes=[
                 pltpu.VMEM(state.shape, f32),
@@ -424,17 +432,17 @@
 
     def forward(early, scaled, row_a, row_b, col_a, col_b):
         above = swaps(row_a, row_b, "row")
-        side_a, side_b = sides(odd, *above, col_a, col_b)
+        side_a, side_b = sides(*above, col_a, col_b)
         other_weight = None
         if early:
             side_b, weight = lax.optimization_barrier((side_b, ray_weight.astype(bf16)))
             other_weight = exchange(weight)
         beside = swaps(side_a, side_b, COL)
-        *parts, taps = inner(odd, mat_idx, send_slot, scaled, *above, kernel, rays)
-        pulled, outgoing, _ = outer(odd, mat_idx, send_slot, *beside, taps, rays, *parts)
+        *parts, taps = inner(routes, scaled, *above, kernel, rays)
+        pulled, outgoing, _ = outer(routes, *beside, taps, rays, *parts)
         return pulled, outgoing, other_weight
 
-    scaled, *rim = start(odd, apart(state), apart(grad))
+    scaled, *rim = start(apart(state), apart(grad))
     for turn in range(ITERS):
         pulled, outgoing, swapped = forward(turn == 0, scaled, *rim)
         if not turn:
@@ -446,7 +454,7 @@
         replies = reply(table, used, total, exchange(mine), ray_weight, other_weight)
         last = turn == ITERS - 1
         scaled, *rim = finish(last)(
-            odd, mat_idx, send_slot, across(replies), pulled, grad, state, rays
+            routes, across(replies), pulled, grad, state, rays
         )
     return scaled
 

time: 175 us -> 173 us (0.989)
  no operation moved by 1% of the time
where the time goes in v13:
time: 173 us
  blocking collectives  103 us (60%)
  waiting for transfers between devices  29.3 us (17%)
  Pallas kernels  23.3 us (13%)
  starting transfers between devices  14.1 us (8%)
    all_to_all x4, blocking collectives, across(): lax.all_to_all(value, GROUP, split_axis=0, concat_axis=0, tiled=True)  103 us
    ppermute x3, waiting for transfers between devices, exchange(): return lax.ppermute(value, 'zh', [(0, 1), (1, 0)])  29 us
    ppermute x4, starting transfers between devices, swaps(): lax.ppermute(value_a, axis, even)  7.73 us
    pallas_call x2, Pallas kernels, forward(): pulled, outgoing, _ = outer(routes, *beside, taps, rays, *parts)  7.42 us
    pallas_call x2, Pallas kernels, forward(): *parts, taps = inner(routes, scaled, *above, kernel, rays)  6.03 us
    pallas_call x2, Pallas kernels, on_device(): finish(last)(routes, across(replies), pulled, grad, state, rays)  4.46 us
    ppermute x3, starting transfers between devices, exchange(): return lax.ppermute(value, 'zh', [(0, 1), (1, 0)])  3.62 us
  transfers between devices with their start and end apart: 11, of which 3 were waited for; matrix products, arithmetic and copies ran while one was open for 1% of the time, Pallas kernels for 6%

profile of v13, /device:TPU:0, one launch (start us, length us, event | category | flops | bytes accessed | tf_op | source)
XLA Modules:
  0.0 172.6 jit_solution(14036938986588142951)
XLA Ops:
  0.0 1.7 %start.1 = (bf16[32,96,128]{2,1,0:T(8,128)(2,1)S(1)}, bf16[96,128]{1,0:T(8,128)(2,1)S(1)}, bf16[96,128]{1,0:T(8,128)(2,1)S(1)}, f32[32,128]{1,0:T(8,128)S(1)}, f32[32,128]{1,0:T(8,128)S(1)}) custom-call(bf16[32,96,128]{2,1,0:T(8,128)(2,1)} %state.5, bf16[32,96,128]{2,1,0:T(8,128)(2,1)} %grad.5), custom_call_target="tpu_custom_call" | custom-call | tf_op jit(solution)/shard_map/start/pallas_call | solution.py:445
  1.8 0.6 collective-permute-start
  2.3 0.7 collective-permute-start.1
  3.2 0.5 select_reduce_fusion
  4.1 0.2 and_reduce_fusion
  4.3 0.5 convert_reduce_fusion
  5.5 0.8 collective-permute-start.3
  6.3 5.5 %collective-permute-start.2 = (f32[48,128]{1,0:T(8,128)S(1)}, f32[48,128]{1,0:T(8,128)S(1)}, u32[]{:S(2)}, u32[]{:S(2)}) collective-permute-start(f32[48,128]{1,0:T(8,128)S(1)} %get-tuple-element.45), channel_id=1, source_target_pairs={{0,1},{1,0},{2,3},{3,2},{4,5},{5,4},{6,7},{7,6},{8,9},{9,8},{10,11... | collective-permute-start | bytes 73736 | tf_op jit(solution)/shard_map/ppermute | solution.py:428
  11.8 2.6 %collective-permute-start.4 = (bf16[8,64,128]{2,1,0:T(8,128)(2,1)S(1)}, bf16[8,64,128]{2,1,0:T(8,128)(2,1)S(1)}, u32[]{:S(2)}, u32[]{:S(2)}) collective-permute-start(bf16[8,64,128]{2,1,0:T(8,128)(2,1)S(1)} %convert_element_type.10), channel_id=1, source_target_pairs={{0,4},{4,0},{1,5},{5,1},{2,6},{6,2},{3,7},{7,3},{8,12},{12,8},{9,1... | collective-permute-start | bytes 393224 | tf_op jit(solution)/shard_map/ppermute | solution.py:275
  14.4 3.0 %inner.2 = (f32[3,16,2,32,128]{4,3,2,1,0:T(8,128)S(1)}, bf16[96,64,128]{2,1,0:T(8,128)(2,1)S(1)}, bf16[17,2,96,384]{3,2,1,0:T(8,128)(2,1)S(1)}, bf16[1536,256]{1,0:T(8,128)(2,1)S(1)}) custom-call(s32[96]{0:T(128)S(1)} %pad_add_fusion.routes, bf16[32,96,128]{2,1,0:T(8,128)(2,1)S(1)} %get-tuple-element.48.scaled, ...), custom_call_target="tpu_custom_call" | custom-call | flops 570425344 | bytes 4194304 | tf_op jit(solution)/shard_map/inner/pallas_call | solution.py:441
  17.4 3.7 %outer.2 = (f32[3,16,2,32,128]{4,3,2,1,0:T(8,128)S(1)}, bf16[96,64,128]{2,1,0:T(8,128)(2,1)S(1)}, bf16[17,2,96,384]{3,2,1,0:T(8,128)(2,1)S(1)}) custom-call(s32[96]{0:T(128)S(1)} %pad_add_fusion.routes, f32[48,128]{1,0:T(8,128)S(1)} %collective-permute-done.2.near_a, ...), custom_call_target="tpu_custom_call", output_to_operand_aliasing={{0}: (5, {}), {1}: (6, {}), {2}: (7, {})} | custom-call | flops 1140850688 | bytes 4194304 | tf_op jit(solution)/shard_map/outer/pallas_call | solution.py:442
  21.1 26.1 %all_to_all.20 = bf16[16,6,64,128]{3,2,1,0:T(8,128)(2,1)S(1)} all-to-all(bf16[16,6,64,128]{3,2,1,0:T(8,128)(2,1)S(1)} %bitcast.28), channel_id=1, replica_groups=mesh['row'=4,'zh'=2,'zl'=2,'x'=2] {'row','zl','x'}, dimensions={0} | all-to-all | bytes 3145728 | tf_op jit(solution)/shard_map/all_to_all | solution.py:421
  47.2 1.0 combine.2
  48.3 0.6 collective-permute-start.5
  48.9 14.4 %collective-permute-done.5.other = bf16[16,64,128]{2,1,0:T(8,128)(2,1)S(1)} collective-permute-done((bf16[16,64,128]{2,1,0:T(8,128)(2,1)S(1)}, bf16[16,64,128]{2,1,0:T(8,128)(2,1)S(1)}, u32[]{:S(2)}, u32[]{:S(2)}) %collective-permute-start.5) | collective-permute-done | bytes 262176 | tf_op jit(solution)/shard_map/ppermute | solution.py:275
  63.3 0.8 reply.2
  64.2 23.3 %all_to_all.21 = bf16[16,6,64,128]{3,2,1,0:T(8,128)(2,1)S(1)} all-to-all(bf16[16,6,64,128]{3,2,1,0:T(8,128)(2,1)S(1)} %bitcast.27), channel_id=1, replica_groups=mesh['row'=4,'zh'=2,'zl'=2,'x'=2] {'row','zl','x'}, dimensions={0} | all-to-all | bytes 3145728 | tf_op jit(solution)/shard_map/all_to_all | solution.py:421
  87.5 1.9 %finish.2 = (bf16[32,96,128]{2,1,0:T(8,128)(2,1)S(1)}, bf16[96,128]{1,0:T(8,128)(2,1)S(1)}, bf16[96,128]{1,0:T(8,128)(2,1)S(1)}, f32[32,128]{1,0:T(8,128)S(1)}, f32[32,128]{1,0:T(8,128)S(1)}) custom-call(s32[96]{0:T(128)S(1)} %pad_add_fusion.routes, bf16[96,64,128]{2,1,0:T(8,128)(2,1)S(1)} %bitcast.23, f32[3,16,2,32,128]{4,3,2,1,0:T(8,128)S(1)} %get-tuple-element.61.pulled, ...), custom_call_target="tpu_custom_call" | custom-call | tf_op jit(solution)/shard_map/finish/pallas_call | solution.py:456
  89.3 0.3 collective-permute-start.6
  89.7 0.7 collective-permute-start.7
  90.3 0.3 collective-permute-done.6.near_a
  90.6 1.4 collective-permute-start.8
  92.0 0.7 collective-permute-start.9
  92.7 3.0 %inner.3 = (f32[3,16,2,32,128]{4,3,2,1,0:T(8,128)S(1)}, bf16[96,64,128]{2,1,0:T(8,128)(2,1)S(1)}, bf16[17,2,96,384]{3,2,1,0:T(8,128)(2,1)S(1)}, bf16[1536,256]{1,0:T(8,128)(2,1)S(1)}) custom-call(s32[96]{0:T(128)S(1)} %pad_add_fusion.routes, bf16[32,96,128]{2,1,0:T(8,128)(2,1)S(1)} %get-tuple-element.68.scaled, ...), custom_call_target="tpu_custom_call" | custom-call | flops 570425344 | bytes 4194304 | tf_op jit(solution)/shard_map/inner/pallas_call | solution.py:441
  95.7 3.7 %outer.3 = (f32[3,16,2,32,128]{4,3,2,1,0:T(8,128)S(1)}, bf16[96,64,128]{2,1,0:T(8,128)(2,1)S(1)}, bf16[17,2,96,384]{3,2,1,0:T(8,128)(2,1)S(1)}) custom-call(s32[96]{0:T(128)S(1)} %pad_add_fusion.routes, f32[48,128]{1,0:T(8,128)S(1)} %collective-permute-done.8.near_a, ...), custom_call_target="tpu_custom_call", output_to_operand_aliasing={{0}: (5, {}), {1}: (6, {}), {2}: (7, {})} | custom-call | flops 1140850688 | bytes 4194304 | tf_op jit(solution)/shard_map/outer/pallas_call | solution.py:442
  99.4 30.6 %all_to_all.22 = bf16[16,6,64,128]{3,2,1,0:T(8,128)(2,1)S(1)} all-to-all(bf16[16,6,64,128]{3,2,1,0:T(8,128)(2,1)S(1)} %bitcast.29), channel_id=1, replica_groups=mesh['row'=4,'zh'=2,'zl'=2,'x'=2] {'row','zl','x'}, dimensions={0} | all-to-all | bytes 3145728 | tf_op jit(solution)/shard_map/all_to_all | solution.py:421
  130.0 1.0 combine.3
  131.0 0.4 collective-permute-start.10
  131.5 14.6 %collective-permute-done.10.other = bf16[16,64,128]{2,1,0:T(8,128)(2,1)S(1)} collective-permute-done((bf16[16,64,128]{2,1,0:T(8,128)(2,1)S(1)}, bf16[16,64,128]{2,1,0:T(8,128)(2,1)S(1)}, u32[]{:S(2)}, u32[]{:S(2)}) %collective-permute-start.10) | collective-permute-done | bytes 262176 | tf_op jit(solution)/shard_map/ppermute | solution.py:275
  146.1 0.8 reply.3
  146.9 23.2 %all_to_all.23 = bf16[16,6,64,128]{3,2,1,0:T(8,128)(2,1)S(1)} all-to-all(bf16[16,6,64,128]{3,2,1,0:T(8,128)(2,1)S(1)} %bitcast.24), channel_id=1, replica_groups=mesh['row'=4,'zh'=2,'zl'=2,'x'=2] {'row','zl','x'}, dimensions={0} | all-to-all | bytes 3145728 | tf_op jit(solution)/shard_map/all_to_all | solution.py:421
  170.0 2.6 %finish.3 = f32[32,96,128]{2,1,0:T(8,128)} custom-call(s32[96]{0:T(128)S(1)} %pad_add_fusion.routes, bf16[96,64,128]{2,1,0:T(8,128)(2,1)S(1)} %bitcast.30, f32[3,16,2,32,128]{4,3,2,1,0:T(8,128)S(1)} %get-tuple-element.76.pulled, bf16[32,96,128]{2,1,0:T(8,128)(2,1)S(1)} %copy-done.2, bf16[32,96,128]{2,1,0:T(8,128)(2,1)S(1)} %copy-done.1, ...), custom_call_target="tpu_custom_call" | custom-call | tf_op jit(solution)/shard_map/finish/pallas_call | solution.py:456
  (50 shorter events, 1.2 us)
Async XLA Ops:
  0.0 3.0 %copy-start.5 = (s32[4,24,16]{1,2,0:T(8,128)S(1)}, s32[4,24,16]{1,2,0:T(8,128)}, u32[]{:S(2)}) copy-start(s32[4,24,16]{1,2,0:T(8,128)} %param.14) | copy-start | bytes 18436
  0.0 3.2 %copy-start.6 = (s32[256]{0:T(256)S(1)}, s32[256]{0:T(256)}, u32[]{:S(2)}) copy-start(s32[256]{0:T(256)} %param.16) | copy-start | bytes 3076
  0.0 3.8 %copy-start.7 = (s32[1,3,16]{2,0,1:T(1,128)S(1)}, s32[1,3,16]{2,0,1:T(1,128)}, u32[]{:S(2)}) copy-start(s32[1,3,16]{2,0,1:T(1,128)} %param.15) | copy-start | bytes 580
  0.0 3.9 %copy-start.8 = (s32[8]{0:T(128)S(1)}, s32[8]{0:T(128)}, u32[]{:S(2)}) copy-start(s32[8]{0:T(128)} %param.17) | copy-start | bytes 100
  0.0 5.4 %copy-start.3 = (f32[8,64,128]{2,1,0:T(8,128)S(1)}, f32[8,64,128]{2,1,0:T(8,128)}, u32[]{:S(2)}) copy-start(f32[8,64,128]{2,1,0:T(8,128)} %own_weight.3) | copy-start | bytes 786436
  1.8 3.6 %collective-permute-start = (bf16[96,128]{1,0:T(8,128)(2,1)S(1)}, bf16[96,128]{1,0:T(8,128)(2,1)S(1)}, u32[]{:S(2)}, u32[]{:S(2)}) collective-permute-start(bf16[96,128]{1,0:T(8,128)(2,1)S(1)} %get-tuple-element.41), channel_id=1, source_target_pairs={{0,8},{8,0},{16,24},{24,16},{1,9},{9,1},{17,25},{25,17},{2,10},{10... | collective-permute-start | bytes 73736 | tf_op jit(solution)/shard_map/ppermute | solution.py:428
  2.3 3.1 %collective-permute-start.1 = (bf16[96,128]{1,0:T(8,128)(2,1)S(1)}, bf16[96,128]{1,0:T(8,128)(2,1)S(1)}, u32[]{:S(2)}, u32[]{:S(2)}) collective-permute-start(bf16[96,128]{1,0:T(8,128)(2,1)S(1)} %get-tuple-element.42), channel_id=1, source_target_pairs={{8,16},{16,8},{9,17},{17,9},{10,18},{18,10},{11,19},{19,11},{12,20... | collective-permute-start | bytes 73736 | tf_op jit(solution)/shard_map/ppermute | solution.py:428
  5.4 8.9 %copy-start = (bf16[8,4,64,1024]{3,2,1,0:T(8,128)(2,1)S(1)}, bf16[8,4,64,1024]{3,2,1,0:T(8,128)(2,1)}, u32[]{:S(2)}) copy-start(bf16[8,4,64,1024]{3,2,1,0:T(8,128)(2,1)} %param.12) | copy-start | bytes 12582916
  5.4 8.9 %copy-start.4 = (bf16[3,3,128,128]{3,2,1,0:T(8,128)(2,1)S(1)}, bf16[3,3,128,128]{3,2,1,0:T(8,128)(2,1)}, u32[]{:S(2)}) copy-start(bf16[3,3,128,128]{3,2,1,0:T(8,128)(2,1)} %kernel.3) | copy-start | bytes 884740
  5.5 11.9 %collective-permute-start.3 = (f32[48,128]{1,0:T(8,128)S(1)}, f32[48,128]{1,0:T(8,128)S(1)}, u32[]{:S(2)}, u32[]{:S(2)}) collective-permute-start(f32[48,128]{1,0:T(8,128)S(1)} %get-tuple-element.47), channel_id=1, source_target_pairs={{1,2},{2,1},{3,4},{4,3},{5,6},{6,5},{9,10},{10,9},{11,12},{12,11},... | collective-permute-start | bytes 73736 | tf_op jit(solution)/shard_map/ppermute | solution.py:428
  6.3 11.1 %collective-permute-start.2 = (f32[48,128]{1,0:T(8,128)S(1)}, f32[48,128]{1,0:T(8,128)S(1)}, u32[]{:S(2)}, u32[]{:S(2)}) collective-permute-start(f32[48,128]{1,0:T(8,128)S(1)} %get-tuple-element.45), channel_id=1, source_target_pairs={{0,1},{1,0},{2,3},{3,2},{4,5},{5,4},{6,7},{7,6},{8,9},{9,8},{10,11... | collective-permute-start | bytes 73736 | tf_op jit(solution)/shard_map/ppermute | solution.py:428
  11.8 9.4 %collective-permute-start.4 = (bf16[8,64,128]{2,1,0:T(8,128)(2,1)S(1)}, bf16[8,64,128]{2,1,0:T(8,128)(2,1)S(1)}, u32[]{:S(2)}, u32[]{:S(2)}) collective-permute-start(bf16[8,64,128]{2,1,0:T(8,128)(2,1)S(1)} %convert_element_type.10), channel_id=1, source_target_pairs={{0,4},{4,0},{1,5},{5,1},{2,6},{6,2},{3,7},{7,3},{8,12},{12,8},{9,1... | collective-permute-start | bytes 393224 | tf_op jit(solution)/shard_map/ppermute | solution.py:275
  48.3 15.0 %collective-permute-start.5 = (bf16[16,64,128]{2,1,0:T(8,128)(2,1)S(1)}, bf16[16,64,128]{2,1,0:T(8,128)(2,1)S(1)}, u32[]{:S(2)}, u32[]{:S(2)}) collective-permute-start(bf16[16,64,128]{2,1,0:T(8,128)(2,1)S(1)} %get-tuple-element.59), channel_id=1, source_target_pairs={{0,4},{4,0},{1,5},{5,1},{2,6},{6,2},{3,7},{7,3},{8,12},{12,8},{9,1... | collective-permute-start | bytes 786440 | tf_op jit(solution)/shard_map/ppermute | solution.py:275
  64.1 23.3 %copy-start.1 = (bf16[32,96,128]{2,1,0:T(8,128)(2,1)S(1)}, bf16[32,96,128]{2,1,0:T(8,128)(2,1)}, u32[]{:S(2)}) copy-start(bf16[32,96,128]{2,1,0:T(8,128)(2,1)} %state.5) | copy-start | bytes 2359300
  64.1 23.3 %copy-start.2 = (bf16[32,96,128]{2,1,0:T(8,128)(2,1)S(1)}, bf16[32,96,128]{2,1,0:T(8,128)(2,1)}, u32[]{:S(2)}) copy-start(bf16[32,96,128]{2,1,0:T(8,128)(2,1)} %grad.5) | copy-start | bytes 2359300
  89.3 1.3 collective-permute-start.6
  89.7 1.0 collective-permute-start.7
  90.6 5.0 %collective-permute-start.8 = (f32[48,128]{1,0:T(8,128)S(1)}, f32[48,128]{1,0:T(8,128)S(1)}, u32[]{:S(2)}, u32[]{:S(2)}) collective-permute-start(f32[48,128]{1,0:T(8,128)S(1)} %get-tuple-element.66), channel_id=1, source_target_pairs={{0,1},{1,0},{2,3},{3,2},{4,5},{5,4},{6,7},{7,6},{8,9},{9,8},{10,11... | collective-permute-start | bytes 73736 | tf_op jit(solution)/shard_map/ppermute | solution.py:428
  92.0 3.7 %collective-permute-start.9 = (f32[48,128]{1,0:T(8,128)S(1)}, f32[48,128]{1,0:T(8,128)S(1)}, u32[]{:S(2)}, u32[]{:S(2)}) collective-permute-start(f32[48,128]{1,0:T(8,128)S(1)} %get-tuple-element.67), channel_id=1, source_target_pairs={{1,2},{2,1},{3,4},{4,3},{5,6},{6,5},{9,10},{10,9},{11,12},{12,11},... | collective-permute-start | bytes 73736 | tf_op jit(solution)/shard_map/ppermute | solution.py:428
  131.0 15.0 %collective-permute-start.10 = (bf16[16,64,128]{2,1,0:T(8,128)(2,1)S(1)}, bf16[16,64,128]{2,1,0:T(8,128)(2,1)S(1)}, u32[]{:S(2)}, u32[]{:S(2)}) collective-permute-start(bf16[16,64,128]{2,1,0:T(8,128)(2,1)S(1)} %get-tuple-element.75), channel_id=1, source_target_pairs={{0,4},{4,0},{1,5},{5,1},{2,6},{6,2},{3,7},{7,3},{8,12},{12,8},{9,1... | collective-permute-start | bytes 786440 | tf_op jit(solution)/shard_map/ppermute | solution.py:275

commit v14 on v13

--- a/solution.py
+++ b/solution.py
@@ -42,6 +42,12 @@
         value = states[where].astype(jnp.float32)
         whole[where] = (1.0 - value * value) * grads[where].astype(jnp.float32)
     emit_edges(whole[...], scaled, row_a, row_b, col_a, col_b)
+
+
+def bring(source, held, mark):
+    copy = pltpu.make_async_copy(source, held, mark)
+    copy.start()
+    return copy
 
 
 def parity(dim):
@@ -120,9 +126,10 @@
 
 
 def inner_kernel(
-    routes, scaled, near_a, near_b, kernel, rays,
-    pulled, out, cols3, taps, wide, *, tile_cols,
+    source, scaled, near_a, near_b, kernel, rays,
+    pulled, out, cols3, taps, wide, routes, mark, *, tile_cols,
 ):
+    coming = bring(source, routes, mark)
     rows, cols, chans = scaled.shape
     f32, bf16 = jnp.float32, jnp.bfloat16
     blank = jnp.zeros((3 * chans, chans), bf16)
@@ -148,14 +155,16 @@
             (rows + 2) // 2, 2, cols, chans
         )
     out[...] = jnp.zeros_like(out)
+    coming.wait()
     for t in tiles_at(pulled.shape[0], tile_cols, True):
         forward_tile(routes, taps, rays, pulled, out, cols3, t, tile_cols)
 
 
 def outer_kernel(
-    routes, near_a, near_b, taps, rays, _pulled, _out, _cols3,
-    pulled, out, cols3, *, tile_cols,
+    source, near_a, near_b, taps, rays, _pulled, _out, _cols3,
+    pulled, out, cols3, routes, mark, *, tile_cols,
 ):
+    coming = bring(source, routes, mark)
     cols = cols3.shape[2]
     chans = pulled.shape[-1]
     group = 16
@@ -168,13 +177,16 @@
             there = (r // 2, r % 2, slice(first, first + group), lanes)
             value = jnp.where(spot == at, edge[7 + r : 8 + r, :], cols3[there].astype(jnp.float32))
             cols3[there] = value.astype(jnp.bfloat16)
+    coming.wait()
     for t in tiles_at(pulled.shape[0], tile_cols, False):
         forward_tile(routes, taps, rays, pulled, out, cols3, t, tile_cols)
 
 
-def combine_kernel(table, recv, total, low, acc_a, acc_b):
+def combine_kernel(source, recv, total, low, acc_a, acc_b, table, mark):
+    coming = bring(source, table, mark)
     acc_a[...] = jnp.zeros_like(acc_a)
     acc_b[...] = jnp.zeros_like(acc_b)
+    coming.wait()
 
     def body(j, carry):
         acc_a[table[2 * j]] += recv[2 * j].astype(jnp.float32)
@@ -188,21 +200,26 @@
     low[...] = value.astype(jnp.bfloat16)
 
 
-def reply_kernel(table, used, total, other, own_weight, other_weight, out, held):
+def reply_kernel(
+    source, flags, total, other, own_weight, other_weight, out, held, table, used, mark
+):
+    coming = [bring(source, table, mark.at[0]), bring(flags, used, mark.at[1])]
     n = total.shape[0]
     own = own_weight.shape[0]
-    place = used[n]
+    place = lax.axis_index("zh") * own
     for half, weight in enumerate((own_weight, other_weight)):
-        first = jnp.where(half == 0, place, n - own - place)
+        first = place if half == 0 else n - own - place
         for b in range(own):
             d = first + b
-            scale = used[d].astype(jnp.float32) * weight[b].astype(jnp.float32)
             value = total[d] + other[d].astype(jnp.float32)
-            held[d] = (scale * value).astype(jnp.bfloat16)
+            held[d] = (weight[b].astype(jnp.float32) * value).astype(jnp.bfloat16)
     held[n] = jnp.zeros(held.shape[1:], jnp.bfloat16)
+    for copy in coming:
+        copy.wait()
 
     def body(j, carry):
-        out[j] = held[table[j]]
+        d = table[j]
+        out[j] = held[jnp.where(used[d] == 1, d, n)]
         return carry
 
     lax.fori_loop(0, out.shape[0], body, 0, unroll=8)
@@ -309,7 +326,7 @@
         (number % blk_ang).reshape(ANGLES, blk_ang) < angle_count[:, None]
     ).reshape(1, blocks)
     used = jnp.any((block_slot[None, :] == dense_place[:, None]) & active, axis=1).astype(i32)
-    used = jnp.concatenate([used, jnp.full((1,), zh * blk_dev, i32)])
+    used = jnp.concatenate([used, jnp.zeros((1,), i32)])
 
     rays = ray_matrix.reshape(angles * spots, bins, tile_pix)
 
@@ -323,6 +340,9 @@
         shape((rows_dev, chans), f32),
         shape((rows_dev, chans), f32),
     )
+
+    def scalars(count):
+        return [pltpu.SMEM((count,), i32), pltpu.SemaphoreType.DMA]
 
     def limit(mib):
         return pltpu.CompilerParams(vmem_limit_bytes=mib << 20)
@@ -366,9 +386,9 @@
     inner = pl.pallas_call(
         functools.partial(inner_kernel, tile_cols=tile_cols),
         out_shape=(pulled_out, slot_out, cols3_out, taps_out),
-        in_specs=[SMEM] + [VMEM] * 5,
+        in_specs=[ANY] + [VMEM] * 5,
         out_specs=(VMEM,) * 4,
-        scratch_shapes=[pltpu.VMEM((rows_dev + 2, cols_dev + 16, chans), f32)],
+        scratch_shapes=[pltpu.VMEM((rows_dev + 2, cols_dev + 16, chans), f32)] + scalars(2 * pairs),
         compiler_params=limit(16),
         cost_estimate=cost(len(tiles_at(tiles, tile_cols, True))),
         name="inner",
@@ -376,8 +396,9 @@
     outer = pl.pallas_call(
         functools.partial(outer_kernel, tile_cols=tile_cols),
         out_shape=(pulled_out, slot_out, cols3_out),
-        in_specs=[SMEM] + [VMEM] * 7,
+        in_specs=[ANY] + [VMEM] * 7,
         out_specs=(VMEM,) * 3,
+        scratch_shapes=scalars(2 * pairs),
         input_output_aliases={5: 0, 6: 1, 7: 2},
         compiler_params=limit(16),
         cost_estimate=cost(len(tiles_at(tiles, tile_cols, False))),
@@ -386,18 +407,23 @@
     combine = pl.pallas_call(
         combine_kernel,
         out_shape=(shape((dense,) + block, f32), shape((dense,) + block, bf16)),
-        in_specs=[SMEM, VMEM],
+        in_specs=[ANY, VMEM],
         out_specs=(VMEM, VMEM),
-        scratch_shapes=[pltpu.VMEM((dense + 1,) + block, f32)] * 2,
+        scratch_shapes=[pltpu.VMEM((dense + 1,) + block, f32)] * 2 + scalars(slots),
         compiler_params=limit(8),
         name="combine",
     )
     reply = pl.pallas_call(
         reply_kernel,
         out_shape=slot_out,
-        in_specs=[SMEM] * 2 + [VMEM] * 4,
+        in_specs=[ANY] * 2 + [VMEM] * 4,
         out_specs=VMEM,
-        scratch_shapes=[pltpu.VMEM((dense + 1,) + block, bf16)],
+        scratch_shapes=[
+            pltpu.VMEM((dense + 1,) + block, bf16),
+            pltpu.SMEM((slots,), i32),
+            pltpu.SMEM((dense + 1,), i32),
+            pltpu.SemaphoreType.DMA((2,)),
+        ],
         compiler_params=limit(8),
         name="reply",
     )

time: 173 us -> 173 us (level)
  transfers between devices with their start and end apart: 11 -> 11, of which waited for: 3 -> 3; matrix products, arithmetic and copies ran while one was open for 1% -> 1% of each run, Pallas kernels for 6% -> 5%
where the time goes in v14:
time: 173 us; the launch traced here: 172 us
  blocking collectives  103 us (60%)
  waiting for transfers between devices  29.3 us (17%)
  Pallas kernels  22.8 us (13%)
  starting transfers between devices  14.3 us (8%)
    all_to_all x4, blocking collectives, across(): lax.all_to_all(value, GROUP, split_axis=0, concat_axis=0, tiled=True)  103 us
    ppermute x3, waiting for transfers between devices, exchange(): return lax.ppermute(value, 'zh', [(0, 1), (1, 0)])  29 us
    ppermute x4, starting transfers between devices, swaps(): lax.ppermute(value_a, axis, even)  7.77 us
    pallas_call x2, Pallas kernels, forward(): pulled, outgoing, _ = outer(routes, *beside, taps, rays, *parts)  7.44 us
    pallas_call x2, Pallas kernels, forward(): *parts, taps = inner(routes, scaled, *above, kernel, rays)  5.58 us
    pallas_call x2, Pallas kernels, on_device(): finish(last)(routes, across(replies), pulled, grad, state, rays)  4.44 us
    ppermute x3, starting transfers between devices, exchange(): return lax.ppermute(value, 'zh', [(0, 1), (1, 0)])  3.65 us
  transfers between devices with their start and end apart: 11, of which 3 were waited for; matrix products, arithmetic and copies ran while one was open for 1% of the time, Pallas kernels for 5%

profile of v14, /device:TPU:0, one launch (start us, length us, event | category | flops | bytes accessed | tf_op | source)
XLA Modules:
  0.0 172.4 jit_solution(1098682257851626468)
XLA Ops:
  0.0 1.7 %start.1 = (bf16[32,96,128]{2,1,0:T(8,128)(2,1)S(1)}, bf16[96,128]{1,0:T(8,128)(2,1)S(1)}, bf16[96,128]{1,0:T(8,128)(2,1)S(1)}, f32[32,128]{1,0:T(8,128)S(1)}, f32[32,128]{1,0:T(8,128)S(1)}) custom-call(bf16[32,96,128]{2,1,0:T(8,128)(2,1)} %state.5, bf16[32,96,128]{2,1,0:T(8,128)(2,1)} %grad.5), custom_call_target="tpu_custom_call" | custom-call | tf_op jit(solution)/shard_map/start/pallas_call | solution.py:471
  1.8 0.6 collective-permute-start
  2.3 0.7 collective-permute-start.1
  3.2 0.5 select_reduce_fusion
  4.1 0.5 convert_reduce_fusion
  4.8 0.2 and_reduce_fusion
  5.5 0.8 collective-permute-start.3
  6.3 5.5 %collective-permute-start.2 = (f32[48,128]{1,0:T(8,128)S(1)}, f32[48,128]{1,0:T(8,128)S(1)}, u32[]{:S(2)}, u32[]{:S(2)}) collective-permute-start(f32[48,128]{1,0:T(8,128)S(1)} %get-tuple-element.45), channel_id=1, source_target_pairs={{0,1},{1,0},{2,3},{3,2},{4,5},{5,4},{6,7},{7,6},{8,9},{9,8},{10,11... | collective-permute-start | bytes 73736 | tf_op jit(solution)/shard_map/ppermute | solution.py:454
  11.8 2.6 %collective-permute-start.4 = (bf16[8,64,128]{2,1,0:T(8,128)(2,1)S(1)}, bf16[8,64,128]{2,1,0:T(8,128)(2,1)S(1)}, u32[]{:S(2)}, u32[]{:S(2)}) collective-permute-start(bf16[8,64,128]{2,1,0:T(8,128)(2,1)S(1)} %convert_element_type.8), channel_id=1, source_target_pairs={{0,4},{4,0},{1,5},{5,1},{2,6},{6,2},{3,7},{7,3},{8,12},{12,8},{9,1... | collective-permute-start | bytes 393224 | tf_op jit(solution)/shard_map/ppermute | solution.py:292
  14.3 2.8 %inner.2 = (f32[3,16,2,32,128]{4,3,2,1,0:T(8,128)S(1)}, bf16[96,64,128]{2,1,0:T(8,128)(2,1)S(1)}, bf16[17,2,96,384]{3,2,1,0:T(8,128)(2,1)S(1)}, bf16[1536,256]{1,0:T(8,128)(2,1)S(1)}) custom-call(s32[96]{0:T(128)S(1)} %pad_add_fusion.source.routes, bf16[32,96,128]{2,1,0:T(8,128)(2,1)S(1)} %get-tuple-element.48.scaled, ...), custom_call_target="tpu_custom_call" | custom-call | flops 570425344 | bytes 4194304 | tf_op jit(solution)/shard_map/inner/pallas_call | solution.py:467
  17.2 3.7 %outer.2 = (f32[3,16,2,32,128]{4,3,2,1,0:T(8,128)S(1)}, bf16[96,64,128]{2,1,0:T(8,128)(2,1)S(1)}, bf16[17,2,96,384]{3,2,1,0:T(8,128)(2,1)S(1)}) custom-call(s32[96]{0:T(128)S(1)} %pad_add_fusion.source.routes, f32[48,128]{1,0:T(8,128)S(1)} %collective-permute-done.2.near_a, ...), custom_call_target="tpu_custom_call", output_to_operand_aliasing={{0}: (5, {}), {1}: (6, {}), {2}: (7, {})} | custom-call | flops 1140850688 | bytes 4194304 | tf_op jit(solution)/shard_map/outer/pallas_call | solution.py:468
  20.9 26.1 %all_to_all.20 = bf16[16,6,64,128]{3,2,1,0:T(8,128)(2,1)S(1)} all-to-all(bf16[16,6,64,128]{3,2,1,0:T(8,128)(2,1)S(1)} %bitcast.27), channel_id=1, replica_groups=mesh['row'=4,'zh'=2,'zl'=2,'x'=2] {'row','zl','x'}, dimensions={0} | all-to-all | bytes 3145728 | tf_op jit(solution)/shard_map/all_to_all | solution.py:447
  47.0 1.0 combine.2
  48.0 0.7 collective-permute-start.5
  48.7 14.3 %collective-permute-done.5.other = bf16[16,64,128]{2,1,0:T(8,128)(2,1)S(1)} collective-permute-done((bf16[16,64,128]{2,1,0:T(8,128)(2,1)S(1)}, bf16[16,64,128]{2,1,0:T(8,128)(2,1)S(1)}, u32[]{:S(2)}, u32[]{:S(2)}) %collective-permute-start.5) | collective-permute-done | bytes 262176 | tf_op jit(solution)/shard_map/ppermute | solution.py:292
  63.0 0.8 reply.2
  63.9 23.3 %all_to_all.21 = bf16[16,6,64,128]{3,2,1,0:T(8,128)(2,1)S(1)} all-to-all(bf16[16,6,64,128]{3,2,1,0:T(8,128)(2,1)S(1)} %bitcast.26), channel_id=1, replica_groups=mesh['row'=4,'zh'=2,'zl'=2,'x'=2] {'row','zl','x'}, dimensions={0} | all-to-all | bytes 3145728 | tf_op jit(solution)/shard_map/all_to_all | solution.py:447
  87.2 1.9 %finish.2 = (bf16[32,96,128]{2,1,0:T(8,128)(2,1)S(1)}, bf16[96,128]{1,0:T(8,128)(2,1)S(1)}, bf16[96,128]{1,0:T(8,128)(2,1)S(1)}, f32[32,128]{1,0:T(8,128)S(1)}, f32[32,128]{1,0:T(8,128)S(1)}) custom-call(s32[96]{0:T(128)S(1)} %pad_add_fusion.source.routes, bf16[96,64,128]{2,1,0:T(8,128)(2,1)S(1)} %bitcast.22, ...), custom_call_target="tpu_custom_call" | custom-call | tf_op jit(solution)/shard_map/finish/pallas_call | solution.py:482
  89.0 0.3 collective-permute-start.6
  89.4 0.7 collective-permute-start.7
  90.0 0.3 collective-permute-done.6.near_a
  90.3 1.4 collective-permute-start.8
  91.7 0.8 collective-permute-start.9
  92.6 2.8 %inner.3 = (f32[3,16,2,32,128]{4,3,2,1,0:T(8,128)S(1)}, bf16[96,64,128]{2,1,0:T(8,128)(2,1)S(1)}, bf16[17,2,96,384]{3,2,1,0:T(8,128)(2,1)S(1)}, bf16[1536,256]{1,0:T(8,128)(2,1)S(1)}) custom-call(s32[96]{0:T(128)S(1)} %pad_add_fusion.source.routes, bf16[32,96,128]{2,1,0:T(8,128)(2,1)S(1)} %get-tuple-element.68.scaled, ...), custom_call_target="tpu_custom_call" | custom-call | flops 570425344 | bytes 4194304 | tf_op jit(solution)/shard_map/inner/pallas_call | solution.py:467
  95.4 3.7 %outer.3 = (f32[3,16,2,32,128]{4,3,2,1,0:T(8,128)S(1)}, bf16[96,64,128]{2,1,0:T(8,128)(2,1)S(1)}, bf16[17,2,96,384]{3,2,1,0:T(8,128)(2,1)S(1)}) custom-call(s32[96]{0:T(128)S(1)} %pad_add_fusion.source.routes, f32[48,128]{1,0:T(8,128)S(1)} %collective-permute-done.8.near_a, ...), custom_call_target="tpu_custom_call", output_to_operand_aliasing={{0}: (5, {}), {1}: (6, {}), {2}: (7, {})} | custom-call | flops 1140850688 | bytes 4194304 | tf_op jit(solution)/shard_map/outer/pallas_call | solution.py:468
  99.1 30.6 %all_to_all.22 = bf16[16,6,64,128]{3,2,1,0:T(8,128)(2,1)S(1)} all-to-all(bf16[16,6,64,128]{3,2,1,0:T(8,128)(2,1)S(1)} %bitcast.28), channel_id=1, replica_groups=mesh['row'=4,'zh'=2,'zl'=2,'x'=2] {'row','zl','x'}, dimensions={0} | all-to-all | bytes 3145728 | tf_op jit(solution)/shard_map/all_to_all | solution.py:447
  129.7 1.0 combine.3
  130.7 0.4 collective-permute-start.10
  131.1 14.7 %collective-permute-done.10.other = bf16[16,64,128]{2,1,0:T(8,128)(2,1)S(1)} collective-permute-done((bf16[16,64,128]{2,1,0:T(8,128)(2,1)S(1)}, bf16[16,64,128]{2,1,0:T(8,128)(2,1)S(1)}, u32[]{:S(2)}, u32[]{:S(2)}) %collective-permute-start.10) | collective-permute-done | bytes 262176 | tf_op jit(solution)/shard_map/ppermute | solution.py:292
  145.7 0.8 reply.3
  146.5 23.2 %all_to_all.23 = bf16[16,6,64,128]{3,2,1,0:T(8,128)(2,1)S(1)} all-to-all(bf16[16,6,64,128]{3,2,1,0:T(8,128)(2,1)S(1)} %bitcast.23), channel_id=1, replica_groups=mesh['row'=4,'zh'=2,'zl'=2,'x'=2] {'row','zl','x'}, dimensions={0} | all-to-all | bytes 3145728 | tf_op jit(solution)/shard_map/all_to_all | solution.py:447
  169.7 2.6 %finish.3 = f32[32,96,128]{2,1,0:T(8,128)} custom-call(s32[96]{0:T(128)S(1)} %pad_add_fusion.source.routes, bf16[96,64,128]{2,1,0:T(8,128)(2,1)S(1)} %bitcast.29, f32[3,16,2,32,128]{4,3,2,1,0:T(8,128)S(1)} %get-tuple-element.76.pulled, bf16[32,96,128]{2,1,0:T(8,128)(2,1)S(1)} %copy-done.2, bf16[32,96,128]{2,1,0:T(8,128)(2,1)S(1)} %copy-done.1, ...), custom_call_target="tpu_custom_call" | custom-call | tf_op jit(solution)/shard_map/finish/pallas_call | solution.py:482
  (49 shorter events, 1.2 us)
Async XLA Ops:
  0.0 3.0 %copy-start.5 = (s32[4,24,16]{1,2,0:T(8,128)S(1)}, s32[4,24,16]{1,2,0:T(8,128)}, u32[]{:S(2)}) copy-start(s32[4,24,16]{1,2,0:T(8,128)} %param.14) | copy-start | bytes 18436
  0.0 3.2 %copy-start.6 = (s32[256]{0:T(256)S(1)}, s32[256]{0:T(256)}, u32[]{:S(2)}) copy-start(s32[256]{0:T(256)} %param.16) | copy-start | bytes 3076
  0.0 3.8 %copy-start.7 = (s32[1,3,16]{2,0,1:T(1,128)S(1)}, s32[1,3,16]{2,0,1:T(1,128)}, u32[]{:S(2)}) copy-start(s32[1,3,16]{2,0,1:T(1,128)} %param.15) | copy-start | bytes 580
  0.0 3.9 %copy-start.8 = (s32[8]{0:T(128)S(1)}, s32[8]{0:T(128)}, u32[]{:S(2)}) copy-start(s32[8]{0:T(128)} %param.17) | copy-start | bytes 100
  0.0 5.3 %copy-start.3 = (f32[8,64,128]{2,1,0:T(8,128)S(1)}, f32[8,64,128]{2,1,0:T(8,128)}, u32[]{:S(2)}) copy-start(f32[8,64,128]{2,1,0:T(8,128)} %own_weight.3) | copy-start | bytes 786436
  1.8 3.6 %collective-permute-start = (bf16[96,128]{1,0:T(8,128)(2,1)S(1)}, bf16[96,128]{1,0:T(8,128)(2,1)S(1)}, u32[]{:S(2)}, u32[]{:S(2)}) collective-permute-start(bf16[96,128]{1,0:T(8,128)(2,1)S(1)} %get-tuple-element.41), channel_id=1, source_target_pairs={{0,8},{8,0},{16,24},{24,16},{1,9},{9,1},{17,25},{25,17},{2,10},{10... | collective-permute-start | bytes 73736 | tf_op jit(solution)/shard_map/ppermute | solution.py:454
  2.3 3.1 %collective-permute-start.1 = (bf16[96,128]{1,0:T(8,128)(2,1)S(1)}, bf16[96,128]{1,0:T(8,128)(2,1)S(1)}, u32[]{:S(2)}, u32[]{:S(2)}) collective-permute-start(bf16[96,128]{1,0:T(8,128)(2,1)S(1)} %get-tuple-element.42), channel_id=1, source_target_pairs={{8,16},{16,8},{9,17},{17,9},{10,18},{18,10},{11,19},{19,11},{12,20... | collective-permute-start | bytes 73736 | tf_op jit(solution)/shard_map/ppermute | solution.py:454
  5.4 8.9 %copy-start = (bf16[8,4,64,1024]{3,2,1,0:T(8,128)(2,1)S(1)}, bf16[8,4,64,1024]{3,2,1,0:T(8,128)(2,1)}, u32[]{:S(2)}) copy-start(bf16[8,4,64,1024]{3,2,1,0:T(8,128)(2,1)} %param.12) | copy-start | bytes 12582916
  5.4 8.9 %copy-start.4 = (bf16[3,3,128,128]{3,2,1,0:T(8,128)(2,1)S(1)}, bf16[3,3,128,128]{3,2,1,0:T(8,128)(2,1)}, u32[]{:S(2)}) copy-start(bf16[3,3,128,128]{3,2,1,0:T(8,128)(2,1)} %kernel.3) | copy-start | bytes 884740
  5.5 11.7 %collective-permute-start.3 = (f32[48,128]{1,0:T(8,128)S(1)}, f32[48,128]{1,0:T(8,128)S(1)}, u32[]{:S(2)}, u32[]{:S(2)}) collective-permute-start(f32[48,128]{1,0:T(8,128)S(1)} %get-tuple-element.47), channel_id=1, source_target_pairs={{1,2},{2,1},{3,4},{4,3},{5,6},{6,5},{9,10},{10,9},{11,12},{12,11},... | collective-permute-start | bytes 73736 | tf_op jit(solution)/shard_map/ppermute | solution.py:454
  6.3 10.9 %collective-permute-start.2 = (f32[48,128]{1,0:T(8,128)S(1)}, f32[48,128]{1,0:T(8,128)S(1)}, u32[]{:S(2)}, u32[]{:S(2)}) collective-permute-start(f32[48,128]{1,0:T(8,128)S(1)} %get-tuple-element.45), channel_id=1, source_target_pairs={{0,1},{1,0},{2,3},{3,2},{4,5},{5,4},{6,7},{7,6},{8,9},{9,8},{10,11... | collective-permute-start | bytes 73736 | tf_op jit(solution)/shard_map/ppermute | solution.py:454
  11.8 9.1 %collective-permute-start.4 = (bf16[8,64,128]{2,1,0:T(8,128)(2,1)S(1)}, bf16[8,64,128]{2,1,0:T(8,128)(2,1)S(1)}, u32[]{:S(2)}, u32[]{:S(2)}) collective-permute-start(bf16[8,64,128]{2,1,0:T(8,128)(2,1)S(1)} %convert_element_type.8), channel_id=1, source_target_pairs={{0,4},{4,0},{1,5},{5,1},{2,6},{6,2},{3,7},{7,3},{8,12},{12,8},{9,1... | collective-permute-start | bytes 393224 | tf_op jit(solution)/shard_map/ppermute | solution.py:292
  48.0 15.0 %collective-permute-start.5 = (bf16[16,64,128]{2,1,0:T(8,128)(2,1)S(1)}, bf16[16,64,128]{2,1,0:T(8,128)(2,1)S(1)}, u32[]{:S(2)}, u32[]{:S(2)}) collective-permute-start(bf16[16,64,128]{2,1,0:T(8,128)(2,1)S(1)} %get-tuple-element.59), channel_id=1, source_target_pairs={{0,4},{4,0},{1,5},{5,1},{2,6},{6,2},{3,7},{7,3},{8,12},{12,8},{9,1... | collective-permute-start | bytes 786440 | tf_op jit(solution)/shard_map/ppermute | solution.py:292
  63.8 23.3 %copy-start.1 = (bf16[32,96,128]{2,1,0:T(8,128)(2,1)S(1)}, bf16[32,96,128]{2,1,0:T(8,128)(2,1)}, u32[]{:S(2)}) copy-start(bf16[32,96,128]{2,1,0:T(8,128)(2,1)} %state.5) | copy-start | bytes 2359300
  63.9 23.3 %copy-start.2 = (bf16[32,96,128]{2,1,0:T(8,128)(2,1)S(1)}, bf16[32,96,128]{2,1,0:T(8,128)(2,1)}, u32[]{:S(2)}) copy-start(bf16[32,96,128]{2,1,0:T(8,128)(2,1)} %grad.5) | copy-start | bytes 2359300
  89.0 1.3 collective-permute-start.6
  89.4 0.9 collective-permute-start.7
  90.3 5.0 %collective-permute-start.8 = (f32[48,128]{1,0:T(8,128)S(1)}, f32[48,128]{1,0:T(8,128)S(1)}, u32[]{:S(2)}, u32[]{:S(2)}) collective-permute-start(f32[48,128]{1,0:T(8,128)S(1)} %get-tuple-element.66), channel_id=1, source_target_pairs={{0,1},{1,0},{2,3},{3,2},{4,5},{5,4},{6,7},{7,6},{8,9},{9,8},{10,11... | collective-permute-start | bytes 73736 | tf_op jit(solution)/shard_map/ppermute | solution.py:454
  91.7 3.6 %collective-permute-start.9 = (f32[48,128]{1,0:T(8,128)S(1)}, f32[48,128]{1,0:T(8,128)S(1)}, u32[]{:S(2)}, u32[]{:S(2)}) collective-permute-start(f32[48,128]{1,0:T(8,128)S(1)} %get-tuple-element.67), channel_id=1, source_target_pairs={{1,2},{2,1},{3,4},{4,3},{5,6},{6,5},{9,10},{10,9},{11,12},{12,11},... | collective-permute-start | bytes 73736 | tf_op jit(solution)/shard_map/ppermute | solution.py:454
  130.7 15.0 %collective-permute-start.10 = (bf16[16,64,128]{2,1,0:T(8,128)(2,1)S(1)}, bf16[16,64,128]{2,1,0:T(8,128)(2,1)S(1)}, u32[]{:S(2)}, u32[]{:S(2)}) collective-permute-start(bf16[16,64,128]{2,1,0:T(8,128)(2,1)S(1)} %get-tuple-element.75), channel_id=1, source_target_pairs={{0,4},{4,0},{1,5},{5,1},{2,6},{6,2},{3,7},{7,3},{8,12},{12,8},{9,1... | collective-permute-start | bytes 786440 | tf_op jit(solution)/shard_map/ppermute | solution.py:292

commit v15 on v14

--- a/solution.py
+++ b/solution.py
@@ -125,14 +125,23 @@
     return [t for t in range(tiles) if (0 < t % tile_cols < tile_cols - 1) == inner]
 
 
-def inner_kernel(
-    source, scaled, near_a, near_b, kernel, rays,
-    pulled, out, cols3, taps, wide, routes, mark, *, tile_cols,
-):
-    coming = bring(source, routes, mark)
-    rows, cols, chans = scaled.shape
+def spread(rows, wide, cols3, first):
+    count, cols, chans = rows.shape
     f32, bf16 = jnp.float32, jnp.bfloat16
-    blank = jnp.zeros((3 * chans, chans), bf16)
+    blank = jnp.zeros((count, 8, chans), f32)
+    wide[:, 0:8, :] = blank
+    wide[:, 8 + cols : 16 + cols, :] = blank
+    wide[:, 8 : 8 + cols, :] = rows.astype(f32)
+    for dc in range(3):
+        lanes = slice(dc * chans, (dc + 1) * chans)
+        value = wide[:, 7 + dc : 7 + dc + cols, :].astype(bf16)
+        for r in range(count):
+            cols3[(first + r) // 2, (first + r) % 2, :, lanes] = value[r]
+
+
+def centre_kernel(scaled, kernel, out, cols3, taps, wide):
+    chans = scaled.shape[2]
+    blank = jnp.zeros((3 * chans, chans), jnp.bfloat16)
     for dr in range(4):
         base = dr * 3 * chans
         for side in range(2):
@@ -143,21 +152,32 @@
                 continue
             for dc in range(3):
                 taps[base + dc * chans : base + (dc + 1) * chans, lanes] = kernel[2 - tap, 2 - dc].T
-    a, b = near_a[...].astype(f32), near_b[...].astype(f32)
-    wide[0, 8 : 8 + cols, :] = pick(0, a, b)
-    wide[rows + 1, 8 : 8 + cols, :] = pick(0, b, a)
-    wide[1 : rows + 1, 8 : 8 + cols, :] = scaled[...].astype(f32)
-    wide[:, 0:8, :] = jnp.zeros((rows + 2, 8, chans), f32)
-    wide[:, 8 + cols :, :] = jnp.zeros((rows + 2, 8, chans), f32)
-    for dc in range(3):
-        value = wide[:, 7 + dc : 7 + dc + cols, :].astype(bf16)
-        cols3[:, :, :, dc * chans : (dc + 1) * chans] = value.reshape(
-            (rows + 2) // 2, 2, cols, chans
-        )
+    spread(scaled[...], wide, cols3, 1)
     out[...] = jnp.zeros_like(out)
+
+
+def inner_kernel(
+    source, near_a, near_b, taps, rays, _out, _cols3,
+    pulled, out, cols3, wide, routes, mark, *, tile_cols,
+):
+    coming = bring(source, routes, mark)
+    a, b = near_a[...], near_b[...]
+    spread(pick(0, a, b)[None], wide, cols3, 0)
+    spread(pick(0, b, a)[None], wide, cols3, 2 * cols3.shape[0] - 1)
     coming.wait()
     for t in tiles_at(pulled.shape[0], tile_cols, True):
         forward_tile(routes, taps, rays, pulled, out, cols3, t, tile_cols)
+
+
+def both_kernel(
+    source, scaled, near_a, near_b, kernel, rays,
+    pulled, out, cols3, taps, wide, line, routes, mark, *, tile_cols,
+):
+    centre_kernel(scaled, kernel, out, cols3, taps, wide)
+    inner_kernel(
+        source, near_a, near_b, taps, rays, None, None,
+        pulled, out, cols3, line, routes, mark, tile_cols=tile_cols,
+    )
 
 
 def outer_kernel(
@@ -383,13 +403,36 @@
 
     taps_out = shape((4 * 3 * chans, 2 * chans), bf16)
 
-    inner = pl.pallas_call(
-        functools.partial(inner_kernel, tile_cols=tile_cols),
+    wide = pltpu.VMEM((rows_dev, cols_dev + 16, chans), f32)
+    line = pltpu.VMEM((1, cols_dev + 16, chans), f32)
+    both = pl.pallas_call(
+        functools.partial(both_kernel, tile_cols=tile_cols),
         out_shape=(pulled_out, slot_out, cols3_out, taps_out),
         in_specs=[ANY] + [VMEM] * 5,
         out_specs=(VMEM,) * 4,
-        scratch_shapes=[pltpu.VMEM((rows_dev + 2, cols_dev + 16, chans), f32)] + scalars(2 * pairs),
+        scratch_shapes=[wide, line] + scalars(2 * pairs),
         compiler_params=limit(16),
+        cost_estimate=cost(len(tiles_at(tiles, tile_cols, True))),
+        name="both",
+    )
+    centre = pl.pallas_call(
+        centre_kernel,
+        out_shape=(slot_out, cols3_out, taps_out),
+        in_specs=[VMEM] * 2,
+        out_specs=(VMEM,) * 3,
+        scratch_shapes=[wide],
+        compiler_params=limit(12),
+        cost_estimate=cost(1),
+        name="centre",
+    )
+    inner = pl.pallas_call(
+        functools.partial(inner_kernel, tile_cols=tile_cols),
+        out_shape=(pulled_out, slot_out, cols3_out),
+        in_specs=[ANY] + [VMEM] * 6,
+        out_specs=(VMEM,) * 3,
+        scratch_shapes=[line] + scalars(2 * pairs),
+        input_output_aliases={5: 1, 6: 2},
+        compiler_params=limit(12),
         cost_estimate=cost(len(tiles_at(tiles, tile_cols, True))),
         name="inner",
     )
@@ -464,7 +507,11 @@
             side_b, weight = lax.optimization_barrier((side_b, ray_weight.astype(bf16)))
             other_weight = exchange(weight)
         beside = swaps(side_a, side_b, COL)
-        *parts, taps = inner(routes, scaled, *above, kernel, rays)
+        if early:
+            *parts, taps = both(routes, scaled, *above, kernel, rays)
+        else:
+            outgoing, cols3, taps = centre(scaled, kernel)
+            parts = inner(routes, *above, taps, rays, outgoing, cols3)
         pulled, outgoing, _ = outer(routes, *beside, taps, rays, *parts)
         return pulled, outgoing, other_weight
 

time: 173 us -> 173 us (level)
    pallas_call x2 -> x3, Pallas kernels: 5.58 us -> 6.07 us  [the longest x1 2.78 us: forward(): *parts, taps = both(routes, scaled, *above, kernel, rays)]
  transfers between devices with their start and end apart: 11 -> 11, of which waited for: 3 -> 2; matrix products, arithmetic and copies ran while one was open for 1% -> 1% of each run, Pallas kernels for 5% -> 6%
where the time goes in v15:
time: 173 us; the launch traced here: 172 us
  blocking collectives  103 us (60%)
  waiting for transfers between devices  29.1 us (17%)
  Pallas kernels  23.3 us (13%)
  starting transfers between devices  14 us (8%)
    all_to_all x4, blocking collectives, across(): lax.all_to_all(value, GROUP, split_axis=0, concat_axis=0, tiled=True)  103 us
    ppermute x3, waiting for transfers between devices, exchange(): return lax.ppermute(value, 'zh', [(0, 1), (1, 0)])  29.1 us
    ppermute x4, starting transfers between devices, swaps(): lax.ppermute(value_a, axis, even)  7.53 us
    pallas_call x2, Pallas kernels, forward(): pulled, outgoing, _ = outer(routes, *beside, taps, rays, *parts)  7.44 us
    pallas_call x2, Pallas kernels, on_device(): finish(last)(routes, across(replies), pulled, grad, state, rays)  4.44 us
    ppermute x3, starting transfers between devices, exchange(): return lax.ppermute(value, 'zh', [(0, 1), (1, 0)])  3.55 us
  transfers between devices with their start and end apart: 11, of which 2 were waited for; matrix products, arithmetic and copies ran while one was open for 1% of the time, Pallas kernels for 6%

profile of v15, /device:TPU:0, one launch (start us, length us, event | category | flops | bytes accessed | tf_op | source)
XLA Modules:
  0.0 172.4 jit_solution(1578742117409149768)
XLA Ops:
  0.0 1.7 %start.1 = (bf16[32,96,128]{2,1,0:T(8,128)(2,1)S(1)}, bf16[96,128]{1,0:T(8,128)(2,1)S(1)}, bf16[96,128]{1,0:T(8,128)(2,1)S(1)}, f32[32,128]{1,0:T(8,128)S(1)}, f32[32,128]{1,0:T(8,128)S(1)}) custom-call(bf16[32,96,128]{2,1,0:T(8,128)(2,1)} %state.5, bf16[32,96,128]{2,1,0:T(8,128)(2,1)} %grad.5), custom_call_target="tpu_custom_call" | custom-call | tf_op jit(solution)/shard_map/start/pallas_call | solution.py:518
  1.8 0.6 collective-permute-start
  2.3 0.7 collective-permute-start.1
  3.2 0.5 select_reduce_fusion
  4.1 0.5 convert_reduce_fusion
  4.8 0.2 and_reduce_fusion
  5.5 0.8 collective-permute-start.3
  6.3 5.5 %collective-permute-start.2 = (f32[48,128]{1,0:T(8,128)S(1)}, f32[48,128]{1,0:T(8,128)S(1)}, u32[]{:S(2)}, u32[]{:S(2)}) collective-permute-start(f32[48,128]{1,0:T(8,128)S(1)} %get-tuple-element.47), channel_id=1, source_target_pairs={{0,1},{1,0},{2,3},{3,2},{4,5},{5,4},{6,7},{7,6},{8,9},{9,8},{10,11... | collective-permute-start | bytes 73736 | tf_op jit(solution)/shard_map/ppermute | solution.py:497
  11.8 2.6 %collective-permute-start.4 = (bf16[8,64,128]{2,1,0:T(8,128)(2,1)S(1)}, bf16[8,64,128]{2,1,0:T(8,128)(2,1)S(1)}, u32[]{:S(2)}, u32[]{:S(2)}) collective-permute-start(bf16[8,64,128]{2,1,0:T(8,128)(2,1)S(1)} %convert_element_type.8), channel_id=1, source_target_pairs={{0,4},{4,0},{1,5},{5,1},{2,6},{6,2},{3,7},{7,3},{8,12},{12,8},{9,1... | collective-permute-start | bytes 393224 | tf_op jit(solution)/shard_map/ppermute | solution.py:312
  14.3 2.8 %both.1 = (f32[3,16,2,32,128]{4,3,2,1,0:T(8,128)S(1)}, bf16[96,64,128]{2,1,0:T(8,128)(2,1)S(1)}, bf16[17,2,96,384]{3,2,1,0:T(8,128)(2,1)S(1)}, bf16[1536,256]{1,0:T(8,128)(2,1)S(1)}) custom-call(s32[96]{0:T(128)S(1)} %pad_add_fusion.source.routes, bf16[32,96,128]{2,1,0:T(8,128)(2,1)S(1)} %get-tuple-element.50.scaled, ...), custom_call_target="tpu_custom_call" | custom-call | flops 570425344 | bytes 4194304 | tf_op jit(solution)/shard_map/both/pallas_call | solution.py:511
  17.2 3.7 %outer.2 = (f32[3,16,2,32,128]{4,3,2,1,0:T(8,128)S(1)}, bf16[96,64,128]{2,1,0:T(8,128)(2,1)S(1)}, bf16[17,2,96,384]{3,2,1,0:T(8,128)(2,1)S(1)}) custom-call(s32[96]{0:T(128)S(1)} %pad_add_fusion.source.routes, f32[48,128]{1,0:T(8,128)S(1)} %collective-permute-done.2.near_a, ...), custom_call_target="tpu_custom_call", output_to_operand_aliasing={{0}: (5, {}), {1}: (6, {}), {2}: (7, {})} | custom-call | flops 1140850688 | bytes 4194304 | tf_op jit(solution)/shard_map/outer/pallas_call | solution.py:515
  20.9 26.1 %all_to_all.20 = bf16[16,6,64,128]{3,2,1,0:T(8,128)(2,1)S(1)} all-to-all(bf16[16,6,64,128]{3,2,1,0:T(8,128)(2,1)S(1)} %bitcast.28), channel_id=1, replica_groups=mesh['row'=4,'zh'=2,'zl'=2,'x'=2] {'row','zl','x'}, dimensions={0} | all-to-all | bytes 3145728 | tf_op jit(solution)/shard_map/all_to_all | solution.py:490
  47.0 1.0 combine.2
  48.0 0.7 collective-permute-start.5
  48.7 14.3 %collective-permute-done.5.other = bf16[16,64,128]{2,1,0:T(8,128)(2,1)S(1)} collective-permute-done((bf16[16,64,128]{2,1,0:T(8,128)(2,1)S(1)}, bf16[16,64,128]{2,1,0:T(8,128)(2,1)S(1)}, u32[]{:S(2)}, u32[]{:S(2)}) %collective-permute-start.5) | collective-permute-done | bytes 262176 | tf_op jit(solution)/shard_map/ppermute | solution.py:312
  63.0 0.8 reply.2
  63.9 23.3 %all_to_all.21 = bf16[16,6,64,128]{3,2,1,0:T(8,128)(2,1)S(1)} all-to-all(bf16[16,6,64,128]{3,2,1,0:T(8,128)(2,1)S(1)} %bitcast.27), channel_id=1, replica_groups=mesh['row'=4,'zh'=2,'zl'=2,'x'=2] {'row','zl','x'}, dimensions={0} | all-to-all | bytes 3145728 | tf_op jit(solution)/shard_map/all_to_all | solution.py:490
  87.2 1.9 %finish.2 = (bf16[32,96,128]{2,1,0:T(8,128)(2,1)S(1)}, bf16[96,128]{1,0:T(8,128)(2,1)S(1)}, bf16[96,128]{1,0:T(8,128)(2,1)S(1)}, f32[32,128]{1,0:T(8,128)S(1)}, f32[32,128]{1,0:T(8,128)S(1)}) custom-call(s32[96]{0:T(128)S(1)} %pad_add_fusion.source.routes, bf16[96,64,128]{2,1,0:T(8,128)(2,1)S(1)} %bitcast.23, ...), custom_call_target="tpu_custom_call" | custom-call | tf_op jit(solution)/shard_map/finish/pallas_call | solution.py:529
  89.0 0.3 collective-permute-start.6
  89.4 0.7 collective-permute-start.7
  90.0 0.8 centre.1
  90.9 1.1 collective-permute-start.8
  92.1 0.8 collective-permute-start.9
  92.9 2.5 %inner.1 = (f32[3,16,2,32,128]{4,3,2,1,0:T(8,128)S(1)}, bf16[96,64,128]{2,1,0:T(8,128)(2,1)S(1)}, bf16[17,2,96,384]{3,2,1,0:T(8,128)(2,1)S(1)}) custom-call(s32[96]{0:T(128)S(1)} %pad_add_fusion.source.routes, bf16[96,128]{1,0:T(8,128)(2,1)S(1)} %collective-permute-done.6.near_a, ...), custom_call_target="tpu_custom_call", output_to_operand_aliasing={{1}: (5, {}), {2}: (6, {})} | custom-call | flops 570425344 | bytes 4194304 | tf_op jit(solution)/shard_map/inner/pallas_call | solution.py:514
  95.4 3.7 %outer.3 = (f32[3,16,2,32,128]{4,3,2,1,0:T(8,128)S(1)}, bf16[96,64,128]{2,1,0:T(8,128)(2,1)S(1)}, bf16[17,2,96,384]{3,2,1,0:T(8,128)(2,1)S(1)}) custom-call(s32[96]{0:T(128)S(1)} %pad_add_fusion.source.routes, f32[48,128]{1,0:T(8,128)S(1)} %collective-permute-done.8.near_a, ...), custom_call_target="tpu_custom_call", output_to_operand_aliasing={{0}: (5, {}), {1}: (6, {}), {2}: (7, {})} | custom-call | flops 1140850688 | bytes 4194304 | tf_op jit(solution)/shard_map/outer/pallas_call | solution.py:515
  99.1 30.6 %all_to_all.22 = bf16[16,6,64,128]{3,2,1,0:T(8,128)(2,1)S(1)} all-to-all(bf16[16,6,64,128]{3,2,1,0:T(8,128)(2,1)S(1)} %bitcast.22), channel_id=1, replica_groups=mesh['row'=4,'zh'=2,'zl'=2,'x'=2] {'row','zl','x'}, dimensions={0} | all-to-all | bytes 3145728 | tf_op jit(solution)/shard_map/all_to_all | solution.py:490
  129.7 1.0 combine.3
  130.7 0.3 collective-permute-start.10
  131.0 14.8 %collective-permute-done.10.other = bf16[16,64,128]{2,1,0:T(8,128)(2,1)S(1)} collective-permute-done((bf16[16,64,128]{2,1,0:T(8,128)(2,1)S(1)}, bf16[16,64,128]{2,1,0:T(8,128)(2,1)S(1)}, u32[]{:S(2)}, u32[]{:S(2)}) %collective-permute-start.10) | collective-permute-done | bytes 262176 | tf_op jit(solution)/shard_map/ppermute | solution.py:312
  145.7 0.8 reply.3
  146.5 23.2 %all_to_all.23 = bf16[16,6,64,128]{3,2,1,0:T(8,128)(2,1)S(1)} all-to-all(bf16[16,6,64,128]{3,2,1,0:T(8,128)(2,1)S(1)} %bitcast.24), channel_id=1, replica_groups=mesh['row'=4,'zh'=2,'zl'=2,'x'=2] {'row','zl','x'}, dimensions={0} | all-to-all | bytes 3145728 | tf_op jit(solution)/shard_map/all_to_all | solution.py:490
  169.7 2.6 %finish.3 = f32[32,96,128]{2,1,0:T(8,128)} custom-call(s32[96]{0:T(128)S(1)} %pad_add_fusion.source.routes, bf16[96,64,128]{2,1,0:T(8,128)(2,1)S(1)} %bitcast.29, f32[3,16,2,32,128]{4,3,2,1,0:T(8,128)S(1)} %get-tuple-element.80.pulled, bf16[32,96,128]{2,1,0:T(8,128)(2,1)S(1)} %copy-done.2, bf16[32,96,128]{2,1,0:T(8,128)(2,1)S(1)} %copy-done.1, ...), custom_call_target="tpu_custom_call" | custom-call | tf_op jit(solution)/shard_map/finish/pallas_call | solution.py:529
  (50 shorter events, 1.2 us)
Async XLA Ops:
  0.0 3.0 %copy-start.5 = (s32[4,24,16]{1,2,0:T(8,128)S(1)}, s32[4,24,16]{1,2,0:T(8,128)}, u32[]{:S(2)}) copy-start(s32[4,24,16]{1,2,0:T(8,128)} %param.14) | copy-start | bytes 18436
  0.0 3.2 %copy-start.6 = (s32[256]{0:T(256)S(1)}, s32[256]{0:T(256)}, u32[]{:S(2)}) copy-start(s32[256]{0:T(256)} %param.16) | copy-start | bytes 3076
  0.0 3.8 %copy-start.7 = (s32[1,3,16]{2,0,1:T(1,128)S(1)}, s32[1,3,16]{2,0,1:T(1,128)}, u32[]{:S(2)}) copy-start(s32[1,3,16]{2,0,1:T(1,128)} %param.15) | copy-start | bytes 580
  0.0 3.9 %copy-start.8 = (s32[8]{0:T(128)S(1)}, s32[8]{0:T(128)}, u32[]{:S(2)}) copy-start(s32[8]{0:T(128)} %param.17) | copy-start | bytes 100
  0.0 5.3 %copy-start.3 = (f32[8,64,128]{2,1,0:T(8,128)S(1)}, f32[8,64,128]{2,1,0:T(8,128)}, u32[]{:S(2)}) copy-start(f32[8,64,128]{2,1,0:T(8,128)} %own_weight.3) | copy-start | bytes 786436
  1.8 3.6 %collective-permute-start = (bf16[96,128]{1,0:T(8,128)(2,1)S(1)}, bf16[96,128]{1,0:T(8,128)(2,1)S(1)}, u32[]{:S(2)}, u32[]{:S(2)}) collective-permute-start(bf16[96,128]{1,0:T(8,128)(2,1)S(1)} %get-tuple-element.43), channel_id=1, source_target_pairs={{0,8},{8,0},{16,24},{24,16},{1,9},{9,1},{17,25},{25,17},{2,10},{10... | collective-permute-start | bytes 73736 | tf_op jit(solution)/shard_map/ppermute | solution.py:497
  2.3 3.1 %collective-permute-start.1 = (bf16[96,128]{1,0:T(8,128)(2,1)S(1)}, bf16[96,128]{1,0:T(8,128)(2,1)S(1)}, u32[]{:S(2)}, u32[]{:S(2)}) collective-permute-start(bf16[96,128]{1,0:T(8,128)(2,1)S(1)} %get-tuple-element.44), channel_id=1, source_target_pairs={{8,16},{16,8},{9,17},{17,9},{10,18},{18,10},{11,19},{19,11},{12,20... | collective-permute-start | bytes 73736 | tf_op jit(solution)/shard_map/ppermute | solution.py:497
  5.4 8.9 %copy-start = (bf16[8,4,64,1024]{3,2,1,0:T(8,128)(2,1)S(1)}, bf16[8,4,64,1024]{3,2,1,0:T(8,128)(2,1)}, u32[]{:S(2)}) copy-start(bf16[8,4,64,1024]{3,2,1,0:T(8,128)(2,1)} %param.12) | copy-start | bytes 12582916
  5.4 8.9 %copy-start.4 = (bf16[3,3,128,128]{3,2,1,0:T(8,128)(2,1)S(1)}, bf16[3,3,128,128]{3,2,1,0:T(8,128)(2,1)}, u32[]{:S(2)}) copy-start(bf16[3,3,128,128]{3,2,1,0:T(8,128)(2,1)} %kernel.3) | copy-start | bytes 884740
  5.5 11.7 %collective-permute-start.3 = (f32[48,128]{1,0:T(8,128)S(1)}, f32[48,128]{1,0:T(8,128)S(1)}, u32[]{:S(2)}, u32[]{:S(2)}) collective-permute-start(f32[48,128]{1,0:T(8,128)S(1)} %get-tuple-element.49), channel_id=1, source_target_pairs={{1,2},{2,1},{3,4},{4,3},{5,6},{6,5},{9,10},{10,9},{11,12},{12,11},... | collective-permute-start | bytes 73736 | tf_op jit(solution)/shard_map/ppermute | solution.py:497
  6.3 10.9 %collective-permute-start.2 = (f32[48,128]{1,0:T(8,128)S(1)}, f32[48,128]{1,0:T(8,128)S(1)}, u32[]{:S(2)}, u32[]{:S(2)}) collective-permute-start(f32[48,128]{1,0:T(8,128)S(1)} %get-tuple-element.47), channel_id=1, source_target_pairs={{0,1},{1,0},{2,3},{3,2},{4,5},{5,4},{6,7},{7,6},{8,9},{9,8},{10,11... | collective-permute-start | bytes 73736 | tf_op jit(solution)/shard_map/ppermute | solution.py:497
  11.8 9.1 %collective-permute-start.4 = (bf16[8,64,128]{2,1,0:T(8,128)(2,1)S(1)}, bf16[8,64,128]{2,1,0:T(8,128)(2,1)S(1)}, u32[]{:S(2)}, u32[]{:S(2)}) collective-permute-start(bf16[8,64,128]{2,1,0:T(8,128)(2,1)S(1)} %convert_element_type.8), channel_id=1, source_target_pairs={{0,4},{4,0},{1,5},{5,1},{2,6},{6,2},{3,7},{7,3},{8,12},{12,8},{9,1... | collective-permute-start | bytes 393224 | tf_op jit(solution)/shard_map/ppermute | solution.py:312
  48.0 15.0 %collective-permute-start.5 = (bf16[16,64,128]{2,1,0:T(8,128)(2,1)S(1)}, bf16[16,64,128]{2,1,0:T(8,128)(2,1)S(1)}, u32[]{:S(2)}, u32[]{:S(2)}) collective-permute-start(bf16[16,64,128]{2,1,0:T(8,128)(2,1)S(1)} %get-tuple-element.61), channel_id=1, source_target_pairs={{0,4},{4,0},{1,5},{5,1},{2,6},{6,2},{3,7},{7,3},{8,12},{12,8},{9,1... | collective-permute-start | bytes 786440 | tf_op jit(solution)/shard_map/ppermute | solution.py:312
  63.8 23.3 %copy-start.1 = (bf16[32,96,128]{2,1,0:T(8,128)(2,1)S(1)}, bf16[32,96,128]{2,1,0:T(8,128)(2,1)}, u32[]{:S(2)}) copy-start(bf16[32,96,128]{2,1,0:T(8,128)(2,1)} %state.5) | copy-start | bytes 2359300
  63.9 23.3 %copy-start.2 = (bf16[32,96,128]{2,1,0:T(8,128)(2,1)S(1)}, bf16[32,96,128]{2,1,0:T(8,128)(2,1)}, u32[]{:S(2)}) copy-start(bf16[32,96,128]{2,1,0:T(8,128)(2,1)} %grad.5) | copy-start | bytes 2359300
  89.0 1.8 %collective-permute-start.6 = (bf16[96,128]{1,0:T(8,128)(2,1)S(1)}, bf16[96,128]{1,0:T(8,128)(2,1)S(1)}, u32[]{:S(2)}, u32[]{:S(2)}) collective-permute-start(bf16[96,128]{1,0:T(8,128)(2,1)S(1)} %get-tuple-element.64), channel_id=1, source_target_pairs={{0,8},{8,0},{16,24},{24,16},{1,9},{9,1},{17,25},{25,17},{2,10},{10... | collective-permute-start | bytes 73736 | tf_op jit(solution)/shard_map/ppermute | solution.py:497
  89.4 1.5 collective-permute-start.7
  90.9 4.5 %collective-permute-start.8 = (f32[48,128]{1,0:T(8,128)S(1)}, f32[48,128]{1,0:T(8,128)S(1)}, u32[]{:S(2)}, u32[]{:S(2)}) collective-permute-start(f32[48,128]{1,0:T(8,128)S(1)} %get-tuple-element.68), channel_id=1, source_target_pairs={{0,1},{1,0},{2,3},{3,2},{4,5},{5,4},{6,7},{7,6},{8,9},{9,8},{10,11... | collective-permute-start | bytes 73736 | tf_op jit(solution)/shard_map/ppermute | solution.py:497
  92.1 3.3 %collective-permute-start.9 = (f32[48,128]{1,0:T(8,128)S(1)}, f32[48,128]{1,0:T(8,128)S(1)}, u32[]{:S(2)}, u32[]{:S(2)}) collective-permute-start(f32[48,128]{1,0:T(8,128)S(1)} %get-tuple-element.69), channel_id=1, source_target_pairs={{1,2},{2,1},{3,4},{4,3},{5,6},{6,5},{9,10},{10,9},{11,12},{12,11},... | collective-permute-start | bytes 73736 | tf_op jit(solution)/shard_map/ppermute | solution.py:497
  130.7 15.0 %collective-permute-start.10 = (bf16[16,64,128]{2,1,0:T(8,128)(2,1)S(1)}, bf16[16,64,128]{2,1,0:T(8,128)(2,1)S(1)}, u32[]{:S(2)}, u32[]{:S(2)}) collective-permute-start(bf16[16,64,128]{2,1,0:T(8,128)(2,1)S(1)} %get-tuple-element.79), channel_id=1, source_target_pairs={{0,4},{4,0},{1,5},{5,1},{2,6},{6,2},{3,7},{7,3},{8,12},{12,8},{9,1... | collective-permute-start | bytes 786440 | tf_op jit(solution)/shard_map/ppermute | solution.py:312

commit v16 on v14

--- a/solution.py
+++ b/solution.py
@@ -149,12 +149,16 @@
     wide[1 : rows + 1, 8 : 8 + cols, :] = scaled[...].astype(f32)
     wide[:, 0:8, :] = jnp.zeros((rows + 2, 8, chans), f32)
     wide[:, 8 + cols :, :] = jnp.zeros((rows + 2, 8, chans), f32)
-    for dc in range(3):
+    for dc in (0, 2):
         value = wide[:, 7 + dc : 7 + dc + cols, :].astype(bf16)
         cols3[:, :, :, dc * chans : (dc + 1) * chans] = value.reshape(
             (rows + 2) // 2, 2, cols, chans
         )
-    out[...] = jnp.zeros_like(out)
+    middle = slice(chans, 2 * chans)
+    cols3[0, 0, :, middle] = pick(0, a, b).astype(bf16)
+    cols3[(rows + 1) // 2, (rows + 1) % 2, :, middle] = pick(0, b, a).astype(bf16)
+    for r in range(1, rows + 1):
+        cols3[r // 2, r % 2, :, middle] = scaled[r - 1]
     coming.wait()
     for t in tiles_at(pulled.shape[0], tile_cols, True):
         forward_tile(routes, taps, rays, pulled, out, cols3, t, tile_cols)

time: 173 us -> 172 us (level)
  transfers between devices with their start and end apart: 11 -> 11, of which waited for: 3 -> 4; matrix products, arithmetic and copies ran while one was open for 1% -> 1% of each run, Pallas kernels for 5% -> 5%
where the time goes in v16:
time: 172 us
  blocking collectives  103 us (60%)
  waiting for transfers between devices  29.1 us (17%)
  Pallas kernels  22.4 us (13%)
  starting transfers between devices  14.4 us (8%)
    all_to_all x4, blocking collectives, across(): lax.all_to_all(value, GROUP, split_axis=0, concat_axis=0, tiled=True)  103 us
    ppermute x3, waiting for transfers between devices, exchange(): return lax.ppermute(value, 'zh', [(0, 1), (1, 0)])  28.8 us
    ppermute x4, starting transfers between devices, swaps(): lax.ppermute(value_a, axis, even)  7.77 us
    pallas_call x2, Pallas kernels, forward(): pulled, outgoing, _ = outer(routes, *beside, taps, rays, *parts)  7.44 us
    pallas_call x2, Pallas kernels, forward(): *parts, taps = inner(routes, scaled, *above, kernel, rays)  5.23 us
    pallas_call x2, Pallas kernels, on_device(): finish(last)(routes, across(replies), pulled, grad, state, rays)  4.44 us
    ppermute x3, starting transfers between devices, exchange(): return lax.ppermute(value, 'zh', [(0, 1), (1, 0)])  3.9 us
  transfers between devices with their start and end apart: 11, of which 4 were waited for; matrix products, arithmetic and copies ran while one was open for 1% of the time, Pallas kernels for 5%

profile of v16, /device:TPU:0, one launch (start us, length us, event | category | flops | bytes accessed | tf_op | source)
XLA Modules:
  0.0 172.1 jit_solution(7204892063443785106)
XLA Ops:
  0.0 1.7 %start.1 = (bf16[32,96,128]{2,1,0:T(8,128)(2,1)S(1)}, bf16[96,128]{1,0:T(8,128)(2,1)S(1)}, bf16[96,128]{1,0:T(8,128)(2,1)S(1)}, f32[32,128]{1,0:T(8,128)S(1)}, f32[32,128]{1,0:T(8,128)S(1)}) custom-call(bf16[32,96,128]{2,1,0:T(8,128)(2,1)} %state.5, bf16[32,96,128]{2,1,0:T(8,128)(2,1)} %grad.5), custom_call_target="tpu_custom_call" | custom-call | tf_op jit(solution)/shard_map/start/pallas_call | solution.py:475
  1.8 0.6 collective-permute-start
  2.3 0.7 collective-permute-start.1
  3.2 0.5 select_reduce_fusion
  4.1 0.5 convert_reduce_fusion
  4.8 0.2 and_reduce_fusion
  5.5 0.8 collective-permute-start.3
  6.3 5.5 %collective-permute-start.2 = (f32[48,128]{1,0:T(8,128)S(1)}, f32[48,128]{1,0:T(8,128)S(1)}, u32[]{:S(2)}, u32[]{:S(2)}) collective-permute-start(f32[48,128]{1,0:T(8,128)S(1)} %get-tuple-element.45), channel_id=1, source_target_pairs={{0,1},{1,0},{2,3},{3,2},{4,5},{5,4},{6,7},{7,6},{8,9},{9,8},{10,11... | collective-permute-start | bytes 73736 | tf_op jit(solution)/shard_map/ppermute | solution.py:458
  11.8 2.6 %collective-permute-start.4 = (bf16[8,64,128]{2,1,0:T(8,128)(2,1)S(1)}, bf16[8,64,128]{2,1,0:T(8,128)(2,1)S(1)}, u32[]{:S(2)}, u32[]{:S(2)}) collective-permute-start(bf16[8,64,128]{2,1,0:T(8,128)(2,1)S(1)} %convert_element_type.8), channel_id=1, source_target_pairs={{0,4},{4,0},{1,5},{5,1},{2,6},{6,2},{3,7},{7,3},{8,12},{12,8},{9,1... | collective-permute-start | bytes 393224 | tf_op jit(solution)/shard_map/ppermute | solution.py:296
  14.3 2.6 %inner.2 = (f32[3,16,2,32,128]{4,3,2,1,0:T(8,128)S(1)}, bf16[96,64,128]{2,1,0:T(8,128)(2,1)S(1)}, bf16[17,2,96,384]{3,2,1,0:T(8,128)(2,1)S(1)}, bf16[1536,256]{1,0:T(8,128)(2,1)S(1)}) custom-call(s32[96]{0:T(128)S(1)} %pad_add_fusion.source.routes, bf16[32,96,128]{2,1,0:T(8,128)(2,1)S(1)} %get-tuple-element.48.scaled, ...), custom_call_target="tpu_custom_call" | custom-call | flops 570425344 | bytes 4194304 | tf_op jit(solution)/shard_map/inner/pallas_call | solution.py:471
  17.0 3.7 %outer.2 = (f32[3,16,2,32,128]{4,3,2,1,0:T(8,128)S(1)}, bf16[96,64,128]{2,1,0:T(8,128)(2,1)S(1)}, bf16[17,2,96,384]{3,2,1,0:T(8,128)(2,1)S(1)}) custom-call(s32[96]{0:T(128)S(1)} %pad_add_fusion.source.routes, f32[48,128]{1,0:T(8,128)S(1)} %collective-permute-done.2.near_a, ...), custom_call_target="tpu_custom_call", output_to_operand_aliasing={{0}: (5, {}), {1}: (6, {}), {2}: (7, {})} | custom-call | flops 1140850688 | bytes 4194304 | tf_op jit(solution)/shard_map/outer/pallas_call | solution.py:472
  20.8 26.0 %all_to_all.20 = bf16[16,6,64,128]{3,2,1,0:T(8,128)(2,1)S(1)} all-to-all(bf16[16,6,64,128]{3,2,1,0:T(8,128)(2,1)S(1)} %bitcast.27), channel_id=1, replica_groups=mesh['row'=4,'zh'=2,'zl'=2,'x'=2] {'row','zl','x'}, dimensions={0} | all-to-all | bytes 3145728 | tf_op jit(solution)/shard_map/all_to_all | solution.py:451
  46.9 1.0 combine.2
  47.8 0.9 collective-permute-start.5
  48.7 14.2 %collective-permute-done.5.other = bf16[16,64,128]{2,1,0:T(8,128)(2,1)S(1)} collective-permute-done((bf16[16,64,128]{2,1,0:T(8,128)(2,1)S(1)}, bf16[16,64,128]{2,1,0:T(8,128)(2,1)S(1)}, u32[]{:S(2)}, u32[]{:S(2)}) %collective-permute-start.5) | collective-permute-done | bytes 262176 | tf_op jit(solution)/shard_map/ppermute | solution.py:296
  62.9 0.8 reply.2
  63.7 23.3 %all_to_all.21 = bf16[16,6,64,128]{3,2,1,0:T(8,128)(2,1)S(1)} all-to-all(bf16[16,6,64,128]{3,2,1,0:T(8,128)(2,1)S(1)} %bitcast.26), channel_id=1, replica_groups=mesh['row'=4,'zh'=2,'zl'=2,'x'=2] {'row','zl','x'}, dimensions={0} | all-to-all | bytes 3145728 | tf_op jit(solution)/shard_map/all_to_all | solution.py:451
  87.0 1.9 %finish.2 = (bf16[32,96,128]{2,1,0:T(8,128)(2,1)S(1)}, bf16[96,128]{1,0:T(8,128)(2,1)S(1)}, bf16[96,128]{1,0:T(8,128)(2,1)S(1)}, f32[32,128]{1,0:T(8,128)S(1)}, f32[32,128]{1,0:T(8,128)S(1)}) custom-call(s32[96]{0:T(128)S(1)} %pad_add_fusion.source.routes, bf16[96,64,128]{2,1,0:T(8,128)(2,1)S(1)} %bitcast.22, ...), custom_call_target="tpu_custom_call" | custom-call | tf_op jit(solution)/shard_map/finish/pallas_call | solution.py:486
  88.9 0.3 collective-permute-start.6
  89.2 0.7 collective-permute-start.7
  89.9 0.3 collective-permute-done.6.near_a
  90.2 1.4 collective-permute-start.8
  91.5 0.7 collective-permute-start.9
  92.2 2.6 %inner.3 = (f32[3,16,2,32,128]{4,3,2,1,0:T(8,128)S(1)}, bf16[96,64,128]{2,1,0:T(8,128)(2,1)S(1)}, bf16[17,2,96,384]{3,2,1,0:T(8,128)(2,1)S(1)}, bf16[1536,256]{1,0:T(8,128)(2,1)S(1)}) custom-call(s32[96]{0:T(128)S(1)} %pad_add_fusion.source.routes, bf16[32,96,128]{2,1,0:T(8,128)(2,1)S(1)} %get-tuple-element.68.scaled, ...), custom_call_target="tpu_custom_call" | custom-call | flops 570425344 | bytes 4194304 | tf_op jit(solution)/shard_map/inner/pallas_call | solution.py:471
  94.8 3.7 %outer.3 = (f32[3,16,2,32,128]{4,3,2,1,0:T(8,128)S(1)}, bf16[96,64,128]{2,1,0:T(8,128)(2,1)S(1)}, bf16[17,2,96,384]{3,2,1,0:T(8,128)(2,1)S(1)}) custom-call(s32[96]{0:T(128)S(1)} %pad_add_fusion.source.routes, f32[48,128]{1,0:T(8,128)S(1)} %collective-permute-done.8.near_a, ...), custom_call_target="tpu_custom_call", output_to_operand_aliasing={{0}: (5, {}), {1}: (6, {}), {2}: (7, {})} | custom-call | flops 1140850688 | bytes 4194304 | tf_op jit(solution)/shard_map/outer/pallas_call | solution.py:472
  98.6 31.0 %all_to_all.22 = bf16[16,6,64,128]{3,2,1,0:T(8,128)(2,1)S(1)} all-to-all(bf16[16,6,64,128]{3,2,1,0:T(8,128)(2,1)S(1)} %bitcast.28), channel_id=1, replica_groups=mesh['row'=4,'zh'=2,'zl'=2,'x'=2] {'row','zl','x'}, dimensions={0} | all-to-all | bytes 3145728 | tf_op jit(solution)/shard_map/all_to_all | solution.py:451
  129.5 1.0 combine.3
  130.5 0.5 collective-permute-start.10
  131.0 14.6 %collective-permute-done.10.other = bf16[16,64,128]{2,1,0:T(8,128)(2,1)S(1)} collective-permute-done((bf16[16,64,128]{2,1,0:T(8,128)(2,1)S(1)}, bf16[16,64,128]{2,1,0:T(8,128)(2,1)S(1)}, u32[]{:S(2)}, u32[]{:S(2)}) %collective-permute-start.10) | collective-permute-done | bytes 262176 | tf_op jit(solution)/shard_map/ppermute | solution.py:296
  145.5 0.8 reply.3
  146.3 23.2 %all_to_all.23 = bf16[16,6,64,128]{3,2,1,0:T(8,128)(2,1)S(1)} all-to-all(bf16[16,6,64,128]{3,2,1,0:T(8,128)(2,1)S(1)} %bitcast.23), channel_id=1, replica_groups=mesh['row'=4,'zh'=2,'zl'=2,'x'=2] {'row','zl','x'}, dimensions={0} | all-to-all | bytes 3145728 | tf_op jit(solution)/shard_map/all_to_all | solution.py:451
  169.5 2.6 %finish.3 = f32[32,96,128]{2,1,0:T(8,128)} custom-call(s32[96]{0:T(128)S(1)} %pad_add_fusion.source.routes, bf16[96,64,128]{2,1,0:T(8,128)(2,1)S(1)} %bitcast.29, f32[3,16,2,32,128]{4,3,2,1,0:T(8,128)S(1)} %get-tuple-element.76.pulled, bf16[32,96,128]{2,1,0:T(8,128)(2,1)S(1)} %copy-done.2, bf16[32,96,128]{2,1,0:T(8,128)(2,1)S(1)} %copy-done.1, ...), custom_call_target="tpu_custom_call" | custom-call | tf_op jit(solution)/shard_map/finish/pallas_call | solution.py:486
  (49 shorter events, 1.3 us)
Async XLA Ops:
  0.0 3.0 %copy-start.5 = (s32[4,24,16]{1,2,0:T(8,128)S(1)}, s32[4,24,16]{1,2,0:T(8,128)}, u32[]{:S(2)}) copy-start(s32[4,24,16]{1,2,0:T(8,128)} %param.14) | copy-start | bytes 18436
  0.0 3.2 %copy-start.6 = (s32[256]{0:T(256)S(1)}, s32[256]{0:T(256)}, u32[]{:S(2)}) copy-start(s32[256]{0:T(256)} %param.16) | copy-start | bytes 3076
  0.0 3.8 %copy-start.7 = (s32[1,3,16]{2,0,1:T(1,128)S(1)}, s32[1,3,16]{2,0,1:T(1,128)}, u32[]{:S(2)}) copy-start(s32[1,3,16]{2,0,1:T(1,128)} %param.15) | copy-start | bytes 580
  0.0 3.9 %copy-start.8 = (s32[8]{0:T(128)S(1)}, s32[8]{0:T(128)}, u32[]{:S(2)}) copy-start(s32[8]{0:T(128)} %param.17) | copy-start | bytes 100
  0.0 5.3 %copy-start.3 = (f32[8,64,128]{2,1,0:T(8,128)S(1)}, f32[8,64,128]{2,1,0:T(8,128)}, u32[]{:S(2)}) copy-start(f32[8,64,128]{2,1,0:T(8,128)} %own_weight.3) | copy-start | bytes 786436
  1.8 3.6 %collective-permute-start = (bf16[96,128]{1,0:T(8,128)(2,1)S(1)}, bf16[96,128]{1,0:T(8,128)(2,1)S(1)}, u32[]{:S(2)}, u32[]{:S(2)}) collective-permute-start(bf16[96,128]{1,0:T(8,128)(2,1)S(1)} %get-tuple-element.41), channel_id=1, source_target_pairs={{0,8},{8,0},{16,24},{24,16},{1,9},{9,1},{17,25},{25,17},{2,10},{10... | collective-permute-start | bytes 73736 | tf_op jit(solution)/shard_map/ppermute | solution.py:458
  2.3 3.1 %collective-permute-start.1 = (bf16[96,128]{1,0:T(8,128)(2,1)S(1)}, bf16[96,128]{1,0:T(8,128)(2,1)S(1)}, u32[]{:S(2)}, u32[]{:S(2)}) collective-permute-start(bf16[96,128]{1,0:T(8,128)(2,1)S(1)} %get-tuple-element.42), channel_id=1, source_target_pairs={{8,16},{16,8},{9,17},{17,9},{10,18},{18,10},{11,19},{19,11},{12,20... | collective-permute-start | bytes 73736 | tf_op jit(solution)/shard_map/ppermute | solution.py:458
  5.4 8.9 %copy-start = (bf16[8,4,64,1024]{3,2,1,0:T(8,128)(2,1)S(1)}, bf16[8,4,64,1024]{3,2,1,0:T(8,128)(2,1)}, u32[]{:S(2)}) copy-start(bf16[8,4,64,1024]{3,2,1,0:T(8,128)(2,1)} %param.12) | copy-start | bytes 12582916
  5.4 8.9 %copy-start.4 = (bf16[3,3,128,128]{3,2,1,0:T(8,128)(2,1)S(1)}, bf16[3,3,128,128]{3,2,1,0:T(8,128)(2,1)}, u32[]{:S(2)}) copy-start(bf16[3,3,128,128]{3,2,1,0:T(8,128)(2,1)} %kernel.3) | copy-start | bytes 884740
  5.5 11.5 %collective-permute-start.3 = (f32[48,128]{1,0:T(8,128)S(1)}, f32[48,128]{1,0:T(8,128)S(1)}, u32[]{:S(2)}, u32[]{:S(2)}) collective-permute-start(f32[48,128]{1,0:T(8,128)S(1)} %get-tuple-element.47), channel_id=1, source_target_pairs={{1,2},{2,1},{3,4},{4,3},{5,6},{6,5},{9,10},{10,9},{11,12},{12,11},... | collective-permute-start | bytes 73736 | tf_op jit(solution)/shard_map/ppermute | solution.py:458
  6.3 10.7 %collective-permute-start.2 = (f32[48,128]{1,0:T(8,128)S(1)}, f32[48,128]{1,0:T(8,128)S(1)}, u32[]{:S(2)}, u32[]{:S(2)}) collective-permute-start(f32[48,128]{1,0:T(8,128)S(1)} %get-tuple-element.45), channel_id=1, source_target_pairs={{0,1},{1,0},{2,3},{3,2},{4,5},{5,4},{6,7},{7,6},{8,9},{9,8},{10,11... | collective-permute-start | bytes 73736 | tf_op jit(solution)/shard_map/ppermute | solution.py:458
  11.8 9.1 %collective-permute-start.4 = (bf16[8,64,128]{2,1,0:T(8,128)(2,1)S(1)}, bf16[8,64,128]{2,1,0:T(8,128)(2,1)S(1)}, u32[]{:S(2)}, u32[]{:S(2)}) collective-permute-start(bf16[8,64,128]{2,1,0:T(8,128)(2,1)S(1)} %convert_element_type.8), channel_id=1, source_target_pairs={{0,4},{4,0},{1,5},{5,1},{2,6},{6,2},{3,7},{7,3},{8,12},{12,8},{9,1... | collective-permute-start | bytes 393224 | tf_op jit(solution)/shard_map/ppermute | solution.py:296
  47.8 15.0 %collective-permute-start.5 = (bf16[16,64,128]{2,1,0:T(8,128)(2,1)S(1)}, bf16[16,64,128]{2,1,0:T(8,128)(2,1)S(1)}, u32[]{:S(2)}, u32[]{:S(2)}) collective-permute-start(bf16[16,64,128]{2,1,0:T(8,128)(2,1)S(1)} %get-tuple-element.59), channel_id=1, source_target_pairs={{0,4},{4,0},{1,5},{5,1},{2,6},{6,2},{3,7},{7,3},{8,12},{12,8},{9,1... | collective-permute-start | bytes 786440 | tf_op jit(solution)/shard_map/ppermute | solution.py:296
  63.7 23.3 %copy-start.1 = (bf16[32,96,128]{2,1,0:T(8,128)(2,1)S(1)}, bf16[32,96,128]{2,1,0:T(8,128)(2,1)}, u32[]{:S(2)}) copy-start(bf16[32,96,128]{2,1,0:T(8,128)(2,1)} %state.5) | copy-start | bytes 2359300
  63.7 23.3 %copy-start.2 = (bf16[32,96,128]{2,1,0:T(8,128)(2,1)S(1)}, bf16[32,96,128]{2,1,0:T(8,128)(2,1)}, u32[]{:S(2)}) copy-start(bf16[32,96,128]{2,1,0:T(8,128)(2,1)} %grad.5) | copy-start | bytes 2359300
  88.9 1.3 collective-permute-start.6
  89.2 0.9 collective-permute-start.7
  90.2 4.7 %collective-permute-start.8 = (f32[48,128]{1,0:T(8,128)S(1)}, f32[48,128]{1,0:T(8,128)S(1)}, u32[]{:S(2)}, u32[]{:S(2)}) collective-permute-start(f32[48,128]{1,0:T(8,128)S(1)} %get-tuple-element.66), channel_id=1, source_target_pairs={{0,1},{1,0},{2,3},{3,2},{4,5},{5,4},{6,7},{7,6},{8,9},{9,8},{10,11... | collective-permute-start | bytes 73736 | tf_op jit(solution)/shard_map/ppermute | solution.py:458
  91.5 3.3 %collective-permute-start.9 = (f32[48,128]{1,0:T(8,128)S(1)}, f32[48,128]{1,0:T(8,128)S(1)}, u32[]{:S(2)}, u32[]{:S(2)}) collective-permute-start(f32[48,128]{1,0:T(8,128)S(1)} %get-tuple-element.67), channel_id=1, source_target_pairs={{1,2},{2,1},{3,4},{4,3},{5,6},{6,5},{9,10},{10,9},{11,12},{12,11},... | collective-permute-start | bytes 73736 | tf_op jit(solution)/shard_map/ppermute | solution.py:458
  130.5 15.0 %collective-permute-start.10 = (bf16[16,64,128]{2,1,0:T(8,128)(2,1)S(1)}, bf16[16,64,128]{2,1,0:T(8,128)(2,1)S(1)}, u32[]{:S(2)}, u32[]{:S(2)}) collective-permute-start(bf16[16,64,128]{2,1,0:T(8,128)(2,1)S(1)} %get-tuple-element.75), channel_id=1, source_target_pairs={{0,4},{4,0},{1,5},{5,1},{2,6},{6,2},{3,7},{7,3},{8,12},{12,8},{9,1... | collective-permute-start | bytes 786440 | tf_op jit(solution)/shard_map/ppermute | solution.py:296

commit v17 on v16

--- a/solution.py
+++ b/solution.py
@@ -40,8 +40,10 @@
             load(a, p).wait()
         where = slice(p * rows, (p + 1) * rows)
         value = states[where].astype(jnp.float32)
-        whole[where] = (1.0 - value * value) * grads[where].astype(jnp.float32)
-    emit_edges(whole[...], scaled, row_a, row_b, col_a, col_b)
+        value = (1.0 - value * value) * grads[where].astype(jnp.float32)
+        whole[where] = value
+        scaled[where] = value.astype(jnp.bfloat16)
+    emit_edges(whole, row_a, row_b, col_a, col_b)
 
 
 def bring(source, held, mark):
@@ -60,9 +62,8 @@
     return jnp.where(parity(dim) == 1, yes, no)
 
 
-def emit_edges(value, scaled, row_a, row_b, col_a, col_b):
+def emit_edges(value, row_a, row_b, col_a, col_b):
     rows, cols = value.shape[:2]
-    scaled[...] = value.astype(jnp.bfloat16)
     row_a[...] = pick(0, value[0], value[rows - 1]).astype(jnp.bfloat16)
     row_b[...] = pick(0, value[rows - 1], value[0]).astype(jnp.bfloat16)
     left, right = value[:, 0, :], value[:, cols - 1, :]
@@ -262,12 +263,14 @@
             leave(t).start()
         else:
             value = state[where].astype(f32)
-            whole[where] = (1.0 - value * value) * adjoint
+            value = (1.0 - value * value) * adjoint
+            whole[where] = value
+            outs[0][where] = value.astype(jnp.bfloat16)
     if last:
         for t in range(tiles):
             leave(t).wait()
     else:
-        emit_edges(whole[...], *outs)
+        emit_edges(whole, *outs[1:])
 
 
 def on_device(state, grad, kernel, ray_matrix, ray_weight, hits, offsets, block_slot, angle_count):

time: 172 us -> 172 us (level)
  no operation moved by 1% of the time
where the time goes in v17:
time: 172 us
  blocking collectives  103 us (60%)
  waiting for transfers between devices  29.1 us (17%)
  Pallas kernels  22.4 us (13%)
  starting transfers between devices  14.4 us (8%)
    all_to_all x4, blocking collectives, across(): lax.all_to_all(value, GROUP, split_axis=0, concat_axis=0, tiled=True)  103 us
    ppermute x3, waiting for transfers between devices, exchange(): return lax.ppermute(value, 'zh', [(0, 1), (1, 0)])  28.9 us
    ppermute x4, starting transfers between devices, swaps(): lax.ppermute(value_a, axis, even)  7.78 us
    pallas_call x2, Pallas kernels, forward(): pulled, outgoing, _ = outer(routes, *beside, taps, rays, *parts)  7.44 us
    pallas_call x2, Pallas kernels, forward(): *parts, taps = inner(routes, scaled, *above, kernel, rays)  5.23 us
    pallas_call x2, Pallas kernels, on_device(): finish(last)(routes, across(replies), pulled, grad, state, rays)  4.44 us
    ppermute x3, starting transfers between devices, exchange(): return lax.ppermute(value, 'zh', [(0, 1), (1, 0)])  3.88 us
  transfers between devices with their start and end apart: 11, of which 4 were waited for; matrix products, arithmetic and copies ran while one was open for 1% of the time, Pallas kernels for 5%

profile of v17, /device:TPU:0, one launch (start us, length us, event | category | flops | bytes accessed | tf_op | source)
XLA Modules:
  0.0 172.1 jit_solution(5122018292254678603)
XLA Ops:
  0.0 1.7 start.1
  1.7 0.6 collective-permute-start
  2.3 0.7 collective-permute-start.1
  3.2 0.5 select_reduce_fusion
  4.1 0.5 convert_reduce_fusion
  4.8 0.2 and_reduce_fusion
  5.4 0.8 collective-permute-start.3
  6.2 5.5 %collective-permute-start.2 = (f32[48,128]{1,0:T(8,128)S(1)}, f32[48,128]{1,0:T(8,128)S(1)}, u32[]{:S(2)}, u32[]{:S(2)}) collective-permute-start(f32[48,128]{1,0:T(8,128)S(1)} %get-tuple-element.45), channel_id=1, source_target_pairs={{0,1},{1,0},{2,3},{3,2},{4,5},{5,4},{6,7},{7,6},{8,9},{9,8},{10,11... | collective-permute-start | bytes 73736 | tf_op jit(solution)/shard_map/ppermute | solution.py:461
  11.7 2.6 %collective-permute-start.4 = (bf16[8,64,128]{2,1,0:T(8,128)(2,1)S(1)}, bf16[8,64,128]{2,1,0:T(8,128)(2,1)S(1)}, u32[]{:S(2)}, u32[]{:S(2)}) collective-permute-start(bf16[8,64,128]{2,1,0:T(8,128)(2,1)S(1)} %convert_element_type.8), channel_id=1, source_target_pairs={{0,4},{4,0},{1,5},{5,1},{2,6},{6,2},{3,7},{7,3},{8,12},{12,8},{9,1... | collective-permute-start | bytes 393224 | tf_op jit(solution)/shard_map/ppermute | solution.py:299
  14.3 2.6 %inner.2 = (f32[3,16,2,32,128]{4,3,2,1,0:T(8,128)S(1)}, bf16[96,64,128]{2,1,0:T(8,128)(2,1)S(1)}, bf16[17,2,96,384]{3,2,1,0:T(8,128)(2,1)S(1)}, bf16[1536,256]{1,0:T(8,128)(2,1)S(1)}) custom-call(s32[96]{0:T(128)S(1)} %pad_add_fusion.source.routes, bf16[32,96,128]{2,1,0:T(8,128)(2,1)S(1)} %get-tuple-element.48.scaled, ...), custom_call_target="tpu_custom_call" | custom-call | flops 570425344 | bytes 4194304 | tf_op jit(solution)/shard_map/inner/pallas_call | solution.py:474
  17.0 3.7 %outer.2 = (f32[3,16,2,32,128]{4,3,2,1,0:T(8,128)S(1)}, bf16[96,64,128]{2,1,0:T(8,128)(2,1)S(1)}, bf16[17,2,96,384]{3,2,1,0:T(8,128)(2,1)S(1)}) custom-call(s32[96]{0:T(128)S(1)} %pad_add_fusion.source.routes, f32[48,128]{1,0:T(8,128)S(1)} %collective-permute-done.2.near_a, ...), custom_call_target="tpu_custom_call", output_to_operand_aliasing={{0}: (5, {}), {1}: (6, {}), {2}: (7, {})} | custom-call | flops 1140850688 | bytes 4194304 | tf_op jit(solution)/shard_map/outer/pallas_call | solution.py:475
  20.8 26.0 %all_to_all.20 = bf16[16,6,64,128]{3,2,1,0:T(8,128)(2,1)S(1)} all-to-all(bf16[16,6,64,128]{3,2,1,0:T(8,128)(2,1)S(1)} %bitcast.27), channel_id=1, replica_groups=mesh['row'=4,'zh'=2,'zl'=2,'x'=2] {'row','zl','x'}, dimensions={0} | all-to-all | bytes 3145728 | tf_op jit(solution)/shard_map/all_to_all | solution.py:454
  46.8 1.0 combine.2
  47.8 0.8 collective-permute-start.5
  48.7 14.2 %collective-permute-done.5.other = bf16[16,64,128]{2,1,0:T(8,128)(2,1)S(1)} collective-permute-done((bf16[16,64,128]{2,1,0:T(8,128)(2,1)S(1)}, bf16[16,64,128]{2,1,0:T(8,128)(2,1)S(1)}, u32[]{:S(2)}, u32[]{:S(2)}) %collective-permute-start.5) | collective-permute-done | bytes 262176 | tf_op jit(solution)/shard_map/ppermute | solution.py:299
  62.9 0.8 reply.2
  63.7 23.3 %all_to_all.21 = bf16[16,6,64,128]{3,2,1,0:T(8,128)(2,1)S(1)} all-to-all(bf16[16,6,64,128]{3,2,1,0:T(8,128)(2,1)S(1)} %bitcast.26), channel_id=1, replica_groups=mesh['row'=4,'zh'=2,'zl'=2,'x'=2] {'row','zl','x'}, dimensions={0} | all-to-all | bytes 3145728 | tf_op jit(solution)/shard_map/all_to_all | solution.py:454
  87.0 1.9 %finish.2 = (bf16[32,96,128]{2,1,0:T(8,128)(2,1)S(1)}, bf16[96,128]{1,0:T(8,128)(2,1)S(1)}, bf16[96,128]{1,0:T(8,128)(2,1)S(1)}, f32[32,128]{1,0:T(8,128)S(1)}, f32[32,128]{1,0:T(8,128)S(1)}) custom-call(s32[96]{0:T(128)S(1)} %pad_add_fusion.source.routes, bf16[96,64,128]{2,1,0:T(8,128)(2,1)S(1)} %bitcast.22, ...), custom_call_target="tpu_custom_call" | custom-call | tf_op jit(solution)/shard_map/finish/pallas_call | solution.py:489
  88.9 0.3 collective-permute-start.6
  89.2 0.7 collective-permute-start.7
  89.9 0.3 collective-permute-done.6.near_a
  90.1 1.4 collective-permute-start.8
  91.5 0.7 collective-permute-start.9
  92.2 2.6 %inner.3 = (f32[3,16,2,32,128]{4,3,2,1,0:T(8,128)S(1)}, bf16[96,64,128]{2,1,0:T(8,128)(2,1)S(1)}, bf16[17,2,96,384]{3,2,1,0:T(8,128)(2,1)S(1)}, bf16[1536,256]{1,0:T(8,128)(2,1)S(1)}) custom-call(s32[96]{0:T(128)S(1)} %pad_add_fusion.source.routes, bf16[32,96,128]{2,1,0:T(8,128)(2,1)S(1)} %get-tuple-element.68.scaled, ...), custom_call_target="tpu_custom_call" | custom-call | flops 570425344 | bytes 4194304 | tf_op jit(solution)/shard_map/inner/pallas_call | solution.py:474
  94.8 3.7 %outer.3 = (f32[3,16,2,32,128]{4,3,2,1,0:T(8,128)S(1)}, bf16[96,64,128]{2,1,0:T(8,128)(2,1)S(1)}, bf16[17,2,96,384]{3,2,1,0:T(8,128)(2,1)S(1)}) custom-call(s32[96]{0:T(128)S(1)} %pad_add_fusion.source.routes, f32[48,128]{1,0:T(8,128)S(1)} %collective-permute-done.8.near_a, ...), custom_call_target="tpu_custom_call", output_to_operand_aliasing={{0}: (5, {}), {1}: (6, {}), {2}: (7, {})} | custom-call | flops 1140850688 | bytes 4194304 | tf_op jit(solution)/shard_map/outer/pallas_call | solution.py:475
  98.5 31.0 %all_to_all.22 = bf16[16,6,64,128]{3,2,1,0:T(8,128)(2,1)S(1)} all-to-all(bf16[16,6,64,128]{3,2,1,0:T(8,128)(2,1)S(1)} %bitcast.28), channel_id=1, replica_groups=mesh['row'=4,'zh'=2,'zl'=2,'x'=2] {'row','zl','x'}, dimensions={0} | all-to-all | bytes 3145728 | tf_op jit(solution)/shard_map/all_to_all | solution.py:454
  129.5 1.0 combine.3
  130.5 0.4 collective-permute-start.10
  130.9 14.6 %collective-permute-done.10.other = bf16[16,64,128]{2,1,0:T(8,128)(2,1)S(1)} collective-permute-done((bf16[16,64,128]{2,1,0:T(8,128)(2,1)S(1)}, bf16[16,64,128]{2,1,0:T(8,128)(2,1)S(1)}, u32[]{:S(2)}, u32[]{:S(2)}) %collective-permute-start.10) | collective-permute-done | bytes 262176 | tf_op jit(solution)/shard_map/ppermute | solution.py:299
  145.5 0.8 reply.3
  146.3 23.2 %all_to_all.23 = bf16[16,6,64,128]{3,2,1,0:T(8,128)(2,1)S(1)} all-to-all(bf16[16,6,64,128]{3,2,1,0:T(8,128)(2,1)S(1)} %bitcast.23), channel_id=1, replica_groups=mesh['row'=4,'zh'=2,'zl'=2,'x'=2] {'row','zl','x'}, dimensions={0} | all-to-all | bytes 3145728 | tf_op jit(solution)/shard_map/all_to_all | solution.py:454
  169.5 2.6 %finish.3 = f32[32,96,128]{2,1,0:T(8,128)} custom-call(s32[96]{0:T(128)S(1)} %pad_add_fusion.source.routes, bf16[96,64,128]{2,1,0:T(8,128)(2,1)S(1)} %bitcast.29, f32[3,16,2,32,128]{4,3,2,1,0:T(8,128)S(1)} %get-tuple-element.76.pulled, bf16[32,96,128]{2,1,0:T(8,128)(2,1)S(1)} %copy-done.2, bf16[32,96,128]{2,1,0:T(8,128)(2,1)S(1)} %copy-done.1, ...), custom_call_target="tpu_custom_call" | custom-call | tf_op jit(solution)/shard_map/finish/pallas_call | solution.py:489
  (49 shorter events, 1.3 us)
Async XLA Ops:
  0.0 3.0 %copy-start.5 = (s32[4,24,16]{1,2,0:T(8,128)S(1)}, s32[4,24,16]{1,2,0:T(8,128)}, u32[]{:S(2)}) copy-start(s32[4,24,16]{1,2,0:T(8,128)} %param.14) | copy-start | bytes 18436
  0.0 3.2 %copy-start.6 = (s32[256]{0:T(256)S(1)}, s32[256]{0:T(256)}, u32[]{:S(2)}) copy-start(s32[256]{0:T(256)} %param.16) | copy-start | bytes 3076
  0.0 3.8 %copy-start.7 = (s32[1,3,16]{2,0,1:T(1,128)S(1)}, s32[1,3,16]{2,0,1:T(1,128)}, u32[]{:S(2)}) copy-start(s32[1,3,16]{2,0,1:T(1,128)} %param.15) | copy-start | bytes 580
  0.0 3.9 %copy-start.8 = (s32[8]{0:T(128)S(1)}, s32[8]{0:T(128)}, u32[]{:S(2)}) copy-start(s32[8]{0:T(128)} %param.17) | copy-start | bytes 100
  0.0 5.3 %copy-start.3 = (f32[8,64,128]{2,1,0:T(8,128)S(1)}, f32[8,64,128]{2,1,0:T(8,128)}, u32[]{:S(2)}) copy-start(f32[8,64,128]{2,1,0:T(8,128)} %own_weight.3) | copy-start | bytes 786436
  1.7 3.6 %collective-permute-start = (bf16[96,128]{1,0:T(8,128)(2,1)S(1)}, bf16[96,128]{1,0:T(8,128)(2,1)S(1)}, u32[]{:S(2)}, u32[]{:S(2)}) collective-permute-start(bf16[96,128]{1,0:T(8,128)(2,1)S(1)} %get-tuple-element.41), channel_id=1, source_target_pairs={{0,8},{8,0},{16,24},{24,16},{1,9},{9,1},{17,25},{25,17},{2,10},{10... | collective-permute-start | bytes 73736 | tf_op jit(solution)/shard_map/ppermute | solution.py:461
  2.3 3.1 %collective-permute-start.1 = (bf16[96,128]{1,0:T(8,128)(2,1)S(1)}, bf16[96,128]{1,0:T(8,128)(2,1)S(1)}, u32[]{:S(2)}, u32[]{:S(2)}) collective-permute-start(bf16[96,128]{1,0:T(8,128)(2,1)S(1)} %get-tuple-element.42), channel_id=1, source_target_pairs={{8,16},{16,8},{9,17},{17,9},{10,18},{18,10},{11,19},{19,11},{12,20... | collective-permute-start | bytes 73736 | tf_op jit(solution)/shard_map/ppermute | solution.py:461
  5.4 8.9 %copy-start = (bf16[8,4,64,1024]{3,2,1,0:T(8,128)(2,1)S(1)}, bf16[8,4,64,1024]{3,2,1,0:T(8,128)(2,1)}, u32[]{:S(2)}) copy-start(bf16[8,4,64,1024]{3,2,1,0:T(8,128)(2,1)} %param.12) | copy-start | bytes 12582916
  5.4 8.9 %copy-start.4 = (bf16[3,3,128,128]{3,2,1,0:T(8,128)(2,1)S(1)}, bf16[3,3,128,128]{3,2,1,0:T(8,128)(2,1)}, u32[]{:S(2)}) copy-start(bf16[3,3,128,128]{3,2,1,0:T(8,128)(2,1)} %kernel.3) | copy-start | bytes 884740
  5.4 11.5 %collective-permute-start.3 = (f32[48,128]{1,0:T(8,128)S(1)}, f32[48,128]{1,0:T(8,128)S(1)}, u32[]{:S(2)}, u32[]{:S(2)}) collective-permute-start(f32[48,128]{1,0:T(8,128)S(1)} %get-tuple-element.47), channel_id=1, source_target_pairs={{1,2},{2,1},{3,4},{4,3},{5,6},{6,5},{9,10},{10,9},{11,12},{12,11},... | collective-permute-start | bytes 73736 | tf_op jit(solution)/shard_map/ppermute | solution.py:461
  6.2 10.7 %collective-permute-start.2 = (f32[48,128]{1,0:T(8,128)S(1)}, f32[48,128]{1,0:T(8,128)S(1)}, u32[]{:S(2)}, u32[]{:S(2)}) collective-permute-start(f32[48,128]{1,0:T(8,128)S(1)} %get-tuple-element.45), channel_id=1, source_target_pairs={{0,1},{1,0},{2,3},{3,2},{4,5},{5,4},{6,7},{7,6},{8,9},{9,8},{10,11... | collective-permute-start | bytes 73736 | tf_op jit(solution)/shard_map/ppermute | solution.py:461
  11.7 9.1 %collective-permute-start.4 = (bf16[8,64,128]{2,1,0:T(8,128)(2,1)S(1)}, bf16[8,64,128]{2,1,0:T(8,128)(2,1)S(1)}, u32[]{:S(2)}, u32[]{:S(2)}) collective-permute-start(bf16[8,64,128]{2,1,0:T(8,128)(2,1)S(1)} %convert_element_type.8), channel_id=1, source_target_pairs={{0,4},{4,0},{1,5},{5,1},{2,6},{6,2},{3,7},{7,3},{8,12},{12,8},{9,1... | collective-permute-start | bytes 393224 | tf_op jit(solution)/shard_map/ppermute | solution.py:299
  47.8 15.0 %collective-permute-start.5 = (bf16[16,64,128]{2,1,0:T(8,128)(2,1)S(1)}, bf16[16,64,128]{2,1,0:T(8,128)(2,1)S(1)}, u32[]{:S(2)}, u32[]{:S(2)}) collective-permute-start(bf16[16,64,128]{2,1,0:T(8,128)(2,1)S(1)} %get-tuple-element.59), channel_id=1, source_target_pairs={{0,4},{4,0},{1,5},{5,1},{2,6},{6,2},{3,7},{7,3},{8,12},{12,8},{9,1... | collective-permute-start | bytes 786440 | tf_op jit(solution)/shard_map/ppermute | solution.py:299
  63.7 23.3 %copy-start.1 = (bf16[32,96,128]{2,1,0:T(8,128)(2,1)S(1)}, bf16[32,96,128]{2,1,0:T(8,128)(2,1)}, u32[]{:S(2)}) copy-start(bf16[32,96,128]{2,1,0:T(8,128)(2,1)} %state.5) | copy-start | bytes 2359300
  63.7 23.3 %copy-start.2 = (bf16[32,96,128]{2,1,0:T(8,128)(2,1)S(1)}, bf16[32,96,128]{2,1,0:T(8,128)(2,1)}, u32[]{:S(2)}) copy-start(bf16[32,96,128]{2,1,0:T(8,128)(2,1)} %grad.5) | copy-start | bytes 2359300
  88.9 1.3 collective-permute-start.6
  89.2 0.9 collective-permute-start.7
  90.1 4.7 %collective-permute-start.8 = (f32[48,128]{1,0:T(8,128)S(1)}, f32[48,128]{1,0:T(8,128)S(1)}, u32[]{:S(2)}, u32[]{:S(2)}) collective-permute-start(f32[48,128]{1,0:T(8,128)S(1)} %get-tuple-element.66), channel_id=1, source_target_pairs={{0,1},{1,0},{2,3},{3,2},{4,5},{5,4},{6,7},{7,6},{8,9},{9,8},{10,11... | collective-permute-start | bytes 73736 | tf_op jit(solution)/shard_map/ppermute | solution.py:461
  91.5 3.3 %collective-permute-start.9 = (f32[48,128]{1,0:T(8,128)S(1)}, f32[48,128]{1,0:T(8,128)S(1)}, u32[]{:S(2)}, u32[]{:S(2)}) collective-permute-start(f32[48,128]{1,0:T(8,128)S(1)} %get-tuple-element.67), channel_id=1, source_target_pairs={{1,2},{2,1},{3,4},{4,3},{5,6},{6,5},{9,10},{10,9},{11,12},{12,11},... | collective-permute-start | bytes 73736 | tf_op jit(solution)/shard_map/ppermute | solution.py:461
  130.5 15.0 %collective-permute-start.10 = (bf16[16,64,128]{2,1,0:T(8,128)(2,1)S(1)}, bf16[16,64,128]{2,1,0:T(8,128)(2,1)S(1)}, u32[]{:S(2)}, u32[]{:S(2)}) collective-permute-start(bf16[16,64,128]{2,1,0:T(8,128)(2,1)S(1)} %get-tuple-element.75), channel_id=1, source_target_pairs={{0,4},{4,0},{1,5},{5,1},{2,6},{6,2},{3,7},{7,3},{8,12},{12,8},{9,1... | collective-permute-start | bytes 786440 | tf_op jit(solution)/shard_map/ppermute | solution.py:299
